TPU v7x, 512 devices: a whole 4x8x8 slice. The times are simulated.
512 devices in a mesh: dp: 16 (over x_hi, y), ctx: 32 (over z, x_lo, core).
Axes of the slice: x: 4 (x_hi: 2, x_lo: 2; x = x_hi * 2 + x_lo), y: 8, z: 8, core: 2. Of those that a mesh axis runs over, the one named last changes fastest.
Arguments:
- tokens: bfloat16 [16, 4096, 8192], P('dp', 'ctx')
- qkv_weight: bfloat16 [8192, 384], P('dp')
- out_grad: bfloat16 [16, 4096, 128], P('dp', 'ctx'), may hold values from -0.0625 to 0.0625
Outputs:
- attn_out: bfloat16 [16, 4096, 128], P('dp', 'ctx')
- qkv_grad: bfloat16 [8192, 384], P('dp')
All inputs are finite; a program needn't handle non-finite values.
Results may differ from a plain program's by a relative error of at most 0.03.
Values may be sent and summed in bfloat16 or wider, within the bound.
No kernel may reach another device: no remote copies, remote signals or barrier semaphores. Data moves between devices by JAX's collectives and lax.ppermute only.
A program may use at most 64 MiB of HBM per device.

v0:
```python
import math

import jax
import jax.numpy as jnp
from jax import lax
from jax.sharding import PartitionSpec as P

z_weight = 0.001
masked_fill = -1e30


def stored_positions(first_row, number, half_rows, ctx_count):
    indices = first_row + jnp.arange(number, dtype=jnp.int32)
    device_index = indices // (2 * half_rows)
    inside = indices % (2 * half_rows)
    block_index = jnp.where(inside < half_rows, device_index, 2 * ctx_count - 1 - device_index)
    return block_index * half_rows + inside % half_rows


def contract_last(left, right):
    return lax.dot_general(
        left, right, (((1,), (1,)), ((), ())), preferred_element_type=jnp.float32
    )


def contract_first(left, right):
    return lax.dot_general(
        left, right, (((0,), (0,)), ((), ())), preferred_element_type=jnp.float32
    )


def on_device(tokens, qkv_weight, out_grad):
    ctx_count = lax.axis_size("ctx")
    feature_rows = tokens[0]
    cotangent = out_grad[0]
    row_count = feature_rows.shape[0]
    half_rows = row_count // 2
    width = qkv_weight.shape[1]
    head_size = width // 3
    score_scale = 1.0 / math.sqrt(head_size)
    columns = lax.all_to_all(tokens, "dp", split_axis=2, concat_axis=0, tiled=True)
    flat_columns = columns.reshape(-1, columns.shape[2])
    projected = jnp.dot(
        feature_rows,
        lax.all_gather(qkv_weight, "dp", axis=0, tiled=True),
        preferred_element_type=jnp.float32,
    )
    qkv = projected.astype(jnp.bfloat16)
    queries = qkv[:, :head_size]
    own_pairs = qkv[:, head_size:]
    gathered = lax.all_gather(own_pairs, "ctx", axis=0, tiled=True)
    key_rows = gathered[:, :head_size]
    value_rows = gathered[:, head_size:]
    own_positions = stored_positions(
        lax.axis_index("ctx") * row_count, row_count, half_rows, ctx_count
    )
    all_positions = stored_positions(0, row_count * ctx_count, half_rows, ctx_count)
    allowed = all_positions[None, :] <= own_positions[:, None]
    scores = jnp.where(allowed, contract_last(queries, key_rows) * score_scale, masked_fill)
    row_top = jnp.max(scores, axis=1)
    log_total = row_top + jnp.log(jnp.sum(jnp.exp(scores - row_top[:, None]), axis=1))
    probs = jnp.where(allowed, jnp.exp(scores - log_total[:, None]), 0.0)
    probs_low = probs.astype(jnp.bfloat16)
    attn_rows = jnp.dot(probs_low, value_rows, preferred_element_type=jnp.float32).astype(
        jnp.bfloat16
    )
    row_delta = jnp.sum(cotangent.astype(jnp.float32) * attn_rows.astype(jnp.float32), axis=1)
    dprob = contract_last(cotangent, value_rows)
    dscore = probs * (dprob - row_delta[:, None] + 2.0 * z_weight * log_total[:, None])
    dscore_low = dscore.astype(jnp.bfloat16)
    grad_query = (
        jnp.dot(dscore_low, key_rows, preferred_element_type=jnp.float32) * score_scale
    ).astype(jnp.bfloat16)
    query_all, cotangent_all = (
        lax.all_gather(queries, "ctx", axis=0, tiled=True),
        lax.all_gather(cotangent, "ctx", axis=0, tiled=True),
    )
    total_all, delta_all = (
        lax.all_gather(log_total, "ctx", axis=0, tiled=True),
        lax.all_gather(row_delta, "ctx", axis=0, tiled=True),
    )
    own_keys = own_pairs[:, :head_size]
    own_values = own_pairs[:, head_size:]
    allowed_back = own_positions[None, :] <= all_positions[:, None]
    scores_back = jnp.where(
        allowed_back, contract_last(query_all, own_keys) * score_scale, masked_fill
    )
    probs_back = jnp.where(allowed_back, jnp.exp(scores_back - total_all[:, None]), 0.0)
    dprob_back = contract_last(cotangent_all, own_values)
    dscore_back = probs_back * (
        dprob_back - delta_all[:, None] + 2.0 * z_weight * total_all[:, None]
    )
    grad_key = (contract_first(dscore_back.astype(jnp.bfloat16), query_all) * score_scale).astype(
        jnp.bfloat16
    )
    grad_value = contract_first(probs_back.astype(jnp.bfloat16), cotangent_all).astype(jnp.bfloat16)
    grad_rows = jnp.concatenate([grad_query, grad_key, grad_value], axis=1)
    partial_sum = contract_first(flat_columns, lax.all_gather(grad_rows, "dp", axis=0, tiled=True))
    weight_total = lax.psum(partial_sum.astype(jnp.bfloat16), "ctx")
    return (attn_rows[None], weight_total)


def solution(mesh):
    placed = (P("dp", "ctx", None), P("dp", None), P("dp", "ctx", None))
    return jax.shard_map(
        on_device,
        mesh=mesh,
        in_specs=placed,
        out_specs=(P("dp", "ctx", None), P("dp", None)),
        check_vma=False,
    )
```

profile of v0, /device:TPU:1, one launch (start us, length us, event | category | flops | bytes accessed | tf_op | source)
XLA Modules:
  0.0 672.0 jit_solution(11417274959753456730)
XLA Ops:
  7.2 0.0 all-gather.9.cloned.1.call-start
  7.2 0.7 all-gather.9.cloned.1.call-update
  7.9 0.0 copy-start
  7.9 0.0 all-gather.11.cloned.1.call-start
  8.0 128.5 %all-gather.9.cloned.1.call-done = bf16[8192,384]{1,0:T(8,128)(2,1)} async-done(((bf16[512,384]{1,0:T(8,128)(2,1)}), bf16[8192,384]{1,0:T(8,128)(2,1)}) %all-gather.9.cloned.1.call-update) | async-done | bytes 6291472 | tf_op jit(solution)/shard_map/all_gather | solution.py:45
  136.5 4.7 fusion.19
  141.2 0.6 slice.27
  141.8 0.0 all-gather.11.cloned.1.call-update
  141.8 0.0 all-gather.13.cloned.1.call-start
  141.9 0.6 slice.26
  142.5 0.1 all-gather.13.cloned.1.call-update
  142.6 0.0 all-gather.17.cloned.1.call-start
  142.6 0.5 all-gather.17.cloned.1.call-update
  143.2 0.0 copy-done
  143.2 6.8 %copy.21 = bf16[1,128,8192]{1,0,2:T(2,128)(2,1)} copy(bf16[1,128,8192]{2,1,0:T(8,128)(2,1)S(1)} %copy-done) | data formatting | bytes 4194304 | tf_op args[0]
  150.0 0.6 broadcast.369
  150.6 45.2 %reduce = bf16[8192,128]{1,0:T(8,128)(2,1)S(1)} reduce(bf16[8192,1,128]{2,1,0:T(2,128)(2,1)} %bitcast.59, bf16[]{:T(256)} %broadcast.369), dimensions={1}, to_apply=%bitcast.52.reduce_sub_computation | reduce | bytes 4194306
  195.8 2.1 reshape.196
  197.8 0.0 copy-start.3
  197.8 4.8 all-to-all-start
  202.7 0.0 all-gather.15.cloned.1.call-start
  202.7 0.0 copy-done.3
  202.8 0.1 copy.18
  202.9 5.9 all-gather.11.cloned.1.call-done
  208.8 0.0 copy-start.4
  208.8 1.9 fusion.69
  210.7 0.0 copy-start.2
  210.7 0.4 exponential_reduce_fusion
  211.1 0.0 copy-done.4
  211.2 0.7 multiply_reduce_fusion
  211.9 0.1 copy-done.2
  212.0 32.2 %all-gather.2 = f32[32,1,128]{2,1,0:T(1,128)S(1)} all-gather(f32[1,1,128]{2,1,0:T(1,128)S(1)} %bitcast.68), channel_id=1, replica_groups=mesh['dp'=16,'ctx'=32] {'ctx'}, dimensions={0}, use_global_device_ids=true | all-gather | bytes 16896 | tf_op jit(solution)/shard_map/all_gather | solution.py:80
  244.2 30.6 %all-gather.1 = f32[32,1,128]{2,1,0:T(1,128)S(1)} all-gather(f32[1,1,128]{2,1,0:T(1,128)S(1)} %bitcast.67), channel_id=1, replica_groups=mesh['dp'=16,'ctx'=32] {'ctx'}, dimensions={0}, use_global_device_ids=true | all-gather | bytes 16896 | tf_op jit(solution)/shard_map/all_gather | solution.py:79
  274.8 2.8 all-gather.13.cloned.1.call-done
  277.6 3.3 fusion.6
  280.9 68.5 %all-gather.17.cloned.1.call-done = bf16[1,4096,128]{2,1,0:T(8,128)(2,1)} async-done(((bf16[1,128,128]{2,1,0:T(8,128)(2,1)}), bf16[1,4096,128]{2,1,0:T(8,128)(2,1)}) %all-gather.17.cloned.1.call-update) | async-done | bytes 1048592 | tf_op jit(solution)/shard_map/all_gather | solution.py:76
  349.4 0.0 copy-start.1
  349.4 2.4 convolution_convert_fusion.1
  351.8 0.0 copy-done.1
  351.8 3.5 fusion.24
  355.4 3.2 fusion.25
  358.5 0.6 pad_maximum_fusion
  359.2 0.0 all-gather.15.cloned.1.call-update
  359.2 0.0 all-reduce.2.cloned.1.call-start
  359.3 0.0 all-to-all-done
  359.3 6.7 %reshape.197 = bf16[8192,1,128]{2,1,0:T(2,128)(2,1)} reshape(bf16[16,2,32768]{2,1,0:T(2,128)(2,1)S(1)} %all-to-all-done) | data formatting | bytes 4194304
  366.0 2.5 copy.27
  368.5 2.6 copy.22
  371.1 69.1 %all-gather.15.cloned.1.call-done = bf16[2048,384]{0,1:T(8,128)(2,1)} async-done(((bf16[128,384]{0,1:T(8,128)(2,1)}), bf16[2048,384]{0,1:T(8,128)(2,1)}) %all-gather.15.cloned.1.call-update) | async-done | bytes 1572880 | tf_op jit(solution)/shard_map/all_gather | solution.py:98
  440.2 3.8 fusion.18
  444.0 0.0 all-reduce.2.cloned.1.call-update
  444.0 0.7 copy.23
  444.7 218.5 %all-reduce.2.cloned.1.call-done = bf16[512,384]{0,1:T(8,128)(2,1)} async-done(((bf16[512,384]{0,1:T(8,128)(2,1)}), bf16[512,384]{0,1:T(8,128)(2,1)}) %all-reduce.2.cloned.1.call-update) | async-done | bytes 393232 | tf_op jit(solution)/shard_map/psum | solution.py:99
  663.2 1.9 copy.24
  (4 shorter events, 0.0 us)
Async XLA Ops:
  7.2 129.3 %all-gather.9.cloned.1.call-start = ((), (), s32[]{:S(2)}) async-start(), calls=%async_computation.1 | async-start | bytes 6684672 | tf_op jit(solution)/shard_map/all_gather | solution.py:45
  7.9 135.3 %copy-start = (bf16[1,128,8192]{2,1,0:T(8,128)(2,1)S(1)}, bf16[1,128,8192]{2,1,0:T(8,128)(2,1)}, u32[]{:S(2)}) copy-start(bf16[1,128,8192]{2,1,0:T(8,128)(2,1)} %param.3) | copy-start | bytes 6291460
  7.9 200.9 %all-gather.11.cloned.1.call-start = ((), (), s32[]{:S(2)}) async-start(), calls=%async_computation.2 | async-start | bytes 2162688 | tf_op jit(solution)/shard_map/all_gather | solution.py:51
  141.8 135.8 %all-gather.13.cloned.1.call-start = ((), (), s32[]{:S(2)}) async-start(), calls=%async_computation.3 | async-start | bytes 1081344 | tf_op jit(solution)/shard_map/all_gather | solution.py:75
  142.6 206.8 %all-gather.17.cloned.1.call-start = ((), (), s32[]{:S(2)}) async-start(), calls=%async_computation.6 | async-start | bytes 1081344 | tf_op jit(solution)/shard_map/all_gather | solution.py:76
  197.8 4.9 copy-start.3
  197.8 161.4 %all-to-all-start = ((bf16[16,2,32768]{2,1,0:T(2,128)(2,1)}), bf16[16,2,32768]{2,1,0:T(2,128)(2,1)S(1)}, u32[]{:S(2)}, u32[]{:S(2)}) async-start(bf16[16,2,32768]{2,1,0:T(2,128)(2,1)} %reshape.196), calls=%async_computation | async-start | bytes 4194304 | tf_op jit(solution)/shard_map/all_to_all | solution.py:41
  202.7 237.5 %all-gather.15.cloned.1.call-start = ((), (), s32[]{:S(2)}) async-start(), calls=%async_computation.4 | async-start | bytes 1671168 | tf_op jit(solution)/shard_map/all_gather | solution.py:98
  208.8 2.4 copy-start.4
  210.7 1.3 copy-start.2
  349.4 2.4 copy-start.1
  359.2 304.0 %all-reduce.2.cloned.1.call-start = ((), (), s32[]{:S(2)}) async-start(), calls=%async_computation.5 | async-start | bytes 786432 | tf_op jit(solution)/shard_map/psum | solution.py:99
Sparse Core Ops, SparseCore 0:
  11.2 125.2 all-gather.8
  142.0 66.7 all-gather.10
  211.5 66.0 all-gather.12
  279.6 69.7 all-gather.16
  359.3 80.8 all-gather.14
  444.1 219.0 all-reduce.1
where the time goes:
time: 672 us
  waiting for transfers between devices  495 us (74%)
  blocking collectives  62.8 us (9%)
  other arithmetic  46.4 us (7%)
  local copies, waits for them, and re-layouts  25.4 us (4%)
  matrix products  23.5 us (3%)
  between operations  14.2 us (2%)
    psum x1, waiting for transfers between devices, on_device(): weight_total = lax.psum(partial_sum.astype(jnp.bfloat16), 'ctx')  219 us
    all_gather x1, waiting for transfers between devices, on_device(): lax.all_gather(qkv_weight, 'dp', axis=0, tiled=True)  129 us
    all_gather x1, waiting for transfers between devices, on_device(): lax.all_gather(grad_rows, 'dp', axis=0, tiled=True)  69.1 us
    all_gather x1, waiting for transfers between devices, on_device(): lax.all_gather(cotangent, 'ctx', axis=0, tiled=True)  68.5 us
    unnamed x1, other arithmetic  45.2 us
    all_gather x1, blocking collectives, on_device(): lax.all_gather(row_delta, 'ctx', axis=0, tiled=True)  32.2 us
    all_gather x1, blocking collectives, on_device(): lax.all_gather(log_total, 'ctx', axis=0, tiled=True)  30.6 us
    unnamed x18, local copies, waits for them, and re-layouts  21.5 us
  transfers between devices with their start and end apart: 7, of which 6 were waited for; matrix products, arithmetic and copies ran while one was open for 13% of the time, Pallas kernels for 0%

commit v1 on v0

v1 whole, which is shorter than its diff:
```python
import math

import jax
import jax.numpy as jnp
from jax import lax
from jax.sharding import Mesh, PartitionSpec as P

z_weight = 0.001
masked_fill = -1e30
low = jnp.bfloat16
ctx_axes = ("z", "xl", "core")


def contract_last(left, right):
    return lax.dot_general(
        left, right, (((1,), (1,)), ((), ())), preferred_element_type=jnp.float32
    )


def contract_first(left, right):
    return lax.dot_general(
        left, right, (((0,), (0,)), ((), ())), preferred_element_type=jnp.float32
    )


def exchange(blocks, axes):
    return lax.all_to_all(blocks, axes, split_axis=0, concat_axis=0, tiled=True)


def spread(block, axes, count):
    return exchange(jnp.broadcast_to(block[None], (count,) + block.shape), axes)


def swap(block, axis):
    return lax.ppermute(block, axis, ((0, 1), (1, 0)))


def gather_rows(block):
    along_z = spread(block, "z", lax.axis_size("z"))
    along_x = jnp.stack([along_z, swap(along_z, "xl")])
    return jnp.stack([along_x, swap(along_x, "core")])


def positions_of(device, inside, half_rows, ctx_count):
    block = jnp.where(inside < half_rows, device, 2 * ctx_count - 1 - device)
    return block * half_rows + inside % half_rows


def on_device(tokens, qkv_weight, out_grad):
    y_count, z_count = lax.axis_size("y"), lax.axis_size("z")
    ctx_count = z_count * 4
    row_count, width = tokens.shape[1], qkv_weight.shape[1]
    shard, head_size = qkv_weight.shape[0], qkv_weight.shape[1] // 3
    half_rows = row_count // 2
    score_scale = 1.0 / math.sqrt(head_size)
    cotangent = out_grad[0]
    x_hi, z_at, x_lo, core = (lax.axis_index(a) for a in ("xh", "z", "xl", "core"))

    other_weight = swap(qkv_weight, "xh")
    first = x_hi == 0
    weight = jnp.concatenate(
        [jnp.where(first, qkv_weight, other_weight), jnp.where(first, other_weight, qkv_weight)]
    )
    split = tokens[0].reshape(row_count, 2, y_count, shard).transpose(2, 0, 1, 3)
    columns = exchange(split.reshape(y_count, row_count, 2 * shard), "y")
    columns = columns.reshape(y_count * row_count, 2 * shard)
    partial_qkv = jnp.dot(columns, weight, preferred_element_type=jnp.float32).astype(low)
    parts = exchange(partial_qkv.reshape(y_count, row_count, width), "y")
    qkv = jnp.sum(parts.astype(jnp.float32), axis=0).astype(low)
    queries, own_keys, own_values = (
        qkv[:, :head_size],
        qkv[:, head_size : 2 * head_size],
        qkv[:, 2 * head_size :],
    )

    gathered = gather_rows(jnp.concatenate([qkv, cotangent], axis=1))
    gathered = gathered.reshape(ctx_count * row_count, 4 * head_size)
    query_all = gathered[:, :head_size]
    key_rows = gathered[:, head_size : 2 * head_size]
    value_rows = gathered[:, 2 * head_size : 3 * head_size]
    cotangent_all = gathered[:, 3 * head_size :]

    own_positions = positions_of(
        z_at * 4 + x_lo * 2 + core, jnp.arange(row_count, dtype=jnp.int32), half_rows, ctx_count
    )
    index = jnp.arange(row_count * ctx_count, dtype=jnp.int32)
    inside, block = index % row_count, index // row_count
    device = (
        (block % z_count) * 4
        + ((block // z_count) % 2 ^ x_lo) * 2
        + (block // (2 * z_count) ^ core)
    )
    all_positions = positions_of(device, inside, half_rows, ctx_count)

    allowed = all_positions[None, :] <= own_positions[:, None]
    scores = jnp.where(allowed, contract_last(queries, key_rows) * score_scale, masked_fill)
    row_top = jnp.max(scores, axis=1)
    log_total = row_top + jnp.log(jnp.sum(jnp.exp(scores - row_top[:, None]), axis=1))
    probs = jnp.where(allowed, jnp.exp(scores - log_total[:, None]), 0.0)
    attn_rows = jnp.dot(probs.astype(low), value_rows, preferred_element_type=jnp.float32)
    attn_rows = attn_rows.astype(low)
    row_delta = jnp.sum(cotangent.astype(jnp.float32) * attn_rows.astype(jnp.float32), axis=1)

    stats = spread(jnp.stack([log_total, row_delta]), ctx_axes, ctx_count)
    stats = stats.reshape(z_count, 2, 2, 2, row_count)
    stats = jnp.where(x_lo == 1, stats[:, ::-1], stats)
    stats = jnp.where(core == 1, stats[:, :, ::-1], stats)
    stats = stats.transpose(3, 2, 1, 0, 4).reshape(2, ctx_count * row_count)
    total_all, delta_all = stats[0], stats[1]

    dprob = contract_last(cotangent, value_rows)
    dscore = probs * (dprob - row_delta[:, None] + 2.0 * z_weight * log_total[:, None])
    grad_query = jnp.dot(dscore.astype(low), key_rows, preferred_element_type=jnp.float32)
    grad_query = (grad_query * score_scale).astype(low)

    allowed_back = own_positions[:, None] <= all_positions[None, :]
    scores_back = jnp.where(
        allowed_back, contract_last(own_keys, query_all) * score_scale, masked_fill
    )
    probs_back = jnp.where(allowed_back, jnp.exp(scores_back - total_all[None, :]), 0.0)
    dprob_back = contract_last(own_values, cotangent_all)
    dscore_back = probs_back * (
        dprob_back - delta_all[None, :] + 2.0 * z_weight * total_all[None, :]
    )
    grad_key = jnp.dot(dscore_back.astype(low), query_all, preferred_element_type=jnp.float32)
    grad_key = (grad_key * score_scale).astype(low)
    grad_value = jnp.dot(
        probs_back.astype(low), cotangent_all, preferred_element_type=jnp.float32
    ).astype(low)
    grad_rows = jnp.concatenate([grad_query, grad_key, grad_value], axis=1)

    grad_all = spread(grad_rows, "y", y_count).reshape(y_count * row_count, width)
    partial_sum = contract_first(columns, grad_all).astype(low)
    pieces = exchange(
        partial_sum.reshape(2 * ctx_count, shard // ctx_count, width), ("xh",) + ctx_axes
    )
    own_piece = jnp.sum(pieces.astype(jnp.float32), axis=0).astype(low)
    weight_total = spread(own_piece, ctx_axes, ctx_count).reshape(shard, width)
    return (attn_rows[None], weight_total)


def solution(mesh):
    grid = Mesh(mesh.devices.reshape(2, 8, 8, 2, 2), ("xh", "y") + ctx_axes)
    rows, weights = P(("xh", "y"), ctx_axes, None), P(("xh", "y"), None)
    return jax.shard_map(
        on_device,
        mesh=grid,
        in_specs=(rows, weights, rows),
        out_specs=(rows, weights),
        check_vma=False,
    )
```

time: 672 us -> 265 us (0.39)
  waiting for transfers between devices: 495 us -> 110 us
  other arithmetic: 46.4 us -> 5.22 us
  starting transfers between devices: 5.08 us -> 38.9 us
  blocking collectives: 62.8 us -> 83.3 us
  between operations: 14.2 us -> 0.93 us
  local copies, waits for them, and re-layouts: 25.4 us -> 12.3 us
  matrix products: 23.5 us -> 13.4 us
    all_gather x5 -> x0, waiting for transfers between devices: 275 us -> none  [the longest x1 129 us: on_device(): lax.all_gather(qkv_weight, 'dp', axis=0, tiled=True)]
    psum x1 -> x0, waiting for transfers between devices: 219 us -> none  [on_device(): weight_total = lax.psum(partial_sum.astype(jnp.bfloat16), 'ctx')]
    all_to_all x0 -> x3, blocking collectives: none -> 83.3 us  [exchange(): return lax.all_to_all(blocks, axes, split_axis=0, concat_axis=0, tiled=True)]
    all_to_all x1 -> x4, waiting for transfers between devices: 0.01 us -> 80.7 us  [exchange(): return lax.all_to_all(blocks, axes, split_axis=0, concat_axis=0, tiled=True)]
    all_gather x2 -> x0, blocking collectives: 62.8 us -> none  [the longest x1 32.2 us: on_device(): lax.all_gather(row_delta, 'ctx', axis=0, tiled=True)]
    unnamed x1 -> x0, other arithmetic: 45.2 us -> none
    ppermute x0 -> x3, waiting for transfers between devices: none -> 29.7 us  [swap(): return lax.ppermute(block, axis, ((0, 1), (1, 0)))]
    all_to_all x1 -> x4, starting transfers between devices: 4.83 us -> 23.1 us  [exchange(): return lax.all_to_all(blocks, axes, split_axis=0, concat_axis=0, tiled=True)]
  transfers between devices with their start and end apart: 7 -> 7, of which waited for: 6 -> 7; matrix products, arithmetic and copies ran while one was open for 13% -> 2% of each run, Pallas kernels for 0% -> 0%
where the time goes in v1:
time: 265 us
  waiting for transfers between devices  110 us (42%)
  blocking collectives  83.3 us (31%)
  starting transfers between devices  38.9 us (15%)
  matrix products  13.4 us (5%)
  local copies, waits for them, and re-layouts  12.3 us (5%)
  other arithmetic  5.22 us (2%)
    all_to_all x3, blocking collectives, exchange(): return lax.all_to_all(blocks, axes, split_axis=0, concat_axis=0, tiled=True)  83.3 us
    all_to_all x4, waiting for transfers between devices, exchange(): return lax.all_to_all(blocks, axes, split_axis=0, concat_axis=0, tiled=True)  80.7 us
    ppermute x3, waiting for transfers between devices, swap(): return lax.ppermute(block, axis, ((0, 1), (1, 0)))  29.7 us
    all_to_all x4, starting transfers between devices, exchange(): return lax.all_to_all(blocks, axes, split_axis=0, concat_axis=0, tiled=True)  23.1 us
    ppermute x3, starting transfers between devices, swap(): return lax.ppermute(block, axis, ((0, 1), (1, 0)))  15.8 us
  transfers between devices with their start and end apart: 7, of which 7 were waited for; matrix products, arithmetic and copies ran while one was open for 2% of the time, Pallas kernels for 0%

profile of v1, /device:TPU:1, one launch (start us, length us, event | category | flops | bytes accessed | tf_op | source)
XLA Modules:
  0.0 264.5 jit_solution(2419594278557387679)
XLA Ops:
  0.6 2.4 copy.36
  3.1 1.6 copy.39
  4.7 2.7 %reshape.175 = bf16[8,128,1024]{2,1,0:T(8,128)(2,1)} reshape(bf16[8,128,2,512]{3,2,1,0:T(2,128)(2,1)S(1)} %bitcast.63) | data formatting | bytes 4194304 | tf_op jit(solution)/shard_map/reshape | solution.py:65
  7.4 0.0 copy-start.3
  7.4 7.8 %all-to-all-start = ((bf16[8,128,1024]{2,1,0:T(8,128)(2,1)}), bf16[8,128,1024]{2,1,0:T(8,128)(2,1)S(1)}, u32[]{:S(2)}, u32[]{:S(2)}) async-start(bf16[8,128,1024]{2,1,0:T(8,128)(2,1)} %reshape.175), calls=%async_computation | async-start | bytes 4194304 | tf_op jit(solution)/shard_map/all_to_all | solution.py:27
  15.2 0.0 copy-done.3
  15.2 4.7 %collective-permute-start = (bf16[512,384]{1,0:T(8,128)(2,1)S(1)}, bf16[512,384]{1,0:T(8,128)(2,1)S(1)}, u32[]{:S(2)}, u32[]{:S(2)}) collective-permute-start(bf16[512,384]{1,0:T(8,128)(2,1)S(1)} %copy-done.3), channel_id=1, source_target_pairs={{0,256},{256,0},{1,257},{257,1},{2,258},{258,2},{3,259},{259,3},{4... | collective-permute-start | bytes 1179656 | tf_op jit(solution)/shard_map/ppermute | solution.py:35
  19.8 7.4 %collective-permute-done = bf16[512,384]{1,0:T(8,128)(2,1)S(1)} collective-permute-done((bf16[512,384]{1,0:T(8,128)(2,1)S(1)}, bf16[512,384]{1,0:T(8,128)(2,1)S(1)}, u32[]{:S(2)}, u32[]{:S(2)}) %collective-permute-start) | collective-permute-done | bytes 393248 | tf_op jit(solution)/shard_map/ppermute | solution.py:35
  27.3 0.8 broadcast_select_fusion.1
  28.1 38.7 %all-to-all-done = bf16[8,128,1024]{2,1,0:T(8,128)(2,1)S(1)} async-done(((bf16[8,128,1024]{2,1,0:T(8,128)(2,1)}), bf16[8,128,1024]{2,1,0:T(8,128)(2,1)S(1)}, u32[]{:S(2)}, u32[]{:S(2)}) %all-to-all-start) | async-done | bytes 2097184 | tf_op jit(solution)/shard_map/all_to_all | solution.py:27
  66.8 0.0 copy-start.1
  66.8 2.3 fusion.14
  69.1 0.0 copy-done.1
  69.1 0.0 copy-start.4
  69.1 1.0 copy.40
  70.2 3.5 %all-to-all-start.1 = ((bf16[8,128,384]{1,2,0:T(8,128)(2,1)}), bf16[8,128,384]{1,2,0:T(8,128)(2,1)S(1)}, u32[]{:S(2)}, u32[]{:S(2)}) async-start(bf16[8,128,384]{1,2,0:T(8,128)(2,1)} %bitcast.56), calls=%async_computation.1 | async-start | bytes 1572864 | tf_op jit(solution)/shard_map/all_to_all | solution.py:27
  73.7 0.0 copy-done.4
  73.7 0.1 copy.25
  73.9 23.4 %all-to-all-done.1 = bf16[8,128,384]{1,2,0:T(8,128)(2,1)S(1)} async-done(((bf16[8,128,384]{1,2,0:T(8,128)(2,1)}), bf16[8,128,384]{1,2,0:T(8,128)(2,1)S(1)}, u32[]{:S(2)}, u32[]{:S(2)}) %all-to-all-start.1) | async-done | bytes 786464 | tf_op jit(solution)/shard_map/all_to_all | solution.py:27
  97.3 0.1 reduce_sum.42
  97.4 0.1 copy.26
  97.5 0.1 broadcast_in_dim.29
  97.6 29.7 %all_to_all.35 = bf16[8,128,512]{2,1,0:T(8,128)(2,1)S(1)} all-to-all(bf16[8,128,512]{2,1,0:T(8,128)(2,1)S(1)} %broadcast_in_dim.29), channel_id=1, replica_groups=mesh['xh'=2,'y'=8,'z'=8,'xl'=2,'core'=2] {'z'}, dimensions={0} | all-to-all | bytes 2097152 | tf_op jit(solution)/shard_map/all_to_all | solution.py:27
  127.3 3.1 %collective-permute-start.1 = (bf16[8,128,512]{2,1,0:T(8,128)(2,1)S(1)}, bf16[8,128,512]{2,1,0:T(8,128)(2,1)S(1)}, u32[]{:S(2)}, u32[]{:S(2)}) collective-permute-start(bf16[8,128,512]{2,1,0:T(8,128)(2,1)S(1)} %all_to_all.35), channel_id=1, source_target_pairs={{0,2},{2,0},{1,3},{3,1},{4,6},{6,4},{5,7},{7,5},{8,10},{10,8},{9,1... | collective-permute-start | bytes 3145736 | tf_op jit(solution)/shard_map/ppermute | solution.py:35
  130.4 18.2 %collective-permute-done.1 = bf16[8,128,512]{2,1,0:T(8,128)(2,1)S(1)} collective-permute-done((bf16[8,128,512]{2,1,0:T(8,128)(2,1)S(1)}, bf16[8,128,512]{2,1,0:T(8,128)(2,1)S(1)}, u32[]{:S(2)}, u32[]{:S(2)}) %collective-permute-start.1) | collective-permute-done | bytes 1048608 | tf_op jit(solution)/shard_map/ppermute | solution.py:35
  148.6 1.6 fusion.83
  150.2 8.0 %collective-permute-start.2 = (bf16[2,8,128,512]{3,2,1,0:T(8,128)(2,1)}, bf16[2,8,128,512]{3,2,1,0:T(8,128)(2,1)}, u32[]{:S(2)}, u32[]{:S(2)}) collective-permute-start(bf16[2,8,128,512]{3,2,1,0:T(8,128)(2,1)} %get-tuple-element.13), channel_id=1, source_target_pairs={{0,1},{1,0},{2,3},{3,2},{4,5},{5,4},{6,7},{7,6},{8,9},{9,8},{10,11... | collective-permute-start | bytes 6291464 | tf_op jit(solution)/shard_map/ppermute | solution.py:35
  158.3 4.1 %collective-permute-done.2 = bf16[2,8,128,512]{3,2,1,0:T(8,128)(2,1)} collective-permute-done((bf16[2,8,128,512]{3,2,1,0:T(8,128)(2,1)}, bf16[2,8,128,512]{3,2,1,0:T(8,128)(2,1)}, u32[]{:S(2)}, u32[]{:S(2)}) %collective-permute-start.2) | collective-permute-done | bytes 2097184 | tf_op jit(solution)/shard_map/ppermute | solution.py:35
  162.4 2.0 pad_maximum_fusion
  164.4 0.0 copy-start
  164.4 0.7 fusion.85
  165.0 0.4 exponential_reduce_fusion
  165.5 0.8 copy-done
  166.3 0.7 multiply_reduce_fusion
  167.0 0.6 broadcast_in_dim.58
  167.7 6.0 %all-to-all-start.3 = ((f32[32,2,128]{2,1,0:T(2,128)}), f32[32,2,128]{2,1,0:T(2,128)S(1)}, u32[]{:S(2)}, u32[]{:S(2)}) async-start(f32[32,2,128]{2,1,0:T(2,128)} %broadcast_in_dim.58), calls=%async_computation.3 | async-start | bytes 65536 | tf_op jit(solution)/shard_map/all_to_all | solution.py:27
  173.6 2.6 fusion.20
  176.2 5.5 %all-to-all-done.3 = f32[32,2,128]{2,1,0:T(2,128)S(1)} async-done(((f32[32,2,128]{2,1,0:T(2,128)}), f32[32,2,128]{2,1,0:T(2,128)S(1)}, u32[]{:S(2)}, u32[]{:S(2)}) %all-to-all-start.3) | async-done | bytes 32800 | tf_op jit(solution)/shard_map/all_to_all | solution.py:27
  181.8 0.1 rev.7
  181.9 2.0 fusion.5
  183.9 1.7 convolution_convert_fusion.1
  185.7 2.4 fusion.19
  188.1 0.0 copy-start.2
  188.2 0.1 broadcast_in_dim.59
  188.3 25.7 %all_to_all.36 = bf16[8,128,384]{1,2,0:T(8,128)(2,1)S(1)} all-to-all(bf16[8,128,384]{1,2,0:T(8,128)(2,1)S(1)} %broadcast_in_dim.59), channel_id=1, replica_groups=mesh['xh'=2,'y'=8,'z'=8,'xl'=2,'core'=2] {'y'}, dimensions={0} | all-to-all | bytes 1572864 | tf_op jit(solution)/shard_map/all_to_all | solution.py:27
  214.0 0.0 copy-done.2
  214.0 1.0 fusion.15
  215.0 0.4 copy.31
  215.3 27.9 %all_to_all.37 = bf16[64,16,384]{2,1,0:T(8,128)(2,1)S(1)} all-to-all(bf16[64,16,384]{2,1,0:T(8,128)(2,1)S(1)} %bitcast.66), channel_id=1, replica_groups=mesh['xh'=2,'y'=8,'z'=8,'xl'=2,'core'=2] {'xh','z','xl','core'}, dimensions={0} | all-to-all | bytes 1572864 | tf_op jit(solution)/shard_map/all_to_all | solution.py:27
  243.2 0.1 reduce_sum.45
  243.4 0.8 broadcast_in_dim.60
  244.1 5.8 %all-to-all-start.6 = ((bf16[32,16,384]{2,1,0:T(8,128)(2,1)}), bf16[32,16,384]{2,1,0:T(8,128)(2,1)S(1)}, u32[]{:S(2)}, u32[]{:S(2)}) async-start(bf16[32,16,384]{2,1,0:T(8,128)(2,1)} %broadcast_in_dim.60), calls=%async_computation.6 | async-start | bytes 786432 | tf_op jit(solution)/shard_map/all_to_all | solution.py:27
  250.0 0.7 copy.32
  250.7 13.0 %all-to-all-done.6 = bf16[32,16,384]{2,1,0:T(8,128)(2,1)S(1)} async-done(((bf16[32,16,384]{2,1,0:T(8,128)(2,1)}), bf16[32,16,384]{2,1,0:T(8,128)(2,1)S(1)}, u32[]{:S(2)}, u32[]{:S(2)}) %all-to-all-start.6) | async-done | bytes 393248 | tf_op jit(solution)/shard_map/all_to_all | solution.py:27
  263.8 0.7 copy.42
  (13 shorter events, 0.1 us)
Async XLA Ops:
  7.4 7.8 %copy-start.3 = (bf16[512,384]{1,0:T(8,128)(2,1)S(1)}, bf16[512,384]{1,0:T(8,128)(2,1)}, u32[]{:S(2)}) copy-start(bf16[512,384]{1,0:T(8,128)(2,1)} %param.4) | copy-start | bytes 1179652
  7.4 59.4 %all-to-all-start = ((bf16[8,128,1024]{2,1,0:T(8,128)(2,1)}), bf16[8,128,1024]{2,1,0:T(8,128)(2,1)S(1)}, u32[]{:S(2)}, u32[]{:S(2)}) async-start(bf16[8,128,1024]{2,1,0:T(8,128)(2,1)} %reshape.175), calls=%async_computation | async-start | bytes 4194304 | tf_op jit(solution)/shard_map/all_to_all | solution.py:27
  15.2 12.1 %collective-permute-start = (bf16[512,384]{1,0:T(8,128)(2,1)S(1)}, bf16[512,384]{1,0:T(8,128)(2,1)S(1)}, u32[]{:S(2)}, u32[]{:S(2)}) collective-permute-start(bf16[512,384]{1,0:T(8,128)(2,1)S(1)} %copy-done.3), channel_id=1, source_target_pairs={{0,256},{256,0},{1,257},{257,1},{2,258},{258,2},{3,259},{259,3},{4... | collective-permute-start | bytes 1179656 | tf_op jit(solution)/shard_map/ppermute | solution.py:35
  66.8 2.3 copy-start.1
  69.1 4.6 %copy-start.4 = (bf16[1,128,128]{2,1,0:T(8,128)(2,1)S(1)}, bf16[1,128,128]{2,1,0:T(8,128)(2,1)}, u32[]{:S(2)}) copy-start(bf16[1,128,128]{2,1,0:T(8,128)(2,1)} %param.5) | copy-start | bytes 98308
  70.2 27.1 %all-to-all-start.1 = ((bf16[8,128,384]{1,2,0:T(8,128)(2,1)}), bf16[8,128,384]{1,2,0:T(8,128)(2,1)S(1)}, u32[]{:S(2)}, u32[]{:S(2)}) async-start(bf16[8,128,384]{1,2,0:T(8,128)(2,1)} %bitcast.56), calls=%async_computation.1 | async-start | bytes 1572864 | tf_op jit(solution)/shard_map/all_to_all | solution.py:27
  127.3 21.3 %collective-permute-start.1 = (bf16[8,128,512]{2,1,0:T(8,128)(2,1)S(1)}, bf16[8,128,512]{2,1,0:T(8,128)(2,1)S(1)}, u32[]{:S(2)}, u32[]{:S(2)}) collective-permute-start(bf16[8,128,512]{2,1,0:T(8,128)(2,1)S(1)} %all_to_all.35), channel_id=1, source_target_pairs={{0,2},{2,0},{1,3},{3,1},{4,6},{6,4},{5,7},{7,5},{8,10},{10,8},{9,1... | collective-permute-start | bytes 3145736 | tf_op jit(solution)/shard_map/ppermute | solution.py:35
  150.2 12.2 %collective-permute-start.2 = (bf16[2,8,128,512]{3,2,1,0:T(8,128)(2,1)}, bf16[2,8,128,512]{3,2,1,0:T(8,128)(2,1)}, u32[]{:S(2)}, u32[]{:S(2)}) collective-permute-start(bf16[2,8,128,512]{3,2,1,0:T(8,128)(2,1)} %get-tuple-element.13), channel_id=1, source_target_pairs={{0,1},{1,0},{2,3},{3,2},{4,5},{5,4},{6,7},{7,6},{8,9},{9,8},{10,11... | collective-permute-start | bytes 6291464 | tf_op jit(solution)/shard_map/ppermute | solution.py:35
  164.4 1.9 copy-start
  167.7 14.1 %all-to-all-start.3 = ((f32[32,2,128]{2,1,0:T(2,128)}), f32[32,2,128]{2,1,0:T(2,128)S(1)}, u32[]{:S(2)}, u32[]{:S(2)}) async-start(f32[32,2,128]{2,1,0:T(2,128)} %broadcast_in_dim.58), calls=%async_computation.3 | async-start | bytes 65536 | tf_op jit(solution)/shard_map/all_to_all | solution.py:27
  188.1 25.9 %copy-start.2 = (bf16[8,128,1024]{2,1,0:T(8,128)(2,1)S(1)}, bf16[8,128,1024]{2,1,0:T(8,128)(2,1)}, u32[]{:S(2)}) copy-start(bf16[8,128,1024]{2,1,0:T(8,128)(2,1)} %copy-done.1) | copy-start | bytes 6291460
  244.1 19.6 %all-to-all-start.6 = ((bf16[32,16,384]{2,1,0:T(8,128)(2,1)}), bf16[32,16,384]{2,1,0:T(8,128)(2,1)S(1)}, u32[]{:S(2)}, u32[]{:S(2)}) async-start(bf16[32,16,384]{2,1,0:T(8,128)(2,1)} %broadcast_in_dim.60), calls=%async_computation.6 | async-start | bytes 786432 | tf_op jit(solution)/shard_map/all_to_all | solution.py:27

commit v2 on v1

v2 whole, which is shorter than its diff:
```python
import functools
import math

import jax
import jax.numpy as jnp
from jax import lax
from jax.experimental import pallas as pl
from jax.experimental.pallas import tpu as pltpu
from jax.sharding import Mesh, PartitionSpec as P

z_weight = 0.001
masked_fill = -1e30
low = jnp.bfloat16
z_axes = ("zh", "zl")
ctx_axes = z_axes + ("xl", "core")
group_axes = ("xh", "zl")
vmem = pltpu.CompilerParams(vmem_limit_bytes=32 * 1024 * 1024)


def dot_f32(left, right, left_dim, right_dim):
    return lax.dot_general(
        left, right, (((left_dim,), (right_dim,)), ((), ())), preferred_element_type=jnp.float32
    )


def exchange(blocks, axes):
    return lax.all_to_all(blocks, axes, split_axis=0, concat_axis=0, tiled=True)


def spread(block, axes, count):
    return exchange(jnp.broadcast_to(block[None], (count,) + block.shape), axes)


def swap(block, axis):
    return lax.ppermute(block, axis, ((0, 1), (1, 0)))


def gather_pieces(block):
    along_z = spread(block, z_axes, lax.axis_size(z_axes))
    along_z = along_z.reshape(-1, block.shape[1])
    by_x = swap(along_z, "xl")
    return along_z, by_x, swap(along_z, "core"), swap(by_x, "core")


def positions(device, inside, half_rows, ctx_count):
    block = jnp.where(inside < half_rows, device, 2 * ctx_count - 1 - device)
    return block * half_rows + inside % half_rows


def piece_device(piece, z):
    return z * 4 + (lax.axis_index("xl") ^ (piece & 1)) * 2 + (lax.axis_index("core") ^ (piece >> 1))


def forward_kernel(
    z_count, q_ref, kv0, kv1, kv2, kv3, cot_ref, attn_ref, stats_ref, dq_ref, held
):
    pieces = (kv0, kv1, kv2, kv3)
    rows, head = q_ref.shape
    half_rows, ctx_count = rows // 2, 4 * z_count
    scale = 1.0 / math.sqrt(head)
    own = piece_device(0, lax.axis_index(z_axes))
    down = lax.broadcasted_iota(jnp.int32, (rows, rows), 0)
    across = lax.broadcasted_iota(jnp.int32, (rows, rows), 1)
    own_positions = positions(own, down, half_rows, ctx_count)
    queries, cotangent = q_ref[...], cot_ref[...]
    top = None
    for piece, kv in enumerate(pieces):
        raw = dot_f32(queries, kv[:, :head], 1, 1) * scale
        for z in range(z_count):
            device = piece_device(piece, z)
            allowed = positions(device, across, half_rows, ctx_count) <= own_positions
            tile = jnp.where(allowed, raw[:, z * rows : (z + 1) * rows], masked_fill)
            held[piece, :, z * rows : (z + 1) * rows] = tile
            top = tile if top is None else jnp.maximum(top, tile)
    row_top = jnp.max(top, axis=1, keepdims=True)
    total = jnp.zeros((rows, rows), jnp.float32)
    for piece in range(4):
        weights = jnp.exp(held[piece] - row_top)
        held[piece] = weights
        for z in range(z_count):
            total = total + weights[:, z * rows : (z + 1) * rows]
    row_sum = jnp.sum(total, axis=1, keepdims=True)
    inverse = 1.0 / row_sum
    log_total = row_top + jnp.log(row_sum)
    attn = jnp.zeros((rows, head), jnp.float32)
    for piece, kv in enumerate(pieces):
        attn = attn + dot_f32((held[piece] * inverse).astype(low), kv[:, head:], 1, 0)
    attn_low = attn.astype(low)
    attn_ref[...] = attn_low
    delta = jnp.sum(
        cotangent.astype(jnp.float32) * attn_low.astype(jnp.float32), axis=1, keepdims=True
    )
    shift = 2.0 * z_weight * log_total - delta
    stats_ref[0:1, :] = jnp.transpose(jnp.broadcast_to(log_total, (rows, rows)))[0:1, :]
    stats_ref[1:2, :] = jnp.transpose(jnp.broadcast_to(shift, (rows, rows)))[0:1, :]
    grad = jnp.zeros((rows, head), jnp.float32)
    for piece, kv in enumerate(pieces):
        dprob = dot_f32(cotangent, kv[:, head:], 1, 1)
        dscore = held[piece] * inverse * (dprob + shift)
        grad = grad + dot_f32(dscore.astype(low), kv[:, :head], 1, 0)
    dq_ref[...] = (grad * scale).astype(low)


def backward_kernel(z_count, kv_ref, qc0, qc1, qc2, qc3, stats_ref, out_ref):
    rows, head = kv_ref.shape[0], kv_ref.shape[1] // 2
    half_rows, ctx_count = rows // 2, 4 * z_count
    scale = 1.0 / math.sqrt(head)
    own = piece_device(0, lax.axis_index(z_axes))
    down = lax.broadcasted_iota(jnp.int32, (rows, rows), 0)
    across = lax.broadcasted_iota(jnp.int32, (rows, rows), 1)
    own_positions = positions(own, down, half_rows, ctx_count)
    keys, values = kv_ref[:, :head], kv_ref[:, head:]
    grad_key = jnp.zeros((rows, head), jnp.float32)
    grad_value = jnp.zeros((rows, head), jnp.float32)
    for piece, both in enumerate((qc0, qc1, qc2, qc3)):
        slot = piece_device(piece, 0)
        queries, cotangent = both[:, :head], both[:, head:]
        scores = dot_f32(keys, queries, 1, 1) * scale
        dprob = dot_f32(values, cotangent, 1, 1)
        probs, dscores = [], []
        for z in range(z_count):
            span = slice(z * rows, (z + 1) * rows)
            stats = stats_ref[4 * z + slot]
            device = piece_device(piece, z)
            allowed = own_positions <= positions(device, across, half_rows, ctx_count)
            masked = jnp.where(allowed, scores[:, span], masked_fill)
            prob = jnp.exp(masked - stats[0:1, :])
            probs.append(prob.astype(low))
            dscores.append((prob * (dprob[:, span] + stats[1:2, :])).astype(low))
        grad_value = grad_value + dot_f32(jnp.concatenate(probs, axis=1), cotangent, 1, 0)
        grad_key = grad_key + dot_f32(jnp.concatenate(dscores, axis=1), queries, 1, 0)
    out_ref[:, :head] = (grad_key * scale).astype(low)
    out_ref[:, head:] = grad_value.astype(low)


def flipped(distance):
    return (lax.axis_index("xh") * 2 + lax.axis_index("zl")) ^ distance


def relayout_kernel(y_count, tokens_ref, out0, out1, out2, out3, sems):
    shard = tokens_ref.shape[1] // (2 * y_count)
    quarter = shard // 4
    core = lax.axis_index("core")
    copies = []
    for distance, out in enumerate((out0, out1, out2, out3)):
        member = flipped(distance)
        for half in range(2):
            for y in range(y_count):
                start = ((member // 2) * y_count + y) * shard
                start = start + ((member % 2) * 2 + (core ^ half)) * quarter
                source = tokens_ref.at[:, pl.ds(pl.multiple_of(start, quarter), quarter)]
                target = out.at[:, pl.ds((half * y_count + y) * quarter, quarter)]
                copies.append(pltpu.make_async_copy(source, target, sems.at[len(copies)]))
    for copy in copies:
        copy.start()
    for copy in copies:
        copy.wait()


def near_kernel(x0, x1, x2, x3, weight_ref, out_ref):
    for distance, x in enumerate((x0, x1, x2, x3)):
        out_ref[distance] = dot_f32(x[...], weight_ref[...], 1, 0)


def far_kernel(x0, x1, x2, x3, weight_ref, sum_ref, out_ref):
    for distance, x in enumerate((x0, x1, x2, x3)):
        total = sum_ref[distance] + dot_f32(x[...], weight_ref[...], 1, 0)
        out_ref[flipped(distance)] = total.astype(low)


def weight_kernel(x0, x1, x2, x3, grad_ref, out_ref):
    rows = jnp.concatenate([x0[...], x1[...], x2[...], x3[...]], axis=0)
    grads = jnp.concatenate([grad_ref[flipped(distance)] for distance in range(4)], axis=0)
    out_ref[...] = dot_f32(rows, grads, 0, 0).astype(out_ref.dtype)


def in_vmem(count):
    return [pl.BlockSpec(memory_space=pltpu.VMEM)] * count


def on_device(tokens, qkv_weight, out_grad):
    y_count, z_count = lax.axis_size("y"), lax.axis_size(z_axes)
    ctx_count = z_count * 4
    row_count, model, width = tokens.shape[1], tokens.shape[2], qkv_weight.shape[1]
    shard, head = qkv_weight.shape[0], qkv_weight.shape[1] // 3
    quarter, depth = shard // 4, model // 8
    cotangent = out_grad[0]

    at = (lax.axis_index("zl") * 2 + lax.axis_index("core")) * quarter
    near = spread(lax.dynamic_slice_in_dim(qkv_weight, at, quarter), "y", y_count)
    near = near.reshape(depth, width)
    x0, x1, x2, x3 = pl.pallas_call(
        functools.partial(relayout_kernel, y_count),
        in_specs=[pl.BlockSpec(memory_space=pl.ANY)],
        out_specs=[pl.BlockSpec(memory_space=pl.ANY)] * 4,
        out_shape=[jax.ShapeDtypeStruct((row_count, 2 * depth), low)] * 4,
        scratch_shapes=[pltpu.SemaphoreType.DMA((8 * y_count,))],
        name="token_columns",
    )(tokens[0])
    columns = (
        x0,
        swap(x1, "zl"),
        swap(x2, "xh"),
        lax.ppermute(x3, group_axes, ((0, 3), (1, 2), (2, 1), (3, 0))),
    )
    near, columns = lax.optimization_barrier((near, columns))
    far = swap(near, "core")

    def column_half(half):
        return [pl.BlockSpec((row_count, depth), lambda i: (0, half))] * 4

    whole_weight = pl.BlockSpec((depth, width), lambda i: (0, 0))
    four_rows = pl.BlockSpec((4, row_count, width), lambda i: (0, 0, 0))
    near_sum = pl.pallas_call(
        near_kernel,
        grid=(1,),
        in_specs=column_half(0) + [whole_weight],
        out_specs=four_rows,
        out_shape=jax.ShapeDtypeStruct((4, row_count, width), jnp.float32),
        compiler_params=vmem,
        name="near_projection",
    )(*columns, near)
    parts = pl.pallas_call(
        far_kernel,
        grid=(1,),
        in_specs=column_half(1) + [whole_weight, four_rows],
        out_specs=four_rows,
        out_shape=jax.ShapeDtypeStruct((4, row_count, width), low),
        compiler_params=vmem,
        name="far_projection",
    )(*columns, far, near_sum)
    parts = exchange(parts, group_axes)
    qkv = jnp.sum(parts.astype(jnp.float32), axis=0).astype(low)
    queries, own_pairs = qkv[:, :head], qkv[:, head:]
    pair_pieces = gather_pieces(own_pairs)
    query_pieces = gather_pieces(jnp.concatenate([queries, cotangent], axis=1))

    attn_rows, stats, grad_query = pl.pallas_call(
        functools.partial(forward_kernel, z_count),
        in_specs=in_vmem(6),
        out_specs=in_vmem(3),
        out_shape=[
            jax.ShapeDtypeStruct((row_count, head), low),
            jax.ShapeDtypeStruct((2, row_count), jnp.float32),
            jax.ShapeDtypeStruct((row_count, head), low),
        ],
        scratch_shapes=[pltpu.VMEM((4, row_count, z_count * row_count), jnp.float32)],
        compiler_params=vmem,
        name="attention_rows",
    )(queries, *pair_pieces, cotangent)

    stats_all = spread(stats, ctx_axes, ctx_count)

    grad_pairs = pl.pallas_call(
        functools.partial(backward_kernel, z_count),
        in_specs=in_vmem(6),
        out_specs=in_vmem(1)[0],
        out_shape=jax.ShapeDtypeStruct((row_count, 2 * head), low),
        compiler_params=vmem,
        name="attention_columns",
    )(own_pairs, *query_pieces, stats_all)

    grad_all = spread(jnp.concatenate([grad_query, grad_pairs], axis=1), group_axes, 4)

    def weight_half(half, dtype):
        return pl.pallas_call(
            weight_kernel,
            grid=(1,),
            in_specs=column_half(half) + [four_rows],
            out_specs=whole_weight,
            out_shape=jax.ShapeDtypeStruct((depth, width), dtype),
            compiler_params=vmem,
            name="weight_gradient",
        )(*columns, grad_all)

    sent = swap(weight_half(1, low), "core")
    summed = (weight_half(0, jnp.float32) + sent.astype(jnp.float32)).astype(low)
    pieces = exchange(summed.reshape(8 * y_count, -1, width), ("y", "zh", "xl"))
    own_piece = jnp.sum(pieces.astype(jnp.float32), axis=0).astype(low)
    total = spread(own_piece, ctx_axes, ctx_count)
    total = total.reshape((z_count // 2, 2, 2, 2) + own_piece.shape).transpose(1, 3, 0, 2, 4, 5)
    return (attn_rows[None], total.reshape(shard, width))


def solution(mesh):
    grid = Mesh(mesh.devices.reshape(2, 8, 4, 2, 2, 2), ("xh", "y") + ctx_axes)
    rows, weights = P(("xh", "y"), ctx_axes, None), P(("xh", "y"), None)
    return jax.shard_map(
        on_device,
        mesh=grid,
        in_specs=(rows, weights, rows),
        out_specs=(rows, weights),
        check_vma=False,
    )
```

time: 265 us -> 279 us (1.053)
  Pallas kernels: 0 us -> 74.2 us
  waiting for transfers between devices: 110 us -> 56.7 us
  starting transfers between devices: 38.9 us -> 63.7 us
  matrix products: 13.4 us -> 0 us
  blocking collectives: 83.3 us -> 75.8 us
  local copies, waits for them, and re-layouts: 12.3 us -> 6.15 us
  other arithmetic: 5.22 us -> 0.38 us
    pallas_call x0 -> x7, Pallas kernels: none -> 74.2 us  [the longest x1 65.2 us: on_device(): pl.pallas_call(functools.partial(relayout_kernel, y_count), in_specs=[pl....]
    all_to_all x4, waiting for transfers between devices: 80.7 us -> 35 us  [exchange(): return lax.all_to_all(blocks, axes, split_axis=0, concat_axis=0, tiled=True)]
    ppermute x3 -> x10, starting transfers between devices: 15.8 us -> 37.2 us  [swap(): return lax.ppermute(block, axis, ((0, 1), (1, 0)))]
    dot_general x8 -> x0, matrix products: 13.4 us -> none  [the longest x2 2.67 us: contract_last(): lax.dot_general(left, right, (((1,), (1,)), ((), ())), preferred_element_...]
    ppermute x3 -> x10, waiting for transfers between devices: 29.7 us -> 21.7 us  [swap(): return lax.ppermute(block, axis, ((0, 1), (1, 0)))]
    all_to_all x3 -> x4, blocking collectives: 83.3 us -> 75.8 us  [exchange(): return lax.all_to_all(blocks, axes, split_axis=0, concat_axis=0, tiled=True)]
    reshape x2 -> x0, local copies, waits for them, and re-layouts: 3.73 us -> none  [the longest x1 2.71 us: on_device(): columns = exchange(split.reshape(y_count, row_count, 2 * shard), 'y')]
    another operation x3 -> x0, other arithmetic: 3.6 us -> none  [the longest x2 3.59 us: gather_rows(): return jnp.stack([along_x, swap(along_x, 'core')])]
  transfers between devices with their start and end apart: 7 -> 15, of which waited for: 7 -> 7; matrix products, arithmetic and copies ran while one was open for 2% -> 0% of each run, Pallas kernels for 0% -> 25%
where the time goes in v2:
time: 279 us; the launch traced here: 278 us
  blocking collectives  75.8 us (27%)
  Pallas kernels  74.2 us (27%)
  starting transfers between devices  63.7 us (23%)
  waiting for transfers between devices  56.7 us (20%)
  local copies, waits for them, and re-layouts  6.15 us (2%)
    all_to_all x4, blocking collectives, exchange(): return lax.all_to_all(blocks, axes, split_axis=0, concat_axis=0, tiled=True)  75.8 us
    pallas_call x1, Pallas kernels, on_device(): pl.pallas_call(functools.partial(relayout_kernel, y_count), in_specs=[pl....  65.2 us
    ppermute x10, starting transfers between devices, swap(): return lax.ppermute(block, axis, ((0, 1), (1, 0)))  37.2 us
    all_to_all x4, waiting for transfers between devices, exchange(): return lax.all_to_all(blocks, axes, split_axis=0, concat_axis=0, tiled=True)  35 us
    all_to_all x4, starting transfers between devices, exchange(): return lax.all_to_all(blocks, axes, split_axis=0, concat_axis=0, tiled=True)  24.5 us
    ppermute x10, waiting for transfers between devices, swap(): return lax.ppermute(block, axis, ((0, 1), (1, 0)))  21.7 us
  transfers between devices with their start and end apart: 15, of which 7 were waited for; matrix products, arithmetic and copies ran while one was open for 0% of the time, Pallas kernels for 25%

profile of v2, /device:TPU:1, one launch (start us, length us, event | category | flops | bytes accessed | tf_op | source)
XLA Modules:
  0.0 277.8 jit_solution(7936368977822652943)
XLA Ops:
  0.6 0.0 copy-start
  0.7 1.0 copy-done
  1.6 1.0 broadcast_in_dim.14
  2.6 7.7 %all-to-all-start = ((bf16[8,128,384]{2,1,0:T(8,128)(2,1)}), bf16[8,128,384]{2,1,0:T(8,128)(2,1)S(1)}, u32[]{:S(2)}, u32[]{:S(2)}) async-start(bf16[8,128,384]{2,1,0:T(8,128)(2,1)} %broadcast_in_dim.14), calls=%async_computation | async-start | bytes 1572864 | tf_op jit(solution)/shard_map/all_to_all | solution.py:27
  10.3 65.2 %token_columns.1 = (bf16[128,2048]{1,0:T(8,128)(2,1)}, bf16[128,2048]{1,0:T(8,128)(2,1)}, bf16[128,2048]{1,0:T(8,128)(2,1)}, bf16[128,2048]{1,0:T(8,128)(2,1)}) custom-call(bf16[128,8192]{1,0:T(8,128)(2,1)} %bitcast.22), custom_call_target="tpu_custom_call" | custom-call | tf_op jit(solution)/shard_map/token_columns/pallas_call | solution.py:192
  75.5 4.0 %collective-permute-start = (bf16[128,2048]{1,0:T(8,128)(2,1)}, bf16[128,2048]{1,0:T(8,128)(2,1)S(1)}, u32[]{:S(2)}, u32[]{:S(2)}) collective-permute-start(bf16[128,2048]{1,0:T(8,128)(2,1)} %get-tuple-element.15), channel_id=1, source_target_pairs={{0,4},{4,0},{1,5},{5,1},{2,6},{6,2},{3,7},{7,3},{8,12},{12,8},{9,1... | collective-permute-start | bytes 1572872 | tf_op jit(solution)/shard_map/ppermute | solution.py:35
  79.5 4.7 %collective-permute-start.1 = (bf16[128,2048]{1,0:T(8,128)(2,1)}, bf16[128,2048]{1,0:T(8,128)(2,1)S(1)}, u32[]{:S(2)}, u32[]{:S(2)}) collective-permute-start(bf16[128,2048]{1,0:T(8,128)(2,1)} %get-tuple-element.16), channel_id=1, source_target_pairs={{0,256},{256,0},{1,257},{257,1},{2,258},{258,2},{3,259},{259,3},{4... | collective-permute-start | bytes 1572872 | tf_op jit(solution)/shard_map/ppermute | solution.py:35
  84.1 1.9 collective-permute-start.2
  86.1 4.0 %collective-permute-done.x1 = bf16[128,2048]{1,0:T(8,128)(2,1)S(1)} collective-permute-done((bf16[128,2048]{1,0:T(8,128)(2,1)}, bf16[128,2048]{1,0:T(8,128)(2,1)S(1)}, u32[]{:S(2)}, u32[]{:S(2)}) %collective-permute-start) | collective-permute-done | bytes 524320 | tf_op jit(solution)/shard_map/ppermute | solution.py:35
  90.0 16.5 %collective-permute-done.1.x2 = bf16[128,2048]{1,0:T(8,128)(2,1)S(1)} collective-permute-done((bf16[128,2048]{1,0:T(8,128)(2,1)}, bf16[128,2048]{1,0:T(8,128)(2,1)S(1)}, u32[]{:S(2)}, u32[]{:S(2)}) %collective-permute-start.1) | collective-permute-done | bytes 524320 | tf_op jit(solution)/shard_map/ppermute | solution.py:35
  106.5 0.0 collective-permute-done.2.x3
  106.5 0.0 all-to-all-done
  106.5 4.1 %collective-permute-start.3 = (bf16[1024,384]{1,0:T(8,128)(2,1)S(1)}, bf16[1024,384]{1,0:T(8,128)(2,1)S(1)}, u32[]{:S(2)}, u32[]{:S(2)}) collective-permute-start(bf16[1024,384]{1,0:T(8,128)(2,1)S(1)} %bitcast.11), channel_id=1, source_target_pairs={{0,1},{1,0},{2,3},{3,2},{4,5},{5,4},{6,7},{7,6},{8,9},{9,8},{10,11... | collective-permute-start | bytes 2359304 | tf_op jit(solution)/shard_map/ppermute | solution.py:35
  110.6 0.0 copy-start.1
  110.6 1.0 copy-done.1
  111.6 0.7 near_projection.1.sum_ref
  112.3 0.1 collective-permute-done.3.weight_ref
  112.5 0.7 far_projection.1
  113.2 0.0 copy-start.3
  113.2 11.2 %all_to_all.40 = bf16[4,128,384]{2,1,0:T(8,128)(2,1)S(1)} all-to-all(bf16[4,128,384]{2,1,0:T(8,128)(2,1)S(1)} %far_projection.1), channel_id=1, replica_groups=mesh['xh'=2,'y'=8,'zh'=4,'zl'=2,'xl'=2,'core'=2] {'xh','zl'}, dimensions={0} | all-to-all | bytes 786432 | tf_op jit(solution)/shard_map/all_to_all | solution.py:27
  124.4 0.1 reduce_sum.24
  124.5 0.8 broadcast_in_dim.15
  125.3 9.1 %all-to-all-start.2 = ((bf16[8,128,256]{2,1,0:T(8,128)(2,1)}), bf16[8,128,256]{2,1,0:T(8,128)(2,1)S(1)}, u32[]{:S(2)}, u32[]{:S(2)}) async-start(bf16[8,128,256]{2,1,0:T(8,128)(2,1)} %broadcast_in_dim.15), calls=%async_computation.2 | async-start | bytes 1048576 | tf_op jit(solution)/shard_map/all_to_all | solution.py:27
  134.4 0.0 copy-done.3
  134.5 15.0 %all-to-all-done.2 = bf16[8,128,256]{2,1,0:T(8,128)(2,1)S(1)} async-done(((bf16[8,128,256]{2,1,0:T(8,128)(2,1)}), bf16[8,128,256]{2,1,0:T(8,128)(2,1)S(1)}, u32[]{:S(2)}, u32[]{:S(2)}) %all-to-all-start.2) | async-done | bytes 524320 | tf_op jit(solution)/shard_map/all_to_all | solution.py:27
  149.5 0.8 broadcast_in_dim.17
  150.3 3.5 %all-to-all-start.3 = ((bf16[8,128,256]{2,1,0:T(8,128)(2,1)}), bf16[8,128,256]{2,1,0:T(8,128)(2,1)S(1)}, u32[]{:S(2)}, u32[]{:S(2)}) async-start(bf16[8,128,256]{2,1,0:T(8,128)(2,1)} %broadcast_in_dim.17), calls=%async_computation.3 | async-start | bytes 1048576 | tf_op jit(solution)/shard_map/all_to_all | solution.py:27
  153.8 2.2 collective-permute-start.4
  156.0 11.9 %all-to-all-done.3 = bf16[8,128,256]{2,1,0:T(8,128)(2,1)S(1)} async-done(((bf16[8,128,256]{2,1,0:T(8,128)(2,1)}), bf16[8,128,256]{2,1,0:T(8,128)(2,1)S(1)}, u32[]{:S(2)}, u32[]{:S(2)}) %all-to-all-start.3) | async-done | bytes 524320 | tf_op jit(solution)/shard_map/all_to_all | solution.py:27
  167.9 2.2 collective-permute-start.7
  170.1 6.5 %collective-permute-start.5 = (bf16[1024,256]{1,0:T(8,128)(2,1)S(1)}, bf16[1024,256]{1,0:T(8,128)(2,1)S(1)}, u32[]{:S(2)}, u32[]{:S(2)}) collective-permute-start(bf16[1024,256]{1,0:T(8,128)(2,1)S(1)} %bitcast.17), channel_id=1, source_target_pairs={{0,1},{1,0},{2,3},{3,2},{4,5},{5,4},{6,7},{7,6},{8,9},{9,8},{10,11... | collective-permute-start | bytes 1572872 | tf_op jit(solution)/shard_map/ppermute | solution.py:35
  176.6 0.0 collective-permute-done.4.kv1
  176.6 1.9 collective-permute-start.6
  178.5 2.4 collective-permute-start.8
  180.9 0.0 collective-permute-done.7.qc1
  180.9 5.2 %collective-permute-start.9 = (bf16[1024,256]{1,0:T(8,128)(2,1)}, bf16[1024,256]{1,0:T(8,128)(2,1)}, u32[]{:S(2)}, u32[]{:S(2)}) collective-permute-start(bf16[1024,256]{1,0:T(8,128)(2,1)} %collective-permute-done.7.qc1), channel_id=1, source_target_pairs={{0,1},{1,0},{2,3},{3,2},{4,5},{5,4},{6,7},{7,6},{8,9},{9,8},{10,11... | collective-permute-start | bytes 1572872 | tf_op jit(solution)/shard_map/ppermute | solution.py:35
  186.1 0.0 collective-permute-done.5.kv2
  186.1 0.0 collective-permute-done.6.kv3
  186.1 3.2 %attention_rows.1 = (bf16[128,128]{1,0:T(8,128)(2,1)}, f32[2,128]{1,0:T(2,128)S(1)}, bf16[128,128]{1,0:T(8,128)(2,1)S(1)}) custom-call(bf16[128,128]{1,0:T(8,128)(2,1)S(1)} %slice.8.q_ref, bf16[1024,256]{1,0:T(8,128)(2,1)S(1)} %bitcast.18, bf16[1024,256]{1,0:T(8,128)(2,1)} %collective-permute-done.4.kv1, bf16[1024,256]{1,0:T(8,128)(2,1)S(1)} %collective-permute-done.5.kv2, ...), custom_call_target="tpu_custom_call" | custom-call | tf_op jit(solution)/shard_map/attention_rows/pallas_call | solution.py:238
  189.3 0.6 broadcast_in_dim.18
  190.0 4.3 %all-to-all-start.4 = ((f32[32,2,128]{2,1,0:T(2,128)}), f32[32,2,128]{2,1,0:T(2,128)S(1)}, u32[]{:S(2)}, u32[]{:S(2)}) async-start(f32[32,2,128]{2,1,0:T(2,128)} %broadcast_in_dim.18), calls=%async_computation.4 | async-start | bytes 65536 | tf_op jit(solution)/shard_map/all_to_all | solution.py:27
  194.2 0.0 copy-start.2
  194.3 0.0 collective-permute-done.8.qc2
  194.3 0.0 collective-permute-done.9.qc3
  194.3 8.1 %all-to-all-done.4.stats_ref = f32[32,2,128]{2,1,0:T(2,128)S(1)} async-done(((f32[32,2,128]{2,1,0:T(2,128)}), f32[32,2,128]{2,1,0:T(2,128)S(1)}, u32[]{:S(2)}, u32[]{:S(2)}) %all-to-all-start.4) | async-done | bytes 32800 | tf_op jit(solution)/shard_map/all_to_all | solution.py:27
  202.4 2.9 %attention_columns.1 = bf16[128,256]{1,0:T(8,128)(2,1)S(1)} custom-call(bf16[128,256]{1,0:T(8,128)(2,1)S(1)} %slice.9.kv_ref, bf16[1024,256]{1,0:T(8,128)(2,1)S(1)} %bitcast.15, bf16[1024,256]{1,0:T(8,128)(2,1)} %collective-permute-done.7.qc1, bf16[1024,256]{1,0:T(8,128)(2,1)} %collective-permute-done.8.qc2, bf16[1024,256]{1,0:T(8,128)(2,1)} %collective-permute-done.9.qc3, ...), custom_call_target="tpu_custom_call" | custom-call | tf_op jit(solution)/shard_map/attention_columns/pallas_call | solution.py:254
  205.3 11.3 %all_to_all.41.grad_ref = bf16[4,128,384]{2,1,0:T(8,128)(2,1)S(1)} all-to-all(bf16[4,128,384]{2,1,0:T(8,128)(2,1)S(1)} %broadcast_in_dim.19), channel_id=1, replica_groups=mesh['xh'=2,'y'=8,'zh'=4,'zl'=2,'xl'=2,'core'=2] {'xh','zl'}, dimensions={0} | all-to-all | bytes 786432 | tf_op jit(solution)/shard_map/all_to_all | solution.py:27
  216.7 0.0 copy-done.2
  216.7 0.7 weight_gradient.3
  217.4 4.1 %collective-permute-start.10 = (bf16[1024,384]{1,0:T(8,128)(2,1)S(1)}, bf16[1024,384]{1,0:T(8,128)(2,1)S(1)}, u32[]{:S(2)}, u32[]{:S(2)}) collective-permute-start(bf16[1024,384]{1,0:T(8,128)(2,1)S(1)} %weight_gradient.3), channel_id=1, source_target_pairs={{0,1},{1,0},{2,3},{3,2},{4,5},{5,4},{6,7},{7,6},{8,9},{9,8},{10,11... | collective-permute-start | bytes 2359304 | tf_op jit(solution)/shard_map/ppermute | solution.py:35
  221.5 0.7 weight_gradient.2
  222.3 1.1 collective-permute-done.10
  223.4 0.2 add_convert_fusion
  223.6 32.1 %all_to_all.42 = bf16[64,16,384]{2,1,0:T(8,128)(2,1)S(1)} all-to-all(bf16[64,16,384]{2,1,0:T(8,128)(2,1)S(1)} %bitcast.21), channel_id=1, replica_groups=mesh['xh'=2,'y'=8,'zh'=4,'zl'=2,'xl'=2,'core'=2] {'y','zh','xl'}, dimensions={0} | all-to-all | bytes 1572864 | tf_op jit(solution)/shard_map/all_to_all | solution.py:27
  255.7 0.1 reduce_sum.25
  255.8 21.2 %all_to_all.43 = bf16[32,16,384]{2,1,0:T(8,128)(2,1)S(1)} all-to-all(bf16[32,16,384]{2,1,0:T(8,128)(2,1)S(1)} %broadcast_in_dim.20), channel_id=1, replica_groups=mesh['xh'=2,'y'=8,'zh'=4,'zl'=2,'xl'=2,'core'=2] {'zh','zl','xl','core'}, dimensions={0} | all-to-all | bytes 786432 | tf_op jit(solution)/shard_map/all_to_all | solution.py:27
  277.0 0.8 copy.5
  (7 shorter events, 0.1 us)
Async XLA Ops:
  0.6 1.0 copy-start
  2.6 103.9 %all-to-all-start = ((bf16[8,128,384]{2,1,0:T(8,128)(2,1)}), bf16[8,128,384]{2,1,0:T(8,128)(2,1)S(1)}, u32[]{:S(2)}, u32[]{:S(2)}) async-start(bf16[8,128,384]{2,1,0:T(8,128)(2,1)} %broadcast_in_dim.14), calls=%async_computation | async-start | bytes 1572864 | tf_op jit(solution)/shard_map/all_to_all | solution.py:27
  75.5 14.6 %collective-permute-start = (bf16[128,2048]{1,0:T(8,128)(2,1)}, bf16[128,2048]{1,0:T(8,128)(2,1)S(1)}, u32[]{:S(2)}, u32[]{:S(2)}) collective-permute-start(bf16[128,2048]{1,0:T(8,128)(2,1)} %get-tuple-element.15), channel_id=1, source_target_pairs={{0,4},{4,0},{1,5},{5,1},{2,6},{6,2},{3,7},{7,3},{8,12},{12,8},{9,1... | collective-permute-start | bytes 1572872 | tf_op jit(solution)/shard_map/ppermute | solution.py:35
  79.5 27.0 %collective-permute-start.1 = (bf16[128,2048]{1,0:T(8,128)(2,1)}, bf16[128,2048]{1,0:T(8,128)(2,1)S(1)}, u32[]{:S(2)}, u32[]{:S(2)}) collective-permute-start(bf16[128,2048]{1,0:T(8,128)(2,1)} %get-tuple-element.16), channel_id=1, source_target_pairs={{0,256},{256,0},{1,257},{257,1},{2,258},{258,2},{3,259},{259,3},{4... | collective-permute-start | bytes 1572872 | tf_op jit(solution)/shard_map/ppermute | solution.py:35
  84.1 22.4 %collective-permute-start.2 = (bf16[128,2048]{1,0:T(8,128)(2,1)}, bf16[128,2048]{1,0:T(8,128)(2,1)S(1)}, u32[]{:S(2)}, u32[]{:S(2)}) collective-permute-start(bf16[128,2048]{1,0:T(8,128)(2,1)} %get-tuple-element.17), channel_id=1, source_target_pairs={{0,260},{4,256},{256,4},{260,0},{1,261},{5,257},{257,5},{261,1},{2... | collective-permute-start | bytes 1572872 | tf_op jit(solution)/shard_map/ppermute | solution.py:204
  106.5 6.0 %collective-permute-start.3 = (bf16[1024,384]{1,0:T(8,128)(2,1)S(1)}, bf16[1024,384]{1,0:T(8,128)(2,1)S(1)}, u32[]{:S(2)}, u32[]{:S(2)}) collective-permute-start(bf16[1024,384]{1,0:T(8,128)(2,1)S(1)} %bitcast.11), channel_id=1, source_target_pairs={{0,1},{1,0},{2,3},{3,2},{4,5},{5,4},{6,7},{7,6},{8,9},{9,8},{10,11... | collective-permute-start | bytes 2359304 | tf_op jit(solution)/shard_map/ppermute | solution.py:35
  110.6 1.0 copy-start.1
  113.2 21.3 %copy-start.3 = (bf16[1,128,128]{2,1,0:T(8,128)(2,1)S(1)}, bf16[1,128,128]{2,1,0:T(8,128)(2,1)}, u32[]{:S(2)}) copy-start(bf16[1,128,128]{2,1,0:T(8,128)(2,1)} %param.5) | copy-start | bytes 98308
  125.3 24.2 %all-to-all-start.2 = ((bf16[8,128,256]{2,1,0:T(8,128)(2,1)}), bf16[8,128,256]{2,1,0:T(8,128)(2,1)S(1)}, u32[]{:S(2)}, u32[]{:S(2)}) async-start(bf16[8,128,256]{2,1,0:T(8,128)(2,1)} %broadcast_in_dim.15), calls=%async_computation.2 | async-start | bytes 1048576 | tf_op jit(solution)/shard_map/all_to_all | solution.py:27
  150.3 17.6 %all-to-all-start.3 = ((bf16[8,128,256]{2,1,0:T(8,128)(2,1)}), bf16[8,128,256]{2,1,0:T(8,128)(2,1)S(1)}, u32[]{:S(2)}, u32[]{:S(2)}) async-start(bf16[8,128,256]{2,1,0:T(8,128)(2,1)} %broadcast_in_dim.17), calls=%async_computation.3 | async-start | bytes 1048576 | tf_op jit(solution)/shard_map/all_to_all | solution.py:27
  153.8 22.8 %collective-permute-start.4 = (bf16[1024,256]{1,0:T(8,128)(2,1)S(1)}, bf16[1024,256]{1,0:T(8,128)(2,1)}, u32[]{:S(2)}, u32[]{:S(2)}) collective-permute-start(bf16[1024,256]{1,0:T(8,128)(2,1)S(1)} %bitcast.16), channel_id=1, source_target_pairs={{0,2},{2,0},{1,3},{3,1},{4,6},{6,4},{5,7},{7,5},{8,10},{10,8},{9,1... | collective-permute-start | bytes 1572872 | tf_op jit(solution)/shard_map/ppermute | solution.py:35
  167.9 13.0 %collective-permute-start.7 = (bf16[1024,256]{1,0:T(8,128)(2,1)S(1)}, bf16[1024,256]{1,0:T(8,128)(2,1)}, u32[]{:S(2)}, u32[]{:S(2)}) collective-permute-start(bf16[1024,256]{1,0:T(8,128)(2,1)S(1)} %bitcast.13), channel_id=1, source_target_pairs={{0,2},{2,0},{1,3},{3,1},{4,6},{6,4},{5,7},{7,5},{8,10},{10,8},{9,1... | collective-permute-start | bytes 1572872 | tf_op jit(solution)/shard_map/ppermute | solution.py:35
  170.1 16.0 %collective-permute-start.5 = (bf16[1024,256]{1,0:T(8,128)(2,1)S(1)}, bf16[1024,256]{1,0:T(8,128)(2,1)S(1)}, u32[]{:S(2)}, u32[]{:S(2)}) collective-permute-start(bf16[1024,256]{1,0:T(8,128)(2,1)S(1)} %bitcast.17), channel_id=1, source_target_pairs={{0,1},{1,0},{2,3},{3,2},{4,5},{5,4},{6,7},{7,6},{8,9},{9,8},{10,11... | collective-permute-start | bytes 1572872 | tf_op jit(solution)/shard_map/ppermute | solution.py:35
  176.6 9.6 %collective-permute-start.6 = (bf16[1024,256]{1,0:T(8,128)(2,1)}, bf16[1024,256]{1,0:T(8,128)(2,1)S(1)}, u32[]{:S(2)}, u32[]{:S(2)}) collective-permute-start(bf16[1024,256]{1,0:T(8,128)(2,1)} %collective-permute-done.4.kv1), channel_id=1, source_target_pairs={{0,1},{1,0},{2,3},{3,2},{4,5},{5,4},{6,7},{7,6},{8,9},{9,8},{10,11... | collective-permute-start | bytes 1572872 | tf_op jit(solution)/shard_map/ppermute | solution.py:35
  178.5 15.8 %collective-permute-start.8 = (bf16[1024,256]{1,0:T(8,128)(2,1)S(1)}, bf16[1024,256]{1,0:T(8,128)(2,1)}, u32[]{:S(2)}, u32[]{:S(2)}) collective-permute-start(bf16[1024,256]{1,0:T(8,128)(2,1)S(1)} %bitcast.14), channel_id=1, source_target_pairs={{0,1},{1,0},{2,3},{3,2},{4,5},{5,4},{6,7},{7,6},{8,9},{9,8},{10,11... | collective-permute-start | bytes 1572872 | tf_op jit(solution)/shard_map/ppermute | solution.py:35
  180.9 13.3 %collective-permute-start.9 = (bf16[1024,256]{1,0:T(8,128)(2,1)}, bf16[1024,256]{1,0:T(8,128)(2,1)}, u32[]{:S(2)}, u32[]{:S(2)}) collective-permute-start(bf16[1024,256]{1,0:T(8,128)(2,1)} %collective-permute-done.7.qc1), channel_id=1, source_target_pairs={{0,1},{1,0},{2,3},{3,2},{4,5},{5,4},{6,7},{7,6},{8,9},{9,8},{10,11... | collective-permute-start | bytes 1572872 | tf_op jit(solution)/shard_map/ppermute | solution.py:35
  190.0 12.4 %all-to-all-start.4 = ((f32[32,2,128]{2,1,0:T(2,128)}), f32[32,2,128]{2,1,0:T(2,128)S(1)}, u32[]{:S(2)}, u32[]{:S(2)}) async-start(f32[32,2,128]{2,1,0:T(2,128)} %broadcast_in_dim.18), calls=%async_computation.4 | async-start | bytes 65536 | tf_op jit(solution)/shard_map/all_to_all | solution.py:27
  194.2 22.4 %copy-start.2 = (bf16[128,2048]{1,0:T(8,128)(2,1)S(1)}, bf16[128,2048]{1,0:T(8,128)(2,1)}, u32[]{:S(2)}) copy-start(bf16[128,2048]{1,0:T(8,128)(2,1)} %get-tuple-element.18.x0) | copy-start | bytes 1572868
  217.4 6.0 %collective-permute-start.10 = (bf16[1024,384]{1,0:T(8,128)(2,1)S(1)}, bf16[1024,384]{1,0:T(8,128)(2,1)S(1)}, u32[]{:S(2)}, u32[]{:S(2)}) collective-permute-start(bf16[1024,384]{1,0:T(8,128)(2,1)S(1)} %weight_gradient.3), channel_id=1, source_target_pairs={{0,1},{1,0},{2,3},{3,2},{4,5},{5,4},{6,7},{7,6},{8,9},{9,8},{10,11... | collective-permute-start | bytes 2359304 | tf_op jit(solution)/shard_map/ppermute | solution.py:35

commit v3 on v2

--- a/solution.py
+++ b/solution.py
@@ -13,7 +13,7 @@
 low = jnp.bfloat16
 z_axes = ("zh", "zl")
 ctx_axes = z_axes + ("xl", "core")
-group_axes = ("xh", "zl")
+group_axes = ("xh", "yl", "zl")
 vmem = pltpu.CompilerParams(vmem_limit_bytes=32 * 1024 * 1024)
 
 
@@ -35,11 +35,9 @@
     return lax.ppermute(block, axis, ((0, 1), (1, 0)))
 
 
-def gather_pieces(block):
-    along_z = spread(block, z_axes, lax.axis_size(z_axes))
-    along_z = along_z.reshape(-1, block.shape[1])
-    by_x = swap(along_z, "xl")
-    return along_z, by_x, swap(along_z, "core"), swap(by_x, "core")
+def gather_x(block):
+    along_z = spread(block, z_axes, lax.axis_size(z_axes)).reshape(-1, block.shape[1])
+    return along_z, swap(along_z, "xl")
 
 
 def positions(device, inside, half_rows, ctx_count):
@@ -133,45 +131,38 @@
     out_ref[:, head:] = grad_value.astype(low)
 
 
-def flipped(distance):
-    return (lax.axis_index("xh") * 2 + lax.axis_index("zl")) ^ distance
-
-
-def relayout_kernel(y_count, tokens_ref, out0, out1, out2, out3, sems):
-    shard = tokens_ref.shape[1] // (2 * y_count)
-    quarter = shard // 4
+def shard_row(step, count):
+    return lax.rem(lax.axis_index("yh") + count - step, count)
+
+
+def relayout_kernel(y_half, tokens_ref, out_ref):
+    members, _, columns = out_ref.shape
+    quarter = columns // (2 * y_half)
     core = lax.axis_index("core")
-    copies = []
-    for distance, out in enumerate((out0, out1, out2, out3)):
-        member = flipped(distance)
+    for member in range(members):
+        x_hi, y_lo, z_lo = member // 4, member // 2 % 2, member % 2
         for half in range(2):
-            for y in range(y_count):
-                start = ((member // 2) * y_count + y) * shard
-                start = start + ((member % 2) * 2 + (core ^ half)) * quarter
-                source = tokens_ref.at[:, pl.ds(pl.multiple_of(start, quarter), quarter)]
-                target = out.at[:, pl.ds((half * y_count + y) * quarter, quarter)]
-                copies.append(pltpu.make_async_copy(source, target, sems.at[len(copies)]))
-    for copy in copies:
-        copy.start()
-    for copy in copies:
-        copy.wait()
-
-
-def near_kernel(x0, x1, x2, x3, weight_ref, out_ref):
-    for distance, x in enumerate((x0, x1, x2, x3)):
-        out_ref[distance] = dot_f32(x[...], weight_ref[...], 1, 0)
-
-
-def far_kernel(x0, x1, x2, x3, weight_ref, sum_ref, out_ref):
-    for distance, x in enumerate((x0, x1, x2, x3)):
-        total = sum_ref[distance] + dot_f32(x[...], weight_ref[...], 1, 0)
-        out_ref[flipped(distance)] = total.astype(low)
-
-
-def weight_kernel(x0, x1, x2, x3, grad_ref, out_ref):
-    rows = jnp.concatenate([x0[...], x1[...], x2[...], x3[...]], axis=0)
-    grads = jnp.concatenate([grad_ref[flipped(distance)] for distance in range(4)], axis=0)
-    out_ref[...] = dot_f32(rows, grads, 0, 0).astype(out_ref.dtype)
+            for step in range(y_half):
+                shard = (x_hi * y_half + shard_row(step, y_half)) * 2 + y_lo
+                start = (shard * 4 + z_lo * 2 + (core ^ half)) * quarter
+                target = (half * y_half + step) * quarter
+                out_ref[member, :, target : target + quarter] = tokens_ref[
+                    :, pl.ds(pl.multiple_of(start, quarter), quarter)
+                ]
+
+
+def project_kernel(x_ref, near_ref, far_ref, out_ref):
+    depth = near_ref.shape[0]
+    total = dot_f32(x_ref[:, :depth], near_ref[...], 1, 0)
+    total = total + dot_f32(x_ref[:, depth:], far_ref[...], 1, 0)
+    out_ref[...] = total.astype(low)
+
+
+def weight_kernel(y_half, x_ref, grad_ref, out_ref):
+    total = dot_f32(x_ref[...], grad_ref[...], 0, 0).astype(out_ref.dtype)
+    quarter = total.shape[0] // y_half
+    for step in range(y_half):
+        out_ref[shard_row(step, y_half)] = total[step * quarter : (step + 1) * quarter]
 
 
 def in_vmem(count):
@@ -179,61 +170,44 @@
 
 
 def on_device(tokens, qkv_weight, out_grad):
-    y_count, z_count = lax.axis_size("y"), lax.axis_size(z_axes)
+    y_half, z_count = lax.axis_size("yh"), lax.axis_size(z_axes)
     ctx_count = z_count * 4
     row_count, model, width = tokens.shape[1], tokens.shape[2], qkv_weight.shape[1]
     shard, head = qkv_weight.shape[0], qkv_weight.shape[1] // 3
-    quarter, depth = shard // 4, model // 8
+    quarter, depth, group_rows = shard // 4, model // 16, 8 * row_count
     cotangent = out_grad[0]
 
     at = (lax.axis_index("zl") * 2 + lax.axis_index("core")) * quarter
-    near = spread(lax.dynamic_slice_in_dim(qkv_weight, at, quarter), "y", y_count)
-    near = near.reshape(depth, width)
-    x0, x1, x2, x3 = pl.pallas_call(
-        functools.partial(relayout_kernel, y_count),
-        in_specs=[pl.BlockSpec(memory_space=pl.ANY)],
-        out_specs=[pl.BlockSpec(memory_space=pl.ANY)] * 4,
-        out_shape=[jax.ShapeDtypeStruct((row_count, 2 * depth), low)] * 4,
-        scratch_shapes=[pltpu.SemaphoreType.DMA((8 * y_count,))],
+    own_weight = lax.dynamic_slice_in_dim(qkv_weight, at, quarter)
+    steps = [own_weight]
+    for step in range(1, y_half):
+        ring = [(i, (i + step) % y_half) for i in range(y_half)]
+        steps.append(lax.ppermute(own_weight, "yh", ring))
+    near = jnp.concatenate(steps)
+    far = swap(near, "core")
+    split = pl.pallas_call(
+        functools.partial(relayout_kernel, y_half),
+        in_specs=in_vmem(1),
+        out_specs=in_vmem(1)[0],
+        out_shape=jax.ShapeDtypeStruct((8, row_count, 2 * depth), low),
+        compiler_params=vmem,
         name="token_columns",
     )(tokens[0])
-    columns = (
-        x0,
-        swap(x1, "zl"),
-        swap(x2, "xh"),
-        lax.ppermute(x3, group_axes, ((0, 3), (1, 2), (2, 1), (3, 0))),
-    )
-    near, columns = lax.optimization_barrier((near, columns))
-    far = swap(near, "core")
-
-    def column_half(half):
-        return [pl.BlockSpec((row_count, depth), lambda i: (0, half))] * 4
-
-    whole_weight = pl.BlockSpec((depth, width), lambda i: (0, 0))
-    four_rows = pl.BlockSpec((4, row_count, width), lambda i: (0, 0, 0))
-    near_sum = pl.pallas_call(
-        near_kernel,
-        grid=(1,),
-        in_specs=column_half(0) + [whole_weight],
-        out_specs=four_rows,
-        out_shape=jax.ShapeDtypeStruct((4, row_count, width), jnp.float32),
-        compiler_params=vmem,
-        name="near_projection",
-    )(*columns, near)
+    columns = exchange(split, group_axes).reshape(group_rows, 2 * depth)
     parts = pl.pallas_call(
-        far_kernel,
-        grid=(1,),
-        in_specs=column_half(1) + [whole_weight, four_rows],
-        out_specs=four_rows,
-        out_shape=jax.ShapeDtypeStruct((4, row_count, width), low),
-        compiler_params=vmem,
-        name="far_projection",
-    )(*columns, far, near_sum)
-    parts = exchange(parts, group_axes)
+        project_kernel,
+        in_specs=in_vmem(3),
+        out_specs=in_vmem(1)[0],
+        out_shape=jax.ShapeDtypeStruct((group_rows, width), low),
+        compiler_params=vmem,
+        name="partial_projection",
+    )(columns, near, far)
+    parts = exchange(parts.reshape(8, row_count, width), group_axes)
     qkv = jnp.sum(parts.astype(jnp.float32), axis=0).astype(low)
     queries, own_pairs = qkv[:, :head], qkv[:, head:]
-    pair_pieces = gather_pieces(own_pairs)
-    query_pieces = gather_pieces(jnp.concatenate([queries, cotangent], axis=1))
+    pair_pieces = gather_x(own_pairs)
+    pair_pieces = pair_pieces + tuple(swap(p, "core") for p in pair_pieces)
+    query_pieces = gather_x(jnp.concatenate([queries, cotangent], axis=1))
 
     attn_rows, stats, grad_query = pl.pallas_call(
         functools.partial(forward_kernel, z_count),
@@ -249,6 +223,8 @@
         name="attention_rows",
     )(queries, *pair_pieces, cotangent)
 
+    query_pieces, stats = lax.optimization_barrier((query_pieces, stats))
+    query_pieces = query_pieces + tuple(swap(p, "core") for p in query_pieces)
     stats_all = spread(stats, ctx_axes, ctx_count)
 
     grad_pairs = pl.pallas_call(
@@ -260,22 +236,26 @@
         name="attention_columns",
     )(own_pairs, *query_pieces, stats_all)
 
-    grad_all = spread(jnp.concatenate([grad_query, grad_pairs], axis=1), group_axes, 4)
+    grad_all = spread(jnp.concatenate([grad_query, grad_pairs], axis=1), group_axes, 8)
+    grad_all = grad_all.reshape(group_rows, width)
 
     def weight_half(half, dtype):
         return pl.pallas_call(
-            weight_kernel,
+            functools.partial(weight_kernel, y_half),
             grid=(1,),
-            in_specs=column_half(half) + [four_rows],
-            out_specs=whole_weight,
-            out_shape=jax.ShapeDtypeStruct((depth, width), dtype),
+            in_specs=[
+                pl.BlockSpec((group_rows, depth), lambda i: (0, half)),
+                pl.BlockSpec((group_rows, width), lambda i: (0, 0)),
+            ],
+            out_specs=pl.BlockSpec((y_half, quarter, width), lambda i: (0, 0, 0)),
+            out_shape=jax.ShapeDtypeStruct((y_half, quarter, width), dtype),
             compiler_params=vmem,
             name="weight_gradient",
-        )(*columns, grad_all)
+        )(columns, grad_all)
 
     sent = swap(weight_half(1, low), "core")
     summed = (weight_half(0, jnp.float32) + sent.astype(jnp.float32)).astype(low)
-    pieces = exchange(summed.reshape(8 * y_count, -1, width), ("y", "zh", "xl"))
+    pieces = exchange(summed.reshape(8 * y_half, -1, width), ("yh", "zh", "xl"))
     own_piece = jnp.sum(pieces.astype(jnp.float32), axis=0).astype(low)
     total = spread(own_piece, ctx_axes, ctx_count)
     total = total.reshape((z_count // 2, 2, 2, 2) + own_piece.shape).transpose(1, 3, 0, 2, 4, 5)
@@ -283,8 +263,8 @@
 
 
 def solution(mesh):
-    grid = Mesh(mesh.devices.reshape(2, 8, 4, 2, 2, 2), ("xh", "y") + ctx_axes)
-    rows, weights = P(("xh", "y"), ctx_axes, None), P(("xh", "y"), None)
+    grid = Mesh(mesh.devices.reshape(2, 4, 2, 4, 2, 2, 2), ("xh", "yh", "yl") + ctx_axes)
+    rows, weights = P(("xh", "yh", "yl"), ctx_axes, None), P(("xh", "yh", "yl"), None)
     return jax.shard_map(
         on_device,
         mesh=grid,

time: 279 us -> 228 us (0.82)
  Pallas kernels: 74.2 us -> 8.35 us
  blocking collectives: 75.8 us -> 91.9 us
  starting transfers between devices: 63.7 us -> 60.4 us
  local copies, waits for them, and re-layouts: 6.15 us -> 9.1 us
    pallas_call x5 -> x4, Pallas kernels: 68.1 us -> 3.28 us  [the longest x2 1.48 us: weight_half(): pl.pallas_call(functools.partial(weight_kernel, y_half), grid=(1,), in_sp...]
    ppermute x1 -> x3, waiting for transfers between devices: 0.01 us -> 25.9 us  [on_device(): steps.append(lax.ppermute(own_weight, 'yh', ring))]
    all_to_all x4 -> x3, waiting for transfers between devices: 35 us -> 14.4 us  [exchange(): return lax.all_to_all(blocks, axes, split_axis=0, concat_axis=0, tiled=True)]
    all_to_all x4 -> x5, blocking collectives: 75.8 us -> 91.9 us  [exchange(): return lax.all_to_all(blocks, axes, split_axis=0, concat_axis=0, tiled=True)]
    ppermute x1 -> x3, starting transfers between devices: 1.92 us -> 12.7 us  [on_device(): steps.append(lax.ppermute(own_weight, 'yh', ring))]
    ppermute x10 -> x8, starting transfers between devices: 37.2 us -> 27.3 us  [swap(): return lax.ppermute(block, axis, ((0, 1), (1, 0)))]
    ppermute x10 -> x8, waiting for transfers between devices: 21.7 us -> 15.6 us  [swap(): return lax.ppermute(block, axis, ((0, 1), (1, 0)))]
    all_to_all x4 -> x3, starting transfers between devices: 24.5 us -> 20.3 us  [exchange(): return lax.all_to_all(blocks, axes, split_axis=0, concat_axis=0, tiled=True)]
  transfers between devices with their start and end apart: 15 -> 14, of which waited for: 7 -> 7; matrix products, arithmetic and copies ran while one was open for 0% -> 0% of each run, Pallas kernels for 25% -> 2%
where the time goes in v3:
time: 228 us; the launch traced here: 227 us
  blocking collectives  91.9 us (40%)
  starting transfers between devices  60.4 us (26%)
  waiting for transfers between devices  55.9 us (25%)
  local copies, waits for them, and re-layouts  9.1 us (4%)
  Pallas kernels  8.35 us (4%)
    all_to_all x5, blocking collectives, exchange(): return lax.all_to_all(blocks, axes, split_axis=0, concat_axis=0, tiled=True)  91.9 us
    ppermute x8, starting transfers between devices, swap(): return lax.ppermute(block, axis, ((0, 1), (1, 0)))  27.3 us
    ppermute x3, waiting for transfers between devices, on_device(): steps.append(lax.ppermute(own_weight, 'yh', ring))  25.9 us
    all_to_all x3, starting transfers between devices, exchange(): return lax.all_to_all(blocks, axes, split_axis=0, concat_axis=0, tiled=True)  20.3 us
    ppermute x8, waiting for transfers between devices, swap(): return lax.ppermute(block, axis, ((0, 1), (1, 0)))  15.6 us
    all_to_all x3, waiting for transfers between devices, exchange(): return lax.all_to_all(blocks, axes, split_axis=0, concat_axis=0, tiled=True)  14.4 us
    ppermute x3, starting transfers between devices, on_device(): steps.append(lax.ppermute(own_weight, 'yh', ring))  12.7 us
    unnamed x20, local copies, waits for them, and re-layouts  5.72 us
  transfers between devices with their start and end apart: 14, of which 7 were waited for; matrix products, arithmetic and copies ran while one was open for 0% of the time, Pallas kernels for 2%

profile of v3, /device:TPU:1, one launch (start us, length us, event | category | flops | bytes accessed | tf_op | source)
XLA Modules:
  0.0 226.8 jit_solution(7366844376965677816)
XLA Ops:
  0.6 0.0 copy-start
  0.6 0.0 copy-start.2
  0.7 1.6 copy-done.2
  2.3 0.6 token_columns.1
  2.8 0.0 copy-start.1
  2.9 1.3 copy-done.1
  4.2 7.7 %all-to-all-start = ((bf16[8,128,1024]{2,1,0:T(8,128)(2,1)}), bf16[8,128,1024]{2,1,0:T(8,128)(2,1)S(1)}, u32[]{:S(2)}, u32[]{:S(2)}) async-start(bf16[8,128,1024]{2,1,0:T(8,128)(2,1)} %copy-done.1), calls=%async_computation | async-start | bytes 4194304 | tf_op jit(solution)/shard_map/all_to_all | solution.py:27
  11.8 0.0 copy-done
  11.9 5.0 %collective-permute-start.2 = (bf16[128,384]{1,0:T(8,128)(2,1)S(1)}, bf16[128,384]{1,0:T(8,128)(2,1)S(1)}, u32[]{:S(2)}, u32[]{:S(2)}) collective-permute-start(bf16[128,384]{1,0:T(8,128)(2,1)S(1)} %constant_dynamic-slice_fusion), channel_id=1, source_target_pairs={{0,192},{64,0},{128,64},{192,128},{1,193},{65,1},{129,65},{193,129... | collective-permute-start | bytes 294920 | tf_op jit(solution)/shard_map/ppermute | solution.py:185
  16.9 4.4 %collective-permute-start.1 = (bf16[128,384]{1,0:T(8,128)(2,1)S(1)}, bf16[128,384]{1,0:T(8,128)(2,1)S(1)}, u32[]{:S(2)}, u32[]{:S(2)}) collective-permute-start(bf16[128,384]{1,0:T(8,128)(2,1)S(1)} %constant_dynamic-slice_fusion), channel_id=1, source_target_pairs={{0,128},{64,192},{128,0},{192,64},{1,129},{65,193},{129,1},{193,65... | collective-permute-start | bytes 294920 | tf_op jit(solution)/shard_map/ppermute | solution.py:185
  21.3 3.3 %collective-permute-start = (bf16[128,384]{1,0:T(8,128)(2,1)S(1)}, bf16[128,384]{1,0:T(8,128)(2,1)S(1)}, u32[]{:S(2)}, u32[]{:S(2)}) collective-permute-start(bf16[128,384]{1,0:T(8,128)(2,1)S(1)} %constant_dynamic-slice_fusion), channel_id=1, source_target_pairs={{0,64},{64,128},{128,192},{192,0},{1,65},{65,129},{129,193},{193,1... | collective-permute-start | bytes 294920 | tf_op jit(solution)/shard_map/ppermute | solution.py:185
  24.6 0.0 collective-permute-done.2
  24.6 23.3 %collective-permute-done.1 = bf16[128,384]{1,0:T(8,128)(2,1)S(1)} collective-permute-done((bf16[128,384]{1,0:T(8,128)(2,1)S(1)}, bf16[128,384]{1,0:T(8,128)(2,1)S(1)}, u32[]{:S(2)}, u32[]{:S(2)}) %collective-permute-start.1) | collective-permute-done | bytes 98336 | tf_op jit(solution)/shard_map/ppermute | solution.py:185
  47.9 2.6 %collective-permute-done = bf16[128,384]{1,0:T(8,128)(2,1)S(1)} collective-permute-done((bf16[128,384]{1,0:T(8,128)(2,1)S(1)}, bf16[128,384]{1,0:T(8,128)(2,1)S(1)}, u32[]{:S(2)}, u32[]{:S(2)}) %collective-permute-start) | collective-permute-done | bytes 98336 | tf_op jit(solution)/shard_map/ppermute | solution.py:185
  50.6 3.9 %collective-permute-start.3 = (bf16[512,384]{1,0:T(8,128)(2,1)S(1)}, bf16[512,384]{1,0:T(8,128)(2,1)S(1)}, u32[]{:S(2)}, u32[]{:S(2)}) collective-permute-start(bf16[512,384]{1,0:T(8,128)(2,1)S(1)} %pad_maximum_fusion.near_ref), channel_id=1, source_target_pairs={{0,1},{1,0},{2,3},{3,2},{4,5},{5,4},{6,7},{7,6},{8,9},{9,8},{10,11... | collective-permute-start | bytes 1179656 | tf_op jit(solution)/shard_map/ppermute | solution.py:35
  54.5 1.3 collective-permute-done.3.far_ref
  55.8 0.0 all-to-all-done
  55.8 1.2 partial_projection.1
  57.1 0.0 copy-start.7
  57.1 19.9 %all_to_all.40 = bf16[8,128,384]{2,1,0:T(8,128)(2,1)S(1)} all-to-all(bf16[8,128,384]{2,1,0:T(8,128)(2,1)S(1)} %bitcast.18), channel_id=1, replica_groups=mesh['xh'=2,'yh'=4,'yl'=2,'zh'=4,'zl'=2,'xl'=2,'core'=2] {'xh','yl','zl'}, dimensions={0} | all-to-all | bytes 1572864 | tf_op jit(solution)/shard_map/all_to_all | solution.py:27
  76.9 0.1 reduce_sum.24
  77.1 0.0 copy-start.9
  77.1 0.8 broadcast_in_dim.12
  77.9 0.6 copy-done.3
  78.5 0.0 copy-done.9
  78.5 9.1 %all-to-all-start.2 = ((bf16[8,128,256]{2,1,0:T(8,128)(2,1)}), bf16[8,128,256]{2,1,0:T(8,128)(2,1)S(1)}, u32[]{:S(2)}, u32[]{:S(2)}) async-start(bf16[8,128,256]{2,1,0:T(8,128)(2,1)} %broadcast_in_dim.12), calls=%async_computation.2 | async-start | bytes 1048576 | tf_op jit(solution)/shard_map/all_to_all | solution.py:27
  87.7 0.8 slice.8.q_ref
  88.4 0.0 copy-done.7
  88.5 0.0 copy-start.5
  88.5 0.6 copy-done.5
  89.1 14.3 %all-to-all-done.2 = bf16[8,128,256]{2,1,0:T(8,128)(2,1)S(1)} async-done(((bf16[8,128,256]{2,1,0:T(8,128)(2,1)}), bf16[8,128,256]{2,1,0:T(8,128)(2,1)S(1)}, u32[]{:S(2)}, u32[]{:S(2)}) %all-to-all-start.2) | async-done | bytes 524320 | tf_op jit(solution)/shard_map/all_to_all | solution.py:27
  103.4 0.8 broadcast_in_dim.14
  104.3 3.5 %all-to-all-start.3 = ((bf16[8,128,256]{2,1,0:T(8,128)(2,1)}), bf16[8,128,256]{2,1,0:T(8,128)(2,1)S(1)}, u32[]{:S(2)}, u32[]{:S(2)}) async-start(bf16[8,128,256]{2,1,0:T(8,128)(2,1)} %broadcast_in_dim.14), calls=%async_computation.3 | async-start | bytes 1048576 | tf_op jit(solution)/shard_map/all_to_all | solution.py:27
  107.8 2.2 collective-permute-start.4
  110.0 4.9 %collective-permute-start.5 = (bf16[1024,256]{1,0:T(8,128)(2,1)S(1)}, bf16[1024,256]{1,0:T(8,128)(2,1)}, u32[]{:S(2)}, u32[]{:S(2)}) collective-permute-start(bf16[1024,256]{1,0:T(8,128)(2,1)S(1)} %bitcast.24), channel_id=1, source_target_pairs={{0,1},{1,0},{2,3},{3,2},{4,5},{5,4},{6,7},{7,6},{8,9},{9,8},{10,11... | collective-permute-start | bytes 1572872 | tf_op jit(solution)/shard_map/ppermute | solution.py:35
  114.9 5.6 %collective-permute-done.4.kv1 = bf16[1024,256]{1,0:T(8,128)(2,1)} collective-permute-done((bf16[1024,256]{1,0:T(8,128)(2,1)S(1)}, bf16[1024,256]{1,0:T(8,128)(2,1)}, u32[]{:S(2)}, u32[]{:S(2)}) %collective-permute-start.4) | collective-permute-done | bytes 524320 | tf_op jit(solution)/shard_map/ppermute | solution.py:35
  120.5 5.5 %collective-permute-start.6 = (bf16[1024,256]{1,0:T(8,128)(2,1)}, bf16[1024,256]{1,0:T(8,128)(2,1)}, u32[]{:S(2)}, u32[]{:S(2)}) collective-permute-start(bf16[1024,256]{1,0:T(8,128)(2,1)} %collective-permute-done.4.kv1), channel_id=1, source_target_pairs={{0,1},{1,0},{2,3},{3,2},{4,5},{5,4},{6,7},{7,6},{8,9},{9,8},{10,11... | collective-permute-start | bytes 1572872 | tf_op jit(solution)/shard_map/ppermute | solution.py:35
  126.0 0.0 all-to-all-done.3
  126.0 0.0 copy-start.4
  126.0 2.3 %collective-permute-start.7 = (bf16[1024,256]{1,0:T(8,128)(2,1)S(1)}, bf16[1024,256]{1,0:T(8,128)(2,1)S(1)}, u32[]{:S(2)}, u32[]{:S(2)}) collective-permute-start(bf16[1024,256]{1,0:T(8,128)(2,1)S(1)} %bitcast.19), channel_id=1, source_target_pairs={{0,2},{2,0},{1,3},{3,1},{4,6},{6,4},{5,7},{7,5},{8,10},{10,8},{9,1... | collective-permute-start | bytes 1572872 | tf_op jit(solution)/shard_map/ppermute | solution.py:35
  128.4 0.0 collective-permute-done.5.kv2
  128.4 0.0 collective-permute-done.6.kv3
  128.4 0.0 copy-start.6
  128.4 0.7 copy-done.6
  129.2 0.8 copy-done.8
  129.9 3.5 %attention_rows.1 = (bf16[128,128]{1,0:T(8,128)(2,1)}, f32[2,128]{1,0:T(2,128)S(1)}, bf16[128,128]{1,0:T(8,128)(2,1)S(1)}) custom-call(bf16[128,128]{1,0:T(8,128)(2,1)S(1)} %copy-done.6, bf16[1024,256]{1,0:T(8,128)(2,1)S(1)} %bitcast.25, bf16[1024,256]{1,0:T(8,128)(2,1)} %collective-permute-done.4.kv1, bf16[1024,256]{1,0:T(8,128)(2,1)} %collective-permute-done.5.kv2, ...), custom_call_target="tpu_custom_call" | custom-call | tf_op jit(solution)/shard_map/attention_rows/pallas_call | solution.py:212
  133.5 8.1 %collective-permute-done.7.qc1 = bf16[1024,256]{1,0:T(8,128)(2,1)S(1)} collective-permute-done((bf16[1024,256]{1,0:T(8,128)(2,1)S(1)}, bf16[1024,256]{1,0:T(8,128)(2,1)S(1)}, u32[]{:S(2)}, u32[]{:S(2)}) %collective-permute-start.7) | collective-permute-done | bytes 524320 | tf_op jit(solution)/shard_map/ppermute | solution.py:35
  141.6 2.8 %collective-permute-start.8 = (bf16[1024,256]{1,0:T(8,128)(2,1)S(1)}, bf16[1024,256]{1,0:T(8,128)(2,1)S(1)}, u32[]{:S(2)}, u32[]{:S(2)}) collective-permute-start(bf16[1024,256]{1,0:T(8,128)(2,1)S(1)} %bitcast.20), channel_id=1, source_target_pairs={{0,1},{1,0},{2,3},{3,2},{4,5},{5,4},{6,7},{7,6},{8,9},{9,8},{10,11... | collective-permute-start | bytes 1572872 | tf_op jit(solution)/shard_map/ppermute | solution.py:35
  144.3 1.9 collective-permute-start.9
  146.3 15.4 %all_to_all.41.stats_ref = f32[32,2,128]{2,1,0:T(2,128)S(1)} all-to-all(f32[32,2,128]{2,1,0:T(2,128)S(1)} %broadcast_in_dim.15), channel_id=1, replica_groups=mesh['xh'=2,'yh'=4,'yl'=2,'zh'=4,'zl'=2,'xl'=2,'core'=2] {'zh','zl','xl'..., dimensions={0} | all-to-all | bytes 65536 | tf_op jit(solution)/shard_map/all_to_all | solution.py:27
  161.7 0.0 collective-permute-done.8.qc2
  161.7 0.0 collective-permute-done.9.qc3
  161.7 1.6 attention_columns.1
  163.3 0.1 broadcast_in_dim.16
  163.3 15.7 %all_to_all.42 = bf16[8,128,384]{2,1,0:T(8,128)(2,1)S(1)} all-to-all(bf16[8,128,384]{2,1,0:T(8,128)(2,1)S(1)} %broadcast_in_dim.16), channel_id=1, replica_groups=mesh['xh'=2,'yh'=4,'yl'=2,'zh'=4,'zl'=2,'xl'=2,'core'=2] {'xh','yl','zl'}, dimensions={0} | all-to-all | bytes 1572864 | tf_op jit(solution)/shard_map/all_to_all | solution.py:27
  179.0 0.7 weight_gradient.3
  179.7 3.8 %collective-permute-start.10 = (bf16[4,128,384]{2,1,0:T(8,128)(2,1)S(1)}, bf16[4,128,384]{2,1,0:T(8,128)(2,1)S(1)}, u32[]{:S(2)}, u32[]{:S(2)}) collective-permute-start(bf16[4,128,384]{2,1,0:T(8,128)(2,1)S(1)} %weight_gradient.3), channel_id=1, source_target_pairs={{0,1},{1,0},{2,3},{3,2},{4,5},{5,4},{6,7},{7,6},{8,9},{9,8},{10,11... | collective-permute-start | bytes 1179656 | tf_op jit(solution)/shard_map/ppermute | solution.py:35
  183.5 0.7 weight_gradient.2
  184.3 0.6 collective-permute-done.10
  184.8 0.1 add_convert_fusion
  184.9 21.0 %all_to_all.43 = bf16[32,16,384]{2,1,0:T(8,128)(2,1)S(1)} all-to-all(bf16[32,16,384]{2,1,0:T(8,128)(2,1)S(1)} %bitcast.29), channel_id=1, replica_groups=mesh['xh'=2,'yh'=4,'yl'=2,'zh'=4,'zl'=2,'xl'=2,'core'=2] {'yh','zh','xl'}, dimensions={0} | all-to-all | bytes 786432 | tf_op jit(solution)/shard_map/all_to_all | solution.py:27
  205.9 0.1 reduce_sum.25
  206.0 20.0 %all_to_all.44 = bf16[32,16,384]{2,1,0:T(8,128)(2,1)S(1)} all-to-all(bf16[32,16,384]{2,1,0:T(8,128)(2,1)S(1)} %broadcast_in_dim.17), channel_id=1, replica_groups=mesh['xh'=2,'yh'=4,'yl'=2,'zh'=4,'zl'=2,'xl'=2,'core'=2] {'zh','zl','xl'..., dimensions={0} | all-to-all | bytes 786432 | tf_op jit(solution)/shard_map/all_to_all | solution.py:27
  226.0 0.8 copy.5
  (10 shorter events, 0.1 us)
Async XLA Ops:
  0.6 11.2 %copy-start = (bf16[512,384]{1,0:T(8,128)(2,1)S(1)}, bf16[512,384]{1,0:T(8,128)(2,1)}, u32[]{:S(2)}) copy-start(bf16[512,384]{1,0:T(8,128)(2,1)} %param.4) | copy-start | bytes 1179652
  0.6 1.6 copy-start.2
  2.8 1.3 copy-start.1
  4.2 51.6 %all-to-all-start = ((bf16[8,128,1024]{2,1,0:T(8,128)(2,1)}), bf16[8,128,1024]{2,1,0:T(8,128)(2,1)S(1)}, u32[]{:S(2)}, u32[]{:S(2)}) async-start(bf16[8,128,1024]{2,1,0:T(8,128)(2,1)} %copy-done.1), calls=%async_computation | async-start | bytes 4194304 | tf_op jit(solution)/shard_map/all_to_all | solution.py:27
  11.9 12.8 %collective-permute-start.2 = (bf16[128,384]{1,0:T(8,128)(2,1)S(1)}, bf16[128,384]{1,0:T(8,128)(2,1)S(1)}, u32[]{:S(2)}, u32[]{:S(2)}) collective-permute-start(bf16[128,384]{1,0:T(8,128)(2,1)S(1)} %constant_dynamic-slice_fusion), channel_id=1, source_target_pairs={{0,192},{64,0},{128,64},{192,128},{1,193},{65,1},{129,65},{193,129... | collective-permute-start | bytes 294920 | tf_op jit(solution)/shard_map/ppermute | solution.py:185
  16.9 31.1 %collective-permute-start.1 = (bf16[128,384]{1,0:T(8,128)(2,1)S(1)}, bf16[128,384]{1,0:T(8,128)(2,1)S(1)}, u32[]{:S(2)}, u32[]{:S(2)}) collective-permute-start(bf16[128,384]{1,0:T(8,128)(2,1)S(1)} %constant_dynamic-slice_fusion), channel_id=1, source_target_pairs={{0,128},{64,192},{128,0},{192,64},{1,129},{65,193},{129,1},{193,65... | collective-permute-start | bytes 294920 | tf_op jit(solution)/shard_map/ppermute | solution.py:185
  21.3 29.2 %collective-permute-start = (bf16[128,384]{1,0:T(8,128)(2,1)S(1)}, bf16[128,384]{1,0:T(8,128)(2,1)S(1)}, u32[]{:S(2)}, u32[]{:S(2)}) collective-permute-start(bf16[128,384]{1,0:T(8,128)(2,1)S(1)} %constant_dynamic-slice_fusion), channel_id=1, source_target_pairs={{0,64},{64,128},{128,192},{192,0},{1,65},{65,129},{129,193},{193,1... | collective-permute-start | bytes 294920 | tf_op jit(solution)/shard_map/ppermute | solution.py:185
  50.6 5.2 %collective-permute-start.3 = (bf16[512,384]{1,0:T(8,128)(2,1)S(1)}, bf16[512,384]{1,0:T(8,128)(2,1)S(1)}, u32[]{:S(2)}, u32[]{:S(2)}) collective-permute-start(bf16[512,384]{1,0:T(8,128)(2,1)S(1)} %pad_maximum_fusion.near_ref), channel_id=1, source_target_pairs={{0,1},{1,0},{2,3},{3,2},{4,5},{5,4},{6,7},{7,6},{8,9},{9,8},{10,11... | collective-permute-start | bytes 1179656 | tf_op jit(solution)/shard_map/ppermute | solution.py:35
  57.1 31.4 %copy-start.7 = (bf16[1,128,128]{2,1,0:T(8,128)(2,1)S(1)}, bf16[1,128,128]{2,1,0:T(8,128)(2,1)}, u32[]{:S(2)}) copy-start(bf16[1,128,128]{2,1,0:T(8,128)(2,1)} %param.5) | copy-start | bytes 98308
  77.1 1.5 copy-start.9
  77.9 0.6 copy-start.3
  78.5 24.9 %all-to-all-start.2 = ((bf16[8,128,256]{2,1,0:T(8,128)(2,1)}), bf16[8,128,256]{2,1,0:T(8,128)(2,1)S(1)}, u32[]{:S(2)}, u32[]{:S(2)}) async-start(bf16[8,128,256]{2,1,0:T(8,128)(2,1)} %broadcast_in_dim.12), calls=%async_computation.2 | async-start | bytes 1048576 | tf_op jit(solution)/shard_map/all_to_all | solution.py:27
  88.5 0.6 copy-start.5
  104.3 21.7 %all-to-all-start.3 = ((bf16[8,128,256]{2,1,0:T(8,128)(2,1)}), bf16[8,128,256]{2,1,0:T(8,128)(2,1)S(1)}, u32[]{:S(2)}, u32[]{:S(2)}) async-start(bf16[8,128,256]{2,1,0:T(8,128)(2,1)} %broadcast_in_dim.14), calls=%async_computation.3 | async-start | bytes 1048576 | tf_op jit(solution)/shard_map/all_to_all | solution.py:27
  107.8 12.7 %collective-permute-start.4 = (bf16[1024,256]{1,0:T(8,128)(2,1)S(1)}, bf16[1024,256]{1,0:T(8,128)(2,1)}, u32[]{:S(2)}, u32[]{:S(2)}) collective-permute-start(bf16[1024,256]{1,0:T(8,128)(2,1)S(1)} %bitcast.23), channel_id=1, source_target_pairs={{0,2},{2,0},{1,3},{3,1},{4,6},{6,4},{5,7},{7,5},{8,10},{10,8},{9,1... | collective-permute-start | bytes 1572872 | tf_op jit(solution)/shard_map/ppermute | solution.py:35
  110.0 18.4 %collective-permute-start.5 = (bf16[1024,256]{1,0:T(8,128)(2,1)S(1)}, bf16[1024,256]{1,0:T(8,128)(2,1)}, u32[]{:S(2)}, u32[]{:S(2)}) collective-permute-start(bf16[1024,256]{1,0:T(8,128)(2,1)S(1)} %bitcast.24), channel_id=1, source_target_pairs={{0,1},{1,0},{2,3},{3,2},{4,5},{5,4},{6,7},{7,6},{8,9},{9,8},{10,11... | collective-permute-start | bytes 1572872 | tf_op jit(solution)/shard_map/ppermute | solution.py:35
  120.5 7.9 %collective-permute-start.6 = (bf16[1024,256]{1,0:T(8,128)(2,1)}, bf16[1024,256]{1,0:T(8,128)(2,1)}, u32[]{:S(2)}, u32[]{:S(2)}) collective-permute-start(bf16[1024,256]{1,0:T(8,128)(2,1)} %collective-permute-done.4.kv1), channel_id=1, source_target_pairs={{0,1},{1,0},{2,3},{3,2},{4,5},{5,4},{6,7},{7,6},{8,9},{9,8},{10,11... | collective-permute-start | bytes 1572872 | tf_op jit(solution)/shard_map/ppermute | solution.py:35
  126.0 35.6 %copy-start.4 = (bf16[128,256]{1,0:T(8,128)(2,1)S(1)}, bf16[128,256]{1,0:T(8,128)(2,1)}, u32[]{:S(2)}) copy-start(bf16[128,256]{1,0:T(8,128)(2,1)} %copy-done.3) | copy-start | bytes 196612
  126.0 15.5 %collective-permute-start.7 = (bf16[1024,256]{1,0:T(8,128)(2,1)S(1)}, bf16[1024,256]{1,0:T(8,128)(2,1)S(1)}, u32[]{:S(2)}, u32[]{:S(2)}) collective-permute-start(bf16[1024,256]{1,0:T(8,128)(2,1)S(1)} %bitcast.19), channel_id=1, source_target_pairs={{0,2},{2,0},{1,3},{3,1},{4,6},{6,4},{5,7},{7,5},{8,10},{10,8},{9,1... | collective-permute-start | bytes 1572872 | tf_op jit(solution)/shard_map/ppermute | solution.py:35
  128.4 0.8 copy-start.6
  129.2 0.8 copy-start.8
  141.6 20.1 %collective-permute-start.8 = (bf16[1024,256]{1,0:T(8,128)(2,1)S(1)}, bf16[1024,256]{1,0:T(8,128)(2,1)S(1)}, u32[]{:S(2)}, u32[]{:S(2)}) collective-permute-start(bf16[1024,256]{1,0:T(8,128)(2,1)S(1)} %bitcast.20), channel_id=1, source_target_pairs={{0,1},{1,0},{2,3},{3,2},{4,5},{5,4},{6,7},{7,6},{8,9},{9,8},{10,11... | collective-permute-start | bytes 1572872 | tf_op jit(solution)/shard_map/ppermute | solution.py:35
  144.3 17.4 %collective-permute-start.9 = (bf16[1024,256]{1,0:T(8,128)(2,1)S(1)}, bf16[1024,256]{1,0:T(8,128)(2,1)S(1)}, u32[]{:S(2)}, u32[]{:S(2)}) collective-permute-start(bf16[1024,256]{1,0:T(8,128)(2,1)S(1)} %collective-permute-done.7.qc1), channel_id=1, source_target_pairs={{0,1},{1,0},{2,3},{3,2},{4,5},{5,4},{6,7},{7,6},{8,9},{9,8},{10,11... | collective-permute-start | bytes 1572872 | tf_op jit(solution)/shard_map/ppermute | solution.py:35
  179.7 5.1 %collective-permute-start.10 = (bf16[4,128,384]{2,1,0:T(8,128)(2,1)S(1)}, bf16[4,128,384]{2,1,0:T(8,128)(2,1)S(1)}, u32[]{:S(2)}, u32[]{:S(2)}) collective-permute-start(bf16[4,128,384]{2,1,0:T(8,128)(2,1)S(1)} %weight_gradient.3), channel_id=1, source_target_pairs={{0,1},{1,0},{2,3},{3,2},{4,5},{5,4},{6,7},{7,6},{8,9},{9,8},{10,11... | collective-permute-start | bytes 1179656 | tf_op jit(solution)/shard_map/ppermute | solution.py:35

commit v4 on v3

--- a/solution.py
+++ b/solution.py
@@ -99,7 +99,7 @@
     dq_ref[...] = (grad * scale).astype(low)
 
 
-def backward_kernel(z_count, kv_ref, qc0, qc1, qc2, qc3, stats_ref, out_ref):
+def backward_kernel(z_count, kv_ref, q0, q1, q2, q3, cot_ref, stats_ref, out_ref):
     rows, head = kv_ref.shape[0], kv_ref.shape[1] // 2
     half_rows, ctx_count = rows // 2, 4 * z_count
     scale = 1.0 / math.sqrt(head)
@@ -110,9 +110,10 @@
     keys, values = kv_ref[:, :head], kv_ref[:, head:]
     grad_key = jnp.zeros((rows, head), jnp.float32)
     grad_value = jnp.zeros((rows, head), jnp.float32)
-    for piece, both in enumerate((qc0, qc1, qc2, qc3)):
+    for piece, queries_ref in enumerate((q0, q1, q2, q3)):
         slot = piece_device(piece, 0)
-        queries, cotangent = both[:, :head], both[:, head:]
+        queries = queries_ref[...]
+        cotangent = jnp.concatenate([cot_ref[4 * z + slot] for z in range(z_count)], axis=0)
         scores = dot_f32(keys, queries, 1, 1) * scale
         dprob = dot_f32(values, cotangent, 1, 1)
         probs, dscores = [], []
@@ -177,13 +178,20 @@
     quarter, depth, group_rows = shard // 4, model // 16, 8 * row_count
     cotangent = out_grad[0]
 
-    at = (lax.axis_index("zl") * 2 + lax.axis_index("core")) * quarter
-    own_weight = lax.dynamic_slice_in_dim(qkv_weight, at, quarter)
+    x_lo, half_quarter = lax.axis_index("xl"), quarter // 2
+    at = (lax.axis_index("zl") * 2 + lax.axis_index("core")) * quarter + x_lo * half_quarter
+    own_weight = lax.dynamic_slice_in_dim(qkv_weight, at, half_quarter)
     steps = [own_weight]
     for step in range(1, y_half):
         ring = [(i, (i + step) % y_half) for i in range(y_half)]
         steps.append(lax.ppermute(own_weight, "yh", ring))
-    near = jnp.concatenate(steps)
+    fetched = jnp.stack(steps)
+    other = swap(fetched, "xl")
+    near = jnp.where(
+        x_lo == 0,
+        jnp.concatenate([fetched, other], axis=1),
+        jnp.concatenate([other, fetched], axis=1),
+    ).reshape(depth, width)
     far = swap(near, "core")
     split = pl.pallas_call(
         functools.partial(relayout_kernel, y_half),
@@ -207,7 +215,10 @@
     queries, own_pairs = qkv[:, :head], qkv[:, head:]
     pair_pieces = gather_x(own_pairs)
     pair_pieces = pair_pieces + tuple(swap(p, "core") for p in pair_pieces)
-    query_pieces = gather_x(jnp.concatenate([queries, cotangent], axis=1))
+    query_pieces = gather_x(queries)
+    pair_pieces, cotangent_all = lax.optimization_barrier(
+        (pair_pieces, lax.all_gather(cotangent, ctx_axes, axis=0, tiled=False))
+    )
 
     attn_rows, stats, grad_query = pl.pallas_call(
         functools.partial(forward_kernel, z_count),
@@ -223,18 +234,18 @@
         name="attention_rows",
     )(queries, *pair_pieces, cotangent)
 
-    query_pieces, stats = lax.optimization_barrier((query_pieces, stats))
+    stats_all = spread(stats, ctx_axes, ctx_count)
+    query_pieces, stats_all = lax.optimization_barrier((query_pieces, stats_all))
     query_pieces = query_pieces + tuple(swap(p, "core") for p in query_pieces)
-    stats_all = spread(stats, ctx_axes, ctx_count)
 
     grad_pairs = pl.pallas_call(
         functools.partial(backward_kernel, z_count),
-        in_specs=in_vmem(6),
+        in_specs=in_vmem(7),
         out_specs=in_vmem(1)[0],
         out_shape=jax.ShapeDtypeStruct((row_count, 2 * head), low),
         compiler_params=vmem,
         name="attention_columns",
-    )(own_pairs, *query_pieces, stats_all)
+    )(own_pairs, *query_pieces, cotangent_all, stats_all)
 
     grad_all = spread(jnp.concatenate([grad_query, grad_pairs], axis=1), group_axes, 8)
     grad_all = grad_all.reshape(group_rows, width)
@@ -257,8 +268,11 @@
     summed = (weight_half(0, jnp.float32) + sent.astype(jnp.float32)).astype(low)
     pieces = exchange(summed.reshape(8 * y_half, -1, width), ("yh", "zh", "xl"))
     own_piece = jnp.sum(pieces.astype(jnp.float32), axis=0).astype(low)
-    total = spread(own_piece, ctx_axes, ctx_count)
-    total = total.reshape((z_count // 2, 2, 2, 2) + own_piece.shape).transpose(1, 3, 0, 2, 4, 5)
+    on_core = spread(own_piece, z_axes + ("xl",), 2 * z_count)
+    on_core = on_core.reshape((z_count // 2, 2, 2) + own_piece.shape).transpose(1, 0, 2, 3, 4)
+    across = swap(on_core, "core")
+    first = lax.axis_index("core") == 0
+    total = jnp.stack([jnp.where(first, on_core, across), jnp.where(first, across, on_core)], axis=1)
     return (attn_rows[None], total.reshape(shard, width))
 
 

time: 228 us -> 251 us (1.10)
  starting transfers between devices: 60.4 us -> 75.3 us
  blocking collectives: 91.9 us -> 77.1 us
  between operations: 0.94 us -> 14.3 us
  waiting for transfers between devices: 55.9 us -> 65.8 us
  local copies, waits for them, and re-layouts: 9.1 us -> 6.52 us
    all_to_all x5 -> x4, blocking collectives: 91.9 us -> 77.1 us  [exchange(): return lax.all_to_all(blocks, axes, split_axis=0, concat_axis=0, tiled=True)]
    all_gather x0 -> x1, waiting for transfers between devices: none -> 14.4 us  [on_device(): lax.all_gather(cotangent, ctx_axes, axis=0, tiled=False)]
    ppermute x8 -> x10, starting transfers between devices: 27.3 us -> 37.3 us  [swap(): return lax.ppermute(block, axis, ((0, 1), (1, 0)))]
    ppermute x8 -> x10, waiting for transfers between devices: 15.6 us -> 8.49 us  [swap(): return lax.ppermute(block, axis, ((0, 1), (1, 0)))]
    all_to_all x3 -> x4, waiting for transfers between devices: 14.4 us -> 21 us  [exchange(): return lax.all_to_all(blocks, axes, split_axis=0, concat_axis=0, tiled=True)]
    all_to_all x3 -> x4, starting transfers between devices: 20.3 us -> 25.2 us  [exchange(): return lax.all_to_all(blocks, axes, split_axis=0, concat_axis=0, tiled=True)]
    ppermute x3, waiting for transfers between devices: 25.9 us -> 21.3 us  [on_device(): steps.append(lax.ppermute(own_weight, 'yh', ring))]
    unnamed x20 -> x10, local copies, waits for them, and re-layouts: 5.72 us -> 4.2 us
  transfers between devices with their start and end apart: 14 -> 18, of which waited for: 7 -> 10; matrix products, arithmetic and copies ran while one was open for 0% -> 1% of each run, Pallas kernels for 2% -> 2%
where the time goes in v4:
time: 251 us; the launch traced here: 250 us
  blocking collectives  77.1 us (31%)
  starting transfers between devices  75.3 us (30%)
  waiting for transfers between devices  65.8 us (26%)
  between operations  14.3 us (6%)
  Pallas kernels  10.2 us (4%)
  local copies, waits for them, and re-layouts  6.52 us (3%)
    all_to_all x4, blocking collectives, exchange(): return lax.all_to_all(blocks, axes, split_axis=0, concat_axis=0, tiled=True)  77.1 us
    ppermute x10, starting transfers between devices, swap(): return lax.ppermute(block, axis, ((0, 1), (1, 0)))  37.3 us
    all_to_all x4, starting transfers between devices, exchange(): return lax.all_to_all(blocks, axes, split_axis=0, concat_axis=0, tiled=True)  25.2 us
    ppermute x3, waiting for transfers between devices, on_device(): steps.append(lax.ppermute(own_weight, 'yh', ring))  21.3 us
    all_to_all x4, waiting for transfers between devices, exchange(): return lax.all_to_all(blocks, axes, split_axis=0, concat_axis=0, tiled=True)  21 us
    all_gather x1, waiting for transfers between devices, on_device(): lax.all_gather(cotangent, ctx_axes, axis=0, tiled=False)  14.4 us
    ppermute x3, starting transfers between devices, on_device(): steps.append(lax.ppermute(own_weight, 'yh', ring))  12.7 us
    ppermute x10, waiting for transfers between devices, swap(): return lax.ppermute(block, axis, ((0, 1), (1, 0)))  8.49 us
  transfers between devices with their start and end apart: 18, of which 10 were waited for; matrix products, arithmetic and copies ran while one was open for 1% of the time, Pallas kernels for 2%

profile of v4, /device:TPU:1, one launch (start us, length us, event | category | flops | bytes accessed | tf_op | source)
XLA Modules:
  0.0 249.8 jit_solution(469223131830223653)
XLA Ops:
  7.2 0.0 copy-start
  7.2 0.0 copy-start.2
  7.2 1.6 copy-done.2
  8.8 0.6 token_columns.1
  9.4 0.0 copy-start.1
  9.4 1.3 copy-done.1
  10.7 7.7 %all-to-all-start = ((bf16[8,128,1024]{2,1,0:T(8,128)(2,1)}), bf16[8,128,1024]{2,1,0:T(8,128)(2,1)S(1)}, u32[]{:S(2)}, u32[]{:S(2)}) async-start(bf16[8,128,1024]{2,1,0:T(8,128)(2,1)} %copy-done.1), calls=%async_computation | async-start | bytes 4194304 | tf_op jit(solution)/shard_map/all_to_all | solution.py:27
  18.4 0.0 copy-done
  18.4 5.0 %collective-permute-start.2 = (bf16[64,384]{1,0:T(8,128)(2,1)S(1)}, bf16[64,384]{1,0:T(8,128)(2,1)S(1)}, u32[]{:S(2)}, u32[]{:S(2)}) collective-permute-start(bf16[64,384]{1,0:T(8,128)(2,1)S(1)} %constant_dynamic-slice_fusion), channel_id=1, source_target_pairs={{0,192},{64,0},{128,64},{192,128},{1,193},{65,1},{129,65},{193,129... | collective-permute-start | bytes 147464 | tf_op jit(solution)/shard_map/ppermute | solution.py:187
  23.4 4.4 %collective-permute-start.1 = (bf16[64,384]{1,0:T(8,128)(2,1)S(1)}, bf16[64,384]{1,0:T(8,128)(2,1)S(1)}, u32[]{:S(2)}, u32[]{:S(2)}) collective-permute-start(bf16[64,384]{1,0:T(8,128)(2,1)S(1)} %constant_dynamic-slice_fusion), channel_id=1, source_target_pairs={{0,128},{64,192},{128,0},{192,64},{1,129},{65,193},{129,1},{193,65... | collective-permute-start | bytes 147464 | tf_op jit(solution)/shard_map/ppermute | solution.py:187
  27.8 3.3 %collective-permute-start = (bf16[64,384]{1,0:T(8,128)(2,1)S(1)}, bf16[64,384]{1,0:T(8,128)(2,1)S(1)}, u32[]{:S(2)}, u32[]{:S(2)}) collective-permute-start(bf16[64,384]{1,0:T(8,128)(2,1)S(1)} %constant_dynamic-slice_fusion), channel_id=1, source_target_pairs={{0,64},{64,128},{128,192},{192,0},{1,65},{65,129},{129,193},{193,1... | collective-permute-start | bytes 147464 | tf_op jit(solution)/shard_map/ppermute | solution.py:187
  31.2 0.0 collective-permute-done.2
  31.2 20.9 %collective-permute-done.1 = bf16[64,384]{1,0:T(8,128)(2,1)S(1)} collective-permute-done((bf16[64,384]{1,0:T(8,128)(2,1)S(1)}, bf16[64,384]{1,0:T(8,128)(2,1)S(1)}, u32[]{:S(2)}, u32[]{:S(2)}) %collective-permute-start.1) | collective-permute-done | bytes 49184 | tf_op jit(solution)/shard_map/ppermute | solution.py:187
  52.1 0.4 collective-permute-done
  52.5 2.5 collective-permute-start.3
  55.0 3.9 %collective-permute-done.3 = bf16[4,64,384]{2,1,0:T(8,128)(2,1)S(1)} collective-permute-done((bf16[4,64,384]{2,1,0:T(8,128)(2,1)S(1)}, bf16[4,64,384]{2,1,0:T(8,128)(2,1)S(1)}, u32[]{:S(2)}, u32[]{:S(2)}) %collective-permute-start.3) | collective-permute-done | bytes 196640 | tf_op jit(solution)/shard_map/ppermute | solution.py:35
  58.9 0.1 maximum_select_fusion
  59.1 5.6 %collective-permute-start.4 = (bf16[512,384]{1,0:T(8,128)(2,1)S(1)}, bf16[512,384]{1,0:T(8,128)(2,1)S(1)}, u32[]{:S(2)}, u32[]{:S(2)}) collective-permute-start(bf16[512,384]{1,0:T(8,128)(2,1)S(1)} %bitcast.32), channel_id=1, source_target_pairs={{0,1},{1,0},{2,3},{3,2},{4,5},{5,4},{6,7},{7,6},{8,9},{9,8},{10,11... | collective-permute-start | bytes 1179656 | tf_op jit(solution)/shard_map/ppermute | solution.py:35
  64.7 1.3 collective-permute-done.4.far_ref
  66.0 0.0 all-to-all-done
  66.0 2.2 partial_projection.1
  68.2 7.1 %all-to-all-start.1 = ((bf16[8,128,384]{2,1,0:T(8,128)(2,1)}), bf16[8,128,384]{2,1,0:T(8,128)(2,1)S(1)}, u32[]{:S(2)}, u32[]{:S(2)}) async-start(bf16[8,128,384]{2,1,0:T(8,128)(2,1)} %bitcast.7), calls=%async_computation.1 | async-start | bytes 1572864 | tf_op jit(solution)/shard_map/all_to_all | solution.py:27
  75.3 0.0 copy-start.4
  75.3 0.0 all-gather.2.cloned.1.call-start
  75.4 0.7 all-gather.2.cloned.1.call-update
  76.1 12.9 %all-to-all-done.1 = bf16[8,128,384]{2,1,0:T(8,128)(2,1)S(1)} async-done(((bf16[8,128,384]{2,1,0:T(8,128)(2,1)}), bf16[8,128,384]{2,1,0:T(8,128)(2,1)S(1)}, u32[]{:S(2)}, u32[]{:S(2)}) %all-to-all-start.1) | async-done | bytes 786464 | tf_op jit(solution)/shard_map/all_to_all | solution.py:27
  88.9 0.1 reduce_sum.24
  89.1 24.1 %all_to_all.40 = bf16[8,128,256]{2,1,0:T(8,128)(2,1)S(1)} all-to-all(bf16[8,128,256]{2,1,0:T(8,128)(2,1)S(1)} %broadcast_in_dim.12), channel_id=1, replica_groups=mesh['xh'=2,'yh'=4,'yl'=2,'zh'=4,'zl'=2,'xl'=2,'core'=2] {'zh','zl'}, dimensions={0} | all-to-all | bytes 1048576 | tf_op jit(solution)/shard_map/all_to_all | solution.py:27
  113.2 2.0 collective-permute-start.5
  115.3 0.7 broadcast_in_dim.14
  116.0 4.3 %all-to-all-start.3 = ((bf16[8,128,128]{2,1,0:T(8,128)(2,1)}), bf16[8,128,128]{2,1,0:T(8,128)(2,1)S(1)}, u32[]{:S(2)}, u32[]{:S(2)}) async-start(bf16[8,128,128]{2,1,0:T(8,128)(2,1)} %broadcast_in_dim.14), calls=%async_computation.3 | async-start | bytes 524288 | tf_op jit(solution)/shard_map/all_to_all | solution.py:27
  120.3 6.0 %collective-permute-start.6 = (bf16[1024,256]{1,0:T(8,128)(2,1)S(1)}, bf16[1024,256]{1,0:T(8,128)(2,1)}, u32[]{:S(2)}, u32[]{:S(2)}) collective-permute-start(bf16[1024,256]{1,0:T(8,128)(2,1)S(1)} %bitcast.30), channel_id=1, source_target_pairs={{0,1},{1,0},{2,3},{3,2},{4,5},{5,4},{6,7},{7,6},{8,9},{9,8},{10,11... | collective-permute-start | bytes 1572872 | tf_op jit(solution)/shard_map/ppermute | solution.py:35
  126.3 0.0 collective-permute-done.5.kv1
  126.3 6.3 %collective-permute-start.7 = (bf16[1024,256]{1,0:T(8,128)(2,1)}, bf16[1024,256]{1,0:T(8,128)(2,1)}, u32[]{:S(2)}, u32[]{:S(2)}) collective-permute-start(bf16[1024,256]{1,0:T(8,128)(2,1)} %collective-permute-done.5.kv1), channel_id=1, source_target_pairs={{0,1},{1,0},{2,3},{3,2},{4,5},{5,4},{6,7},{7,6},{8,9},{9,8},{10,11... | collective-permute-start | bytes 1572872 | tf_op jit(solution)/shard_map/ppermute | solution.py:35
  132.7 0.0 all-to-all-done.3
  132.7 2.3 collective-permute-start.8
  134.9 14.4 %all-gather.2.cloned.1.call-done.cot_ref = bf16[32,128,128]{2,1,0:T(8,128)(2,1)} async-done(((bf16[1,128,128]{2,1,0:T(8,128)(2,1)}), bf16[32,128,128]{2,1,0:T(8,128)(2,1)}) %all-gather.2.cloned.1.call-update) | async-done | bytes 1048592 | tf_op jit(solution)/shard_map/all_gather | solution.py:220
  149.3 0.0 collective-permute-done.6.kv2
  149.3 0.0 collective-permute-done.7.kv3
  149.3 0.0 copy-done.4
  149.3 3.5 %attention_rows.1 = (bf16[128,128]{1,0:T(8,128)(2,1)}, f32[2,128]{1,0:T(2,128)S(1)}, bf16[128,128]{1,0:T(8,128)(2,1)S(1)}) custom-call(bf16[128,128]{1,0:T(8,128)(2,1)S(1)} %slice.8.q_ref, bf16[1024,256]{1,0:T(8,128)(2,1)S(1)} %bitcast.31, bf16[1024,256]{1,0:T(8,128)(2,1)} %collective-permute-done.5.kv1, bf16[1024,256]{1,0:T(8,128)(2,1)} %collective-permute-done.6.kv2, ...), custom_call_target="tpu_custom_call" | custom-call | tf_op jit(solution)/shard_map/attention_rows/pallas_call | solution.py:223
  152.9 0.6 broadcast_in_dim.15
  153.5 6.2 %all-to-all-start.4 = ((f32[32,2,128]{2,1,0:T(2,128)}), f32[32,2,128]{2,1,0:T(2,128)S(1)}, u32[]{:S(2)}, u32[]{:S(2)}) async-start(f32[32,2,128]{2,1,0:T(2,128)} %broadcast_in_dim.15), calls=%async_computation.4 | async-start | bytes 65536 | tf_op jit(solution)/shard_map/all_to_all | solution.py:27
  159.7 0.0 collective-permute-done.8.q1
  159.7 8.1 %all-to-all-done.4.stats_ref = f32[32,2,128]{2,1,0:T(2,128)S(1)} async-done(((f32[32,2,128]{2,1,0:T(2,128)}), f32[32,2,128]{2,1,0:T(2,128)S(1)}, u32[]{:S(2)}, u32[]{:S(2)}) %all-to-all-start.4) | async-done | bytes 32800 | tf_op jit(solution)/shard_map/all_to_all | solution.py:27
  167.8 2.3 collective-permute-start.9
  170.1 2.0 collective-permute-start.10
  172.1 0.0 collective-permute-done.9.q2
  172.1 1.6 collective-permute-done.10.q3
  173.7 1.2 copy-done.3
  175.0 2.5 attention_columns.1
  177.5 0.1 broadcast_in_dim.16
  177.5 17.3 %all_to_all.41 = bf16[8,128,384]{2,1,0:T(8,128)(2,1)S(1)} all-to-all(bf16[8,128,384]{2,1,0:T(8,128)(2,1)S(1)} %broadcast_in_dim.16), channel_id=1, replica_groups=mesh['xh'=2,'yh'=4,'yl'=2,'zh'=4,'zl'=2,'xl'=2,'core'=2] {'xh','yl','zl'}, dimensions={0} | all-to-all | bytes 1572864 | tf_op jit(solution)/shard_map/all_to_all | solution.py:27
  194.9 0.7 weight_gradient.3
  195.6 3.3 %collective-permute-start.11 = (bf16[4,128,384]{2,1,0:T(8,128)(2,1)S(1)}, bf16[4,128,384]{2,1,0:T(8,128)(2,1)S(1)}, u32[]{:S(2)}, u32[]{:S(2)}) collective-permute-start(bf16[4,128,384]{2,1,0:T(8,128)(2,1)S(1)} %weight_gradient.3), channel_id=1, source_target_pairs={{0,1},{1,0},{2,3},{3,2},{4,5},{5,4},{6,7},{7,6},{8,9},{9,8},{10,11... | collective-permute-start | bytes 1179656 | tf_op jit(solution)/shard_map/ppermute | solution.py:35
  198.9 0.7 weight_gradient.2
  199.7 0.6 collective-permute-done.11
  200.2 0.1 add_convert_fusion
  200.3 24.0 %all_to_all.42 = bf16[32,16,384]{2,1,0:T(8,128)(2,1)S(1)} all-to-all(bf16[32,16,384]{2,1,0:T(8,128)(2,1)S(1)} %bitcast.38), channel_id=1, replica_groups=mesh['xh'=2,'yh'=4,'yl'=2,'zh'=4,'zl'=2,'xl'=2,'core'=2] {'yh','zh','xl'}, dimensions={0} | all-to-all | bytes 786432 | tf_op jit(solution)/shard_map/all_to_all | solution.py:27
  224.3 0.1 reduce_sum.25
  224.4 11.7 %all_to_all.43 = bf16[16,16,384]{2,1,0:T(8,128)(2,1)S(1)} all-to-all(bf16[16,16,384]{2,1,0:T(8,128)(2,1)S(1)} %broadcast_in_dim.17), channel_id=1, replica_groups=mesh['xh'=2,'yh'=4,'yl'=2,'zh'=4,'zl'=2,'xl'=2,'core'=2] {'zh','zl','xl'}, dimensions={0} | all-to-all | bytes 393216 | tf_op jit(solution)/shard_map/all_to_all | solution.py:27
  236.1 5.0 %collective-permute-start.12 = (bf16[2,4,2,16,384]{4,3,2,0,1:T(8,128)(2,1)S(1)}, bf16[2,4,2,16,384]{4,3,2,0,1:T(8,128)(2,1)S(1)}, u32[]{:S(2)}, u32[]{:S(2)}) collective-permute-start(bf16[2,4,2,16,384]{4,3,2,0,1:T(8,128)(2,1)S(1)} %bitcast.39), channel_id=1, source_target_pairs={{0,1},{1,0},{2,3},{3,2},{4,5},{5,4},{6,7},{7,6},{8,9},{9,8},{10,11... | collective-permute-start | bytes 589832 | tf_op jit(solution)/shard_map/ppermute | solution.py:35
  241.0 1.0 collective-permute-done.12
  242.2 0.8 copy.7
  (11 shorter events, 0.2 us)
Async XLA Ops:
  7.2 11.2 %copy-start = (bf16[512,384]{1,0:T(8,128)(2,1)S(1)}, bf16[512,384]{1,0:T(8,128)(2,1)}, u32[]{:S(2)}) copy-start(bf16[512,384]{1,0:T(8,128)(2,1)} %param.4) | copy-start | bytes 1179652
  7.2 1.6 copy-start.2
  9.4 1.3 copy-start.1
  10.7 55.3 %all-to-all-start = ((bf16[8,128,1024]{2,1,0:T(8,128)(2,1)}), bf16[8,128,1024]{2,1,0:T(8,128)(2,1)S(1)}, u32[]{:S(2)}, u32[]{:S(2)}) async-start(bf16[8,128,1024]{2,1,0:T(8,128)(2,1)} %copy-done.1), calls=%async_computation | async-start | bytes 4194304 | tf_op jit(solution)/shard_map/all_to_all | solution.py:27
  18.4 12.8 %collective-permute-start.2 = (bf16[64,384]{1,0:T(8,128)(2,1)S(1)}, bf16[64,384]{1,0:T(8,128)(2,1)S(1)}, u32[]{:S(2)}, u32[]{:S(2)}) collective-permute-start(bf16[64,384]{1,0:T(8,128)(2,1)S(1)} %constant_dynamic-slice_fusion), channel_id=1, source_target_pairs={{0,192},{64,0},{128,64},{192,128},{1,193},{65,1},{129,65},{193,129... | collective-permute-start | bytes 147464 | tf_op jit(solution)/shard_map/ppermute | solution.py:187
  23.4 28.7 %collective-permute-start.1 = (bf16[64,384]{1,0:T(8,128)(2,1)S(1)}, bf16[64,384]{1,0:T(8,128)(2,1)S(1)}, u32[]{:S(2)}, u32[]{:S(2)}) collective-permute-start(bf16[64,384]{1,0:T(8,128)(2,1)S(1)} %constant_dynamic-slice_fusion), channel_id=1, source_target_pairs={{0,128},{64,192},{128,0},{192,64},{1,129},{65,193},{129,1},{193,65... | collective-permute-start | bytes 147464 | tf_op jit(solution)/shard_map/ppermute | solution.py:187
  27.8 24.6 %collective-permute-start = (bf16[64,384]{1,0:T(8,128)(2,1)S(1)}, bf16[64,384]{1,0:T(8,128)(2,1)S(1)}, u32[]{:S(2)}, u32[]{:S(2)}) collective-permute-start(bf16[64,384]{1,0:T(8,128)(2,1)S(1)} %constant_dynamic-slice_fusion), channel_id=1, source_target_pairs={{0,64},{64,128},{128,192},{192,0},{1,65},{65,129},{129,193},{193,1... | collective-permute-start | bytes 147464 | tf_op jit(solution)/shard_map/ppermute | solution.py:187
  52.5 6.4 %collective-permute-start.3 = (bf16[4,64,384]{2,1,0:T(8,128)(2,1)S(1)}, bf16[4,64,384]{2,1,0:T(8,128)(2,1)S(1)}, u32[]{:S(2)}, u32[]{:S(2)}) collective-permute-start(bf16[4,64,384]{2,1,0:T(8,128)(2,1)S(1)} %pad_maximum_fusion.1), channel_id=1, source_target_pairs={{0,2},{2,0},{1,3},{3,1},{4,6},{6,4},{5,7},{7,5},{8,10},{10,8},{9,1... | collective-permute-start | bytes 589832 | tf_op jit(solution)/shard_map/ppermute | solution.py:35
  59.1 6.9 %collective-permute-start.4 = (bf16[512,384]{1,0:T(8,128)(2,1)S(1)}, bf16[512,384]{1,0:T(8,128)(2,1)S(1)}, u32[]{:S(2)}, u32[]{:S(2)}) collective-permute-start(bf16[512,384]{1,0:T(8,128)(2,1)S(1)} %bitcast.32), channel_id=1, source_target_pairs={{0,1},{1,0},{2,3},{3,2},{4,5},{5,4},{6,7},{7,6},{8,9},{9,8},{10,11... | collective-permute-start | bytes 1179656 | tf_op jit(solution)/shard_map/ppermute | solution.py:35
  68.2 20.7 %all-to-all-start.1 = ((bf16[8,128,384]{2,1,0:T(8,128)(2,1)}), bf16[8,128,384]{2,1,0:T(8,128)(2,1)S(1)}, u32[]{:S(2)}, u32[]{:S(2)}) async-start(bf16[8,128,384]{2,1,0:T(8,128)(2,1)} %bitcast.7), calls=%async_computation.1 | async-start | bytes 1572864 | tf_op jit(solution)/shard_map/all_to_all | solution.py:27
  75.3 74.0 %copy-start.4 = (bf16[1,128,128]{2,1,0:T(8,128)(2,1)S(1)}, bf16[1,128,128]{2,1,0:T(8,128)(2,1)}, u32[]{:S(2)}) copy-start(bf16[1,128,128]{2,1,0:T(8,128)(2,1)} %param.5) | copy-start | bytes 98308
  75.3 74.0 %all-gather.2.cloned.1.call-start = ((), (), s32[]{:S(2)}) async-start(), calls=%async_computation.8 | async-start | bytes 1081344 | tf_op jit(solution)/shard_map/all_gather | solution.py:220
  113.2 13.1 %collective-permute-start.5 = (bf16[1024,256]{1,0:T(8,128)(2,1)S(1)}, bf16[1024,256]{1,0:T(8,128)(2,1)}, u32[]{:S(2)}, u32[]{:S(2)}) collective-permute-start(bf16[1024,256]{1,0:T(8,128)(2,1)S(1)} %bitcast.29), channel_id=1, source_target_pairs={{0,2},{2,0},{1,3},{3,1},{4,6},{6,4},{5,7},{7,5},{8,10},{10,8},{9,1... | collective-permute-start | bytes 1572872 | tf_op jit(solution)/shard_map/ppermute | solution.py:35
  116.0 16.7 %all-to-all-start.3 = ((bf16[8,128,128]{2,1,0:T(8,128)(2,1)}), bf16[8,128,128]{2,1,0:T(8,128)(2,1)S(1)}, u32[]{:S(2)}, u32[]{:S(2)}) async-start(bf16[8,128,128]{2,1,0:T(8,128)(2,1)} %broadcast_in_dim.14), calls=%async_computation.3 | async-start | bytes 524288 | tf_op jit(solution)/shard_map/all_to_all | solution.py:27
  120.3 29.0 %collective-permute-start.6 = (bf16[1024,256]{1,0:T(8,128)(2,1)S(1)}, bf16[1024,256]{1,0:T(8,128)(2,1)}, u32[]{:S(2)}, u32[]{:S(2)}) collective-permute-start(bf16[1024,256]{1,0:T(8,128)(2,1)S(1)} %bitcast.30), channel_id=1, source_target_pairs={{0,1},{1,0},{2,3},{3,2},{4,5},{5,4},{6,7},{7,6},{8,9},{9,8},{10,11... | collective-permute-start | bytes 1572872 | tf_op jit(solution)/shard_map/ppermute | solution.py:35
  126.3 23.0 %collective-permute-start.7 = (bf16[1024,256]{1,0:T(8,128)(2,1)}, bf16[1024,256]{1,0:T(8,128)(2,1)}, u32[]{:S(2)}, u32[]{:S(2)}) collective-permute-start(bf16[1024,256]{1,0:T(8,128)(2,1)} %collective-permute-done.5.kv1), channel_id=1, source_target_pairs={{0,1},{1,0},{2,3},{3,2},{4,5},{5,4},{6,7},{7,6},{8,9},{9,8},{10,11... | collective-permute-start | bytes 1572872 | tf_op jit(solution)/shard_map/ppermute | solution.py:35
  132.7 27.0 %collective-permute-start.8 = (bf16[1024,128]{1,0:T(8,128)(2,1)S(1)}, bf16[1024,128]{1,0:T(8,128)(2,1)}, u32[]{:S(2)}, u32[]{:S(2)}) collective-permute-start(bf16[1024,128]{1,0:T(8,128)(2,1)S(1)} %bitcast.34), channel_id=1, source_target_pairs={{0,2},{2,0},{1,3},{3,1},{4,6},{6,4},{5,7},{7,5},{8,10},{10,8},{9,1... | collective-permute-start | bytes 786440 | tf_op jit(solution)/shard_map/ppermute | solution.py:35
  153.5 14.3 %all-to-all-start.4 = ((f32[32,2,128]{2,1,0:T(2,128)}), f32[32,2,128]{2,1,0:T(2,128)S(1)}, u32[]{:S(2)}, u32[]{:S(2)}) async-start(f32[32,2,128]{2,1,0:T(2,128)} %broadcast_in_dim.15), calls=%async_computation.4 | async-start | bytes 65536 | tf_op jit(solution)/shard_map/all_to_all | solution.py:27
  167.8 4.3 %collective-permute-start.9 = (bf16[1024,128]{1,0:T(8,128)(2,1)S(1)}, bf16[1024,128]{1,0:T(8,128)(2,1)S(1)}, u32[]{:S(2)}, u32[]{:S(2)}) collective-permute-start(bf16[1024,128]{1,0:T(8,128)(2,1)S(1)} %bitcast.35), channel_id=1, source_target_pairs={{0,1},{1,0},{2,3},{3,2},{4,5},{5,4},{6,7},{7,6},{8,9},{9,8},{10,11... | collective-permute-start | bytes 786440 | tf_op jit(solution)/shard_map/ppermute | solution.py:35
  170.1 3.6 %collective-permute-start.10 = (bf16[1024,128]{1,0:T(8,128)(2,1)}, bf16[1024,128]{1,0:T(8,128)(2,1)S(1)}, u32[]{:S(2)}, u32[]{:S(2)}) collective-permute-start(bf16[1024,128]{1,0:T(8,128)(2,1)} %collective-permute-done.8.q1), channel_id=1, source_target_pairs={{0,1},{1,0},{2,3},{3,2},{4,5},{5,4},{6,7},{7,6},{8,9},{9,8},{10,11... | collective-permute-start | bytes 786440 | tf_op jit(solution)/shard_map/ppermute | solution.py:35
  173.7 1.2 copy-start.3
  195.6 4.6 %collective-permute-start.11 = (bf16[4,128,384]{2,1,0:T(8,128)(2,1)S(1)}, bf16[4,128,384]{2,1,0:T(8,128)(2,1)S(1)}, u32[]{:S(2)}, u32[]{:S(2)}) collective-permute-start(bf16[4,128,384]{2,1,0:T(8,128)(2,1)S(1)} %weight_gradient.3), channel_id=1, source_target_pairs={{0,1},{1,0},{2,3},{3,2},{4,5},{5,4},{6,7},{7,6},{8,9},{9,8},{10,11... | collective-permute-start | bytes 1179656 | tf_op jit(solution)/shard_map/ppermute | solution.py:35
  236.1 6.0 %collective-permute-start.12 = (bf16[2,4,2,16,384]{4,3,2,0,1:T(8,128)(2,1)S(1)}, bf16[2,4,2,16,384]{4,3,2,0,1:T(8,128)(2,1)S(1)}, u32[]{:S(2)}, u32[]{:S(2)}) collective-permute-start(bf16[2,4,2,16,384]{4,3,2,0,1:T(8,128)(2,1)S(1)} %bitcast.39), channel_id=1, source_target_pairs={{0,1},{1,0},{2,3},{3,2},{4,5},{5,4},{6,7},{7,6},{8,9},{9,8},{10,11... | collective-permute-start | bytes 589832 | tf_op jit(solution)/shard_map/ppermute | solution.py:35
Sparse Core Ops, SparseCore 0:
  78.3 70.9 all-gather.1

commit v5 on v4

--- a/solution.py
+++ b/solution.py
@@ -33,6 +33,11 @@
 
 def swap(block, axis):
     return lax.ppermute(block, axis, ((0, 1), (1, 0)))
+
+
+def doubled(blocks, axis, flip):
+    pairs = [(i, i ^ flip) for i in range(lax.axis_size(axis))]
+    return jnp.concatenate([blocks, lax.ppermute(blocks, axis, pairs)])
 
 
 def gather_x(block):
@@ -103,7 +108,8 @@
     rows, head = kv_ref.shape[0], kv_ref.shape[1] // 2
     half_rows, ctx_count = rows // 2, 4 * z_count
     scale = 1.0 / math.sqrt(head)
-    own = piece_device(0, lax.axis_index(z_axes))
+    z_own = lax.axis_index(z_axes)
+    own = piece_device(0, z_own)
     down = lax.broadcasted_iota(jnp.int32, (rows, rows), 0)
     across = lax.broadcasted_iota(jnp.int32, (rows, rows), 1)
     own_positions = positions(own, down, half_rows, ctx_count)
@@ -113,7 +119,9 @@
     for piece, queries_ref in enumerate((q0, q1, q2, q3)):
         slot = piece_device(piece, 0)
         queries = queries_ref[...]
-        cotangent = jnp.concatenate([cot_ref[4 * z + slot] for z in range(z_count)], axis=0)
+        cotangent = jnp.concatenate(
+            [cot_ref[piece * z_count + (z ^ z_own)] for z in range(z_count)], axis=0
+        )
         scores = dot_f32(keys, queries, 1, 1) * scale
         dprob = dot_f32(values, cotangent, 1, 1)
         probs, dscores = [], []
@@ -132,10 +140,6 @@
     out_ref[:, head:] = grad_value.astype(low)
 
 
-def shard_row(step, count):
-    return lax.rem(lax.axis_index("yh") + count - step, count)
-
-
 def relayout_kernel(y_half, tokens_ref, out_ref):
     members, _, columns = out_ref.shape
     quarter = columns // (2 * y_half)
@@ -144,7 +148,7 @@
         x_hi, y_lo, z_lo = member // 4, member // 2 % 2, member % 2
         for half in range(2):
             for step in range(y_half):
-                shard = (x_hi * y_half + shard_row(step, y_half)) * 2 + y_lo
+                shard = (x_hi * y_half + step) * 2 + y_lo
                 start = (shard * 4 + z_lo * 2 + (core ^ half)) * quarter
                 target = (half * y_half + step) * quarter
                 out_ref[member, :, target : target + quarter] = tokens_ref[
@@ -159,11 +163,8 @@
     out_ref[...] = total.astype(low)
 
 
-def weight_kernel(y_half, x_ref, grad_ref, out_ref):
-    total = dot_f32(x_ref[...], grad_ref[...], 0, 0).astype(out_ref.dtype)
-    quarter = total.shape[0] // y_half
-    for step in range(y_half):
-        out_ref[shard_row(step, y_half)] = total[step * quarter : (step + 1) * quarter]
+def weight_kernel(x_ref, grad_ref, out_ref):
+    out_ref[...] = dot_f32(x_ref[...], grad_ref[...], 0, 0).astype(out_ref.dtype)
 
 
 def in_vmem(count):
@@ -178,21 +179,9 @@
     quarter, depth, group_rows = shard // 4, model // 16, 8 * row_count
     cotangent = out_grad[0]
 
-    x_lo, half_quarter = lax.axis_index("xl"), quarter // 2
-    at = (lax.axis_index("zl") * 2 + lax.axis_index("core")) * quarter + x_lo * half_quarter
-    own_weight = lax.dynamic_slice_in_dim(qkv_weight, at, half_quarter)
-    steps = [own_weight]
-    for step in range(1, y_half):
-        ring = [(i, (i + step) % y_half) for i in range(y_half)]
-        steps.append(lax.ppermute(own_weight, "yh", ring))
-    fetched = jnp.stack(steps)
-    other = swap(fetched, "xl")
-    near = jnp.where(
-        x_lo == 0,
-        jnp.concatenate([fetched, other], axis=1),
-        jnp.concatenate([other, fetched], axis=1),
-    ).reshape(depth, width)
-    far = swap(near, "core")
+    at = (lax.axis_index("zl") * 2 + lax.axis_index("core")) * quarter
+    own_weight = lax.dynamic_slice_in_dim(qkv_weight, at, quarter)
+    near = spread(own_weight, "yh", y_half).reshape(depth, width)
     split = pl.pallas_call(
         functools.partial(relayout_kernel, y_half),
         in_specs=in_vmem(1),
@@ -201,7 +190,13 @@
         compiler_params=vmem,
         name="token_columns",
     )(tokens[0])
+    split, near = lax.optimization_barrier((split, near))
+    far = swap(near, "core")
     columns = exchange(split, group_axes).reshape(group_rows, 2 * depth)
+    cotangent_all = cotangent[None]
+    for axis, flip in (("zl", 1), ("zh", 1), ("zh", 2)):
+        cotangent_all = doubled(cotangent_all, axis, flip)
+    columns, cotangent_all = lax.optimization_barrier((columns, cotangent_all))
     parts = pl.pallas_call(
         project_kernel,
         in_specs=in_vmem(3),
@@ -211,14 +206,13 @@
         name="partial_projection",
     )(columns, near, far)
     parts = exchange(parts.reshape(8, row_count, width), group_axes)
+    cotangent_all = doubled(doubled(cotangent_all, "xl", 1), "core", 1)
+    parts, cotangent_all = lax.optimization_barrier((parts, cotangent_all))
     qkv = jnp.sum(parts.astype(jnp.float32), axis=0).astype(low)
     queries, own_pairs = qkv[:, :head], qkv[:, head:]
     pair_pieces = gather_x(own_pairs)
     pair_pieces = pair_pieces + tuple(swap(p, "core") for p in pair_pieces)
     query_pieces = gather_x(queries)
-    pair_pieces, cotangent_all = lax.optimization_barrier(
-        (pair_pieces, lax.all_gather(cotangent, ctx_axes, axis=0, tiled=False))
-    )
 
     attn_rows, stats, grad_query = pl.pallas_call(
         functools.partial(forward_kernel, z_count),
@@ -252,14 +246,14 @@
 
     def weight_half(half, dtype):
         return pl.pallas_call(
-            functools.partial(weight_kernel, y_half),
+            weight_kernel,
             grid=(1,),
             in_specs=[
                 pl.BlockSpec((group_rows, depth), lambda i: (0, half)),
                 pl.BlockSpec((group_rows, width), lambda i: (0, 0)),
             ],
-            out_specs=pl.BlockSpec((y_half, quarter, width), lambda i: (0, 0, 0)),
-            out_shape=jax.ShapeDtypeStruct((y_half, quarter, width), dtype),
+            out_specs=pl.BlockSpec((depth, width), lambda i: (0, 0)),
+            out_shape=jax.ShapeDtypeStruct((depth, width), dtype),
             compiler_params=vmem,
             name="weight_gradient",
         )(columns, grad_all)

time: 251 us -> 257 us (1.024)
  starting transfers between devices: 75.3 us -> 89.1 us
  between operations: 14.3 us -> 0.98 us
  waiting for transfers between devices: 65.8 us -> 58.5 us
  local copies, waits for them, and re-layouts: 6.52 us -> 12.8 us
  other arithmetic: 0.54 us -> 4.96 us
    ppermute x3 -> x5, waiting for transfers between devices: 21.3 us -> 38.8 us  [doubled(): return jnp.concatenate([blocks, lax.ppermute(blocks, axis, pairs)])]
    all_gather x1 -> x0, waiting for transfers between devices: 14.4 us -> none  [on_device(): lax.all_gather(cotangent, ctx_axes, axis=0, tiled=False)]
    all_to_all x4 -> x5, starting transfers between devices: 25.2 us -> 35.3 us  [exchange(): return lax.all_to_all(blocks, axes, split_axis=0, concat_axis=0, tiled=True)]
    ppermute x3 -> x5, starting transfers between devices: 12.7 us -> 22.6 us  [doubled(): return jnp.concatenate([blocks, lax.ppermute(blocks, axis, pairs)])]
    ppermute x10 -> x9, starting transfers between devices: 37.3 us -> 31.1 us  [swap(): return lax.ppermute(block, axis, ((0, 1), (1, 0)))]
    all_to_all x4 -> x5, waiting for transfers between devices: 21 us -> 15.8 us  [exchange(): return lax.all_to_all(blocks, axes, split_axis=0, concat_axis=0, tiled=True)]
    ppermute x10 -> x9, waiting for transfers between devices: 8.49 us -> 3.94 us  [swap(): return lax.ppermute(block, axis, ((0, 1), (1, 0)))]
    unnamed x10 -> x22, local copies, waits for them, and re-layouts: 4.2 us -> 8.1 us
  transfers between devices with their start and end apart: 18 -> 19, of which waited for: 10 -> 10; matrix products, arithmetic and copies ran while one was open for 1% -> 2% of each run, Pallas kernels for 2% -> 2%
where the time goes in v5:
time: 257 us; the launch traced here: 255 us
  starting transfers between devices  89.1 us (35%)
  blocking collectives  78.8 us (31%)
  waiting for transfers between devices  58.5 us (23%)
  local copies, waits for them, and re-layouts  12.8 us (5%)
  Pallas kernels  10.4 us (4%)
  other arithmetic  4.96 us (2%)
    all_to_all x4, blocking collectives, exchange(): return lax.all_to_all(blocks, axes, split_axis=0, concat_axis=0, tiled=True)  78.8 us
    ppermute x5, waiting for transfers between devices, doubled(): return jnp.concatenate([blocks, lax.ppermute(blocks, axis, pairs)])  38.8 us
    all_to_all x5, starting transfers between devices, exchange(): return lax.all_to_all(blocks, axes, split_axis=0, concat_axis=0, tiled=True)  35.3 us
    ppermute x9, starting transfers between devices, swap(): return lax.ppermute(block, axis, ((0, 1), (1, 0)))  31.1 us
    ppermute x5, starting transfers between devices, doubled(): return jnp.concatenate([blocks, lax.ppermute(blocks, axis, pairs)])  22.6 us
    all_to_all x5, waiting for transfers between devices, exchange(): return lax.all_to_all(blocks, axes, split_axis=0, concat_axis=0, tiled=True)  15.8 us
    unnamed x22, local copies, waits for them, and re-layouts  8.1 us
  transfers between devices with their start and end apart: 19, of which 10 were waited for; matrix products, arithmetic and copies ran while one was open for 2% of the time, Pallas kernels for 2%

profile of v5, /device:TPU:1, one launch (start us, length us, event | category | flops | bytes accessed | tf_op | source)
XLA Modules:
  0.0 255.5 jit_solution(7921038922831206665)
XLA Ops:
  0.6 0.0 copy-start
  0.7 1.0 copy-done
  1.6 0.8 broadcast_in_dim.14
  2.4 7.6 %all-to-all-start = ((bf16[4,128,384]{2,1,0:T(8,128)(2,1)}), bf16[4,128,384]{2,1,0:T(8,128)(2,1)S(1)}, u32[]{:S(2)}, u32[]{:S(2)}) async-start(bf16[4,128,384]{2,1,0:T(8,128)(2,1)} %broadcast_in_dim.14), calls=%async_computation | async-start | bytes 786432 | tf_op jit(solution)/shard_map/all_to_all | solution.py:27
  10.1 1.6 copy-done.2
  11.7 0.6 token_columns.1
  12.2 1.3 copy-done.1
  13.6 7.5 %all-to-all-done = bf16[4,128,384]{2,1,0:T(8,128)(2,1)S(1)} async-done(((bf16[4,128,384]{2,1,0:T(8,128)(2,1)}), bf16[4,128,384]{2,1,0:T(8,128)(2,1)S(1)}, u32[]{:S(2)}, u32[]{:S(2)}) %all-to-all-start) | async-done | bytes 393248 | tf_op jit(solution)/shard_map/all_to_all | solution.py:27
  21.0 6.0 %all-to-all-start.1 = ((bf16[8,128,1024]{2,1,0:T(8,128)(2,1)}), bf16[8,128,1024]{2,1,0:T(8,128)(2,1)S(1)}, u32[]{:S(2)}, u32[]{:S(2)}) async-start(bf16[8,128,1024]{2,1,0:T(8,128)(2,1)} %copy-done.1), calls=%async_computation.1 | async-start | bytes 4194304 | tf_op jit(solution)/shard_map/all_to_all | solution.py:27
  27.0 3.4 %collective-permute-start = (bf16[1,128,128]{2,1,0:T(8,128)(2,1)S(1)}, bf16[1,128,128]{2,1,0:T(8,128)(2,1)S(1)}, u32[]{:S(2)}, u32[]{:S(2)}) collective-permute-start(bf16[1,128,128]{2,1,0:T(8,128)(2,1)S(1)} %copy-done.5), channel_id=1, source_target_pairs={{0,4},{4,0},{1,5},{5,1},{2,6},{6,2},{3,7},{7,3},{8,12},{12,8},{9,1... | collective-permute-start | bytes 98312 | tf_op jit(solution)/shard_map/ppermute | solution.py:40
  30.4 21.9 %collective-permute-done = bf16[1,128,128]{2,1,0:T(8,128)(2,1)S(1)} collective-permute-done((bf16[1,128,128]{2,1,0:T(8,128)(2,1)S(1)}, bf16[1,128,128]{2,1,0:T(8,128)(2,1)S(1)}, u32[]{:S(2)}, u32[]{:S(2)}) %collective-permute-start) | collective-permute-done | bytes 32800 | tf_op jit(solution)/shard_map/ppermute | solution.py:40
  52.3 5.8 %collective-permute-start.1 = (bf16[2,128,128]{2,1,0:T(8,128)(2,1)S(1)}, bf16[2,128,128]{2,1,0:T(8,128)(2,1)S(1)}, u32[]{:S(2)}, u32[]{:S(2)}) collective-permute-start(bf16[2,128,128]{2,1,0:T(8,128)(2,1)S(1)} %pad_maximum_fusion.6), channel_id=1, source_target_pairs={{0,8},{8,0},{16,24},{24,16},{1,9},{9,1},{17,25},{25,17},{2,10},{10... | collective-permute-start | bytes 196616 | tf_op jit(solution)/shard_map/ppermute | solution.py:40
  58.1 3.9 %collective-permute-start.3 = (bf16[512,384]{1,0:T(8,128)(2,1)S(1)}, bf16[512,384]{1,0:T(8,128)(2,1)S(1)}, u32[]{:S(2)}, u32[]{:S(2)}) collective-permute-start(bf16[512,384]{1,0:T(8,128)(2,1)S(1)} %bitcast.24), channel_id=1, source_target_pairs={{0,1},{1,0},{2,3},{3,2},{4,5},{5,4},{6,7},{7,6},{8,9},{9,8},{10,11... | collective-permute-start | bytes 1179656 | tf_op jit(solution)/shard_map/ppermute | solution.py:35
  62.1 7.9 %collective-permute-start.2 = (bf16[4,128,128]{2,1,0:T(8,128)(2,1)S(1)}, bf16[4,128,128]{2,1,0:T(8,128)(2,1)S(1)}, u32[]{:S(2)}, u32[]{:S(2)}) collective-permute-start(bf16[4,128,128]{2,1,0:T(8,128)(2,1)S(1)} %pad_maximum_fusion.4), channel_id=1, source_target_pairs={{0,16},{8,24},{16,0},{24,8},{1,17},{9,25},{17,1},{25,9},{2,18},{10... | collective-permute-start | bytes 393224 | tf_op jit(solution)/shard_map/ppermute | solution.py:40
  70.0 2.4 collective-permute-done.2
  72.4 0.7 pad_maximum_fusion.3
  73.1 0.0 all-to-all-done.1
  73.2 2.2 partial_projection.1
  75.3 10.5 %all-to-all-start.2 = ((bf16[8,128,384]{2,1,0:T(8,128)(2,1)}), bf16[8,128,384]{2,1,0:T(8,128)(2,1)}, u32[]{:S(2)}, u32[]{:S(2)}) async-start(bf16[8,128,384]{2,1,0:T(8,128)(2,1)} %bitcast.3), calls=%async_computation.2 | async-start | bytes 1572864 | tf_op jit(solution)/shard_map/all_to_all | solution.py:27
  85.8 2.2 collective-permute-start.4
  88.1 12.9 %collective-permute-done.4 = bf16[8,128,128]{2,1,0:T(8,128)(2,1)S(1)} collective-permute-done((bf16[8,128,128]{2,1,0:T(8,128)(2,1)}, bf16[8,128,128]{2,1,0:T(8,128)(2,1)S(1)}, u32[]{:S(2)}, u32[]{:S(2)}) %collective-permute-start.4) | collective-permute-done | bytes 262176 | tf_op jit(solution)/shard_map/ppermute | solution.py:40
  101.0 1.0 pad_maximum_fusion.1
  102.0 3.3 %collective-permute-start.5 = (bf16[16,128,128]{2,1,0:T(8,128)(2,1)S(1)}, bf16[16,128,128]{2,1,0:T(8,128)(2,1)S(1)}, u32[]{:S(2)}, u32[]{:S(2)}) collective-permute-start(bf16[16,128,128]{2,1,0:T(8,128)(2,1)S(1)} %pad_maximum_fusion.1), channel_id=1, source_target_pairs={{0,1},{1,0},{2,3},{3,2},{4,5},{5,4},{6,7},{7,6},{8,9},{9,8},{10,11... | collective-permute-start | bytes 1572872 | tf_op jit(solution)/shard_map/ppermute | solution.py:40
  105.3 1.5 collective-permute-done.5
  106.8 1.1 pad_maximum_fusion.cot_ref
  107.9 1.9 reduce_sum.24
  109.8 0.8 slice.9.kv_ref
  110.7 0.6 copy-done.3
  111.3 22.8 %all_to_all.45 = bf16[8,128,256]{2,1,0:T(8,128)(2,1)} all-to-all(bf16[8,128,256]{2,1,0:T(8,128)(2,1)S(1)} %broadcast_in_dim.15), channel_id=1, replica_groups=mesh['xh'=2,'yh'=4,'yl'=2,'zh'=4,'zl'=2,'xl'=2,'core'=2] {'zh','zl'}, dimensions={0} | all-to-all | bytes 1048576 | tf_op jit(solution)/shard_map/all_to_all | solution.py:27
  134.1 3.0 %collective-permute-start.6 = (bf16[1024,256]{1,0:T(8,128)(2,1)}, bf16[1024,256]{1,0:T(8,128)(2,1)}, u32[]{:S(2)}, u32[]{:S(2)}) collective-permute-start(bf16[1024,256]{1,0:T(8,128)(2,1)} %bitcast.4.kv0), channel_id=1, source_target_pairs={{0,2},{2,0},{1,3},{3,1},{4,6},{6,4},{5,7},{7,5},{8,10},{10,8},{9,1... | collective-permute-start | bytes 1572872 | tf_op jit(solution)/shard_map/ppermute | solution.py:35
  137.2 0.8 slice.8.q_ref
  137.9 0.7 broadcast_in_dim.17
  138.7 0.6 copy-done.7
  139.3 4.0 %all-to-all-start.4 = ((bf16[8,128,128]{2,1,0:T(8,128)(2,1)}), bf16[8,128,128]{2,1,0:T(8,128)(2,1)}, u32[]{:S(2)}, u32[]{:S(2)}) async-start(bf16[8,128,128]{2,1,0:T(8,128)(2,1)} %broadcast_in_dim.17), calls=%async_computation.4 | async-start | bytes 524288 | tf_op jit(solution)/shard_map/all_to_all | solution.py:27
  143.3 3.9 %collective-permute-start.7 = (bf16[1024,256]{1,0:T(8,128)(2,1)}, bf16[1024,256]{1,0:T(8,128)(2,1)}, u32[]{:S(2)}, u32[]{:S(2)}) collective-permute-start(bf16[1024,256]{1,0:T(8,128)(2,1)} %bitcast.4.kv0), channel_id=1, source_target_pairs={{0,1},{1,0},{2,3},{3,2},{4,5},{5,4},{6,7},{7,6},{8,9},{9,8},{10,11... | collective-permute-start | bytes 1572872 | tf_op jit(solution)/shard_map/ppermute | solution.py:35
  147.3 0.7 collective-permute-done.6.kv1
  148.0 4.6 %collective-permute-start.8 = (bf16[1024,256]{1,0:T(8,128)(2,1)}, bf16[1024,256]{1,0:T(8,128)(2,1)}, u32[]{:S(2)}, u32[]{:S(2)}) collective-permute-start(bf16[1024,256]{1,0:T(8,128)(2,1)} %collective-permute-done.6.kv1), channel_id=1, source_target_pairs={{0,1},{1,0},{2,3},{3,2},{4,5},{5,4},{6,7},{7,6},{8,9},{9,8},{10,11... | collective-permute-start | bytes 1572872 | tf_op jit(solution)/shard_map/ppermute | solution.py:35
  152.6 3.1 %collective-permute-start.9 = (bf16[1024,128]{1,0:T(8,128)(2,1)}, bf16[1024,128]{1,0:T(8,128)(2,1)}, u32[]{:S(2)}, u32[]{:S(2)}) collective-permute-start(bf16[1024,128]{1,0:T(8,128)(2,1)} %bitcast.7.q0), channel_id=1, source_target_pairs={{0,2},{2,0},{1,3},{3,1},{4,6},{6,4},{5,7},{7,5},{8,10},{10,8},{9,1... | collective-permute-start | bytes 786440 | tf_op jit(solution)/shard_map/ppermute | solution.py:35
  155.6 0.0 copy-start.6
  155.7 0.7 copy-done.6
  156.4 0.8 copy-done.8
  157.2 3.7 %attention_rows.1 = (bf16[128,128]{1,0:T(8,128)(2,1)}, f32[2,128]{1,0:T(2,128)S(1)}, bf16[128,128]{1,0:T(8,128)(2,1)S(1)}) custom-call(bf16[128,128]{1,0:T(8,128)(2,1)S(1)} %copy-done.8, bf16[1024,256]{1,0:T(8,128)(2,1)} %bitcast.4.kv0, bf16[1024,256]{1,0:T(8,128)(2,1)} %collective-permute-done.6.kv1, bf16[1024,256]{1,0:T(8,128)(2,1)} %collective-permute-done.7.kv2, ...), custom_call_target="tpu_custom_call" | custom-call | tf_op jit(solution)/shard_map/attention_rows/pallas_call | solution.py:217
  160.8 0.6 copy-done.9
  161.4 0.6 broadcast_in_dim.18
  162.1 7.2 %all-to-all-start.5 = ((f32[32,2,128]{2,1,0:T(2,128)}), f32[32,2,128]{2,1,0:T(2,128)}, u32[]{:S(2)}, u32[]{:S(2)}) async-start(f32[32,2,128]{2,1,0:T(2,128)} %broadcast_in_dim.18), calls=%async_computation.5 | async-start | bytes 65536 | tf_op jit(solution)/shard_map/all_to_all | solution.py:27
  169.3 8.3 %all-to-all-done.5.stats_ref = f32[32,2,128]{2,1,0:T(2,128)} async-done(((f32[32,2,128]{2,1,0:T(2,128)}), f32[32,2,128]{2,1,0:T(2,128)}, u32[]{:S(2)}, u32[]{:S(2)}) %all-to-all-start.5) | async-done | bytes 32800 | tf_op jit(solution)/shard_map/all_to_all | solution.py:27
  177.6 2.3 collective-permute-start.10
  179.9 2.0 collective-permute-start.11
  181.9 1.6 collective-permute-done.11.q3
  183.5 0.8 copy-done.4
  184.4 2.5 attention_columns.1
  186.9 0.1 broadcast_in_dim.19
  187.0 19.6 %all_to_all.46 = bf16[8,128,384]{2,1,0:T(8,128)(2,1)S(1)} all-to-all(bf16[8,128,384]{2,1,0:T(8,128)(2,1)S(1)} %broadcast_in_dim.19), channel_id=1, replica_groups=mesh['xh'=2,'yh'=4,'yl'=2,'zh'=4,'zl'=2,'xl'=2,'core'=2] {'xh','yl','zl'}, dimensions={0} | all-to-all | bytes 1572864 | tf_op jit(solution)/shard_map/all_to_all | solution.py:27
  206.6 0.7 weight_gradient.3
  207.4 3.3 %collective-permute-start.12 = (bf16[512,384]{1,0:T(8,128)(2,1)S(1)}, bf16[512,384]{1,0:T(8,128)(2,1)S(1)}, u32[]{:S(2)}, u32[]{:S(2)}) collective-permute-start(bf16[512,384]{1,0:T(8,128)(2,1)S(1)} %weight_gradient.3), channel_id=1, source_target_pairs={{0,1},{1,0},{2,3},{3,2},{4,5},{5,4},{6,7},{7,6},{8,9},{9,8},{10,11... | collective-permute-start | bytes 1179656 | tf_op jit(solution)/shard_map/ppermute | solution.py:35
  210.7 0.7 weight_gradient.2
  211.4 0.6 collective-permute-done.12
  212.0 0.1 add_convert_fusion
  212.1 24.7 %all_to_all.47 = bf16[32,16,384]{2,1,0:T(8,128)(2,1)S(1)} all-to-all(bf16[32,16,384]{2,1,0:T(8,128)(2,1)S(1)} %bitcast.27), channel_id=1, replica_groups=mesh['xh'=2,'yh'=4,'yl'=2,'zh'=4,'zl'=2,'xl'=2,'core'=2] {'yh','zh','xl'}, dimensions={0} | all-to-all | bytes 786432 | tf_op jit(solution)/shard_map/all_to_all | solution.py:27
  236.8 0.1 reduce_sum.25
  236.9 11.7 %all_to_all.48 = bf16[16,16,384]{2,1,0:T(8,128)(2,1)S(1)} all-to-all(bf16[16,16,384]{2,1,0:T(8,128)(2,1)S(1)} %broadcast_in_dim.20), channel_id=1, replica_groups=mesh['xh'=2,'yh'=4,'yl'=2,'zh'=4,'zl'=2,'xl'=2,'core'=2] {'zh','zl','xl'}, dimensions={0} | all-to-all | bytes 393216 | tf_op jit(solution)/shard_map/all_to_all | solution.py:27
  248.6 5.0 %collective-permute-start.13 = (bf16[2,4,2,16,384]{4,3,2,0,1:T(8,128)(2,1)S(1)}, bf16[2,4,2,16,384]{4,3,2,0,1:T(8,128)(2,1)S(1)}, u32[]{:S(2)}, u32[]{:S(2)}) collective-permute-start(bf16[2,4,2,16,384]{4,3,2,0,1:T(8,128)(2,1)S(1)} %bitcast.28), channel_id=1, source_target_pairs={{0,1},{1,0},{2,3},{3,2},{4,5},{5,4},{6,7},{7,6},{8,9},{9,8},{10,11... | collective-permute-start | bytes 589832 | tf_op jit(solution)/shard_map/ppermute | solution.py:35
  253.6 1.0 collective-permute-done.13
  254.7 0.8 copy.6
  (27 shorter events, 0.2 us)
Async XLA Ops:
  0.6 1.0 copy-start
  2.4 18.6 %all-to-all-start = ((bf16[4,128,384]{2,1,0:T(8,128)(2,1)}), bf16[4,128,384]{2,1,0:T(8,128)(2,1)S(1)}, u32[]{:S(2)}, u32[]{:S(2)}) async-start(bf16[4,128,384]{2,1,0:T(8,128)(2,1)} %broadcast_in_dim.14), calls=%async_computation | async-start | bytes 786432 | tf_op jit(solution)/shard_map/all_to_all | solution.py:27
  10.1 1.6 copy-start.2
  12.2 1.3 copy-start.1
  21.0 6.0 %copy-start.5 = (bf16[1,128,128]{2,1,0:T(8,128)(2,1)S(1)}, bf16[1,128,128]{2,1,0:T(8,128)(2,1)}, u32[]{:S(2)}) copy-start(bf16[1,128,128]{2,1,0:T(8,128)(2,1)} %param.5) | copy-start | bytes 98308
  21.0 52.1 %all-to-all-start.1 = ((bf16[8,128,1024]{2,1,0:T(8,128)(2,1)}), bf16[8,128,1024]{2,1,0:T(8,128)(2,1)S(1)}, u32[]{:S(2)}, u32[]{:S(2)}) async-start(bf16[8,128,1024]{2,1,0:T(8,128)(2,1)} %copy-done.1), calls=%async_computation.1 | async-start | bytes 4194304 | tf_op jit(solution)/shard_map/all_to_all | solution.py:27
  27.0 25.3 %collective-permute-start = (bf16[1,128,128]{2,1,0:T(8,128)(2,1)S(1)}, bf16[1,128,128]{2,1,0:T(8,128)(2,1)S(1)}, u32[]{:S(2)}, u32[]{:S(2)}) collective-permute-start(bf16[1,128,128]{2,1,0:T(8,128)(2,1)S(1)} %copy-done.5), channel_id=1, source_target_pairs={{0,4},{4,0},{1,5},{5,1},{2,6},{6,2},{3,7},{7,3},{8,12},{12,8},{9,1... | collective-permute-start | bytes 98312 | tf_op jit(solution)/shard_map/ppermute | solution.py:40
  52.3 9.7 %collective-permute-start.1 = (bf16[2,128,128]{2,1,0:T(8,128)(2,1)S(1)}, bf16[2,128,128]{2,1,0:T(8,128)(2,1)S(1)}, u32[]{:S(2)}, u32[]{:S(2)}) collective-permute-start(bf16[2,128,128]{2,1,0:T(8,128)(2,1)S(1)} %pad_maximum_fusion.6), channel_id=1, source_target_pairs={{0,8},{8,0},{16,24},{24,16},{1,9},{9,1},{17,25},{25,17},{2,10},{10... | collective-permute-start | bytes 196616 | tf_op jit(solution)/shard_map/ppermute | solution.py:40
  58.1 15.0 %collective-permute-start.3 = (bf16[512,384]{1,0:T(8,128)(2,1)S(1)}, bf16[512,384]{1,0:T(8,128)(2,1)S(1)}, u32[]{:S(2)}, u32[]{:S(2)}) collective-permute-start(bf16[512,384]{1,0:T(8,128)(2,1)S(1)} %bitcast.24), channel_id=1, source_target_pairs={{0,1},{1,0},{2,3},{3,2},{4,5},{5,4},{6,7},{7,6},{8,9},{9,8},{10,11... | collective-permute-start | bytes 1179656 | tf_op jit(solution)/shard_map/ppermute | solution.py:35
  62.1 10.3 %collective-permute-start.2 = (bf16[4,128,128]{2,1,0:T(8,128)(2,1)S(1)}, bf16[4,128,128]{2,1,0:T(8,128)(2,1)S(1)}, u32[]{:S(2)}, u32[]{:S(2)}) collective-permute-start(bf16[4,128,128]{2,1,0:T(8,128)(2,1)S(1)} %pad_maximum_fusion.4), channel_id=1, source_target_pairs={{0,16},{8,24},{16,0},{24,8},{1,17},{9,25},{17,1},{25,9},{2,18},{10... | collective-permute-start | bytes 393224 | tf_op jit(solution)/shard_map/ppermute | solution.py:40
  75.3 32.5 %all-to-all-start.2 = ((bf16[8,128,384]{2,1,0:T(8,128)(2,1)}), bf16[8,128,384]{2,1,0:T(8,128)(2,1)}, u32[]{:S(2)}, u32[]{:S(2)}) async-start(bf16[8,128,384]{2,1,0:T(8,128)(2,1)} %bitcast.3), calls=%async_computation.2 | async-start | bytes 1572864 | tf_op jit(solution)/shard_map/all_to_all | solution.py:27
  85.8 15.2 %collective-permute-start.4 = (bf16[8,128,128]{2,1,0:T(8,128)(2,1)}, bf16[8,128,128]{2,1,0:T(8,128)(2,1)S(1)}, u32[]{:S(2)}, u32[]{:S(2)}) collective-permute-start(bf16[8,128,128]{2,1,0:T(8,128)(2,1)} %pad_maximum_fusion.3), channel_id=1, source_target_pairs={{0,2},{2,0},{1,3},{3,1},{4,6},{6,4},{5,7},{7,5},{8,10},{10,8},{9,1... | collective-permute-start | bytes 786440 | tf_op jit(solution)/shard_map/ppermute | solution.py:40
  102.0 4.8 %collective-permute-start.5 = (bf16[16,128,128]{2,1,0:T(8,128)(2,1)S(1)}, bf16[16,128,128]{2,1,0:T(8,128)(2,1)S(1)}, u32[]{:S(2)}, u32[]{:S(2)}) collective-permute-start(bf16[16,128,128]{2,1,0:T(8,128)(2,1)S(1)} %pad_maximum_fusion.1), channel_id=1, source_target_pairs={{0,1},{1,0},{2,3},{3,2},{4,5},{5,4},{6,7},{7,6},{8,9},{9,8},{10,11... | collective-permute-start | bytes 1572872 | tf_op jit(solution)/shard_map/ppermute | solution.py:40
  110.7 0.6 copy-start.3
  134.1 13.9 %collective-permute-start.6 = (bf16[1024,256]{1,0:T(8,128)(2,1)}, bf16[1024,256]{1,0:T(8,128)(2,1)}, u32[]{:S(2)}, u32[]{:S(2)}) collective-permute-start(bf16[1024,256]{1,0:T(8,128)(2,1)} %bitcast.4.kv0), channel_id=1, source_target_pairs={{0,2},{2,0},{1,3},{3,1},{4,6},{6,4},{5,7},{7,5},{8,10},{10,8},{9,1... | collective-permute-start | bytes 1572872 | tf_op jit(solution)/shard_map/ppermute | solution.py:35
  138.7 0.6 copy-start.7
  139.3 13.3 %all-to-all-start.4 = ((bf16[8,128,128]{2,1,0:T(8,128)(2,1)}), bf16[8,128,128]{2,1,0:T(8,128)(2,1)}, u32[]{:S(2)}, u32[]{:S(2)}) async-start(bf16[8,128,128]{2,1,0:T(8,128)(2,1)} %broadcast_in_dim.17), calls=%async_computation.4 | async-start | bytes 524288 | tf_op jit(solution)/shard_map/all_to_all | solution.py:27
  143.3 12.3 %collective-permute-start.7 = (bf16[1024,256]{1,0:T(8,128)(2,1)}, bf16[1024,256]{1,0:T(8,128)(2,1)}, u32[]{:S(2)}, u32[]{:S(2)}) collective-permute-start(bf16[1024,256]{1,0:T(8,128)(2,1)} %bitcast.4.kv0), channel_id=1, source_target_pairs={{0,1},{1,0},{2,3},{3,2},{4,5},{5,4},{6,7},{7,6},{8,9},{9,8},{10,11... | collective-permute-start | bytes 1572872 | tf_op jit(solution)/shard_map/ppermute | solution.py:35
  148.0 7.7 %collective-permute-start.8 = (bf16[1024,256]{1,0:T(8,128)(2,1)}, bf16[1024,256]{1,0:T(8,128)(2,1)}, u32[]{:S(2)}, u32[]{:S(2)}) collective-permute-start(bf16[1024,256]{1,0:T(8,128)(2,1)} %collective-permute-done.6.kv1), channel_id=1, source_target_pairs={{0,1},{1,0},{2,3},{3,2},{4,5},{5,4},{6,7},{7,6},{8,9},{9,8},{10,11... | collective-permute-start | bytes 1572872 | tf_op jit(solution)/shard_map/ppermute | solution.py:35
  152.6 16.7 %collective-permute-start.9 = (bf16[1024,128]{1,0:T(8,128)(2,1)}, bf16[1024,128]{1,0:T(8,128)(2,1)}, u32[]{:S(2)}, u32[]{:S(2)}) collective-permute-start(bf16[1024,128]{1,0:T(8,128)(2,1)} %bitcast.7.q0), channel_id=1, source_target_pairs={{0,2},{2,0},{1,3},{3,1},{4,6},{6,4},{5,7},{7,5},{8,10},{10,8},{9,1... | collective-permute-start | bytes 786440 | tf_op jit(solution)/shard_map/ppermute | solution.py:35
  155.6 0.8 copy-start.6
  156.4 0.8 copy-start.8
  160.8 0.6 copy-start.9
  162.1 15.5 %all-to-all-start.5 = ((f32[32,2,128]{2,1,0:T(2,128)}), f32[32,2,128]{2,1,0:T(2,128)}, u32[]{:S(2)}, u32[]{:S(2)}) async-start(f32[32,2,128]{2,1,0:T(2,128)} %broadcast_in_dim.18), calls=%async_computation.5 | async-start | bytes 65536 | tf_op jit(solution)/shard_map/all_to_all | solution.py:27
  177.6 4.3 %collective-permute-start.10 = (bf16[1024,128]{1,0:T(8,128)(2,1)}, bf16[1024,128]{1,0:T(8,128)(2,1)S(1)}, u32[]{:S(2)}, u32[]{:S(2)}) collective-permute-start(bf16[1024,128]{1,0:T(8,128)(2,1)} %bitcast.7.q0), channel_id=1, source_target_pairs={{0,1},{1,0},{2,3},{3,2},{4,5},{5,4},{6,7},{7,6},{8,9},{9,8},{10,11... | collective-permute-start | bytes 786440 | tf_op jit(solution)/shard_map/ppermute | solution.py:35
  179.9 3.6 %collective-permute-start.11 = (bf16[1024,128]{1,0:T(8,128)(2,1)}, bf16[1024,128]{1,0:T(8,128)(2,1)S(1)}, u32[]{:S(2)}, u32[]{:S(2)}) collective-permute-start(bf16[1024,128]{1,0:T(8,128)(2,1)} %collective-permute-done.9.q1), channel_id=1, source_target_pairs={{0,1},{1,0},{2,3},{3,2},{4,5},{5,4},{6,7},{7,6},{8,9},{9,8},{10,11... | collective-permute-start | bytes 786440 | tf_op jit(solution)/shard_map/ppermute | solution.py:35
  183.5 0.8 copy-start.4
  184.3 2.6 copy-start.10
  207.4 4.6 %collective-permute-start.12 = (bf16[512,384]{1,0:T(8,128)(2,1)S(1)}, bf16[512,384]{1,0:T(8,128)(2,1)S(1)}, u32[]{:S(2)}, u32[]{:S(2)}) collective-permute-start(bf16[512,384]{1,0:T(8,128)(2,1)S(1)} %weight_gradient.3), channel_id=1, source_target_pairs={{0,1},{1,0},{2,3},{3,2},{4,5},{5,4},{6,7},{7,6},{8,9},{9,8},{10,11... | collective-permute-start | bytes 1179656 | tf_op jit(solution)/shard_map/ppermute | solution.py:35
  248.6 6.0 %collective-permute-start.13 = (bf16[2,4,2,16,384]{4,3,2,0,1:T(8,128)(2,1)S(1)}, bf16[2,4,2,16,384]{4,3,2,0,1:T(8,128)(2,1)S(1)}, u32[]{:S(2)}, u32[]{:S(2)}) collective-permute-start(bf16[2,4,2,16,384]{4,3,2,0,1:T(8,128)(2,1)S(1)} %bitcast.28), channel_id=1, source_target_pairs={{0,1},{1,0},{2,3},{3,2},{4,5},{5,4},{6,7},{7,6},{8,9},{9,8},{10,11... | collective-permute-start | bytes 589832 | tf_op jit(solution)/shard_map/ppermute | solution.py:35

commit v6 on v3

--- a/solution.py
+++ b/solution.py
@@ -99,36 +99,46 @@
     dq_ref[...] = (grad * scale).astype(low)
 
 
-def backward_kernel(z_count, kv_ref, qc0, qc1, qc2, qc3, stats_ref, out_ref):
+def backward_kernel(z_count, kv_ref, across_ref, qc0, qc1, stats_ref, own_ref, other_ref):
     rows, head = kv_ref.shape[0], kv_ref.shape[1] // 2
     half_rows, ctx_count = rows // 2, 4 * z_count
     scale = 1.0 / math.sqrt(head)
-    own = piece_device(0, lax.axis_index(z_axes))
+    z_own = lax.axis_index(z_axes)
     down = lax.broadcasted_iota(jnp.int32, (rows, rows), 0)
     across = lax.broadcasted_iota(jnp.int32, (rows, rows), 1)
-    own_positions = positions(own, down, half_rows, ctx_count)
-    keys, values = kv_ref[:, :head], kv_ref[:, head:]
-    grad_key = jnp.zeros((rows, head), jnp.float32)
-    grad_value = jnp.zeros((rows, head), jnp.float32)
-    for piece, both in enumerate((qc0, qc1, qc2, qc3)):
-        slot = piece_device(piece, 0)
+    key_positions = jnp.concatenate(
+        [
+            positions(piece_device(0, z_own), down, half_rows, ctx_count),
+            positions(piece_device(2, z_own), down, half_rows, ctx_count),
+        ],
+        axis=0,
+    )
+    pairs = jnp.concatenate(
+        [kv_ref[...], across_ref[pl.ds(pl.multiple_of(z_own * rows, rows), rows), :]], axis=0
+    )
+    keys, values = pairs[:, :head], pairs[:, head:]
+    grad_key = jnp.zeros((2 * rows, head), jnp.float32)
+    grad_value = jnp.zeros((2 * rows, head), jnp.float32)
+    for piece, both in enumerate((qc0, qc1)):
+        slot = lax.axis_index("xl") ^ piece
         queries, cotangent = both[:, :head], both[:, head:]
         scores = dot_f32(keys, queries, 1, 1) * scale
         dprob = dot_f32(values, cotangent, 1, 1)
         probs, dscores = [], []
         for z in range(z_count):
             span = slice(z * rows, (z + 1) * rows)
-            stats = stats_ref[4 * z + slot]
-            device = piece_device(piece, z)
-            allowed = own_positions <= positions(device, across, half_rows, ctx_count)
+            stats = stats_ref[2 * z + slot]
+            row_positions = positions(piece_device(piece, z), across, half_rows, ctx_count)
+            allowed = key_positions <= jnp.concatenate([row_positions, row_positions], axis=0)
             masked = jnp.where(allowed, scores[:, span], masked_fill)
             prob = jnp.exp(masked - stats[0:1, :])
             probs.append(prob.astype(low))
             dscores.append((prob * (dprob[:, span] + stats[1:2, :])).astype(low))
         grad_value = grad_value + dot_f32(jnp.concatenate(probs, axis=1), cotangent, 1, 0)
         grad_key = grad_key + dot_f32(jnp.concatenate(dscores, axis=1), queries, 1, 0)
-    out_ref[:, :head] = (grad_key * scale).astype(low)
-    out_ref[:, head:] = grad_value.astype(low)
+    grad_key = grad_key * scale
+    own_ref[:, :head], own_ref[:, head:] = grad_key[:rows], grad_value[:rows]
+    other_ref[:, :head], other_ref[:, head:] = grad_key[rows:], grad_value[rows:]
 
 
 def shard_row(step, count):
@@ -184,7 +194,6 @@
         ring = [(i, (i + step) % y_half) for i in range(y_half)]
         steps.append(lax.ppermute(own_weight, "yh", ring))
     near = jnp.concatenate(steps)
-    far = swap(near, "core")
     split = pl.pallas_call(
         functools.partial(relayout_kernel, y_half),
         in_specs=in_vmem(1),
@@ -193,6 +202,8 @@
         compiler_params=vmem,
         name="token_columns",
     )(tokens[0])
+    split, near = lax.optimization_barrier((split, near))
+    far = swap(near, "core")
     columns = exchange(split, group_axes).reshape(group_rows, 2 * depth)
     parts = pl.pallas_call(
         project_kernel,
@@ -223,18 +234,17 @@
         name="attention_rows",
     )(queries, *pair_pieces, cotangent)
 
-    query_pieces, stats = lax.optimization_barrier((query_pieces, stats))
-    query_pieces = query_pieces + tuple(swap(p, "core") for p in query_pieces)
-    stats_all = spread(stats, ctx_axes, ctx_count)
-
-    grad_pairs = pl.pallas_call(
+    stats_all = spread(stats, z_axes + ("xl",), 2 * z_count)
+
+    own_part, other_part = pl.pallas_call(
         functools.partial(backward_kernel, z_count),
-        in_specs=in_vmem(6),
-        out_specs=in_vmem(1)[0],
-        out_shape=jax.ShapeDtypeStruct((row_count, 2 * head), low),
+        in_specs=in_vmem(5),
+        out_specs=in_vmem(2),
+        out_shape=[jax.ShapeDtypeStruct((row_count, 2 * head), jnp.float32)] * 2,
         compiler_params=vmem,
         name="attention_columns",
-    )(own_pairs, *query_pieces, stats_all)
+    )(own_pairs, pair_pieces[2], *query_pieces, stats_all)
+    grad_pairs = (own_part + swap(other_part, "core")).astype(low)
 
     grad_all = spread(jnp.concatenate([grad_query, grad_pairs], axis=1), group_axes, 8)
     grad_all = grad_all.reshape(group_rows, width)
@@ -257,8 +267,11 @@
     summed = (weight_half(0, jnp.float32) + sent.astype(jnp.float32)).astype(low)
     pieces = exchange(summed.reshape(8 * y_half, -1, width), ("yh", "zh", "xl"))
     own_piece = jnp.sum(pieces.astype(jnp.float32), axis=0).astype(low)
-    total = spread(own_piece, ctx_axes, ctx_count)
-    total = total.reshape((z_count // 2, 2, 2, 2) + own_piece.shape).transpose(1, 3, 0, 2, 4, 5)
+    on_core = spread(own_piece, z_axes + ("xl",), 2 * z_count)
+    on_core = on_core.reshape((z_count // 2, 2, 2) + own_piece.shape).transpose(1, 0, 2, 3, 4)
+    across = swap(on_core, "core")
+    first = lax.axis_index("core") == 0
+    total = jnp.stack([jnp.where(first, on_core, across), jnp.where(first, across, on_core)], axis=1)
     return (attn_rows[None], total.reshape(shard, width))
 
 

time: 228 us -> 223 us (0.978)
  blocking collectives: 91.9 us -> 67.1 us
  starting transfers between devices: 60.4 us -> 75.5 us
    all_to_all x3 -> x4, waiting for transfers between devices: 14.4 us -> 49.2 us  [exchange(): return lax.all_to_all(blocks, axes, split_axis=0, concat_axis=0, tiled=True)]
    ppermute x3, waiting for transfers between devices: 25.9 us -> 0.91 us  [on_device(): steps.append(lax.ppermute(own_weight, 'yh', ring))]
    all_to_all x5 -> x4, blocking collectives: 91.9 us -> 67.1 us  [exchange(): return lax.all_to_all(blocks, axes, split_axis=0, concat_axis=0, tiled=True)]
    ppermute x8, waiting for transfers between devices: 15.6 us -> 6.58 us  [swap(): return lax.ppermute(block, axis, ((0, 1), (1, 0)))]
    all_to_all x3 -> x4, starting transfers between devices: 20.3 us -> 27.1 us  [exchange(): return lax.all_to_all(blocks, axes, split_axis=0, concat_axis=0, tiled=True)]
    ppermute x8, starting transfers between devices: 27.3 us -> 32.8 us  [swap(): return lax.ppermute(block, axis, ((0, 1), (1, 0)))]
    ppermute x3, starting transfers between devices: 12.7 us -> 15.7 us  [on_device(): steps.append(lax.ppermute(own_weight, 'yh', ring))]
    unnamed x20, local copies, waits for them, and re-layouts: 5.72 us -> 8.09 us
  transfers between devices with their start and end apart: 14 -> 15, of which waited for: 7 -> 9; matrix products, arithmetic and copies ran while one was open for 0% -> 0% of each run, Pallas kernels for 2% -> 2%
where the time goes in v6:
time: 223 us; the launch traced here: 222 us
  starting transfers between devices  75.5 us (34%)
  blocking collectives  67.1 us (30%)
  waiting for transfers between devices  56.7 us (25%)
  local copies, waits for them, and re-layouts  11.3 us (5%)
  Pallas kernels  9.32 us (4%)
    all_to_all x4, blocking collectives, exchange(): return lax.all_to_all(blocks, axes, split_axis=0, concat_axis=0, tiled=True)  67.1 us
    all_to_all x4, waiting for transfers between devices, exchange(): return lax.all_to_all(blocks, axes, split_axis=0, concat_axis=0, tiled=True)  49.2 us
    ppermute x8, starting transfers between devices, swap(): return lax.ppermute(block, axis, ((0, 1), (1, 0)))  32.8 us
    all_to_all x4, starting transfers between devices, exchange(): return lax.all_to_all(blocks, axes, split_axis=0, concat_axis=0, tiled=True)  27.1 us
    ppermute x3, starting transfers between devices, on_device(): steps.append(lax.ppermute(own_weight, 'yh', ring))  15.7 us
    unnamed x20, local copies, waits for them, and re-layouts  8.09 us
    ppermute x8, waiting for transfers between devices, swap(): return lax.ppermute(block, axis, ((0, 1), (1, 0)))  6.58 us
  transfers between devices with their start and end apart: 15, of which 9 were waited for; matrix products, arithmetic and copies ran while one was open for 0% of the time, Pallas kernels for 2%

profile of v6, /device:TPU:1, one launch (start us, length us, event | category | flops | bytes accessed | tf_op | source)
XLA Modules:
  0.0 222.0 jit_solution(90481645168046255)
XLA Ops:
  0.6 0.0 copy-start
  0.7 1.0 copy-done
  1.6 5.0 %collective-permute-start = (bf16[128,384]{1,0:T(8,128)(2,1)S(1)}, bf16[128,384]{1,0:T(8,128)(2,1)S(1)}, u32[]{:S(2)}, u32[]{:S(2)}) collective-permute-start(bf16[128,384]{1,0:T(8,128)(2,1)S(1)} %constant_dynamic-slice_fusion), channel_id=1, source_target_pairs={{0,64},{64,128},{128,192},{192,0},{1,65},{65,129},{129,193},{193,1... | collective-permute-start | bytes 294920 | tf_op jit(solution)/shard_map/ppermute | solution.py:195
  6.7 5.7 %collective-permute-start.1 = (bf16[128,384]{1,0:T(8,128)(2,1)S(1)}, bf16[128,384]{1,0:T(8,128)(2,1)S(1)}, u32[]{:S(2)}, u32[]{:S(2)}) collective-permute-start(bf16[128,384]{1,0:T(8,128)(2,1)S(1)} %constant_dynamic-slice_fusion), channel_id=1, source_target_pairs={{0,128},{64,192},{128,0},{192,64},{1,129},{65,193},{129,1},{193,65... | collective-permute-start | bytes 294920 | tf_op jit(solution)/shard_map/ppermute | solution.py:195
  12.4 5.0 %collective-permute-start.2 = (bf16[128,384]{1,0:T(8,128)(2,1)S(1)}, bf16[128,384]{1,0:T(8,128)(2,1)S(1)}, u32[]{:S(2)}, u32[]{:S(2)}) collective-permute-start(bf16[128,384]{1,0:T(8,128)(2,1)S(1)} %constant_dynamic-slice_fusion), channel_id=1, source_target_pairs={{0,192},{64,0},{128,64},{192,128},{1,193},{65,1},{129,65},{193,129... | collective-permute-start | bytes 294920 | tf_op jit(solution)/shard_map/ppermute | solution.py:195
  17.3 0.0 copy-start.2
  17.4 1.6 copy-done.2
  18.9 0.6 token_columns.1
  19.5 0.0 copy-start.1
  19.5 1.3 copy-done.1
  20.8 0.0 collective-permute-done
  20.8 0.0 collective-permute-done.1
  20.8 0.9 collective-permute-done.2
  21.8 6.9 %all-to-all-start = ((bf16[8,128,1024]{2,1,0:T(8,128)(2,1)}), bf16[8,128,1024]{2,1,0:T(8,128)(2,1)S(1)}, u32[]{:S(2)}, u32[]{:S(2)}) async-start(bf16[8,128,1024]{2,1,0:T(8,128)(2,1)} %copy-done.1), calls=%async_computation | async-start | bytes 4194304 | tf_op jit(solution)/shard_map/all_to_all | solution.py:27
  28.7 2.8 %collective-permute-start.3 = (bf16[512,384]{1,0:T(8,128)(2,1)S(1)}, bf16[512,384]{1,0:T(8,128)(2,1)S(1)}, u32[]{:S(2)}, u32[]{:S(2)}) collective-permute-start(bf16[512,384]{1,0:T(8,128)(2,1)S(1)} %pad_maximum_fusion.near_ref), channel_id=1, source_target_pairs={{0,1},{1,0},{2,3},{3,2},{4,5},{5,4},{6,7},{7,6},{8,9},{9,8},{10,11... | collective-permute-start | bytes 1179656 | tf_op jit(solution)/shard_map/ppermute | solution.py:35
  31.5 1.3 collective-permute-done.3.far_ref
  32.9 28.1 %all-to-all-done = bf16[8,128,1024]{2,1,0:T(8,128)(2,1)S(1)} async-done(((bf16[8,128,1024]{2,1,0:T(8,128)(2,1)}), bf16[8,128,1024]{2,1,0:T(8,128)(2,1)S(1)}, u32[]{:S(2)}, u32[]{:S(2)}) %all-to-all-start) | async-done | bytes 2097184 | tf_op jit(solution)/shard_map/all_to_all | solution.py:27
  61.0 1.2 partial_projection.1
  62.3 0.0 copy-start.7
  62.3 15.2 %all_to_all.40 = bf16[8,128,384]{2,1,0:T(8,128)(2,1)S(1)} all-to-all(bf16[8,128,384]{2,1,0:T(8,128)(2,1)S(1)} %bitcast.22), channel_id=1, replica_groups=mesh['xh'=2,'yh'=4,'yl'=2,'zh'=4,'zl'=2,'xl'=2,'core'=2] {'xh','yl','zl'}, dimensions={0} | all-to-all | bytes 1572864 | tf_op jit(solution)/shard_map/all_to_all | solution.py:27
  77.4 0.1 reduce_sum.24
  77.6 0.8 broadcast_in_dim.12
  78.4 0.6 copy-done.3
  79.0 9.1 %all-to-all-start.2 = ((bf16[8,128,256]{2,1,0:T(8,128)(2,1)}), bf16[8,128,256]{2,1,0:T(8,128)(2,1)}, u32[]{:S(2)}, u32[]{:S(2)}) async-start(bf16[8,128,256]{2,1,0:T(8,128)(2,1)} %broadcast_in_dim.12), calls=%async_computation.2 | async-start | bytes 1048576 | tf_op jit(solution)/shard_map/all_to_all | solution.py:27
  88.2 0.0 copy-start.5
  88.2 0.6 copy-done.5
  88.8 13.6 %all-to-all-done.2 = bf16[8,128,256]{2,1,0:T(8,128)(2,1)} async-done(((bf16[8,128,256]{2,1,0:T(8,128)(2,1)}), bf16[8,128,256]{2,1,0:T(8,128)(2,1)}, u32[]{:S(2)}, u32[]{:S(2)}) %all-to-all-start.2) | async-done | bytes 524320 | tf_op jit(solution)/shard_map/all_to_all | solution.py:27
  102.4 0.8 broadcast_in_dim.14
  103.3 3.5 %all-to-all-start.3 = ((bf16[8,128,256]{2,1,0:T(8,128)(2,1)}), bf16[8,128,256]{2,1,0:T(8,128)(2,1)S(1)}, u32[]{:S(2)}, u32[]{:S(2)}) async-start(bf16[8,128,256]{2,1,0:T(8,128)(2,1)} %broadcast_in_dim.14), calls=%async_computation.3 | async-start | bytes 1048576 | tf_op jit(solution)/shard_map/all_to_all | solution.py:27
  106.8 2.2 %collective-permute-start.4 = (bf16[1024,256]{1,0:T(8,128)(2,1)}, bf16[1024,256]{1,0:T(8,128)(2,1)}, u32[]{:S(2)}, u32[]{:S(2)}) collective-permute-start(bf16[1024,256]{1,0:T(8,128)(2,1)} %bitcast.3.kv0), channel_id=1, source_target_pairs={{0,2},{2,0},{1,3},{3,1},{4,6},{6,4},{5,7},{7,5},{8,10},{10,8},{9,1... | collective-permute-start | bytes 1572872 | tf_op jit(solution)/shard_map/ppermute | solution.py:35
  109.0 6.5 %collective-permute-start.5 = (bf16[1024,256]{1,0:T(8,128)(2,1)}, bf16[1024,256]{1,0:T(8,128)(2,1)S(1)}, u32[]{:S(2)}, u32[]{:S(2)}) collective-permute-start(bf16[1024,256]{1,0:T(8,128)(2,1)} %bitcast.3.kv0), channel_id=1, source_target_pairs={{0,1},{1,0},{2,3},{3,2},{4,5},{5,4},{6,7},{7,6},{8,9},{9,8},{10,11... | collective-permute-start | bytes 1572872 | tf_op jit(solution)/shard_map/ppermute | solution.py:35
  115.5 2.7 %collective-permute-done.4.kv1 = bf16[1024,256]{1,0:T(8,128)(2,1)} collective-permute-done((bf16[1024,256]{1,0:T(8,128)(2,1)}, bf16[1024,256]{1,0:T(8,128)(2,1)}, u32[]{:S(2)}, u32[]{:S(2)}) %collective-permute-start.4) | collective-permute-done | bytes 524320 | tf_op jit(solution)/shard_map/ppermute | solution.py:35
  118.1 7.1 %collective-permute-start.6 = (bf16[1024,256]{1,0:T(8,128)(2,1)}, bf16[1024,256]{1,0:T(8,128)(2,1)}, u32[]{:S(2)}, u32[]{:S(2)}) collective-permute-start(bf16[1024,256]{1,0:T(8,128)(2,1)} %collective-permute-done.4.kv1), channel_id=1, source_target_pairs={{0,1},{1,0},{2,3},{3,2},{4,5},{5,4},{6,7},{7,6},{8,9},{9,8},{10,11... | collective-permute-start | bytes 1572872 | tf_op jit(solution)/shard_map/ppermute | solution.py:35
  125.2 0.0 all-to-all-done.3
  125.3 2.2 %collective-permute-start.7 = (bf16[1024,256]{1,0:T(8,128)(2,1)S(1)}, bf16[1024,256]{1,0:T(8,128)(2,1)}, u32[]{:S(2)}, u32[]{:S(2)}) collective-permute-start(bf16[1024,256]{1,0:T(8,128)(2,1)S(1)} %bitcast.23), channel_id=1, source_target_pairs={{0,2},{2,0},{1,3},{3,1},{4,6},{6,4},{5,7},{7,5},{8,10},{10,8},{9,1... | collective-permute-start | bytes 1572872 | tf_op jit(solution)/shard_map/ppermute | solution.py:35
  127.5 0.0 collective-permute-done.5.kv2.across_ref
  127.5 0.0 collective-permute-done.6.kv3
  127.5 0.0 copy-start.6
  127.5 0.7 copy-done.6
  128.3 0.8 copy-done.8
  129.0 3.5 %attention_rows.1 = (bf16[128,128]{1,0:T(8,128)(2,1)}, f32[2,128]{1,0:T(2,128)S(1)}, bf16[128,128]{1,0:T(8,128)(2,1)S(1)}) custom-call(bf16[128,128]{1,0:T(8,128)(2,1)S(1)} %copy-done.6, bf16[1024,256]{1,0:T(8,128)(2,1)} %bitcast.3.kv0, bf16[1024,256]{1,0:T(8,128)(2,1)} %collective-permute-done.4.kv1, ...), custom_call_target="tpu_custom_call" | custom-call | tf_op jit(solution)/shard_map/attention_rows/pallas_call | solution.py:223
  132.6 0.6 copy-done.9
  133.2 0.6 broadcast_in_dim.15
  133.8 7.5 %all-to-all-start.4 = ((f32[16,2,128]{2,1,0:T(2,128)}), f32[16,2,128]{2,1,0:T(2,128)S(1)}, u32[]{:S(2)}, u32[]{:S(2)}) async-start(f32[16,2,128]{2,1,0:T(2,128)} %broadcast_in_dim.15), calls=%async_computation.4 | async-start | bytes 32768 | tf_op jit(solution)/shard_map/all_to_all | solution.py:27
  141.3 0.0 collective-permute-done.7.qc1
  141.3 7.4 %all-to-all-done.4.stats_ref = f32[16,2,128]{2,1,0:T(2,128)S(1)} async-done(((f32[16,2,128]{2,1,0:T(2,128)}), f32[16,2,128]{2,1,0:T(2,128)S(1)}, u32[]{:S(2)}, u32[]{:S(2)}) %all-to-all-start.4) | async-done | bytes 16416 | tf_op jit(solution)/shard_map/all_to_all | solution.py:27
  148.7 0.8 copy-done.4
  149.6 2.5 %attention_columns.1 = (f32[128,256]{1,0:T(8,128)S(1)}, f32[128,256]{1,0:T(8,128)S(1)}) custom-call(bf16[128,256]{1,0:T(8,128)(2,1)S(1)} %copy-done.4, bf16[1024,256]{1,0:T(8,128)(2,1)S(1)} %collective-permute-done.5.kv2.across_ref, bf16[1024,256]{1,0:T(8,128)(2,1)S(1)} %bitcast.24, bf16[1024,256]{1,0:T(8,128)(2,1)} %collective-permute-done.7.qc1, ...), custom_call_target="tpu_custom_call" | custom-call | tf_op jit(solution)/shard_map/attention_columns/pallas_call | solution.py:239
  152.1 3.6 %collective-permute-start.8 = (f32[128,256]{1,0:T(8,128)S(1)}, f32[128,256]{1,0:T(8,128)S(1)}, u32[]{:S(2)}, u32[]{:S(2)}) collective-permute-start(f32[128,256]{1,0:T(8,128)S(1)} %get-tuple-element.15), channel_id=1, source_target_pairs={{0,1},{1,0},{2,3},{3,2},{4,5},{5,4},{6,7},{7,6},{8,9},{9,8},{10,11... | collective-permute-start | bytes 393224 | tf_op jit(solution)/shard_map/ppermute | solution.py:35
  155.7 1.0 collective-permute-done.8
  156.7 0.8 pad_maximum_fusion.2
  157.5 0.1 broadcast_in_dim.16
  157.6 15.9 %all_to_all.41 = bf16[8,128,384]{2,1,0:T(8,128)(2,1)S(1)} all-to-all(bf16[8,128,384]{2,1,0:T(8,128)(2,1)S(1)} %broadcast_in_dim.16), channel_id=1, replica_groups=mesh['xh'=2,'yh'=4,'yl'=2,'zh'=4,'zl'=2,'xl'=2,'core'=2] {'xh','yl','zl'}, dimensions={0} | all-to-all | bytes 1572864 | tf_op jit(solution)/shard_map/all_to_all | solution.py:27
  173.5 0.7 weight_gradient.3
  174.2 3.4 %collective-permute-start.9 = (bf16[4,128,384]{2,1,0:T(8,128)(2,1)S(1)}, bf16[4,128,384]{2,1,0:T(8,128)(2,1)S(1)}, u32[]{:S(2)}, u32[]{:S(2)}) collective-permute-start(bf16[4,128,384]{2,1,0:T(8,128)(2,1)S(1)} %weight_gradient.3), channel_id=1, source_target_pairs={{0,1},{1,0},{2,3},{3,2},{4,5},{5,4},{6,7},{7,6},{8,9},{9,8},{10,11... | collective-permute-start | bytes 1179656 | tf_op jit(solution)/shard_map/ppermute | solution.py:35
  177.7 0.7 weight_gradient.2
  178.4 0.6 collective-permute-done.9
  179.0 0.1 add_convert_fusion
  179.1 24.3 %all_to_all.42 = bf16[32,16,384]{2,1,0:T(8,128)(2,1)S(1)} all-to-all(bf16[32,16,384]{2,1,0:T(8,128)(2,1)S(1)} %bitcast.28), channel_id=1, replica_groups=mesh['xh'=2,'yh'=4,'yl'=2,'zh'=4,'zl'=2,'xl'=2,'core'=2] {'yh','zh','xl'}, dimensions={0} | all-to-all | bytes 786432 | tf_op jit(solution)/shard_map/all_to_all | solution.py:27
  203.4 0.1 reduce_sum.25
  203.5 11.7 %all_to_all.43 = bf16[16,16,384]{2,1,0:T(8,128)(2,1)S(1)} all-to-all(bf16[16,16,384]{2,1,0:T(8,128)(2,1)S(1)} %broadcast_in_dim.17), channel_id=1, replica_groups=mesh['xh'=2,'yh'=4,'yl'=2,'zh'=4,'zl'=2,'xl'=2,'core'=2] {'zh','zl','xl'}, dimensions={0} | all-to-all | bytes 393216 | tf_op jit(solution)/shard_map/all_to_all | solution.py:27
  215.2 4.9 %collective-permute-start.10 = (bf16[2,4,2,16,384]{4,3,2,0,1:T(8,128)(2,1)S(1)}, bf16[2,4,2,16,384]{4,3,2,0,1:T(8,128)(2,1)S(1)}, u32[]{:S(2)}, u32[]{:S(2)}) collective-permute-start(bf16[2,4,2,16,384]{4,3,2,0,1:T(8,128)(2,1)S(1)} %bitcast.29), channel_id=1, source_target_pairs={{0,1},{1,0},{2,3},{3,2},{4,5},{5,4},{6,7},{7,6},{8,9},{9,8},{10,11... | collective-permute-start | bytes 589832 | tf_op jit(solution)/shard_map/ppermute | solution.py:35
  220.1 1.0 collective-permute-done.10
  221.2 0.8 copy.6
  (14 shorter events, 0.2 us)
Async XLA Ops:
  0.6 1.0 copy-start
  1.6 19.2 %collective-permute-start = (bf16[128,384]{1,0:T(8,128)(2,1)S(1)}, bf16[128,384]{1,0:T(8,128)(2,1)S(1)}, u32[]{:S(2)}, u32[]{:S(2)}) collective-permute-start(bf16[128,384]{1,0:T(8,128)(2,1)S(1)} %constant_dynamic-slice_fusion), channel_id=1, source_target_pairs={{0,64},{64,128},{128,192},{192,0},{1,65},{65,129},{129,193},{193,1... | collective-permute-start | bytes 294920 | tf_op jit(solution)/shard_map/ppermute | solution.py:195
  6.7 14.1 %collective-permute-start.1 = (bf16[128,384]{1,0:T(8,128)(2,1)S(1)}, bf16[128,384]{1,0:T(8,128)(2,1)S(1)}, u32[]{:S(2)}, u32[]{:S(2)}) collective-permute-start(bf16[128,384]{1,0:T(8,128)(2,1)S(1)} %constant_dynamic-slice_fusion), channel_id=1, source_target_pairs={{0,128},{64,192},{128,0},{192,64},{1,129},{65,193},{129,1},{193,65... | collective-permute-start | bytes 294920 | tf_op jit(solution)/shard_map/ppermute | solution.py:195
  12.4 9.4 %collective-permute-start.2 = (bf16[128,384]{1,0:T(8,128)(2,1)S(1)}, bf16[128,384]{1,0:T(8,128)(2,1)S(1)}, u32[]{:S(2)}, u32[]{:S(2)}) collective-permute-start(bf16[128,384]{1,0:T(8,128)(2,1)S(1)} %constant_dynamic-slice_fusion), channel_id=1, source_target_pairs={{0,192},{64,0},{128,64},{192,128},{1,193},{65,1},{129,65},{193,129... | collective-permute-start | bytes 294920 | tf_op jit(solution)/shard_map/ppermute | solution.py:195
  17.3 1.6 copy-start.2
  19.5 1.3 copy-start.1
  21.8 39.2 %all-to-all-start = ((bf16[8,128,1024]{2,1,0:T(8,128)(2,1)}), bf16[8,128,1024]{2,1,0:T(8,128)(2,1)S(1)}, u32[]{:S(2)}, u32[]{:S(2)}) async-start(bf16[8,128,1024]{2,1,0:T(8,128)(2,1)} %copy-done.1), calls=%async_computation | async-start | bytes 4194304 | tf_op jit(solution)/shard_map/all_to_all | solution.py:27
  28.7 4.1 %collective-permute-start.3 = (bf16[512,384]{1,0:T(8,128)(2,1)S(1)}, bf16[512,384]{1,0:T(8,128)(2,1)S(1)}, u32[]{:S(2)}, u32[]{:S(2)}) collective-permute-start(bf16[512,384]{1,0:T(8,128)(2,1)S(1)} %pad_maximum_fusion.near_ref), channel_id=1, source_target_pairs={{0,1},{1,0},{2,3},{3,2},{4,5},{5,4},{6,7},{7,6},{8,9},{9,8},{10,11... | collective-permute-start | bytes 1179656 | tf_op jit(solution)/shard_map/ppermute | solution.py:35
  62.3 25.9 %copy-start.7 = (bf16[1,128,128]{2,1,0:T(8,128)(2,1)S(1)}, bf16[1,128,128]{2,1,0:T(8,128)(2,1)}, u32[]{:S(2)}) copy-start(bf16[1,128,128]{2,1,0:T(8,128)(2,1)} %param.5) | copy-start | bytes 98308
  78.4 0.6 copy-start.3
  79.0 23.4 %all-to-all-start.2 = ((bf16[8,128,256]{2,1,0:T(8,128)(2,1)}), bf16[8,128,256]{2,1,0:T(8,128)(2,1)}, u32[]{:S(2)}, u32[]{:S(2)}) async-start(bf16[8,128,256]{2,1,0:T(8,128)(2,1)} %broadcast_in_dim.12), calls=%async_computation.2 | async-start | bytes 1048576 | tf_op jit(solution)/shard_map/all_to_all | solution.py:27
  88.2 0.6 copy-start.5
  103.3 22.0 %all-to-all-start.3 = ((bf16[8,128,256]{2,1,0:T(8,128)(2,1)}), bf16[8,128,256]{2,1,0:T(8,128)(2,1)S(1)}, u32[]{:S(2)}, u32[]{:S(2)}) async-start(bf16[8,128,256]{2,1,0:T(8,128)(2,1)} %broadcast_in_dim.14), calls=%async_computation.3 | async-start | bytes 1048576 | tf_op jit(solution)/shard_map/all_to_all | solution.py:27
  106.8 11.4 %collective-permute-start.4 = (bf16[1024,256]{1,0:T(8,128)(2,1)}, bf16[1024,256]{1,0:T(8,128)(2,1)}, u32[]{:S(2)}, u32[]{:S(2)}) collective-permute-start(bf16[1024,256]{1,0:T(8,128)(2,1)} %bitcast.3.kv0), channel_id=1, source_target_pairs={{0,2},{2,0},{1,3},{3,1},{4,6},{6,4},{5,7},{7,5},{8,10},{10,8},{9,1... | collective-permute-start | bytes 1572872 | tf_op jit(solution)/shard_map/ppermute | solution.py:35
  109.0 18.5 %collective-permute-start.5 = (bf16[1024,256]{1,0:T(8,128)(2,1)}, bf16[1024,256]{1,0:T(8,128)(2,1)S(1)}, u32[]{:S(2)}, u32[]{:S(2)}) collective-permute-start(bf16[1024,256]{1,0:T(8,128)(2,1)} %bitcast.3.kv0), channel_id=1, source_target_pairs={{0,1},{1,0},{2,3},{3,2},{4,5},{5,4},{6,7},{7,6},{8,9},{9,8},{10,11... | collective-permute-start | bytes 1572872 | tf_op jit(solution)/shard_map/ppermute | solution.py:35
  118.1 9.4 %collective-permute-start.6 = (bf16[1024,256]{1,0:T(8,128)(2,1)}, bf16[1024,256]{1,0:T(8,128)(2,1)}, u32[]{:S(2)}, u32[]{:S(2)}) collective-permute-start(bf16[1024,256]{1,0:T(8,128)(2,1)} %collective-permute-done.4.kv1), channel_id=1, source_target_pairs={{0,1},{1,0},{2,3},{3,2},{4,5},{5,4},{6,7},{7,6},{8,9},{9,8},{10,11... | collective-permute-start | bytes 1572872 | tf_op jit(solution)/shard_map/ppermute | solution.py:35
  125.3 16.1 %collective-permute-start.7 = (bf16[1024,256]{1,0:T(8,128)(2,1)S(1)}, bf16[1024,256]{1,0:T(8,128)(2,1)}, u32[]{:S(2)}, u32[]{:S(2)}) collective-permute-start(bf16[1024,256]{1,0:T(8,128)(2,1)S(1)} %bitcast.23), channel_id=1, source_target_pairs={{0,2},{2,0},{1,3},{3,1},{4,6},{6,4},{5,7},{7,5},{8,10},{10,8},{9,1... | collective-permute-start | bytes 1572872 | tf_op jit(solution)/shard_map/ppermute | solution.py:35
  127.5 0.8 copy-start.6
  128.3 0.8 copy-start.8
  132.6 0.6 copy-start.9
  133.8 14.9 %all-to-all-start.4 = ((f32[16,2,128]{2,1,0:T(2,128)}), f32[16,2,128]{2,1,0:T(2,128)S(1)}, u32[]{:S(2)}, u32[]{:S(2)}) async-start(f32[16,2,128]{2,1,0:T(2,128)} %broadcast_in_dim.15), calls=%async_computation.4 | async-start | bytes 32768 | tf_op jit(solution)/shard_map/all_to_all | solution.py:27
  148.7 0.8 copy-start.4
  152.1 4.6 %collective-permute-start.8 = (f32[128,256]{1,0:T(8,128)S(1)}, f32[128,256]{1,0:T(8,128)S(1)}, u32[]{:S(2)}, u32[]{:S(2)}) collective-permute-start(f32[128,256]{1,0:T(8,128)S(1)} %get-tuple-element.15), channel_id=1, source_target_pairs={{0,1},{1,0},{2,3},{3,2},{4,5},{5,4},{6,7},{7,6},{8,9},{9,8},{10,11... | collective-permute-start | bytes 393224 | tf_op jit(solution)/shard_map/ppermute | solution.py:35
  174.2 4.8 %collective-permute-start.9 = (bf16[4,128,384]{2,1,0:T(8,128)(2,1)S(1)}, bf16[4,128,384]{2,1,0:T(8,128)(2,1)S(1)}, u32[]{:S(2)}, u32[]{:S(2)}) collective-permute-start(bf16[4,128,384]{2,1,0:T(8,128)(2,1)S(1)} %weight_gradient.3), channel_id=1, source_target_pairs={{0,1},{1,0},{2,3},{3,2},{4,5},{5,4},{6,7},{7,6},{8,9},{9,8},{10,11... | collective-permute-start | bytes 1179656 | tf_op jit(solution)/shard_map/ppermute | solution.py:35
  215.2 5.9 %collective-permute-start.10 = (bf16[2,4,2,16,384]{4,3,2,0,1:T(8,128)(2,1)S(1)}, bf16[2,4,2,16,384]{4,3,2,0,1:T(8,128)(2,1)S(1)}, u32[]{:S(2)}, u32[]{:S(2)}) collective-permute-start(bf16[2,4,2,16,384]{4,3,2,0,1:T(8,128)(2,1)S(1)} %bitcast.29), channel_id=1, source_target_pairs={{0,1},{1,0},{2,3},{3,2},{4,5},{5,4},{6,7},{7,6},{8,9},{9,8},{10,11... | collective-permute-start | bytes 589832 | tf_op jit(solution)/shard_map/ppermute | solution.py:35

commit v7 on v6

--- a/solution.py
+++ b/solution.py
@@ -35,9 +35,8 @@
     return lax.ppermute(block, axis, ((0, 1), (1, 0)))
 
 
-def gather_x(block):
-    along_z = spread(block, z_axes, lax.axis_size(z_axes)).reshape(-1, block.shape[1])
-    return along_z, swap(along_z, "xl")
+def gather_z(block):
+    return spread(block, z_axes, lax.axis_size(z_axes)).reshape(-1, block.shape[1])
 
 
 def positions(device, inside, half_rows, ctx_count):
@@ -99,7 +98,7 @@
     dq_ref[...] = (grad * scale).astype(low)
 
 
-def backward_kernel(z_count, kv_ref, across_ref, qc0, qc1, stats_ref, own_ref, other_ref):
+def backward_kernel(z_count, kv_ref, across_ref, q0, q1, cot_ref, stats_ref, own_ref, other_ref):
     rows, head = kv_ref.shape[0], kv_ref.shape[1] // 2
     half_rows, ctx_count = rows // 2, 4 * z_count
     scale = 1.0 / math.sqrt(head)
@@ -119,9 +118,12 @@
     keys, values = pairs[:, :head], pairs[:, head:]
     grad_key = jnp.zeros((2 * rows, head), jnp.float32)
     grad_value = jnp.zeros((2 * rows, head), jnp.float32)
-    for piece, both in enumerate((qc0, qc1)):
+    for piece, queries_ref in enumerate((q0, q1)):
         slot = lax.axis_index("xl") ^ piece
-        queries, cotangent = both[:, :head], both[:, head:]
+        queries = queries_ref[...]
+        cotangent = jnp.concatenate(
+            [cot_ref[2 * z + slot, :, :head] for z in range(z_count)], axis=0
+        )
         scores = dot_f32(keys, queries, 1, 1) * scale
         dprob = dot_f32(values, cotangent, 1, 1)
         probs, dscores = [], []
@@ -141,38 +143,29 @@
     other_ref[:, :head], other_ref[:, head:] = grad_key[rows:], grad_value[rows:]
 
 
-def shard_row(step, count):
-    return lax.rem(lax.axis_index("yh") + count - step, count)
-
-
 def relayout_kernel(y_half, tokens_ref, out_ref):
     members, _, columns = out_ref.shape
-    quarter = columns // (2 * y_half)
-    core = lax.axis_index("core")
+    span = columns // y_half
     for member in range(members):
         x_hi, y_lo, z_lo = member // 4, member // 2 % 2, member % 2
-        for half in range(2):
-            for step in range(y_half):
-                shard = (x_hi * y_half + shard_row(step, y_half)) * 2 + y_lo
-                start = (shard * 4 + z_lo * 2 + (core ^ half)) * quarter
-                target = (half * y_half + step) * quarter
-                out_ref[member, :, target : target + quarter] = tokens_ref[
-                    :, pl.ds(pl.multiple_of(start, quarter), quarter)
-                ]
-
-
-def project_kernel(x_ref, near_ref, far_ref, out_ref):
-    depth = near_ref.shape[0]
-    total = dot_f32(x_ref[:, :depth], near_ref[...], 1, 0)
-    total = total + dot_f32(x_ref[:, depth:], far_ref[...], 1, 0)
-    out_ref[...] = total.astype(low)
-
-
-def weight_kernel(y_half, x_ref, grad_ref, out_ref):
-    total = dot_f32(x_ref[...], grad_ref[...], 0, 0).astype(out_ref.dtype)
-    quarter = total.shape[0] // y_half
-    for step in range(y_half):
-        out_ref[shard_row(step, y_half)] = total[step * quarter : (step + 1) * quarter]
+        for y_hi in range(y_half):
+            start = (((x_hi * y_half + y_hi) * 2 + y_lo) * 2 + z_lo) * span
+            out_ref[member, :, y_hi * span : (y_hi + 1) * span] = tokens_ref[:, start : start + span]
+
+
+def project_kernel(x_ref, weight_ref, out_ref):
+    out_ref[...] = dot_f32(x_ref[...], weight_ref[...], 1, 0).astype(low)
+
+
+def weight_kernel(y_half, half, x_ref, grad_ref, out_ref):
+    quarter = x_ref.shape[1] // (2 * y_half)
+    core = lax.axis_index("core") ^ half
+    columns = []
+    for y_hi in range(y_half):
+        start = pl.multiple_of((y_hi * 2 + core) * quarter, quarter)
+        columns.append(x_ref[:, pl.ds(start, quarter)])
+    total = dot_f32(jnp.concatenate(columns, axis=1), grad_ref[...], 0, 0)
+    out_ref[...] = total.astype(out_ref.dtype)
 
 
 def in_vmem(count):
@@ -187,13 +180,6 @@
     quarter, depth, group_rows = shard // 4, model // 16, 8 * row_count
     cotangent = out_grad[0]
 
-    at = (lax.axis_index("zl") * 2 + lax.axis_index("core")) * quarter
-    own_weight = lax.dynamic_slice_in_dim(qkv_weight, at, quarter)
-    steps = [own_weight]
-    for step in range(1, y_half):
-        ring = [(i, (i + step) % y_half) for i in range(y_half)]
-        steps.append(lax.ppermute(own_weight, "yh", ring))
-    near = jnp.concatenate(steps)
     split = pl.pallas_call(
         functools.partial(relayout_kernel, y_half),
         in_specs=in_vmem(1),
@@ -202,23 +188,29 @@
         compiler_params=vmem,
         name="token_columns",
     )(tokens[0])
-    split, near = lax.optimization_barrier((split, near))
-    far = swap(near, "core")
     columns = exchange(split, group_axes).reshape(group_rows, 2 * depth)
+    at = (lax.axis_index("zl") * 2 + lax.axis_index("core")) * quarter
+    own_weight = lax.dynamic_slice_in_dim(qkv_weight, at, quarter)
+    weight = lax.all_gather(own_weight, ("yh", "core"), axis=0, tiled=True)
     parts = pl.pallas_call(
         project_kernel,
-        in_specs=in_vmem(3),
+        in_specs=in_vmem(2),
         out_specs=in_vmem(1)[0],
         out_shape=jax.ShapeDtypeStruct((group_rows, width), low),
         compiler_params=vmem,
         name="partial_projection",
-    )(columns, near, far)
+    )(columns, weight)
     parts = exchange(parts.reshape(8, row_count, width), group_axes)
     qkv = jnp.sum(parts.astype(jnp.float32), axis=0).astype(low)
     queries, own_pairs = qkv[:, :head], qkv[:, head:]
-    pair_pieces = gather_x(own_pairs)
+    cotangent_all = lax.all_gather(
+        jnp.concatenate([cotangent, cotangent], axis=1), z_axes + ("xl",), axis=0, tiled=False
+    )
+    along_z, cotangent_all = lax.optimization_barrier((gather_z(own_pairs), cotangent_all))
+    pair_pieces = (along_z, swap(along_z, "xl"))
     pair_pieces = pair_pieces + tuple(swap(p, "core") for p in pair_pieces)
-    query_pieces = gather_x(jnp.concatenate([queries, cotangent], axis=1))
+    queries_z = gather_z(queries)
+    query_pieces = (queries_z, swap(queries_z, "xl"))
 
     attn_rows, stats, grad_query = pl.pallas_call(
         functools.partial(forward_kernel, z_count),
@@ -238,12 +230,12 @@
 
     own_part, other_part = pl.pallas_call(
         functools.partial(backward_kernel, z_count),
-        in_specs=in_vmem(5),
+        in_specs=in_vmem(6),
         out_specs=in_vmem(2),
         out_shape=[jax.ShapeDtypeStruct((row_count, 2 * head), jnp.float32)] * 2,
         compiler_params=vmem,
         name="attention_columns",
-    )(own_pairs, pair_pieces[2], *query_pieces, stats_all)
+    )(own_pairs, pair_pieces[2], *query_pieces, cotangent_all, stats_all)
     grad_pairs = (own_part + swap(other_part, "core")).astype(low)
 
     grad_all = spread(jnp.concatenate([grad_query, grad_pairs], axis=1), group_axes, 8)
@@ -251,14 +243,10 @@
 
     def weight_half(half, dtype):
         return pl.pallas_call(
-            functools.partial(weight_kernel, y_half),
-            grid=(1,),
-            in_specs=[
-                pl.BlockSpec((group_rows, depth), lambda i: (0, half)),
-                pl.BlockSpec((group_rows, width), lambda i: (0, 0)),
-            ],
-            out_specs=pl.BlockSpec((y_half, quarter, width), lambda i: (0, 0, 0)),
-            out_shape=jax.ShapeDtypeStruct((y_half, quarter, width), dtype),
+            functools.partial(weight_kernel, y_half, half),
+            in_specs=in_vmem(2),
+            out_specs=in_vmem(1)[0],
+            out_shape=jax.ShapeDtypeStruct((depth, width), dtype),
             compiler_params=vmem,
             name="weight_gradient",
         )(columns, grad_all)

time: 223 us -> 273 us (1.22)
  blocking collectives: 67.1 us -> 96.8 us
  between operations: 0.95 us -> 14.3 us
  waiting for transfers between devices: 56.7 us -> 68.8 us
  starting transfers between devices: 75.5 us -> 69.3 us
    all_gather x0 -> x1, waiting for transfers between devices: none -> 45.3 us  [on_device(): lax.all_gather(jnp.concatenate([cotangent, cotangent], axis=1), z_axes +...]
    all_gather x0 -> x1, blocking collectives: none -> 42.6 us  [on_device(): weight = lax.all_gather(own_weight, ('yh', 'core'), axis=0, tiled=True)]
    all_to_all x4 -> x5, waiting for transfers between devices: 49.2 us -> 20.8 us  [exchange(): return lax.all_to_all(blocks, axes, split_axis=0, concat_axis=0, tiled=True)]
    ppermute x3 -> x0, starting transfers between devices: 15.7 us -> none  [on_device(): steps.append(lax.ppermute(own_weight, 'yh', ring))]
    all_to_all x4 -> x3, blocking collectives: 67.1 us -> 54.2 us  [exchange(): return lax.all_to_all(blocks, axes, split_axis=0, concat_axis=0, tiled=True)]
    all_to_all x4 -> x5, starting transfers between devices: 27.1 us -> 35.7 us  [exchange(): return lax.all_to_all(blocks, axes, split_axis=0, concat_axis=0, tiled=True)]
    ppermute x8 -> x7, waiting for transfers between devices: 6.58 us -> 2.59 us  [swap(): return lax.ppermute(block, axis, ((0, 1), (1, 0)))]
    ppermute x8 -> x7, starting transfers between devices: 32.8 us -> 33.6 us  [swap(): return lax.ppermute(block, axis, ((0, 1), (1, 0)))]
  transfers between devices with their start and end apart: 15 -> 13, of which waited for: 9 -> 6; matrix products, arithmetic and copies ran while one was open for 0% -> 1% of each run, Pallas kernels for 2% -> 2%
where the time goes in v7:
time: 273 us; the launch traced here: 271 us
  blocking collectives  96.8 us (35%)
  starting transfers between devices  69.3 us (25%)
  waiting for transfers between devices  68.8 us (25%)
  between operations  14.3 us (5%)
  local copies, waits for them, and re-layouts  11.5 us (4%)
  Pallas kernels  9.78 us (4%)
    all_to_all x3, blocking collectives, exchange(): return lax.all_to_all(blocks, axes, split_axis=0, concat_axis=0, tiled=True)  54.2 us
    all_gather x1, waiting for transfers between devices, on_device(): lax.all_gather(jnp.concatenate([cotangent, cotangent], axis=1), z_axes +...  45.3 us
    all_gather x1, blocking collectives, on_device(): weight = lax.all_gather(own_weight, ('yh', 'core'), axis=0, tiled=True)  42.6 us
    all_to_all x5, starting transfers between devices, exchange(): return lax.all_to_all(blocks, axes, split_axis=0, concat_axis=0, tiled=True)  35.7 us
    ppermute x7, starting transfers between devices, swap(): return lax.ppermute(block, axis, ((0, 1), (1, 0)))  33.6 us
    all_to_all x5, waiting for transfers between devices, exchange(): return lax.all_to_all(blocks, axes, split_axis=0, concat_axis=0, tiled=True)  20.8 us
    unnamed x24, local copies, waits for them, and re-layouts  8.4 us
  transfers between devices with their start and end apart: 13, of which 6 were waited for; matrix products, arithmetic and copies ran while one was open for 1% of the time, Pallas kernels for 2%

profile of v7, /device:TPU:1, one launch (start us, length us, event | category | flops | bytes accessed | tf_op | source)
XLA Modules:
  0.0 271.5 jit_solution(2756991710211084920)
XLA Ops:
  7.2 0.0 copy-start
  7.2 0.0 copy-start.2
  7.2 1.6 copy-done.2
  8.8 0.3 token_columns.1
  9.1 0.0 copy-start.1
  9.1 1.3 copy-done.1
  10.4 7.7 %all-to-all-start = ((bf16[8,128,1024]{2,1,0:T(8,128)(2,1)}), bf16[8,128,1024]{2,1,0:T(8,128)(2,1)S(1)}, u32[]{:S(2)}, u32[]{:S(2)}) async-start(bf16[8,128,1024]{2,1,0:T(8,128)(2,1)} %copy-done.1), calls=%async_computation | async-start | bytes 4194304 | tf_op jit(solution)/shard_map/all_to_all | solution.py:27
  18.1 0.0 copy-done
  18.1 42.6 %all_gather.9.weight_ref = bf16[1024,384]{1,0:T(8,128)(2,1)S(1)} all-gather(bf16[128,384]{1,0:T(8,128)(2,1)S(1)} %constant_dynamic-slice_fusion), channel_id=1, replica_groups=mesh['xh'=2,'yh'=4,'yl'=2,'zh'=4,'zl'=2,'xl'=2,'core'=2] {'yh','core'}, dimensions={0}, use_global_device_ids=true | all-gather | bytes 884736 | tf_op jit(solution)/shard_map/all_gather | solution.py:194
  60.7 0.0 all-to-all-done
  60.7 0.0 copy-start.8
  60.7 2.1 partial_projection.1
  62.8 7.4 %all-to-all-start.1 = ((bf16[8,128,384]{2,1,0:T(8,128)(2,1)}), bf16[8,128,384]{2,1,0:T(8,128)(2,1)S(1)}, u32[]{:S(2)}, u32[]{:S(2)}) async-start(bf16[8,128,384]{2,1,0:T(8,128)(2,1)} %bitcast.2), calls=%async_computation.1 | async-start | bytes 1572864 | tf_op jit(solution)/shard_map/all_to_all | solution.py:27
  70.2 0.0 all-gather.3.cloned.1.call-start
  70.2 0.0 copy-done.8
  70.2 0.6 pad_maximum_fusion.2
  70.9 0.0 all-gather.3.cloned.1.call-update
  70.9 13.4 %all-to-all-done.1 = bf16[8,128,384]{2,1,0:T(8,128)(2,1)S(1)} async-done(((bf16[8,128,384]{2,1,0:T(8,128)(2,1)}), bf16[8,128,384]{2,1,0:T(8,128)(2,1)S(1)}, u32[]{:S(2)}, u32[]{:S(2)}) %all-to-all-start.1) | async-done | bytes 786464 | tf_op jit(solution)/shard_map/all_to_all | solution.py:27
  84.4 0.1 reduce_sum.24
  84.5 0.8 broadcast_in_dim.12
  85.3 0.6 copy-done.4
  85.9 9.1 %all-to-all-start.2 = ((bf16[8,128,256]{2,1,0:T(8,128)(2,1)}), bf16[8,128,256]{2,1,0:T(8,128)(2,1)S(1)}, u32[]{:S(2)}, u32[]{:S(2)}) async-start(bf16[8,128,256]{2,1,0:T(8,128)(2,1)} %broadcast_in_dim.12), calls=%async_computation.2 | async-start | bytes 1048576 | tf_op jit(solution)/shard_map/all_to_all | solution.py:27
  95.1 45.3 %all-gather.3.cloned.1.call-done = bf16[2048,256]{1,0:T(8,128)(2,1)} async-done(((bf16[128,256]{1,0:T(8,128)(2,1)}), bf16[2048,256]{1,0:T(8,128)(2,1)}) %all-gather.3.cloned.1.call-update) | async-done | bytes 1048592 | tf_op jit(solution)/shard_map/all_gather | solution.py:206
  140.4 0.0 all-to-all-done.2
  140.4 3.0 %collective-permute-start = (bf16[1024,256]{1,0:T(8,128)(2,1)S(1)}, bf16[1024,256]{1,0:T(8,128)(2,1)}, u32[]{:S(2)}, u32[]{:S(2)}) collective-permute-start(bf16[1024,256]{1,0:T(8,128)(2,1)S(1)} %bitcast.24), channel_id=1, source_target_pairs={{0,2},{2,0},{1,3},{3,1},{4,6},{6,4},{5,7},{7,5},{8,10},{10,8},{9,1... | collective-permute-start | bytes 1572872 | tf_op jit(solution)/shard_map/ppermute | solution.py:35
  143.4 0.7 broadcast_in_dim.14
  144.2 0.6 copy-done.6
  144.8 4.2 %all-to-all-start.3 = ((bf16[8,128,128]{2,1,0:T(8,128)(2,1)}), bf16[8,128,128]{2,1,0:T(8,128)(2,1)}, u32[]{:S(2)}, u32[]{:S(2)}) async-start(bf16[8,128,128]{2,1,0:T(8,128)(2,1)} %broadcast_in_dim.14), calls=%async_computation.3 | async-start | bytes 524288 | tf_op jit(solution)/shard_map/all_to_all | solution.py:27
  149.0 11.7 %collective-permute-start.1 = (bf16[1024,256]{1,0:T(8,128)(2,1)S(1)}, bf16[1024,256]{1,0:T(8,128)(2,1)S(1)}, u32[]{:S(2)}, u32[]{:S(2)}) collective-permute-start(bf16[1024,256]{1,0:T(8,128)(2,1)S(1)} %bitcast.25), channel_id=1, source_target_pairs={{0,1},{1,0},{2,3},{3,2},{4,5},{5,4},{6,7},{7,6},{8,9},{9,8},{10,11... | collective-permute-start | bytes 1572872 | tf_op jit(solution)/shard_map/ppermute | solution.py:35
  160.7 0.0 collective-permute-done.kv1
  160.7 1.9 collective-permute-start.2
  162.6 0.0 all-to-all-done.3
  162.6 2.8 %collective-permute-start.3 = (bf16[1024,128]{1,0:T(8,128)(2,1)}, bf16[1024,128]{1,0:T(8,128)(2,1)}, u32[]{:S(2)}, u32[]{:S(2)}) collective-permute-start(bf16[1024,128]{1,0:T(8,128)(2,1)} %bitcast.7.q0), channel_id=1, source_target_pairs={{0,2},{2,0},{1,3},{3,1},{4,6},{6,4},{5,7},{7,5},{8,10},{10,8},{9,1... | collective-permute-start | bytes 786440 | tf_op jit(solution)/shard_map/ppermute | solution.py:35
  165.5 0.0 collective-permute-done.1.kv2.across_ref
  165.5 0.0 collective-permute-done.2.kv3
  165.5 0.0 copy-start.7
  165.5 0.7 copy-done.7
  166.3 0.8 copy-done.9
  167.0 3.4 %attention_rows.1 = (bf16[128,128]{1,0:T(8,128)(2,1)}, f32[2,128]{1,0:T(2,128)S(1)}, bf16[128,128]{1,0:T(8,128)(2,1)S(1)}) custom-call(bf16[128,128]{1,0:T(8,128)(2,1)S(1)} %copy-done.7, bf16[1024,256]{1,0:T(8,128)(2,1)S(1)} %bitcast.26, bf16[1024,256]{1,0:T(8,128)(2,1)} %collective-permute-done.kv1, ...), custom_call_target="tpu_custom_call" | custom-call | tf_op jit(solution)/shard_map/attention_rows/pallas_call | solution.py:215
  170.4 0.0 copy-start.10
  170.4 0.6 copy-done.10
  171.0 0.6 broadcast_in_dim.15
  171.6 7.3 %all-to-all-start.4 = ((f32[16,2,128]{2,1,0:T(2,128)}), f32[16,2,128]{2,1,0:T(2,128)S(1)}, u32[]{:S(2)}, u32[]{:S(2)}) async-start(f32[16,2,128]{2,1,0:T(2,128)} %broadcast_in_dim.15), calls=%async_computation.4 | async-start | bytes 32768 | tf_op jit(solution)/shard_map/all_to_all | solution.py:27
  178.9 0.0 collective-permute-done.3.q1
  178.9 7.4 %all-to-all-done.4.stats_ref = f32[16,2,128]{2,1,0:T(2,128)S(1)} async-done(((f32[16,2,128]{2,1,0:T(2,128)}), f32[16,2,128]{2,1,0:T(2,128)S(1)}, u32[]{:S(2)}, u32[]{:S(2)}) %all-to-all-start.4) | async-done | bytes 16416 | tf_op jit(solution)/shard_map/all_to_all | solution.py:27
  186.3 1.2 copy-done.3
  187.6 0.8 copy-done.5
  188.4 2.5 attention_columns.1
  190.9 5.7 %collective-permute-start.4 = (f32[128,256]{1,0:T(8,128)S(1)}, f32[128,256]{1,0:T(8,128)S(1)}, u32[]{:S(2)}, u32[]{:S(2)}) collective-permute-start(f32[128,256]{1,0:T(8,128)S(1)} %get-tuple-element.15), channel_id=1, source_target_pairs={{0,1},{1,0},{2,3},{3,2},{4,5},{5,4},{6,7},{7,6},{8,9},{9,8},{10,11... | collective-permute-start | bytes 393224 | tf_op jit(solution)/shard_map/ppermute | solution.py:35
  196.6 1.0 collective-permute-done.4
  197.6 0.0 copy-done.11
  197.6 0.1 broadcast_in_dim.16
  197.7 19.3 %all_to_all.40 = bf16[8,128,384]{2,1,0:T(8,128)(2,1)S(1)} all-to-all(bf16[8,128,384]{2,1,0:T(8,128)(2,1)S(1)} %broadcast_in_dim.16), channel_id=1, replica_groups=mesh['xh'=2,'yh'=4,'yl'=2,'zh'=4,'zl'=2,'xl'=2,'core'=2] {'xh','yl','zl'}, dimensions={0} | all-to-all | bytes 1572864 | tf_op jit(solution)/shard_map/all_to_all | solution.py:27
  217.0 0.8 weight_gradient.3
  217.7 3.6 %collective-permute-start.5 = (bf16[512,384]{1,0:T(8,128)(2,1)S(1)}, bf16[512,384]{1,0:T(8,128)(2,1)S(1)}, u32[]{:S(2)}, u32[]{:S(2)}) collective-permute-start(bf16[512,384]{1,0:T(8,128)(2,1)S(1)} %weight_gradient.3), channel_id=1, source_target_pairs={{0,1},{1,0},{2,3},{3,2},{4,5},{5,4},{6,7},{7,6},{8,9},{9,8},{10,11... | collective-permute-start | bytes 1179656 | tf_op jit(solution)/shard_map/ppermute | solution.py:35
  221.4 0.8 weight_gradient.2
  222.1 0.6 collective-permute-done.5
  222.7 0.1 add_convert_fusion
  222.8 23.2 %all_to_all.41 = bf16[32,16,384]{2,1,0:T(8,128)(2,1)S(1)} all-to-all(bf16[32,16,384]{2,1,0:T(8,128)(2,1)S(1)} %bitcast.30), channel_id=1, replica_groups=mesh['xh'=2,'yh'=4,'yl'=2,'zh'=4,'zl'=2,'xl'=2,'core'=2] {'yh','zh','xl'}, dimensions={0} | all-to-all | bytes 786432 | tf_op jit(solution)/shard_map/all_to_all | solution.py:27
  246.0 0.1 reduce_sum.25
  246.1 11.7 %all_to_all.42 = bf16[16,16,384]{2,1,0:T(8,128)(2,1)S(1)} all-to-all(bf16[16,16,384]{2,1,0:T(8,128)(2,1)S(1)} %broadcast_in_dim.17), channel_id=1, replica_groups=mesh['xh'=2,'yh'=4,'yl'=2,'zh'=4,'zl'=2,'xl'=2,'core'=2] {'zh','zl','xl'}, dimensions={0} | all-to-all | bytes 393216 | tf_op jit(solution)/shard_map/all_to_all | solution.py:27
  257.8 4.9 %collective-permute-start.6 = (bf16[2,4,2,16,384]{4,3,2,0,1:T(8,128)(2,1)S(1)}, bf16[2,4,2,16,384]{4,3,2,0,1:T(8,128)(2,1)S(1)}, u32[]{:S(2)}, u32[]{:S(2)}) collective-permute-start(bf16[2,4,2,16,384]{4,3,2,0,1:T(8,128)(2,1)S(1)} %bitcast.31), channel_id=1, source_target_pairs={{0,1},{1,0},{2,3},{3,2},{4,5},{5,4},{6,7},{7,6},{8,9},{9,8},{10,11... | collective-permute-start | bytes 589832 | tf_op jit(solution)/shard_map/ppermute | solution.py:35
  262.7 1.0 collective-permute-done.6
  263.8 0.8 copy.6
  (14 shorter events, 0.2 us)
Async XLA Ops:
  7.2 10.9 %copy-start = (bf16[512,384]{1,0:T(8,128)(2,1)S(1)}, bf16[512,384]{1,0:T(8,128)(2,1)}, u32[]{:S(2)}) copy-start(bf16[512,384]{1,0:T(8,128)(2,1)} %param.4) | copy-start | bytes 1179652
  7.2 1.6 copy-start.2
  9.1 1.3 copy-start.1
  10.4 50.3 %all-to-all-start = ((bf16[8,128,1024]{2,1,0:T(8,128)(2,1)}), bf16[8,128,1024]{2,1,0:T(8,128)(2,1)S(1)}, u32[]{:S(2)}, u32[]{:S(2)}) async-start(bf16[8,128,1024]{2,1,0:T(8,128)(2,1)} %copy-done.1), calls=%async_computation | async-start | bytes 4194304 | tf_op jit(solution)/shard_map/all_to_all | solution.py:27
  60.7 9.5 %copy-start.8 = (bf16[1,128,128]{2,1,0:T(8,128)(2,1)S(1)}, bf16[1,128,128]{2,1,0:T(8,128)(2,1)}, u32[]{:S(2)}) copy-start(bf16[1,128,128]{2,1,0:T(8,128)(2,1)} %param.5) | copy-start | bytes 98308
  62.8 21.5 %all-to-all-start.1 = ((bf16[8,128,384]{2,1,0:T(8,128)(2,1)}), bf16[8,128,384]{2,1,0:T(8,128)(2,1)S(1)}, u32[]{:S(2)}, u32[]{:S(2)}) async-start(bf16[8,128,384]{2,1,0:T(8,128)(2,1)} %bitcast.2), calls=%async_computation.1 | async-start | bytes 1572864 | tf_op jit(solution)/shard_map/all_to_all | solution.py:27
  70.2 70.2 %all-gather.3.cloned.1.call-start = ((), (), s32[]{:S(2)}) async-start(), calls=%async_computation.8 | async-start | bytes 1114112 | tf_op jit(solution)/shard_map/all_gather | solution.py:206
  85.3 0.6 copy-start.4
  85.9 54.5 %all-to-all-start.2 = ((bf16[8,128,256]{2,1,0:T(8,128)(2,1)}), bf16[8,128,256]{2,1,0:T(8,128)(2,1)S(1)}, u32[]{:S(2)}, u32[]{:S(2)}) async-start(bf16[8,128,256]{2,1,0:T(8,128)(2,1)} %broadcast_in_dim.12), calls=%async_computation.2 | async-start | bytes 1048576 | tf_op jit(solution)/shard_map/all_to_all | solution.py:27
  140.4 20.3 %collective-permute-start = (bf16[1024,256]{1,0:T(8,128)(2,1)S(1)}, bf16[1024,256]{1,0:T(8,128)(2,1)}, u32[]{:S(2)}, u32[]{:S(2)}) collective-permute-start(bf16[1024,256]{1,0:T(8,128)(2,1)S(1)} %bitcast.24), channel_id=1, source_target_pairs={{0,2},{2,0},{1,3},{3,1},{4,6},{6,4},{5,7},{7,5},{8,10},{10,8},{9,1... | collective-permute-start | bytes 1572872 | tf_op jit(solution)/shard_map/ppermute | solution.py:35
  144.2 0.6 copy-start.6
  144.8 17.9 %all-to-all-start.3 = ((bf16[8,128,128]{2,1,0:T(8,128)(2,1)}), bf16[8,128,128]{2,1,0:T(8,128)(2,1)}, u32[]{:S(2)}, u32[]{:S(2)}) async-start(bf16[8,128,128]{2,1,0:T(8,128)(2,1)} %broadcast_in_dim.14), calls=%async_computation.3 | async-start | bytes 524288 | tf_op jit(solution)/shard_map/all_to_all | solution.py:27
  149.0 16.5 %collective-permute-start.1 = (bf16[1024,256]{1,0:T(8,128)(2,1)S(1)}, bf16[1024,256]{1,0:T(8,128)(2,1)S(1)}, u32[]{:S(2)}, u32[]{:S(2)}) collective-permute-start(bf16[1024,256]{1,0:T(8,128)(2,1)S(1)} %bitcast.25), channel_id=1, source_target_pairs={{0,1},{1,0},{2,3},{3,2},{4,5},{5,4},{6,7},{7,6},{8,9},{9,8},{10,11... | collective-permute-start | bytes 1572872 | tf_op jit(solution)/shard_map/ppermute | solution.py:35
  160.7 4.8 %collective-permute-start.2 = (bf16[1024,256]{1,0:T(8,128)(2,1)}, bf16[1024,256]{1,0:T(8,128)(2,1)}, u32[]{:S(2)}, u32[]{:S(2)}) collective-permute-start(bf16[1024,256]{1,0:T(8,128)(2,1)} %collective-permute-done.kv1), channel_id=1, source_target_pairs={{0,1},{1,0},{2,3},{3,2},{4,5},{5,4},{6,7},{7,6},{8,9},{9,8},{10,11... | collective-permute-start | bytes 1572872 | tf_op jit(solution)/shard_map/ppermute | solution.py:35
  162.6 16.3 %collective-permute-start.3 = (bf16[1024,128]{1,0:T(8,128)(2,1)}, bf16[1024,128]{1,0:T(8,128)(2,1)}, u32[]{:S(2)}, u32[]{:S(2)}) collective-permute-start(bf16[1024,128]{1,0:T(8,128)(2,1)} %bitcast.7.q0), channel_id=1, source_target_pairs={{0,2},{2,0},{1,3},{3,1},{4,6},{6,4},{5,7},{7,5},{8,10},{10,8},{9,1... | collective-permute-start | bytes 786440 | tf_op jit(solution)/shard_map/ppermute | solution.py:35
  165.5 0.8 copy-start.7
  166.3 0.8 copy-start.9
  170.4 0.6 copy-start.10
  171.0 26.6 %copy-start.11 = (bf16[128,128]{1,0:T(8,128)(2,1)S(1)}, bf16[128,128]{1,0:T(8,128)(2,1)}, u32[]{:S(2)}) copy-start(bf16[128,128]{1,0:T(8,128)(2,1)} %copy-done.10) | copy-start | bytes 98308
  171.6 14.7 %all-to-all-start.4 = ((f32[16,2,128]{2,1,0:T(2,128)}), f32[16,2,128]{2,1,0:T(2,128)S(1)}, u32[]{:S(2)}, u32[]{:S(2)}) async-start(f32[16,2,128]{2,1,0:T(2,128)} %broadcast_in_dim.15), calls=%async_computation.4 | async-start | bytes 32768 | tf_op jit(solution)/shard_map/all_to_all | solution.py:27
  186.3 1.2 copy-start.3
  187.6 0.8 copy-start.5
  190.9 6.6 %collective-permute-start.4 = (f32[128,256]{1,0:T(8,128)S(1)}, f32[128,256]{1,0:T(8,128)S(1)}, u32[]{:S(2)}, u32[]{:S(2)}) collective-permute-start(f32[128,256]{1,0:T(8,128)S(1)} %get-tuple-element.15), channel_id=1, source_target_pairs={{0,1},{1,0},{2,3},{3,2},{4,5},{5,4},{6,7},{7,6},{8,9},{9,8},{10,11... | collective-permute-start | bytes 393224 | tf_op jit(solution)/shard_map/ppermute | solution.py:35
  217.7 5.0 %collective-permute-start.5 = (bf16[512,384]{1,0:T(8,128)(2,1)S(1)}, bf16[512,384]{1,0:T(8,128)(2,1)S(1)}, u32[]{:S(2)}, u32[]{:S(2)}) collective-permute-start(bf16[512,384]{1,0:T(8,128)(2,1)S(1)} %weight_gradient.3), channel_id=1, source_target_pairs={{0,1},{1,0},{2,3},{3,2},{4,5},{5,4},{6,7},{7,6},{8,9},{9,8},{10,11... | collective-permute-start | bytes 1179656 | tf_op jit(solution)/shard_map/ppermute | solution.py:35
  257.8 5.9 %collective-permute-start.6 = (bf16[2,4,2,16,384]{4,3,2,0,1:T(8,128)(2,1)S(1)}, bf16[2,4,2,16,384]{4,3,2,0,1:T(8,128)(2,1)S(1)}, u32[]{:S(2)}, u32[]{:S(2)}) collective-permute-start(bf16[2,4,2,16,384]{4,3,2,0,1:T(8,128)(2,1)S(1)} %bitcast.31), channel_id=1, source_target_pairs={{0,1},{1,0},{2,3},{3,2},{4,5},{5,4},{6,7},{7,6},{8,9},{9,8},{10,11... | collective-permute-start | bytes 589832 | tf_op jit(solution)/shard_map/ppermute | solution.py:35
Sparse Core Ops, SparseCore 0:
  73.7 66.6 all-gather.2

commit v8 on v6

--- a/solution.py
+++ b/solution.py
@@ -13,7 +13,7 @@
 low = jnp.bfloat16
 z_axes = ("zh", "zl")
 ctx_axes = z_axes + ("xl", "core")
-group_axes = ("xh", "yl", "zl")
+group_axes = ("xh", "zl")
 vmem = pltpu.CompilerParams(vmem_limit_bytes=32 * 1024 * 1024)
 
 
@@ -141,21 +141,16 @@
     other_ref[:, :head], other_ref[:, head:] = grad_key[rows:], grad_value[rows:]
 
 
-def shard_row(step, count):
-    return lax.rem(lax.axis_index("yh") + count - step, count)
-
-
-def relayout_kernel(y_half, tokens_ref, out_ref):
+def relayout_kernel(y_count, tokens_ref, out_ref):
     members, _, columns = out_ref.shape
-    quarter = columns // (2 * y_half)
+    quarter = columns // (2 * y_count)
     core = lax.axis_index("core")
     for member in range(members):
-        x_hi, y_lo, z_lo = member // 4, member // 2 % 2, member % 2
+        x_hi, z_lo = member // 2, member % 2
         for half in range(2):
-            for step in range(y_half):
-                shard = (x_hi * y_half + shard_row(step, y_half)) * 2 + y_lo
-                start = (shard * 4 + z_lo * 2 + (core ^ half)) * quarter
-                target = (half * y_half + step) * quarter
+            for y in range(y_count):
+                start = ((x_hi * y_count + y) * 4 + z_lo * 2 + (core ^ half)) * quarter
+                target = (half * y_count + y) * quarter
                 out_ref[member, :, target : target + quarter] = tokens_ref[
                     :, pl.ds(pl.multiple_of(start, quarter), quarter)
                 ]
@@ -168,11 +163,8 @@
     out_ref[...] = total.astype(low)
 
 
-def weight_kernel(y_half, x_ref, grad_ref, out_ref):
-    total = dot_f32(x_ref[...], grad_ref[...], 0, 0).astype(out_ref.dtype)
-    quarter = total.shape[0] // y_half
-    for step in range(y_half):
-        out_ref[shard_row(step, y_half)] = total[step * quarter : (step + 1) * quarter]
+def weight_kernel(x_ref, grad_ref, out_ref):
+    out_ref[...] = dot_f32(x_ref[...], grad_ref[...], 0, 0).astype(out_ref.dtype)
 
 
 def in_vmem(count):
@@ -180,30 +172,25 @@
 
 
 def on_device(tokens, qkv_weight, out_grad):
-    y_half, z_count = lax.axis_size("yh"), lax.axis_size(z_axes)
+    y_count, z_count = lax.axis_size("y"), lax.axis_size(z_axes)
     ctx_count = z_count * 4
     row_count, model, width = tokens.shape[1], tokens.shape[2], qkv_weight.shape[1]
     shard, head = qkv_weight.shape[0], qkv_weight.shape[1] // 3
-    quarter, depth, group_rows = shard // 4, model // 16, 8 * row_count
+    quarter, depth, group_rows = shard // 4, model // 8, 4 * row_count
     cotangent = out_grad[0]
 
     at = (lax.axis_index("zl") * 2 + lax.axis_index("core")) * quarter
     own_weight = lax.dynamic_slice_in_dim(qkv_weight, at, quarter)
-    steps = [own_weight]
-    for step in range(1, y_half):
-        ring = [(i, (i + step) % y_half) for i in range(y_half)]
-        steps.append(lax.ppermute(own_weight, "yh", ring))
-    near = jnp.concatenate(steps)
+    near = lax.all_gather(own_weight, "y", axis=0, tiled=True)
+    far = swap(near, "core")
     split = pl.pallas_call(
-        functools.partial(relayout_kernel, y_half),
+        functools.partial(relayout_kernel, y_count),
         in_specs=in_vmem(1),
         out_specs=in_vmem(1)[0],
-        out_shape=jax.ShapeDtypeStruct((8, row_count, 2 * depth), low),
+        out_shape=jax.ShapeDtypeStruct((4, row_count, 2 * depth), low),
         compiler_params=vmem,
         name="token_columns",
     )(tokens[0])
-    split, near = lax.optimization_barrier((split, near))
-    far = swap(near, "core")
     columns = exchange(split, group_axes).reshape(group_rows, 2 * depth)
     parts = pl.pallas_call(
         project_kernel,
@@ -213,7 +200,7 @@
         compiler_params=vmem,
         name="partial_projection",
     )(columns, near, far)
-    parts = exchange(parts.reshape(8, row_count, width), group_axes)
+    parts = exchange(parts.reshape(4, row_count, width), group_axes)
     qkv = jnp.sum(parts.astype(jnp.float32), axis=0).astype(low)
     queries, own_pairs = qkv[:, :head], qkv[:, head:]
     pair_pieces = gather_x(own_pairs)
@@ -246,26 +233,26 @@
     )(own_pairs, pair_pieces[2], *query_pieces, stats_all)
     grad_pairs = (own_part + swap(other_part, "core")).astype(low)
 
-    grad_all = spread(jnp.concatenate([grad_query, grad_pairs], axis=1), group_axes, 8)
+    grad_all = spread(jnp.concatenate([grad_query, grad_pairs], axis=1), group_axes, 4)
     grad_all = grad_all.reshape(group_rows, width)
 
     def weight_half(half, dtype):
         return pl.pallas_call(
-            functools.partial(weight_kernel, y_half),
+            weight_kernel,
             grid=(1,),
             in_specs=[
                 pl.BlockSpec((group_rows, depth), lambda i: (0, half)),
                 pl.BlockSpec((group_rows, width), lambda i: (0, 0)),
             ],
-            out_specs=pl.BlockSpec((y_half, quarter, width), lambda i: (0, 0, 0)),
-            out_shape=jax.ShapeDtypeStruct((y_half, quarter, width), dtype),
+            out_specs=pl.BlockSpec((depth, width), lambda i: (0, 0)),
+            out_shape=jax.ShapeDtypeStruct((depth, width), dtype),
             compiler_params=vmem,
             name="weight_gradient",
         )(columns, grad_all)
 
     sent = swap(weight_half(1, low), "core")
     summed = (weight_half(0, jnp.float32) + sent.astype(jnp.float32)).astype(low)
-    pieces = exchange(summed.reshape(8 * y_half, -1, width), ("yh", "zh", "xl"))
+    pieces = exchange(summed.reshape(z_count * y_count, -1, width), ("y", "zh", "xl"))
     own_piece = jnp.sum(pieces.astype(jnp.float32), axis=0).astype(low)
     on_core = spread(own_piece, z_axes + ("xl",), 2 * z_count)
     on_core = on_core.reshape((z_count // 2, 2, 2) + own_piece.shape).transpose(1, 0, 2, 3, 4)
@@ -276,8 +263,8 @@
 
 
 def solution(mesh):
-    grid = Mesh(mesh.devices.reshape(2, 4, 2, 4, 2, 2, 2), ("xh", "yh", "yl") + ctx_axes)
-    rows, weights = P(("xh", "yh", "yl"), ctx_axes, None), P(("xh", "yh", "yl"), None)
+    grid = Mesh(mesh.devices.reshape(2, 8, 4, 2, 2, 2), ("xh", "y") + ctx_axes)
+    rows, weights = P(("xh", "y"), ctx_axes, None), P(("xh", "y"), None)
     return jax.shard_map(
         on_device,
         mesh=grid,

time: 223 us -> 210 us (0.942)
  waiting for transfers between devices: 56.7 us -> 31.4 us
  blocking collectives: 67.1 us -> 90.9 us
  starting transfers between devices: 75.5 us -> 63.6 us
    all_to_all x4, waiting for transfers between devices: 49.2 us -> 21.9 us  [exchange(): return lax.all_to_all(blocks, axes, split_axis=0, concat_axis=0, tiled=True)]
    all_gather x0 -> x1, blocking collectives: none -> 23.3 us  [on_device(): near = lax.all_gather(own_weight, 'y', axis=0, tiled=True)]
    ppermute x3 -> x0, starting transfers between devices: 15.7 us -> none  [on_device(): steps.append(lax.ppermute(own_weight, 'yh', ring))]
    ppermute x8, starting transfers between devices: 32.8 us -> 38.2 us  [swap(): return lax.ppermute(block, axis, ((0, 1), (1, 0)))]
    ppermute x8, waiting for transfers between devices: 6.58 us -> 9.49 us  [swap(): return lax.ppermute(block, axis, ((0, 1), (1, 0)))]
    unnamed x20 -> x26, local copies, waits for them, and re-layouts: 8.09 us -> 9.19 us
  transfers between devices with their start and end apart: 15 -> 12, of which waited for: 9 -> 7; matrix products, arithmetic and copies ran while one was open for 0% -> 0% of each run, Pallas kernels for 2% -> 2%
where the time goes in v8:
time: 210 us; the launch traced here: 209 us
  blocking collectives  90.9 us (43%)
  starting transfers between devices  63.6 us (30%)
  waiting for transfers between devices  31.4 us (15%)
  local copies, waits for them, and re-layouts  12.3 us (6%)
  Pallas kernels  9.33 us (4%)
    all_to_all x4, blocking collectives, exchange(): return lax.all_to_all(blocks, axes, split_axis=0, concat_axis=0, tiled=True)  67.6 us
    ppermute x8, starting transfers between devices, swap(): return lax.ppermute(block, axis, ((0, 1), (1, 0)))  38.2 us
    all_to_all x4, starting transfers between devices, exchange(): return lax.all_to_all(blocks, axes, split_axis=0, concat_axis=0, tiled=True)  25.4 us
    all_gather x1, blocking collectives, on_device(): near = lax.all_gather(own_weight, 'y', axis=0, tiled=True)  23.3 us
    all_to_all x4, waiting for transfers between devices, exchange(): return lax.all_to_all(blocks, axes, split_axis=0, concat_axis=0, tiled=True)  21.9 us
    ppermute x8, waiting for transfers between devices, swap(): return lax.ppermute(block, axis, ((0, 1), (1, 0)))  9.49 us
    unnamed x26, local copies, waits for them, and re-layouts  9.19 us
  transfers between devices with their start and end apart: 12, of which 7 were waited for; matrix products, arithmetic and copies ran while one was open for 0% of the time, Pallas kernels for 2%

profile of v8, /device:TPU:1, one launch (start us, length us, event | category | flops | bytes accessed | tf_op | source)
XLA Modules:
  0.0 209.0 jit_solution(15245536071991291871)
XLA Ops:
  0.6 0.0 copy-start
  0.6 0.0 copy-start.2
  0.7 1.6 copy-done.2
  2.3 0.5 token_columns.1
  2.8 0.0 copy-start.1
  2.9 1.3 copy-done.1
  4.2 6.7 %all-to-all-start = ((bf16[4,128,2048]{2,1,0:T(8,128)(2,1)}), bf16[4,128,2048]{2,1,0:T(8,128)(2,1)S(1)}, u32[]{:S(2)}, u32[]{:S(2)}) async-start(bf16[4,128,2048]{2,1,0:T(8,128)(2,1)} %copy-done.1), calls=%async_computation | async-start | bytes 4194304 | tf_op jit(solution)/shard_map/all_to_all | solution.py:27
  10.8 0.0 copy-done
  10.8 23.3 %all_gather.3.near_ref = bf16[1024,384]{1,0:T(8,128)(2,1)S(1)} all-gather(bf16[128,384]{1,0:T(8,128)(2,1)S(1)} %constant_dynamic-slice_fusion), channel_id=1, replica_groups=mesh['xh'=2,'y'=8,'zh'=4,'zl'=2,'xl'=2,'core'=2] {'y'}, dimensions={0}, use_global_device_ids=true | all-gather | bytes 884736 | tf_op jit(solution)/shard_map/all_gather | solution.py:184
  34.2 8.7 %collective-permute-start = (bf16[1024,384]{1,0:T(8,128)(2,1)S(1)}, bf16[1024,384]{1,0:T(8,128)(2,1)S(1)}, u32[]{:S(2)}, u32[]{:S(2)}) collective-permute-start(bf16[1024,384]{1,0:T(8,128)(2,1)S(1)} %all_gather.3.near_ref), channel_id=1, source_target_pairs={{0,1},{1,0},{2,3},{3,2},{4,5},{5,4},{6,7},{7,6},{8,9},{9,8},{10,11... | collective-permute-start | bytes 2359304 | tf_op jit(solution)/shard_map/ppermute | solution.py:35
  42.9 1.9 collective-permute-done.far_ref
  44.8 0.0 copy-start.3
  44.8 0.9 copy-done.3
  45.7 0.0 all-to-all-done
  45.7 1.1 copy-done.4
  46.8 1.2 partial_projection.1
  48.0 0.0 copy-start.9
  48.1 12.6 %all_to_all.40 = bf16[4,128,384]{2,1,0:T(8,128)(2,1)S(1)} all-to-all(bf16[4,128,384]{2,1,0:T(8,128)(2,1)S(1)} %bitcast.25), channel_id=1, replica_groups=mesh['xh'=2,'y'=8,'zh'=4,'zl'=2,'xl'=2,'core'=2] {'xh','zl'}, dimensions={0} | all-to-all | bytes 786432 | tf_op jit(solution)/shard_map/all_to_all | solution.py:27
  60.6 0.1 reduce_sum.24
  60.7 0.8 broadcast_in_dim.12
  61.5 0.0 copy-start.5
  61.5 0.6 copy-done.5
  62.2 7.7 %all-to-all-start.2 = ((bf16[8,128,256]{2,1,0:T(8,128)(2,1)}), bf16[8,128,256]{2,1,0:T(8,128)(2,1)}, u32[]{:S(2)}, u32[]{:S(2)}) async-start(bf16[8,128,256]{2,1,0:T(8,128)(2,1)} %broadcast_in_dim.12), calls=%async_computation.2 | async-start | bytes 1048576 | tf_op jit(solution)/shard_map/all_to_all | solution.py:27
  69.9 0.0 copy-done.9
  69.9 0.0 copy-start.7
  69.9 0.6 copy-done.7
  70.5 14.5 %all-to-all-done.2 = bf16[8,128,256]{2,1,0:T(8,128)(2,1)} async-done(((bf16[8,128,256]{2,1,0:T(8,128)(2,1)}), bf16[8,128,256]{2,1,0:T(8,128)(2,1)}, u32[]{:S(2)}, u32[]{:S(2)}) %all-to-all-start.2) | async-done | bytes 524320 | tf_op jit(solution)/shard_map/all_to_all | solution.py:27
  85.0 0.8 broadcast_in_dim.14
  85.9 3.5 %all-to-all-start.3 = ((bf16[8,128,256]{2,1,0:T(8,128)(2,1)}), bf16[8,128,256]{2,1,0:T(8,128)(2,1)S(1)}, u32[]{:S(2)}, u32[]{:S(2)}) async-start(bf16[8,128,256]{2,1,0:T(8,128)(2,1)} %broadcast_in_dim.14), calls=%async_computation.3 | async-start | bytes 1048576 | tf_op jit(solution)/shard_map/all_to_all | solution.py:27
  89.4 2.2 %collective-permute-start.1 = (bf16[1024,256]{1,0:T(8,128)(2,1)}, bf16[1024,256]{1,0:T(8,128)(2,1)}, u32[]{:S(2)}, u32[]{:S(2)}) collective-permute-start(bf16[1024,256]{1,0:T(8,128)(2,1)} %bitcast.3.kv0), channel_id=1, source_target_pairs={{0,2},{2,0},{1,3},{3,1},{4,6},{6,4},{5,7},{7,5},{8,10},{10,8},{9,1... | collective-permute-start | bytes 1572872 | tf_op jit(solution)/shard_map/ppermute | solution.py:35
  91.5 5.6 %collective-permute-start.2 = (bf16[1024,256]{1,0:T(8,128)(2,1)}, bf16[1024,256]{1,0:T(8,128)(2,1)S(1)}, u32[]{:S(2)}, u32[]{:S(2)}) collective-permute-start(bf16[1024,256]{1,0:T(8,128)(2,1)} %bitcast.3.kv0), channel_id=1, source_target_pairs={{0,1},{1,0},{2,3},{3,2},{4,5},{5,4},{6,7},{7,6},{8,9},{9,8},{10,11... | collective-permute-start | bytes 1572872 | tf_op jit(solution)/shard_map/ppermute | solution.py:35
  97.1 4.4 %collective-permute-done.1.kv1 = bf16[1024,256]{1,0:T(8,128)(2,1)} collective-permute-done((bf16[1024,256]{1,0:T(8,128)(2,1)}, bf16[1024,256]{1,0:T(8,128)(2,1)}, u32[]{:S(2)}, u32[]{:S(2)}) %collective-permute-start.1) | collective-permute-done | bytes 524320 | tf_op jit(solution)/shard_map/ppermute | solution.py:35
  101.6 6.2 %collective-permute-start.3 = (bf16[1024,256]{1,0:T(8,128)(2,1)}, bf16[1024,256]{1,0:T(8,128)(2,1)}, u32[]{:S(2)}, u32[]{:S(2)}) collective-permute-start(bf16[1024,256]{1,0:T(8,128)(2,1)} %collective-permute-done.1.kv1), channel_id=1, source_target_pairs={{0,1},{1,0},{2,3},{3,2},{4,5},{5,4},{6,7},{7,6},{8,9},{9,8},{10,11... | collective-permute-start | bytes 1572872 | tf_op jit(solution)/shard_map/ppermute | solution.py:35
  107.8 0.0 all-to-all-done.3
  107.8 2.2 %collective-permute-start.4 = (bf16[1024,256]{1,0:T(8,128)(2,1)S(1)}, bf16[1024,256]{1,0:T(8,128)(2,1)}, u32[]{:S(2)}, u32[]{:S(2)}) collective-permute-start(bf16[1024,256]{1,0:T(8,128)(2,1)S(1)} %bitcast.22), channel_id=1, source_target_pairs={{0,2},{2,0},{1,3},{3,1},{4,6},{6,4},{5,7},{7,5},{8,10},{10,8},{9,1... | collective-permute-start | bytes 1572872 | tf_op jit(solution)/shard_map/ppermute | solution.py:35
  110.0 0.0 collective-permute-done.2.kv2.across_ref
  110.0 0.0 collective-permute-done.3.kv3
  110.0 0.0 copy-start.8
  110.0 0.7 copy-done.8
  110.8 0.8 copy-done.10
  111.5 3.5 %attention_rows.1 = (bf16[128,128]{1,0:T(8,128)(2,1)}, f32[2,128]{1,0:T(2,128)S(1)}, bf16[128,128]{1,0:T(8,128)(2,1)S(1)}) custom-call(bf16[128,128]{1,0:T(8,128)(2,1)S(1)} %copy-done.8, bf16[1024,256]{1,0:T(8,128)(2,1)} %bitcast.3.kv0, bf16[1024,256]{1,0:T(8,128)(2,1)} %collective-permute-done.1.kv1, ...), custom_call_target="tpu_custom_call" | custom-call | tf_op jit(solution)/shard_map/attention_rows/pallas_call | solution.py:210
  115.1 0.0 copy-start.11
  115.1 0.6 copy-done.11
  115.7 0.6 broadcast_in_dim.15
  116.3 7.6 %all-to-all-start.4 = ((f32[16,2,128]{2,1,0:T(2,128)}), f32[16,2,128]{2,1,0:T(2,128)S(1)}, u32[]{:S(2)}, u32[]{:S(2)}) async-start(f32[16,2,128]{2,1,0:T(2,128)} %broadcast_in_dim.15), calls=%async_computation.4 | async-start | bytes 32768 | tf_op jit(solution)/shard_map/all_to_all | solution.py:27
  123.9 0.0 collective-permute-done.4.qc1
  123.9 7.4 %all-to-all-done.4.stats_ref = f32[16,2,128]{2,1,0:T(2,128)S(1)} async-done(((f32[16,2,128]{2,1,0:T(2,128)}), f32[16,2,128]{2,1,0:T(2,128)S(1)}, u32[]{:S(2)}, u32[]{:S(2)}) %all-to-all-start.4) | async-done | bytes 16416 | tf_op jit(solution)/shard_map/all_to_all | solution.py:27
  131.3 0.8 copy-done.6
  132.1 2.5 %attention_columns.1 = (f32[128,256]{1,0:T(8,128)S(1)}, f32[128,256]{1,0:T(8,128)S(1)}) custom-call(bf16[128,256]{1,0:T(8,128)(2,1)S(1)} %copy-done.6, bf16[1024,256]{1,0:T(8,128)(2,1)S(1)} %collective-permute-done.2.kv2.across_ref, bf16[1024,256]{1,0:T(8,128)(2,1)S(1)} %bitcast.23, bf16[1024,256]{1,0:T(8,128)(2,1)} %collective-permute-done.4.qc1, ...), custom_call_target="tpu_custom_call" | custom-call | tf_op jit(solution)/shard_map/attention_columns/pallas_call | solution.py:226
  134.7 3.6 %collective-permute-start.5 = (f32[128,256]{1,0:T(8,128)S(1)}, f32[128,256]{1,0:T(8,128)S(1)}, u32[]{:S(2)}, u32[]{:S(2)}) collective-permute-start(f32[128,256]{1,0:T(8,128)S(1)} %get-tuple-element.11), channel_id=1, source_target_pairs={{0,1},{1,0},{2,3},{3,2},{4,5},{5,4},{6,7},{7,6},{8,9},{9,8},{10,11... | collective-permute-start | bytes 393224 | tf_op jit(solution)/shard_map/ppermute | solution.py:35
  138.3 1.0 collective-permute-done.5
  139.3 0.0 copy-done.12
  139.4 10.7 %all_to_all.41 = bf16[4,128,384]{2,1,0:T(8,128)(2,1)S(1)} all-to-all(bf16[4,128,384]{2,1,0:T(8,128)(2,1)S(1)} %broadcast_in_dim.16), channel_id=1, replica_groups=mesh['xh'=2,'y'=8,'zh'=4,'zl'=2,'xl'=2,'core'=2] {'xh','zl'}, dimensions={0} | all-to-all | bytes 786432 | tf_op jit(solution)/shard_map/all_to_all | solution.py:27
  150.1 0.7 weight_gradient.3
  150.8 4.1 %collective-permute-start.6 = (bf16[1024,384]{1,0:T(8,128)(2,1)S(1)}, bf16[1024,384]{1,0:T(8,128)(2,1)S(1)}, u32[]{:S(2)}, u32[]{:S(2)}) collective-permute-start(bf16[1024,384]{1,0:T(8,128)(2,1)S(1)} %weight_gradient.3), channel_id=1, source_target_pairs={{0,1},{1,0},{2,3},{3,2},{4,5},{5,4},{6,7},{7,6},{8,9},{9,8},{10,11... | collective-permute-start | bytes 2359304 | tf_op jit(solution)/shard_map/ppermute | solution.py:35
  154.9 0.7 weight_gradient.2
  155.7 1.1 collective-permute-done.6
  156.8 0.2 add_convert_fusion
  157.0 30.5 %all_to_all.42 = bf16[64,16,384]{2,1,0:T(8,128)(2,1)S(1)} all-to-all(bf16[64,16,384]{2,1,0:T(8,128)(2,1)S(1)} %bitcast.28), channel_id=1, replica_groups=mesh['xh'=2,'y'=8,'zh'=4,'zl'=2,'xl'=2,'core'=2] {'y','zh','xl'}, dimensions={0} | all-to-all | bytes 1572864 | tf_op jit(solution)/shard_map/all_to_all | solution.py:27
  187.5 0.1 reduce_sum.25
  187.6 13.8 %all_to_all.43 = bf16[16,16,384]{2,1,0:T(8,128)(2,1)S(1)} all-to-all(bf16[16,16,384]{2,1,0:T(8,128)(2,1)S(1)} %broadcast_in_dim.17), channel_id=1, replica_groups=mesh['xh'=2,'y'=8,'zh'=4,'zl'=2,'xl'=2,'core'=2] {'zh','zl','xl'}, dimensions={0} | all-to-all | bytes 393216 | tf_op jit(solution)/shard_map/all_to_all | solution.py:27
  201.4 5.6 %collective-permute-start.7 = (bf16[2,4,2,16,384]{4,3,2,0,1:T(8,128)(2,1)S(1)}, bf16[2,4,2,16,384]{4,3,2,0,1:T(8,128)(2,1)S(1)}, u32[]{:S(2)}, u32[]{:S(2)}) collective-permute-start(bf16[2,4,2,16,384]{4,3,2,0,1:T(8,128)(2,1)S(1)} %bitcast.29), channel_id=1, source_target_pairs={{0,1},{1,0},{2,3},{3,2},{4,5},{5,4},{6,7},{7,6},{8,9},{9,8},{10,11... | collective-permute-start | bytes 589832 | tf_op jit(solution)/shard_map/ppermute | solution.py:35
  207.1 1.0 collective-permute-done.7
  208.2 0.8 copy.6
  (14 shorter events, 0.2 us)
Async XLA Ops:
  0.6 10.2 %copy-start = (bf16[512,384]{1,0:T(8,128)(2,1)S(1)}, bf16[512,384]{1,0:T(8,128)(2,1)}, u32[]{:S(2)}) copy-start(bf16[512,384]{1,0:T(8,128)(2,1)} %param.4) | copy-start | bytes 1179652
  0.6 1.6 copy-start.2
  2.8 1.3 copy-start.1
  4.2 41.5 %all-to-all-start = ((bf16[4,128,2048]{2,1,0:T(8,128)(2,1)}), bf16[4,128,2048]{2,1,0:T(8,128)(2,1)S(1)}, u32[]{:S(2)}, u32[]{:S(2)}) async-start(bf16[4,128,2048]{2,1,0:T(8,128)(2,1)} %copy-done.1), calls=%async_computation | async-start | bytes 4194304 | tf_op jit(solution)/shard_map/all_to_all | solution.py:27
  34.2 10.6 %collective-permute-start = (bf16[1024,384]{1,0:T(8,128)(2,1)S(1)}, bf16[1024,384]{1,0:T(8,128)(2,1)S(1)}, u32[]{:S(2)}, u32[]{:S(2)}) collective-permute-start(bf16[1024,384]{1,0:T(8,128)(2,1)S(1)} %all_gather.3.near_ref), channel_id=1, source_target_pairs={{0,1},{1,0},{2,3},{3,2},{4,5},{5,4},{6,7},{7,6},{8,9},{9,8},{10,11... | collective-permute-start | bytes 2359304 | tf_op jit(solution)/shard_map/ppermute | solution.py:35
  44.8 0.9 copy-start.3
  45.7 1.1 copy-start.4
  48.0 21.8 %copy-start.9 = (bf16[1,128,128]{2,1,0:T(8,128)(2,1)S(1)}, bf16[1,128,128]{2,1,0:T(8,128)(2,1)}, u32[]{:S(2)}) copy-start(bf16[1,128,128]{2,1,0:T(8,128)(2,1)} %param.5) | copy-start | bytes 98308
  61.5 0.6 copy-start.5
  62.2 22.8 %all-to-all-start.2 = ((bf16[8,128,256]{2,1,0:T(8,128)(2,1)}), bf16[8,128,256]{2,1,0:T(8,128)(2,1)}, u32[]{:S(2)}, u32[]{:S(2)}) async-start(bf16[8,128,256]{2,1,0:T(8,128)(2,1)} %broadcast_in_dim.12), calls=%async_computation.2 | async-start | bytes 1048576 | tf_op jit(solution)/shard_map/all_to_all | solution.py:27
  69.9 0.6 copy-start.7
  85.9 22.0 %all-to-all-start.3 = ((bf16[8,128,256]{2,1,0:T(8,128)(2,1)}), bf16[8,128,256]{2,1,0:T(8,128)(2,1)S(1)}, u32[]{:S(2)}, u32[]{:S(2)}) async-start(bf16[8,128,256]{2,1,0:T(8,128)(2,1)} %broadcast_in_dim.14), calls=%async_computation.3 | async-start | bytes 1048576 | tf_op jit(solution)/shard_map/all_to_all | solution.py:27
  89.4 12.2 %collective-permute-start.1 = (bf16[1024,256]{1,0:T(8,128)(2,1)}, bf16[1024,256]{1,0:T(8,128)(2,1)}, u32[]{:S(2)}, u32[]{:S(2)}) collective-permute-start(bf16[1024,256]{1,0:T(8,128)(2,1)} %bitcast.3.kv0), channel_id=1, source_target_pairs={{0,2},{2,0},{1,3},{3,1},{4,6},{6,4},{5,7},{7,5},{8,10},{10,8},{9,1... | collective-permute-start | bytes 1572872 | tf_op jit(solution)/shard_map/ppermute | solution.py:35
  91.5 18.5 %collective-permute-start.2 = (bf16[1024,256]{1,0:T(8,128)(2,1)}, bf16[1024,256]{1,0:T(8,128)(2,1)S(1)}, u32[]{:S(2)}, u32[]{:S(2)}) collective-permute-start(bf16[1024,256]{1,0:T(8,128)(2,1)} %bitcast.3.kv0), channel_id=1, source_target_pairs={{0,1},{1,0},{2,3},{3,2},{4,5},{5,4},{6,7},{7,6},{8,9},{9,8},{10,11... | collective-permute-start | bytes 1572872 | tf_op jit(solution)/shard_map/ppermute | solution.py:35
  101.6 8.4 %collective-permute-start.3 = (bf16[1024,256]{1,0:T(8,128)(2,1)}, bf16[1024,256]{1,0:T(8,128)(2,1)}, u32[]{:S(2)}, u32[]{:S(2)}) collective-permute-start(bf16[1024,256]{1,0:T(8,128)(2,1)} %collective-permute-done.1.kv1), channel_id=1, source_target_pairs={{0,1},{1,0},{2,3},{3,2},{4,5},{5,4},{6,7},{7,6},{8,9},{9,8},{10,11... | collective-permute-start | bytes 1572872 | tf_op jit(solution)/shard_map/ppermute | solution.py:35
  107.8 16.1 %collective-permute-start.4 = (bf16[1024,256]{1,0:T(8,128)(2,1)S(1)}, bf16[1024,256]{1,0:T(8,128)(2,1)}, u32[]{:S(2)}, u32[]{:S(2)}) collective-permute-start(bf16[1024,256]{1,0:T(8,128)(2,1)S(1)} %bitcast.22), channel_id=1, source_target_pairs={{0,2},{2,0},{1,3},{3,1},{4,6},{6,4},{5,7},{7,5},{8,10},{10,8},{9,1... | collective-permute-start | bytes 1572872 | tf_op jit(solution)/shard_map/ppermute | solution.py:35
  110.0 0.8 copy-start.8
  110.8 0.8 copy-start.10
  115.1 0.6 copy-start.11
  116.3 15.0 %all-to-all-start.4 = ((f32[16,2,128]{2,1,0:T(2,128)}), f32[16,2,128]{2,1,0:T(2,128)S(1)}, u32[]{:S(2)}, u32[]{:S(2)}) async-start(f32[16,2,128]{2,1,0:T(2,128)} %broadcast_in_dim.15), calls=%async_computation.4 | async-start | bytes 32768 | tf_op jit(solution)/shard_map/all_to_all | solution.py:27
  131.3 0.8 copy-start.6
  132.1 7.2 %copy-start.12 = (bf16[128,128]{1,0:T(8,128)(2,1)S(1)}, bf16[128,128]{1,0:T(8,128)(2,1)}, u32[]{:S(2)}) copy-start(bf16[128,128]{1,0:T(8,128)(2,1)} %copy-done.11) | copy-start | bytes 98308
  134.7 4.6 %collective-permute-start.5 = (f32[128,256]{1,0:T(8,128)S(1)}, f32[128,256]{1,0:T(8,128)S(1)}, u32[]{:S(2)}, u32[]{:S(2)}) collective-permute-start(f32[128,256]{1,0:T(8,128)S(1)} %get-tuple-element.11), channel_id=1, source_target_pairs={{0,1},{1,0},{2,3},{3,2},{4,5},{5,4},{6,7},{7,6},{8,9},{9,8},{10,11... | collective-permute-start | bytes 393224 | tf_op jit(solution)/shard_map/ppermute | solution.py:35
  150.8 6.0 %collective-permute-start.6 = (bf16[1024,384]{1,0:T(8,128)(2,1)S(1)}, bf16[1024,384]{1,0:T(8,128)(2,1)S(1)}, u32[]{:S(2)}, u32[]{:S(2)}) collective-permute-start(bf16[1024,384]{1,0:T(8,128)(2,1)S(1)} %weight_gradient.3), channel_id=1, source_target_pairs={{0,1},{1,0},{2,3},{3,2},{4,5},{5,4},{6,7},{7,6},{8,9},{9,8},{10,11... | collective-permute-start | bytes 2359304 | tf_op jit(solution)/shard_map/ppermute | solution.py:35
  201.4 6.7 %collective-permute-start.7 = (bf16[2,4,2,16,384]{4,3,2,0,1:T(8,128)(2,1)S(1)}, bf16[2,4,2,16,384]{4,3,2,0,1:T(8,128)(2,1)S(1)}, u32[]{:S(2)}, u32[]{:S(2)}) collective-permute-start(bf16[2,4,2,16,384]{4,3,2,0,1:T(8,128)(2,1)S(1)} %bitcast.29), channel_id=1, source_target_pairs={{0,1},{1,0},{2,3},{3,2},{4,5},{5,4},{6,7},{7,6},{8,9},{9,8},{10,11... | collective-permute-start | bytes 589832 | tf_op jit(solution)/shard_map/ppermute | solution.py:35

commit v9 on v8

--- a/solution.py
+++ b/solution.py
@@ -35,11 +35,6 @@
     return lax.ppermute(block, axis, ((0, 1), (1, 0)))
 
 
-def gather_x(block):
-    along_z = spread(block, z_axes, lax.axis_size(z_axes)).reshape(-1, block.shape[1])
-    return along_z, swap(along_z, "xl")
-
-
 def positions(device, inside, half_rows, ctx_count):
     block = jnp.where(inside < half_rows, device, 2 * ctx_count - 1 - device)
     return block * half_rows + inside % half_rows
@@ -49,10 +44,7 @@
     return z * 4 + (lax.axis_index("xl") ^ (piece & 1)) * 2 + (lax.axis_index("core") ^ (piece >> 1))
 
 
-def forward_kernel(
-    z_count, q_ref, kv0, kv1, kv2, kv3, cot_ref, attn_ref, stats_ref, dq_ref, held
-):
-    pieces = (kv0, kv1, kv2, kv3)
+def row_scores(z_count, q_ref, kv_refs):
     rows, head = q_ref.shape
     half_rows, ctx_count = rows // 2, 4 * z_count
     scale = 1.0 / math.sqrt(head)
@@ -60,14 +52,24 @@
     down = lax.broadcasted_iota(jnp.int32, (rows, rows), 0)
     across = lax.broadcasted_iota(jnp.int32, (rows, rows), 1)
     own_positions = positions(own, down, half_rows, ctx_count)
-    queries, cotangent = q_ref[...], cot_ref[...]
-    top = None
-    for piece, kv in enumerate(pieces):
-        raw = dot_f32(queries, kv[:, :head], 1, 1) * scale
+    for piece, kv in enumerate(kv_refs):
+        raw = dot_f32(q_ref[...], kv[:, :head], 1, 1) * scale
+        tiles = []
         for z in range(z_count):
             device = piece_device(piece, z)
             allowed = positions(device, across, half_rows, ctx_count) <= own_positions
-            tile = jnp.where(allowed, raw[:, z * rows : (z + 1) * rows], masked_fill)
+            tiles.append(jnp.where(allowed, raw[:, z * rows : (z + 1) * rows], masked_fill))
+        yield tiles
+
+
+def forward_kernel(
+    z_count, q_ref, kv0, kv1, kv2, kv3, cot_ref, attn_ref, stats_ref, columns_ref, held
+):
+    pieces = (kv0, kv1, kv2, kv3)
+    rows, head = q_ref.shape
+    top = None
+    for piece, tiles in enumerate(row_scores(z_count, q_ref, pieces)):
+        for z, tile in enumerate(tiles):
             held[piece, :, z * rows : (z + 1) * rows] = tile
             top = tile if top is None else jnp.maximum(top, tile)
     row_top = jnp.max(top, axis=1, keepdims=True)
@@ -86,20 +88,33 @@
     attn_low = attn.astype(low)
     attn_ref[...] = attn_low
     delta = jnp.sum(
-        cotangent.astype(jnp.float32) * attn_low.astype(jnp.float32), axis=1, keepdims=True
+        cot_ref[...].astype(jnp.float32) * attn_low.astype(jnp.float32), axis=1, keepdims=True
     )
     shift = 2.0 * z_weight * log_total - delta
-    stats_ref[0:1, :] = jnp.transpose(jnp.broadcast_to(log_total, (rows, rows)))[0:1, :]
-    stats_ref[1:2, :] = jnp.transpose(jnp.broadcast_to(shift, (rows, rows)))[0:1, :]
+    for place, column in enumerate((log_total, shift)):
+        wide = jnp.broadcast_to(column, (rows, rows))
+        columns_ref[place] = wide
+        line = jnp.transpose(wide)[0:1, :]
+        for copy in range(stats_ref.shape[0]):
+            stats_ref[copy, place : place + 1, :] = line
+
+
+def query_kernel(z_count, q_ref, kv0, kv1, kv2, kv3, cot_ref, columns_ref, dq_ref):
+    pieces = (kv0, kv1, kv2, kv3)
+    rows, head = q_ref.shape
+    log_total, shift = columns_ref[0], columns_ref[1]
     grad = jnp.zeros((rows, head), jnp.float32)
-    for piece, kv in enumerate(pieces):
-        dprob = dot_f32(cotangent, kv[:, head:], 1, 1)
-        dscore = held[piece] * inverse * (dprob + shift)
-        grad = grad + dot_f32(dscore.astype(low), kv[:, :head], 1, 0)
-    dq_ref[...] = (grad * scale).astype(low)
-
-
-def backward_kernel(z_count, kv_ref, across_ref, qc0, qc1, stats_ref, own_ref, other_ref):
+    for kv, tiles in zip(pieces, row_scores(z_count, q_ref, pieces)):
+        dprob = dot_f32(cot_ref[...], kv[:, head:], 1, 1)
+        dscores = []
+        for z, tile in enumerate(tiles):
+            prob = jnp.exp(tile - log_total)
+            dscores.append((prob * (dprob[:, z * rows : (z + 1) * rows] + shift)).astype(low))
+        grad = grad + dot_f32(jnp.concatenate(dscores, axis=1), kv[:, :head], 1, 0)
+    dq_ref[...] = (grad * (1.0 / math.sqrt(head))).astype(low)
+
+
+def backward_kernel(z_count, kv_ref, across_ref, q0, q1, cot0, cot1, stats_ref, own_ref, other_ref):
     rows, head = kv_ref.shape[0], kv_ref.shape[1] // 2
     half_rows, ctx_count = rows // 2, 4 * z_count
     scale = 1.0 / math.sqrt(head)
@@ -119,9 +134,9 @@
     keys, values = pairs[:, :head], pairs[:, head:]
     grad_key = jnp.zeros((2 * rows, head), jnp.float32)
     grad_value = jnp.zeros((2 * rows, head), jnp.float32)
-    for piece, both in enumerate((qc0, qc1)):
+    for piece, (q_ref, cot_ref) in enumerate(((q0, cot0), (q1, cot1))):
         slot = lax.axis_index("xl") ^ piece
-        queries, cotangent = both[:, :head], both[:, head:]
+        queries, cotangent = q_ref[...], cot_ref[...]
         scores = dot_f32(keys, queries, 1, 1) * scale
         dprob = dot_f32(values, cotangent, 1, 1)
         probs, dscores = [], []
@@ -156,11 +171,33 @@
                 ]
 
 
-def project_kernel(x_ref, near_ref, far_ref, out_ref):
-    depth = near_ref.shape[0]
-    total = dot_f32(x_ref[:, :depth], near_ref[...], 1, 0)
-    total = total + dot_f32(x_ref[:, depth:], far_ref[...], 1, 0)
-    out_ref[...] = total.astype(low)
+def near_kernel(x_ref, weight_ref, out_ref):
+    out_ref[...] = dot_f32(x_ref[...], weight_ref[...], 1, 0)
+
+
+def far_kernel(x_ref, weight_ref, sum_ref, out_ref):
+    out_ref[...] = (sum_ref[...] + dot_f32(x_ref[...], weight_ref[...], 1, 0)).astype(low)
+
+
+def split_kernel(parts_ref, q_ref, kv_ref, kv_copies, q_copies):
+    head = q_ref.shape[1]
+    total = parts_ref[0].astype(jnp.float32)
+    for part in range(1, parts_ref.shape[0]):
+        total = total + parts_ref[part].astype(jnp.float32)
+    qkv = total.astype(low)
+    queries, pairs = qkv[:, :head], qkv[:, head:]
+    q_ref[...] = queries
+    kv_ref[...] = pairs
+    for copy in range(kv_copies.shape[0]):
+        kv_copies[copy] = pairs
+        q_copies[copy] = queries
+
+
+def join_kernel(dq_ref, own_ref, other_ref, out_ref):
+    pairs = (own_ref[...] + other_ref[...]).astype(low)
+    rows = jnp.concatenate([dq_ref[...], pairs], axis=1)
+    for copy in range(out_ref.shape[0]):
+        out_ref[copy] = rows
 
 
 def weight_kernel(x_ref, grad_ref, out_ref):
@@ -192,49 +229,102 @@
         name="token_columns",
     )(tokens[0])
     columns = exchange(split, group_axes).reshape(group_rows, 2 * depth)
+    whole = pl.BlockSpec((depth, width), lambda i: (0, 0))
+    summed_rows = pl.BlockSpec((group_rows, width), lambda i: (0, 0))
+
+    def column_half(half):
+        return pl.BlockSpec((group_rows, depth), lambda i: (0, half))
+
+    near_sum = pl.pallas_call(
+        near_kernel,
+        grid=(1,),
+        in_specs=[column_half(0), whole],
+        out_specs=summed_rows,
+        out_shape=jax.ShapeDtypeStruct((group_rows, width), jnp.float32),
+        compiler_params=vmem,
+        name="near_projection",
+    )(columns, near)
     parts = pl.pallas_call(
-        project_kernel,
-        in_specs=in_vmem(3),
-        out_specs=in_vmem(1)[0],
+        far_kernel,
+        grid=(1,),
+        in_specs=[column_half(1), whole, summed_rows],
+        out_specs=summed_rows,
         out_shape=jax.ShapeDtypeStruct((group_rows, width), low),
         compiler_params=vmem,
-        name="partial_projection",
-    )(columns, near, far)
+        name="far_projection",
+    )(columns, far, near_sum)
     parts = exchange(parts.reshape(4, row_count, width), group_axes)
-    qkv = jnp.sum(parts.astype(jnp.float32), axis=0).astype(low)
-    queries, own_pairs = qkv[:, :head], qkv[:, head:]
-    pair_pieces = gather_x(own_pairs)
-    pair_pieces = pair_pieces + tuple(swap(p, "core") for p in pair_pieces)
-    query_pieces = gather_x(jnp.concatenate([queries, cotangent], axis=1))
-
-    attn_rows, stats, grad_query = pl.pallas_call(
+    cotangent_z = lax.all_gather(
+        jnp.concatenate([cotangent] * 4, axis=1), z_axes, axis=0, tiled=True
+    )
+    parts, cotangent_z = lax.optimization_barrier((parts, cotangent_z))
+    cotangent_z = cotangent_z[:, :head]
+    cotangent_x = swap(cotangent_z, "xl")
+    queries, own_pairs, pair_copies, query_copies = pl.pallas_call(
+        split_kernel,
+        in_specs=in_vmem(1),
+        out_specs=in_vmem(4),
+        out_shape=[
+            jax.ShapeDtypeStruct(shape, low)
+            for shape in (
+                (row_count, head),
+                (row_count, 2 * head),
+                (z_count, row_count, 2 * head),
+                (z_count, row_count, head),
+            )
+        ],
+        compiler_params=vmem,
+        name="projection_sum",
+    )(parts)
+
+    along_z = exchange(pair_copies, z_axes).reshape(-1, 2 * head)
+    along_z, cotangent_x = lax.optimization_barrier((along_z, cotangent_x))
+    by_x, by_core = swap(along_z, "xl"), swap(along_z, "core")
+    pair_pieces = (along_z, by_x, by_core, swap(by_x, "core"))
+    queries_z = exchange(query_copies, z_axes).reshape(-1, head)
+    query_pieces = (queries_z, swap(queries_z, "xl"))
+
+    attn_rows, stats, stat_columns = pl.pallas_call(
         functools.partial(forward_kernel, z_count),
         in_specs=in_vmem(6),
         out_specs=in_vmem(3),
         out_shape=[
             jax.ShapeDtypeStruct((row_count, head), low),
-            jax.ShapeDtypeStruct((2, row_count), jnp.float32),
-            jax.ShapeDtypeStruct((row_count, head), low),
+            jax.ShapeDtypeStruct((2 * z_count, 2, row_count), jnp.float32),
+            jax.ShapeDtypeStruct((2, row_count, row_count), jnp.float32),
         ],
         scratch_shapes=[pltpu.VMEM((4, row_count, z_count * row_count), jnp.float32)],
         compiler_params=vmem,
         name="attention_rows",
     )(queries, *pair_pieces, cotangent)
-
-    stats_all = spread(stats, z_axes + ("xl",), 2 * z_count)
+    stats_all = exchange(stats, z_axes + ("xl",))
+    grad_query = pl.pallas_call(
+        functools.partial(query_kernel, z_count),
+        in_specs=in_vmem(7),
+        out_specs=in_vmem(1)[0],
+        out_shape=jax.ShapeDtypeStruct((row_count, head), low),
+        compiler_params=vmem,
+        name="query_gradient",
+    )(queries, *pair_pieces, cotangent, stat_columns)
+    grad_query, stats_all = lax.optimization_barrier((grad_query, stats_all))
 
     own_part, other_part = pl.pallas_call(
         functools.partial(backward_kernel, z_count),
-        in_specs=in_vmem(5),
+        in_specs=in_vmem(7),
         out_specs=in_vmem(2),
         out_shape=[jax.ShapeDtypeStruct((row_count, 2 * head), jnp.float32)] * 2,
         compiler_params=vmem,
         name="attention_columns",
-    )(own_pairs, pair_pieces[2], *query_pieces, stats_all)
-    grad_pairs = (own_part + swap(other_part, "core")).astype(low)
-
-    grad_all = spread(jnp.concatenate([grad_query, grad_pairs], axis=1), group_axes, 4)
-    grad_all = grad_all.reshape(group_rows, width)
+    )(own_pairs, pair_pieces[2], *query_pieces, cotangent_z, cotangent_x, stats_all)
+    grad_copies = pl.pallas_call(
+        join_kernel,
+        in_specs=in_vmem(3),
+        out_specs=in_vmem(1)[0],
+        out_shape=jax.ShapeDtypeStruct((4, row_count, width), low),
+        compiler_params=vmem,
+        name="join_gradients",
+    )(grad_query, own_part, swap(other_part, "core"))
+    grad_all = exchange(grad_copies, group_axes).reshape(group_rows, width)
 
     def weight_half(half, dtype):
         return pl.pallas_call(

time: 210 us -> 222 us (1.057)
  between operations: 0.93 us -> 14.3 us
  blocking collectives: 90.9 us -> 80.5 us
  Pallas kernels: 9.33 us -> 14.6 us
  waiting for transfers between devices: 31.4 us -> 26.8 us
  starting transfers between devices: 63.6 us -> 67.8 us
  local copies, waits for them, and re-layouts: 12.3 us -> 15.9 us
    all_to_all x4 -> x5, waiting for transfers between devices: 21.9 us -> 11.3 us  [exchange(): return lax.all_to_all(blocks, axes, split_axis=0, concat_axis=0, tiled=True)]
    all_to_all x4 -> x3, blocking collectives: 67.6 us -> 57.1 us  [exchange(): return lax.all_to_all(blocks, axes, split_axis=0, concat_axis=0, tiled=True)]
    pallas_call x1 -> x5, Pallas kernels: 1.24 us -> 6.9 us  [the longest x1 2.66 us: on_device(): pl.pallas_call(far_kernel, grid=(1,), in_specs=[column_half(1), whole, su...]
    unnamed x26 -> x40, local copies, waits for them, and re-layouts: 9.19 us -> 14.2 us
    all_gather x0 -> x1, waiting for transfers between devices: none -> 3.74 us  [on_device(): lax.all_gather(jnp.concatenate([cotangent] * 4, axis=1), z_axes, axis=0,...]
    all_to_all x4 -> x5, starting transfers between devices: 25.4 us -> 28.3 us  [exchange(): return lax.all_to_all(blocks, axes, split_axis=0, concat_axis=0, tiled=True)]
    broadcast_in_dim x5 -> x1, local copies, waits for them, and re-layouts: 2.34 us -> 0.02 us  [spread(): return exchange(jnp.broadcast_to(block[None], (count,) + block.shape), axes)]
    ppermute x8 -> x9, waiting for transfers between devices: 9.49 us -> 11.8 us  [swap(): return lax.ppermute(block, axis, ((0, 1), (1, 0)))]
  transfers between devices with their start and end apart: 12 -> 15, of which waited for: 7 -> 10; matrix products, arithmetic and copies ran while one was open for 0% -> 1% of each run, Pallas kernels for 2% -> 4%
where the time goes in v9:
time: 222 us; the launch traced here: 221 us
  blocking collectives  80.5 us (36%)
  starting transfers between devices  67.8 us (31%)
  waiting for transfers between devices  26.8 us (12%)
  local copies, waits for them, and re-layouts  15.9 us (7%)
  Pallas kernels  14.6 us (7%)
  between operations  14.3 us (6%)
    all_to_all x3, blocking collectives, exchange(): return lax.all_to_all(blocks, axes, split_axis=0, concat_axis=0, tiled=True)  57.1 us
    ppermute x9, starting transfers between devices, swap(): return lax.ppermute(block, axis, ((0, 1), (1, 0)))  39.5 us
    all_to_all x5, starting transfers between devices, exchange(): return lax.all_to_all(blocks, axes, split_axis=0, concat_axis=0, tiled=True)  28.3 us
    all_gather x1, blocking collectives, on_device(): near = lax.all_gather(own_weight, 'y', axis=0, tiled=True)  23.3 us
    unnamed x40, local copies, waits for them, and re-layouts  14.2 us
    ppermute x9, waiting for transfers between devices, swap(): return lax.ppermute(block, axis, ((0, 1), (1, 0)))  11.8 us
    all_to_all x5, waiting for transfers between devices, exchange(): return lax.all_to_all(blocks, axes, split_axis=0, concat_axis=0, tiled=True)  11.3 us
  transfers between devices with their start and end apart: 15, of which 10 were waited for; matrix products, arithmetic and copies ran while one was open for 1% of the time, Pallas kernels for 4%

profile of v9, /device:TPU:1, one launch (start us, length us, event | category | flops | bytes accessed | tf_op | source)
XLA Modules:
  0.0 221.0 jit_solution(5611946627032430152)
XLA Ops:
  7.2 0.0 copy-start
  7.2 1.6 copy-done.2
  8.8 0.5 token_columns.1
  9.4 1.4 copy-done.1
  10.7 6.8 %all-to-all-start = ((bf16[4,128,2048]{2,1,0:T(8,128)(2,1)}), bf16[4,128,2048]{2,1,0:T(8,128)(2,1)S(1)}, u32[]{:S(2)}, u32[]{:S(2)}) async-start(bf16[4,128,2048]{2,1,0:T(8,128)(2,1)} %copy-done.1), calls=%async_computation | async-start | bytes 4194304 | tf_op jit(solution)/shard_map/all_to_all | solution.py:27
  17.5 0.7 pad_maximum_fusion.1
  18.2 0.0 all-gather.2.cloned.1.call-update
  18.3 23.3 %all_gather.6.weight_ref = bf16[1024,384]{1,0:T(8,128)(2,1)S(1)} all-gather(bf16[128,384]{1,0:T(8,128)(2,1)S(1)} %constant_dynamic-slice_fusion), channel_id=1, replica_groups=mesh['xh'=2,'y'=8,'zh'=4,'zl'=2,'xl'=2,'core'=2] {'y'}, dimensions={0}, use_global_device_ids=true | all-gather | bytes 884736 | tf_op jit(solution)/shard_map/all_gather | solution.py:221
  41.6 8.7 %collective-permute-start = (bf16[1024,384]{1,0:T(8,128)(2,1)S(1)}, bf16[1024,384]{1,0:T(8,128)(2,1)}, u32[]{:S(2)}, u32[]{:S(2)}) collective-permute-start(bf16[1024,384]{1,0:T(8,128)(2,1)S(1)} %all_gather.6.weight_ref), channel_id=1, source_target_pairs={{0,1},{1,0},{2,3},{3,2},{4,5},{5,4},{6,7},{7,6},{8,9},{9,8},{10,11... | collective-permute-start | bytes 2359304 | tf_op jit(solution)/shard_map/ppermute | solution.py:35
  50.3 0.7 near_projection.1.sum_ref
  51.0 1.3 collective-permute-done.weight_ref
  52.3 2.7 %far_projection.1 = bf16[512,384]{1,0:T(8,128)(2,1)} custom-call(bf16[512,2048]{1,0:T(8,128)(2,1)S(1)} %bitcast.18, bf16[1024,384]{1,0:T(8,128)(2,1)} %collective-permute-done.weight_ref, f32[512,384]{1,0:T(8,128)S(1)} %near_projection.1.sum_ref), custom_call_target="tpu_custom_call" | custom-call | tf_op jit(solution)/shard_map/far_projection/pallas_call | solution.py:247
  55.0 5.4 %all-to-all-start.1 = ((bf16[4,128,384]{2,1,0:T(8,128)(2,1)}), bf16[4,128,384]{2,1,0:T(8,128)(2,1)S(1)}, u32[]{:S(2)}, u32[]{:S(2)}) async-start(bf16[4,128,384]{2,1,0:T(8,128)(2,1)} %bitcast.2), calls=%async_computation.1 | async-start | bytes 786432 | tf_op jit(solution)/shard_map/all_to_all | solution.py:27
  60.4 3.7 %all-gather.2.cloned.1.call-done = bf16[1024,512]{1,0:T(8,128)(2,1)} async-done(((bf16[128,512]{1,0:T(8,128)(2,1)}), bf16[1024,512]{1,0:T(8,128)(2,1)}) %all-gather.2.cloned.1.call-update) | async-done | bytes 1048592 | tf_op jit(solution)/shard_map/all_gather | solution.py:257
  64.1 3.2 %all-to-all-done.1.parts_ref = bf16[4,128,384]{2,1,0:T(8,128)(2,1)S(1)} async-done(((bf16[4,128,384]{2,1,0:T(8,128)(2,1)}), bf16[4,128,384]{2,1,0:T(8,128)(2,1)S(1)}, u32[]{:S(2)}, u32[]{:S(2)}) %all-to-all-start.1) | async-done | bytes 393248 | tf_op jit(solution)/shard_map/all_to_all | solution.py:27
  67.3 0.9 projection_sum.1
  68.3 0.6 copy-done.10
  68.9 0.6 copy-done.17
  69.5 8.6 %all-to-all-start.2 = ((bf16[8,128,256]{2,1,0:T(8,128)(2,1)}), bf16[8,128,256]{2,1,0:T(8,128)(2,1)S(1)}, u32[]{:S(2)}, u32[]{:S(2)}) async-start(bf16[8,128,256]{2,1,0:T(8,128)(2,1)} %get-tuple-element.19), calls=%async_computation.2 | async-start | bytes 1048576 | tf_op jit(solution)/shard_map/all_to_all | solution.py:27
  78.1 1.0 slice.3.cot0
  79.0 2.2 collective-permute-start.1
  81.2 0.7 copy-done.3
  81.9 5.2 %collective-permute-done.1.cot1 = bf16[1024,128]{1,0:T(8,128)(2,1)S(1)} collective-permute-done((bf16[1024,128]{1,0:T(8,128)(2,1)S(1)}, bf16[1024,128]{1,0:T(8,128)(2,1)S(1)}, u32[]{:S(2)}, u32[]{:S(2)}) %collective-permute-start.1) | collective-permute-done | bytes 262176 | tf_op jit(solution)/shard_map/ppermute | solution.py:35
  87.1 0.7 copy-done.8
  87.8 6.3 %all-to-all-done.2 = bf16[8,128,256]{2,1,0:T(8,128)(2,1)S(1)} async-done(((bf16[8,128,256]{2,1,0:T(8,128)(2,1)}), bf16[8,128,256]{2,1,0:T(8,128)(2,1)S(1)}, u32[]{:S(2)}, u32[]{:S(2)}) %all-to-all-start.2) | async-done | bytes 524320 | tf_op jit(solution)/shard_map/all_to_all | solution.py:27
  94.1 2.1 collective-permute-start.2
  96.2 4.1 %all-to-all-start.4 = ((bf16[8,128,128]{2,1,0:T(8,128)(2,1)}), bf16[8,128,128]{2,1,0:T(8,128)(2,1)}, u32[]{:S(2)}, u32[]{:S(2)}) async-start(bf16[8,128,128]{2,1,0:T(8,128)(2,1)} %get-tuple-element.27), calls=%async_computation.4 | async-start | bytes 524288 | tf_op jit(solution)/shard_map/all_to_all | solution.py:27
  100.3 4.6 %collective-permute-start.3 = (bf16[1024,256]{1,0:T(8,128)(2,1)S(1)}, bf16[1024,256]{1,0:T(8,128)(2,1)S(1)}, u32[]{:S(2)}, u32[]{:S(2)}) collective-permute-start(bf16[1024,256]{1,0:T(8,128)(2,1)S(1)} %bitcast.22), channel_id=1, source_target_pairs={{0,1},{1,0},{2,3},{3,2},{4,5},{5,4},{6,7},{7,6},{8,9},{9,8},{10,11... | collective-permute-start | bytes 1572872 | tf_op jit(solution)/shard_map/ppermute | solution.py:35
  104.9 2.1 collective-permute-done.2.kv1
  107.0 5.3 %collective-permute-start.4 = (bf16[1024,256]{1,0:T(8,128)(2,1)}, bf16[1024,256]{1,0:T(8,128)(2,1)}, u32[]{:S(2)}, u32[]{:S(2)}) collective-permute-start(bf16[1024,256]{1,0:T(8,128)(2,1)} %collective-permute-done.2.kv1), channel_id=1, source_target_pairs={{0,1},{1,0},{2,3},{3,2},{4,5},{5,4},{6,7},{7,6},{8,9},{9,8},{10,11... | collective-permute-start | bytes 1572872 | tf_op jit(solution)/shard_map/ppermute | solution.py:35
  112.3 2.2 collective-permute-start.5
  114.5 0.0 copy-start.6
  114.5 0.7 copy-done.6
  115.3 0.8 copy-done.11
  116.0 3.2 %attention_rows.1 = (bf16[128,128]{1,0:T(8,128)(2,1)}, f32[16,2,128]{2,1,0:T(2,128)S(1)}, f32[2,128,128]{2,1,0:T(8,128)S(1)}) custom-call(bf16[128,128]{1,0:T(8,128)(2,1)S(1)} %copy-done.11, bf16[1024,256]{1,0:T(8,128)(2,1)S(1)} %bitcast.23, bf16[1024,256]{1,0:T(8,128)(2,1)} %collective-permute-done.2.kv1, ...), custom_call_target="tpu_custom_call" | custom-call | tf_op jit(solution)/shard_map/attention_rows/pallas_call | solution.py:287
  119.2 0.7 copy-done.15
  119.8 0.6 copy-done.19
  120.4 3.5 %all-to-all-start.3 = ((f32[16,2,128]{2,1,0:T(2,128)}), f32[16,2,128]{2,1,0:T(2,128)S(1)}, u32[]{:S(2)}, u32[]{:S(2)}) async-start(f32[16,2,128]{2,1,0:T(2,128)} %copy-done.19), calls=%async_computation.3 | async-start | bytes 32768 | tf_op jit(solution)/shard_map/all_to_all | solution.py:27
  123.9 0.0 copy-start.7
  123.9 0.7 copy-done.7
  124.7 0.8 copy-done.12
  125.4 0.9 copy-done.16
  126.3 2.6 %query_gradient.1.dq_ref = bf16[128,128]{1,0:T(8,128)(2,1)S(1)} custom-call(bf16[128,128]{1,0:T(8,128)(2,1)S(1)} %copy-done.12, bf16[1024,256]{1,0:T(8,128)(2,1)S(1)} %bitcast.24, bf16[1024,256]{1,0:T(8,128)(2,1)} %collective-permute-done.2.kv1, bf16[1024,256]{1,0:T(8,128)(2,1)S(1)} %collective-permute-done.3.kv2.across_ref, ...), custom_call_target="tpu_custom_call" | custom-call | tf_op jit(solution)/shard_map/query_gradient/pallas_call | solution.py:301
  128.9 0.0 copy-start.13
  128.9 0.6 copy-done.13
  129.5 1.8 all-to-all-done.3.stats_ref
  131.3 0.9 copy-done.4
  132.3 0.9 copy-done.9
  133.2 0.8 copy-done.18
  134.1 2.5 %attention_columns.1 = (f32[128,256]{1,0:T(8,128)S(1)}, f32[128,256]{1,0:T(8,128)S(1)}) custom-call(bf16[128,256]{1,0:T(8,128)(2,1)S(1)} %copy-done.18, bf16[1024,256]{1,0:T(8,128)(2,1)S(1)} %collective-permute-done.3.kv2.across_ref, bf16[1024,128]{1,0:T(8,128)(2,1)} %bitcast.6.q0, bf16[1024,128]{1,0:T(8,128)(2,1)} %collective-permute-done.5.q1, ...), custom_call_target="tpu_custom_call" | custom-call | tf_op jit(solution)/shard_map/attention_columns/pallas_call | solution.py:311
  136.6 5.4 %collective-permute-start.6 = (f32[128,256]{1,0:T(8,128)S(1)}, f32[128,256]{1,0:T(8,128)S(1)}, u32[]{:S(2)}, u32[]{:S(2)}) collective-permute-start(f32[128,256]{1,0:T(8,128)S(1)} %get-tuple-element.31), channel_id=1, source_target_pairs={{0,1},{1,0},{2,3},{3,2},{4,5},{5,4},{6,7},{7,6},{8,9},{9,8},{10,11... | collective-permute-start | bytes 393224 | tf_op jit(solution)/shard_map/ppermute | solution.py:35
  142.0 1.0 collective-permute-done.6.other_ref
  143.0 10.4 %all_to_all.40 = bf16[4,128,384]{2,1,0:T(8,128)(2,1)S(1)} all-to-all(bf16[4,128,384]{2,1,0:T(8,128)(2,1)S(1)} %join_gradients.1), channel_id=1, replica_groups=mesh['xh'=2,'y'=8,'zh'=4,'zl'=2,'xl'=2,'core'=2] {'xh','zl'}, dimensions={0} | all-to-all | bytes 786432 | tf_op jit(solution)/shard_map/all_to_all | solution.py:27
  153.4 0.7 weight_gradient.3
  154.2 3.5 %collective-permute-start.7 = (bf16[1024,384]{1,0:T(8,128)(2,1)S(1)}, bf16[1024,384]{1,0:T(8,128)(2,1)S(1)}, u32[]{:S(2)}, u32[]{:S(2)}) collective-permute-start(bf16[1024,384]{1,0:T(8,128)(2,1)S(1)} %weight_gradient.3), channel_id=1, source_target_pairs={{0,1},{1,0},{2,3},{3,2},{4,5},{5,4},{6,7},{7,6},{8,9},{9,8},{10,11... | collective-permute-start | bytes 2359304 | tf_op jit(solution)/shard_map/ppermute | solution.py:35
  157.6 0.7 weight_gradient.2
  158.4 1.1 collective-permute-done.7
  159.5 0.2 add_convert_fusion
  159.7 32.9 %all_to_all.41 = bf16[64,16,384]{2,1,0:T(8,128)(2,1)S(1)} all-to-all(bf16[64,16,384]{2,1,0:T(8,128)(2,1)S(1)} %bitcast.31), channel_id=1, replica_groups=mesh['xh'=2,'y'=8,'zh'=4,'zl'=2,'xl'=2,'core'=2] {'y','zh','xl'}, dimensions={0} | all-to-all | bytes 1572864 | tf_op jit(solution)/shard_map/all_to_all | solution.py:27
  192.6 0.1 reduce_sum.12
  192.8 13.8 %all_to_all.42 = bf16[16,16,384]{2,1,0:T(8,128)(2,1)S(1)} all-to-all(bf16[16,16,384]{2,1,0:T(8,128)(2,1)S(1)} %broadcast_in_dim.10), channel_id=1, replica_groups=mesh['xh'=2,'y'=8,'zh'=4,'zl'=2,'xl'=2,'core'=2] {'zh','zl','xl'}, dimensions={0} | all-to-all | bytes 393216 | tf_op jit(solution)/shard_map/all_to_all | solution.py:27
  206.6 5.6 %collective-permute-start.8 = (bf16[2,4,2,16,384]{4,3,2,0,1:T(8,128)(2,1)S(1)}, bf16[2,4,2,16,384]{4,3,2,0,1:T(8,128)(2,1)S(1)}, u32[]{:S(2)}, u32[]{:S(2)}) collective-permute-start(bf16[2,4,2,16,384]{4,3,2,0,1:T(8,128)(2,1)S(1)} %bitcast.32), channel_id=1, source_target_pairs={{0,1},{1,0},{2,3},{3,2},{4,5},{5,4},{6,7},{7,6},{8,9},{9,8},{10,11... | collective-permute-start | bytes 589832 | tf_op jit(solution)/shard_map/ppermute | solution.py:35
  212.2 1.0 collective-permute-done.8
  213.4 0.8 copy.6
  (30 shorter events, 0.2 us)
Async XLA Ops:
  7.2 11.1 %copy-start = (bf16[512,384]{1,0:T(8,128)(2,1)S(1)}, bf16[512,384]{1,0:T(8,128)(2,1)}, u32[]{:S(2)}) copy-start(bf16[512,384]{1,0:T(8,128)(2,1)} %param.4) | copy-start | bytes 1179652
  7.2 1.6 copy-start.2
  9.4 1.4 copy-start.1
  10.7 6.8 %copy-start.5 = (bf16[1,128,128]{2,1,0:T(8,128)(2,1)S(1)}, bf16[1,128,128]{2,1,0:T(8,128)(2,1)}, u32[]{:S(2)}) copy-start(bf16[1,128,128]{2,1,0:T(8,128)(2,1)} %param.5) | copy-start | bytes 98308
  10.7 39.6 %all-to-all-start = ((bf16[4,128,2048]{2,1,0:T(8,128)(2,1)}), bf16[4,128,2048]{2,1,0:T(8,128)(2,1)S(1)}, u32[]{:S(2)}, u32[]{:S(2)}) async-start(bf16[4,128,2048]{2,1,0:T(8,128)(2,1)} %copy-done.1), calls=%async_computation | async-start | bytes 4194304 | tf_op jit(solution)/shard_map/all_to_all | solution.py:27
  17.5 46.6 %all-gather.2.cloned.1.call-start = ((), (), s32[]{:S(2)}) async-start(), calls=%async_computation.8 | async-start | bytes 1179648 | tf_op jit(solution)/shard_map/all_gather | solution.py:257
  41.6 10.7 %collective-permute-start = (bf16[1024,384]{1,0:T(8,128)(2,1)S(1)}, bf16[1024,384]{1,0:T(8,128)(2,1)}, u32[]{:S(2)}, u32[]{:S(2)}) collective-permute-start(bf16[1024,384]{1,0:T(8,128)(2,1)S(1)} %all_gather.6.weight_ref), channel_id=1, source_target_pairs={{0,1},{1,0},{2,3},{3,2},{4,5},{5,4},{6,7},{7,6},{8,9},{9,8},{10,11... | collective-permute-start | bytes 2359304 | tf_op jit(solution)/shard_map/ppermute | solution.py:35
  55.0 12.3 %all-to-all-start.1 = ((bf16[4,128,384]{2,1,0:T(8,128)(2,1)}), bf16[4,128,384]{2,1,0:T(8,128)(2,1)S(1)}, u32[]{:S(2)}, u32[]{:S(2)}) async-start(bf16[4,128,384]{2,1,0:T(8,128)(2,1)} %bitcast.2), calls=%async_computation.1 | async-start | bytes 786432 | tf_op jit(solution)/shard_map/all_to_all | solution.py:27
  68.3 0.6 copy-start.10
  68.8 0.6 copy-start.17
  69.5 24.6 %all-to-all-start.2 = ((bf16[8,128,256]{2,1,0:T(8,128)(2,1)}), bf16[8,128,256]{2,1,0:T(8,128)(2,1)S(1)}, u32[]{:S(2)}, u32[]{:S(2)}) async-start(bf16[8,128,256]{2,1,0:T(8,128)(2,1)} %get-tuple-element.19), calls=%async_computation.2 | async-start | bytes 1048576 | tf_op jit(solution)/shard_map/all_to_all | solution.py:27
  79.0 8.1 %collective-permute-start.1 = (bf16[1024,128]{1,0:T(8,128)(2,1)S(1)}, bf16[1024,128]{1,0:T(8,128)(2,1)S(1)}, u32[]{:S(2)}, u32[]{:S(2)}) collective-permute-start(bf16[1024,128]{1,0:T(8,128)(2,1)S(1)} %slice.3.cot0), channel_id=1, source_target_pairs={{0,2},{2,0},{1,3},{3,1},{4,6},{6,4},{5,7},{7,5},{8,10},{10,8},{9,1... | collective-permute-start | bytes 786440 | tf_op jit(solution)/shard_map/ppermute | solution.py:35
  81.2 0.7 copy-start.3
  87.1 0.7 copy-start.8
  94.1 13.0 %collective-permute-start.2 = (bf16[1024,256]{1,0:T(8,128)(2,1)S(1)}, bf16[1024,256]{1,0:T(8,128)(2,1)}, u32[]{:S(2)}, u32[]{:S(2)}) collective-permute-start(bf16[1024,256]{1,0:T(8,128)(2,1)S(1)} %bitcast.21), channel_id=1, source_target_pairs={{0,2},{2,0},{1,3},{3,1},{4,6},{6,4},{5,7},{7,5},{8,10},{10,8},{9,1... | collective-permute-start | bytes 1572872 | tf_op jit(solution)/shard_map/ppermute | solution.py:35
  96.2 16.1 %all-to-all-start.4 = ((bf16[8,128,128]{2,1,0:T(8,128)(2,1)}), bf16[8,128,128]{2,1,0:T(8,128)(2,1)}, u32[]{:S(2)}, u32[]{:S(2)}) async-start(bf16[8,128,128]{2,1,0:T(8,128)(2,1)} %get-tuple-element.27), calls=%async_computation.4 | async-start | bytes 524288 | tf_op jit(solution)/shard_map/all_to_all | solution.py:27
  100.3 14.2 %collective-permute-start.3 = (bf16[1024,256]{1,0:T(8,128)(2,1)S(1)}, bf16[1024,256]{1,0:T(8,128)(2,1)S(1)}, u32[]{:S(2)}, u32[]{:S(2)}) collective-permute-start(bf16[1024,256]{1,0:T(8,128)(2,1)S(1)} %bitcast.22), channel_id=1, source_target_pairs={{0,1},{1,0},{2,3},{3,2},{4,5},{5,4},{6,7},{7,6},{8,9},{9,8},{10,11... | collective-permute-start | bytes 1572872 | tf_op jit(solution)/shard_map/ppermute | solution.py:35
  107.0 7.5 %collective-permute-start.4 = (bf16[1024,256]{1,0:T(8,128)(2,1)}, bf16[1024,256]{1,0:T(8,128)(2,1)}, u32[]{:S(2)}, u32[]{:S(2)}) collective-permute-start(bf16[1024,256]{1,0:T(8,128)(2,1)} %collective-permute-done.2.kv1), channel_id=1, source_target_pairs={{0,1},{1,0},{2,3},{3,2},{4,5},{5,4},{6,7},{7,6},{8,9},{9,8},{10,11... | collective-permute-start | bytes 1572872 | tf_op jit(solution)/shard_map/ppermute | solution.py:35
  112.3 19.0 %collective-permute-start.5 = (bf16[1024,128]{1,0:T(8,128)(2,1)}, bf16[1024,128]{1,0:T(8,128)(2,1)}, u32[]{:S(2)}, u32[]{:S(2)}) collective-permute-start(bf16[1024,128]{1,0:T(8,128)(2,1)} %bitcast.6.q0), channel_id=1, source_target_pairs={{0,2},{2,0},{1,3},{3,1},{4,6},{6,4},{5,7},{7,5},{8,10},{10,8},{9,1... | collective-permute-start | bytes 786440 | tf_op jit(solution)/shard_map/ppermute | solution.py:35
  114.5 0.8 copy-start.6
  115.3 0.8 copy-start.11
  119.2 0.7 copy-start.15
  119.8 0.6 copy-start.19
  120.4 10.9 %all-to-all-start.3 = ((f32[16,2,128]{2,1,0:T(2,128)}), f32[16,2,128]{2,1,0:T(2,128)S(1)}, u32[]{:S(2)}, u32[]{:S(2)}) async-start(f32[16,2,128]{2,1,0:T(2,128)} %copy-done.19), calls=%async_computation.3 | async-start | bytes 32768 | tf_op jit(solution)/shard_map/all_to_all | solution.py:27
  123.9 0.8 copy-start.7
  124.7 0.8 copy-start.12
  125.4 0.9 copy-start.16
  128.9 0.6 copy-start.13
  131.3 1.0 copy-start.4
  132.3 0.9 copy-start.9
  133.2 0.8 copy-start.18
  134.1 8.9 %copy-start.14 = (bf16[128,128]{1,0:T(8,128)(2,1)S(1)}, bf16[128,128]{1,0:T(8,128)(2,1)}, u32[]{:S(2)}) copy-start(bf16[128,128]{1,0:T(8,128)(2,1)} %copy-done.13) | copy-start | bytes 98308
  136.6 6.4 %collective-permute-start.6 = (f32[128,256]{1,0:T(8,128)S(1)}, f32[128,256]{1,0:T(8,128)S(1)}, u32[]{:S(2)}, u32[]{:S(2)}) collective-permute-start(f32[128,256]{1,0:T(8,128)S(1)} %get-tuple-element.31), channel_id=1, source_target_pairs={{0,1},{1,0},{2,3},{3,2},{4,5},{5,4},{6,7},{7,6},{8,9},{9,8},{10,11... | collective-permute-start | bytes 393224 | tf_op jit(solution)/shard_map/ppermute | solution.py:35
  154.2 5.3 %collective-permute-start.7 = (bf16[1024,384]{1,0:T(8,128)(2,1)S(1)}, bf16[1024,384]{1,0:T(8,128)(2,1)S(1)}, u32[]{:S(2)}, u32[]{:S(2)}) collective-permute-start(bf16[1024,384]{1,0:T(8,128)(2,1)S(1)} %weight_gradient.3), channel_id=1, source_target_pairs={{0,1},{1,0},{2,3},{3,2},{4,5},{5,4},{6,7},{7,6},{8,9},{9,8},{10,11... | collective-permute-start | bytes 2359304 | tf_op jit(solution)/shard_map/ppermute | solution.py:35
  206.6 6.7 %collective-permute-start.8 = (bf16[2,4,2,16,384]{4,3,2,0,1:T(8,128)(2,1)S(1)}, bf16[2,4,2,16,384]{4,3,2,0,1:T(8,128)(2,1)S(1)}, u32[]{:S(2)}, u32[]{:S(2)}) collective-permute-start(bf16[2,4,2,16,384]{4,3,2,0,1:T(8,128)(2,1)S(1)} %bitcast.32), channel_id=1, source_target_pairs={{0,1},{1,0},{2,3},{3,2},{4,5},{5,4},{6,7},{7,6},{8,9},{9,8},{10,11... | collective-permute-start | bytes 589832 | tf_op jit(solution)/shard_map/ppermute | solution.py:35
Sparse Core Ops, SparseCore 0:
  20.4 43.6 all-gather.1

commit v10 on v9

--- a/solution.py
+++ b/solution.py
@@ -44,7 +44,10 @@
     return z * 4 + (lax.axis_index("xl") ^ (piece & 1)) * 2 + (lax.axis_index("core") ^ (piece >> 1))
 
 
-def row_scores(z_count, q_ref, kv_refs):
+def forward_kernel(
+    z_count, q_ref, kv0, kv1, kv2, kv3, cot_ref, attn_ref, stats_ref, dq_ref, held
+):
+    pieces = (kv0, kv1, kv2, kv3)
     rows, head = q_ref.shape
     half_rows, ctx_count = rows // 2, 4 * z_count
     scale = 1.0 / math.sqrt(head)
@@ -52,24 +55,14 @@
     down = lax.broadcasted_iota(jnp.int32, (rows, rows), 0)
     across = lax.broadcasted_iota(jnp.int32, (rows, rows), 1)
     own_positions = positions(own, down, half_rows, ctx_count)
-    for piece, kv in enumerate(kv_refs):
-        raw = dot_f32(q_ref[...], kv[:, :head], 1, 1) * scale
-        tiles = []
+    queries, cotangent = q_ref[...], cot_ref[...]
+    top = None
+    for piece, kv in enumerate(pieces):
+        raw = dot_f32(queries, kv[:, :head], 1, 1) * scale
         for z in range(z_count):
             device = piece_device(piece, z)
             allowed = positions(device, across, half_rows, ctx_count) <= own_positions
-            tiles.append(jnp.where(allowed, raw[:, z * rows : (z + 1) * rows], masked_fill))
-        yield tiles
-
-
-def forward_kernel(
-    z_count, q_ref, kv0, kv1, kv2, kv3, cot_ref, attn_ref, stats_ref, columns_ref, held
-):
-    pieces = (kv0, kv1, kv2, kv3)
-    rows, head = q_ref.shape
-    top = None
-    for piece, tiles in enumerate(row_scores(z_count, q_ref, pieces)):
-        for z, tile in enumerate(tiles):
+            tile = jnp.where(allowed, raw[:, z * rows : (z + 1) * rows], masked_fill)
             held[piece, :, z * rows : (z + 1) * rows] = tile
             top = tile if top is None else jnp.maximum(top, tile)
     row_top = jnp.max(top, axis=1, keepdims=True)
@@ -88,34 +81,23 @@
     attn_low = attn.astype(low)
     attn_ref[...] = attn_low
     delta = jnp.sum(
-        cot_ref[...].astype(jnp.float32) * attn_low.astype(jnp.float32), axis=1, keepdims=True
+        cotangent.astype(jnp.float32) * attn_low.astype(jnp.float32), axis=1, keepdims=True
     )
     shift = 2.0 * z_weight * log_total - delta
     for place, column in enumerate((log_total, shift)):
-        wide = jnp.broadcast_to(column, (rows, rows))
-        columns_ref[place] = wide
-        line = jnp.transpose(wide)[0:1, :]
+        line = jnp.transpose(jnp.broadcast_to(column, (rows, rows)))[0:1, :]
         for copy in range(stats_ref.shape[0]):
             stats_ref[copy, place : place + 1, :] = line
-
-
-def query_kernel(z_count, q_ref, kv0, kv1, kv2, kv3, cot_ref, columns_ref, dq_ref):
-    pieces = (kv0, kv1, kv2, kv3)
-    rows, head = q_ref.shape
-    log_total, shift = columns_ref[0], columns_ref[1]
     grad = jnp.zeros((rows, head), jnp.float32)
-    for kv, tiles in zip(pieces, row_scores(z_count, q_ref, pieces)):
-        dprob = dot_f32(cot_ref[...], kv[:, head:], 1, 1)
-        dscores = []
-        for z, tile in enumerate(tiles):
-            prob = jnp.exp(tile - log_total)
-            dscores.append((prob * (dprob[:, z * rows : (z + 1) * rows] + shift)).astype(low))
-        grad = grad + dot_f32(jnp.concatenate(dscores, axis=1), kv[:, :head], 1, 0)
-    dq_ref[...] = (grad * (1.0 / math.sqrt(head))).astype(low)
-
-
-def backward_kernel(z_count, kv_ref, across_ref, q0, q1, cot0, cot1, stats_ref, own_ref, other_ref):
-    rows, head = kv_ref.shape[0], kv_ref.shape[1] // 2
+    for piece, kv in enumerate(pieces):
+        dprob = dot_f32(cotangent, kv[:, head:], 1, 1)
+        dscore = held[piece] * inverse * (dprob + shift)
+        grad = grad + dot_f32(dscore.astype(low), kv[:, :head], 1, 0)
+    dq_ref[...] = (grad * scale).astype(low)
+
+
+def backward_kernel(z_count, along_ref, across_ref, qc0, qc1, stats_ref, own_ref, other_ref):
+    rows, head = along_ref.shape[0] // z_count, along_ref.shape[1] // 2
     half_rows, ctx_count = rows // 2, 4 * z_count
     scale = 1.0 / math.sqrt(head)
     z_own = lax.axis_index(z_axes)
@@ -128,15 +110,14 @@
         ],
         axis=0,
     )
-    pairs = jnp.concatenate(
-        [kv_ref[...], across_ref[pl.ds(pl.multiple_of(z_own * rows, rows), rows), :]], axis=0
-    )
+    place = pl.ds(pl.multiple_of(z_own * rows, rows), rows)
+    pairs = jnp.concatenate([along_ref[place, :], across_ref[place, :]], axis=0)
     keys, values = pairs[:, :head], pairs[:, head:]
     grad_key = jnp.zeros((2 * rows, head), jnp.float32)
     grad_value = jnp.zeros((2 * rows, head), jnp.float32)
-    for piece, (q_ref, cot_ref) in enumerate(((q0, cot0), (q1, cot1))):
+    for piece, both in enumerate((qc0, qc1)):
         slot = lax.axis_index("xl") ^ piece
-        queries, cotangent = q_ref[...], cot_ref[...]
+        queries, cotangent = both[:, :head], both[:, head:]
         scores = dot_f32(keys, queries, 1, 1) * scale
         dprob = dot_f32(values, cotangent, 1, 1)
         probs, dscores = [], []
@@ -179,7 +160,7 @@
     out_ref[...] = (sum_ref[...] + dot_f32(x_ref[...], weight_ref[...], 1, 0)).astype(low)
 
 
-def split_kernel(parts_ref, q_ref, kv_ref, kv_copies, q_copies):
+def split_kernel(parts_ref, cot_ref, q_ref, kv_copies, qc_copies):
     head = q_ref.shape[1]
     total = parts_ref[0].astype(jnp.float32)
     for part in range(1, parts_ref.shape[0]):
@@ -187,10 +168,10 @@
     qkv = total.astype(low)
     queries, pairs = qkv[:, :head], qkv[:, head:]
     q_ref[...] = queries
-    kv_ref[...] = pairs
+    both = jnp.concatenate([queries, cot_ref[...]], axis=1)
     for copy in range(kv_copies.shape[0]):
         kv_copies[copy] = pairs
-        q_copies[copy] = queries
+        qc_copies[copy] = both
 
 
 def join_kernel(dq_ref, own_ref, other_ref, out_ref):
@@ -254,68 +235,51 @@
         name="far_projection",
     )(columns, far, near_sum)
     parts = exchange(parts.reshape(4, row_count, width), group_axes)
-    cotangent_z = lax.all_gather(
-        jnp.concatenate([cotangent] * 4, axis=1), z_axes, axis=0, tiled=True
-    )
-    parts, cotangent_z = lax.optimization_barrier((parts, cotangent_z))
-    cotangent_z = cotangent_z[:, :head]
-    cotangent_x = swap(cotangent_z, "xl")
-    queries, own_pairs, pair_copies, query_copies = pl.pallas_call(
+    queries, pair_copies, query_copies = pl.pallas_call(
         split_kernel,
-        in_specs=in_vmem(1),
-        out_specs=in_vmem(4),
+        in_specs=in_vmem(2),
+        out_specs=in_vmem(3),
         out_shape=[
             jax.ShapeDtypeStruct(shape, low)
             for shape in (
                 (row_count, head),
-                (row_count, 2 * head),
                 (z_count, row_count, 2 * head),
-                (z_count, row_count, head),
+                (z_count, row_count, 2 * head),
             )
         ],
         compiler_params=vmem,
         name="projection_sum",
-    )(parts)
+    )(parts, cotangent)
 
     along_z = exchange(pair_copies, z_axes).reshape(-1, 2 * head)
-    along_z, cotangent_x = lax.optimization_barrier((along_z, cotangent_x))
     by_x, by_core = swap(along_z, "xl"), swap(along_z, "core")
     pair_pieces = (along_z, by_x, by_core, swap(by_x, "core"))
-    queries_z = exchange(query_copies, z_axes).reshape(-1, head)
+    queries_z = exchange(query_copies, z_axes).reshape(-1, 2 * head)
     query_pieces = (queries_z, swap(queries_z, "xl"))
 
-    attn_rows, stats, stat_columns = pl.pallas_call(
+    attn_rows, stats, grad_query = pl.pallas_call(
         functools.partial(forward_kernel, z_count),
         in_specs=in_vmem(6),
         out_specs=in_vmem(3),
         out_shape=[
             jax.ShapeDtypeStruct((row_count, head), low),
             jax.ShapeDtypeStruct((2 * z_count, 2, row_count), jnp.float32),
-            jax.ShapeDtypeStruct((2, row_count, row_count), jnp.float32),
+            jax.ShapeDtypeStruct((row_count, head), low),
         ],
         scratch_shapes=[pltpu.VMEM((4, row_count, z_count * row_count), jnp.float32)],
         compiler_params=vmem,
         name="attention_rows",
     )(queries, *pair_pieces, cotangent)
     stats_all = exchange(stats, z_axes + ("xl",))
-    grad_query = pl.pallas_call(
-        functools.partial(query_kernel, z_count),
-        in_specs=in_vmem(7),
-        out_specs=in_vmem(1)[0],
-        out_shape=jax.ShapeDtypeStruct((row_count, head), low),
-        compiler_params=vmem,
-        name="query_gradient",
-    )(queries, *pair_pieces, cotangent, stat_columns)
-    grad_query, stats_all = lax.optimization_barrier((grad_query, stats_all))
 
     own_part, other_part = pl.pallas_call(
         functools.partial(backward_kernel, z_count),
-        in_specs=in_vmem(7),
+        in_specs=in_vmem(5),
         out_specs=in_vmem(2),
         out_shape=[jax.ShapeDtypeStruct((row_count, 2 * head), jnp.float32)] * 2,
         compiler_params=vmem,
         name="attention_columns",
-    )(own_pairs, pair_pieces[2], *query_pieces, cotangent_z, cotangent_x, stats_all)
+    )(pair_pieces[0], pair_pieces[2], *query_pieces, stats_all)
     grad_copies = pl.pallas_call(
         join_kernel,
         in_specs=in_vmem(3),

time: 222 us -> 204 us (0.919)
  blocking collectives: 80.5 us -> 112 us
  between operations: 14.3 us -> 0.91 us
  waiting for transfers between devices: 26.8 us -> 14.9 us
  starting transfers between devices: 67.8 us -> 57.1 us
  local copies, waits for them, and re-layouts: 15.9 us -> 6.53 us
  Pallas kernels: 14.6 us -> 11 us
    all_to_all x3 -> x5, blocking collectives: 57.1 us -> 89 us  [exchange(): return lax.all_to_all(blocks, axes, split_axis=0, concat_axis=0, tiled=True)]
    all_to_all x5 -> x3, starting transfers between devices: 28.3 us -> 17.7 us  [exchange(): return lax.all_to_all(blocks, axes, split_axis=0, concat_axis=0, tiled=True)]
    unnamed x40 -> x22, local copies, waits for them, and re-layouts: 14.2 us -> 5.71 us
    ppermute x9 -> x8, waiting for transfers between devices: 11.8 us -> 7.49 us  [swap(): return lax.ppermute(block, axis, ((0, 1), (1, 0)))]
    all_to_all x5 -> x3, waiting for transfers between devices: 11.3 us -> 7.4 us  [exchange(): return lax.all_to_all(blocks, axes, split_axis=0, concat_axis=0, tiled=True)]
    all_gather x1 -> x0, waiting for transfers between devices: 3.74 us -> none  [on_device(): lax.all_gather(jnp.concatenate([cotangent] * 4, axis=1), z_axes, axis=0,...]
    pallas_call x2 -> x1, Pallas kernels: 3.49 us -> 0.09 us  [on_device(): pl.pallas_call(split_kernel, in_specs=in_vmem(2), out_specs=in_vmem(3), o...]
    ppermute x9 -> x8, starting transfers between devices: 39.5 us -> 39.4 us  [swap(): return lax.ppermute(block, axis, ((0, 1), (1, 0)))]
  transfers between devices with their start and end apart: 15 -> 11, of which waited for: 10 -> 6; matrix products, arithmetic and copies ran while one was open for 1% -> 0% of each run, Pallas kernels for 4% -> 2%
where the time goes in v10:
time: 204 us; the launch traced here: 203 us
  blocking collectives  112 us (55%)
  starting transfers between devices  57.1 us (28%)
  waiting for transfers between devices  14.9 us (7%)
  Pallas kernels  11 us (5%)
  local copies, waits for them, and re-layouts  6.53 us (3%)
    all_to_all x5, blocking collectives, exchange(): return lax.all_to_all(blocks, axes, split_axis=0, concat_axis=0, tiled=True)  89 us
    ppermute x8, starting transfers between devices, swap(): return lax.ppermute(block, axis, ((0, 1), (1, 0)))  39.4 us
    all_gather x1, blocking collectives, on_device(): near = lax.all_gather(own_weight, 'y', axis=0, tiled=True)  23.3 us
    all_to_all x3, starting transfers between devices, exchange(): return lax.all_to_all(blocks, axes, split_axis=0, concat_axis=0, tiled=True)  17.7 us
    ppermute x8, waiting for transfers between devices, swap(): return lax.ppermute(block, axis, ((0, 1), (1, 0)))  7.49 us
    all_to_all x3, waiting for transfers between devices, exchange(): return lax.all_to_all(blocks, axes, split_axis=0, concat_axis=0, tiled=True)  7.4 us
    unnamed x22, local copies, waits for them, and re-layouts  5.71 us
  transfers between devices with their start and end apart: 11, of which 6 were waited for; matrix products, arithmetic and copies ran while one was open for 0% of the time, Pallas kernels for 2%

profile of v10, /device:TPU:1, one launch (start us, length us, event | category | flops | bytes accessed | tf_op | source)
XLA Modules:
  0.0 203.1 jit_solution(15627705770967016456)
XLA Ops:
  0.6 0.0 copy-start
  0.6 0.0 copy-start.2
  0.7 1.6 copy-done.2
  2.3 0.5 token_columns.1
  2.8 0.0 copy-start.1
  2.9 1.3 copy-done.1
  4.2 6.7 %all-to-all-start = ((bf16[4,128,2048]{2,1,0:T(8,128)(2,1)}), bf16[4,128,2048]{2,1,0:T(8,128)(2,1)S(1)}, u32[]{:S(2)}, u32[]{:S(2)}) async-start(bf16[4,128,2048]{2,1,0:T(8,128)(2,1)} %copy-done.1), calls=%async_computation | async-start | bytes 4194304 | tf_op jit(solution)/shard_map/all_to_all | solution.py:27
  10.8 0.0 copy-done
  10.8 23.3 %all_gather.3.weight_ref = bf16[1024,384]{1,0:T(8,128)(2,1)S(1)} all-gather(bf16[128,384]{1,0:T(8,128)(2,1)S(1)} %constant_dynamic-slice_fusion), channel_id=1, replica_groups=mesh['xh'=2,'y'=8,'zh'=4,'zl'=2,'xl'=2,'core'=2] {'y'}, dimensions={0}, use_global_device_ids=true | all-gather | bytes 884736 | tf_op jit(solution)/shard_map/all_gather | solution.py:202
  34.2 8.7 %collective-permute-start = (bf16[1024,384]{1,0:T(8,128)(2,1)S(1)}, bf16[1024,384]{1,0:T(8,128)(2,1)}, u32[]{:S(2)}, u32[]{:S(2)}) collective-permute-start(bf16[1024,384]{1,0:T(8,128)(2,1)S(1)} %all_gather.3.weight_ref), channel_id=1, source_target_pairs={{0,1},{1,0},{2,3},{3,2},{4,5},{5,4},{6,7},{7,6},{8,9},{9,8},{10,11... | collective-permute-start | bytes 2359304 | tf_op jit(solution)/shard_map/ppermute | solution.py:35
  42.9 0.0 all-to-all-done
  42.9 0.7 near_projection.1.sum_ref
  43.6 0.0 copy-start.4
  43.6 1.3 collective-permute-done.weight_ref
  44.9 1.9 far_projection.1
  46.8 12.6 %all_to_all.40.parts_ref = bf16[4,128,384]{2,1,0:T(8,128)(2,1)S(1)} all-to-all(bf16[4,128,384]{2,1,0:T(8,128)(2,1)S(1)} %bitcast.30), channel_id=1, replica_groups=mesh['xh'=2,'y'=8,'zh'=4,'zl'=2,'xl'=2,'core'=2] {'xh','zl'}, dimensions={0} | all-to-all | bytes 786432 | tf_op jit(solution)/shard_map/all_to_all | solution.py:27
  59.4 0.0 copy-done.4
  59.4 0.1 projection_sum.1
  59.5 0.0 copy-start.3
  59.5 0.0 copy-start.6
  59.5 21.9 %all_to_all.41 = bf16[8,128,256]{2,1,0:T(8,128)(2,1)S(1)} all-to-all(bf16[8,128,256]{2,1,0:T(8,128)(2,1)S(1)} %get-tuple-element.11), channel_id=1, replica_groups=mesh['xh'=2,'y'=8,'zh'=4,'zl'=2,'xl'=2,'core'=2] {'zh','zl'}, dimensions={0} | all-to-all | bytes 1048576 | tf_op jit(solution)/shard_map/all_to_all | solution.py:27
  81.5 0.0 copy-done.3
  81.5 0.0 copy-done.6
  81.5 3.5 %all-to-all-start.3 = ((bf16[8,128,256]{2,1,0:T(8,128)(2,1)}), bf16[8,128,256]{2,1,0:T(8,128)(2,1)S(1)}, u32[]{:S(2)}, u32[]{:S(2)}) async-start(bf16[8,128,256]{2,1,0:T(8,128)(2,1)} %copy-done.3), calls=%async_computation.3 | async-start | bytes 1048576 | tf_op jit(solution)/shard_map/all_to_all | solution.py:27
  85.0 2.2 %collective-permute-start.1 = (bf16[1024,256]{1,0:T(8,128)(2,1)S(1)}, bf16[1024,256]{1,0:T(8,128)(2,1)}, u32[]{:S(2)}, u32[]{:S(2)}) collective-permute-start(bf16[1024,256]{1,0:T(8,128)(2,1)S(1)} %bitcast.21), channel_id=1, source_target_pairs={{0,2},{2,0},{1,3},{3,1},{4,6},{6,4},{5,7},{7,5},{8,10},{10,8},{9,1... | collective-permute-start | bytes 1572872 | tf_op jit(solution)/shard_map/ppermute | solution.py:35
  87.1 6.2 %collective-permute-start.2 = (bf16[1024,256]{1,0:T(8,128)(2,1)S(1)}, bf16[1024,256]{1,0:T(8,128)(2,1)}, u32[]{:S(2)}, u32[]{:S(2)}) collective-permute-start(bf16[1024,256]{1,0:T(8,128)(2,1)S(1)} %bitcast.22), channel_id=1, source_target_pairs={{0,1},{1,0},{2,3},{3,2},{4,5},{5,4},{6,7},{7,6},{8,9},{9,8},{10,11... | collective-permute-start | bytes 1572872 | tf_op jit(solution)/shard_map/ppermute | solution.py:35
  93.3 3.0 %collective-permute-done.1.kv1 = bf16[1024,256]{1,0:T(8,128)(2,1)} collective-permute-done((bf16[1024,256]{1,0:T(8,128)(2,1)S(1)}, bf16[1024,256]{1,0:T(8,128)(2,1)}, u32[]{:S(2)}, u32[]{:S(2)}) %collective-permute-start.1) | collective-permute-done | bytes 524320 | tf_op jit(solution)/shard_map/ppermute | solution.py:35
  96.4 6.8 %collective-permute-start.3 = (bf16[1024,256]{1,0:T(8,128)(2,1)}, bf16[1024,256]{1,0:T(8,128)(2,1)}, u32[]{:S(2)}, u32[]{:S(2)}) collective-permute-start(bf16[1024,256]{1,0:T(8,128)(2,1)} %collective-permute-done.1.kv1), channel_id=1, source_target_pairs={{0,1},{1,0},{2,3},{3,2},{4,5},{5,4},{6,7},{7,6},{8,9},{9,8},{10,11... | collective-permute-start | bytes 1572872 | tf_op jit(solution)/shard_map/ppermute | solution.py:35
  103.2 0.0 all-to-all-done.3
  103.2 2.2 %collective-permute-start.4 = (bf16[1024,256]{1,0:T(8,128)(2,1)S(1)}, bf16[1024,256]{1,0:T(8,128)(2,1)}, u32[]{:S(2)}, u32[]{:S(2)}) collective-permute-start(bf16[1024,256]{1,0:T(8,128)(2,1)S(1)} %bitcast.28), channel_id=1, source_target_pairs={{0,2},{2,0},{1,3},{3,1},{4,6},{6,4},{5,7},{7,5},{8,10},{10,8},{9,1... | collective-permute-start | bytes 1572872 | tf_op jit(solution)/shard_map/ppermute | solution.py:35
  105.4 0.0 collective-permute-done.2.kv2.across_ref
  105.4 0.0 collective-permute-done.3.kv3
  105.4 0.0 copy-start.5
  105.4 0.7 copy-done.5
  106.2 0.0 copy-start.7
  106.2 0.8 copy-done.7
  107.0 3.5 %attention_rows.1 = (bf16[128,128]{1,0:T(8,128)(2,1)}, f32[16,2,128]{2,1,0:T(2,128)S(1)}, bf16[128,128]{1,0:T(8,128)(2,1)S(1)}) custom-call(bf16[128,128]{1,0:T(8,128)(2,1)S(1)} %copy-done.7, bf16[1024,256]{1,0:T(8,128)(2,1)S(1)} %bitcast.23, bf16[1024,256]{1,0:T(8,128)(2,1)} %collective-permute-done.1.kv1, ...), custom_call_target="tpu_custom_call" | custom-call | tf_op jit(solution)/shard_map/attention_rows/pallas_call | solution.py:260
  110.5 0.0 copy-start.8
  110.5 0.6 copy-done.8
  111.1 0.0 copy-start.10
  111.1 0.6 copy-done.10
  111.7 7.6 %all-to-all-start.4 = ((f32[16,2,128]{2,1,0:T(2,128)}), f32[16,2,128]{2,1,0:T(2,128)S(1)}, u32[]{:S(2)}, u32[]{:S(2)}) async-start(f32[16,2,128]{2,1,0:T(2,128)} %copy-done.10), calls=%async_computation.4 | async-start | bytes 32768 | tf_op jit(solution)/shard_map/all_to_all | solution.py:27
  119.3 0.0 collective-permute-done.4.qc1
  119.3 7.4 %all-to-all-done.4.stats_ref = f32[16,2,128]{2,1,0:T(2,128)S(1)} async-done(((f32[16,2,128]{2,1,0:T(2,128)}), f32[16,2,128]{2,1,0:T(2,128)S(1)}, u32[]{:S(2)}, u32[]{:S(2)}) %all-to-all-start.4) | async-done | bytes 16416 | tf_op jit(solution)/shard_map/all_to_all | solution.py:27
  126.7 0.0 copy-start.9
  126.7 2.7 %attention_columns.1 = (f32[128,256]{1,0:T(8,128)S(1)}, f32[128,256]{1,0:T(8,128)S(1)}) custom-call(bf16[1024,256]{1,0:T(8,128)(2,1)S(1)} %bitcast.24, bf16[1024,256]{1,0:T(8,128)(2,1)} %collective-permute-done.2.kv2.across_ref, bf16[1024,256]{1,0:T(8,128)(2,1)S(1)} %bitcast.29, bf16[1024,256]{1,0:T(8,128)(2,1)} %collective-permute-done.4.qc1, ...), custom_call_target="tpu_custom_call" | custom-call | tf_op jit(solution)/shard_map/attention_columns/pallas_call | solution.py:275
  129.4 3.6 %collective-permute-start.5 = (f32[128,256]{1,0:T(8,128)S(1)}, f32[128,256]{1,0:T(8,128)S(1)}, u32[]{:S(2)}, u32[]{:S(2)}) collective-permute-start(f32[128,256]{1,0:T(8,128)S(1)} %get-tuple-element.17), channel_id=1, source_target_pairs={{0,1},{1,0},{2,3},{3,2},{4,5},{5,4},{6,7},{7,6},{8,9},{9,8},{10,11... | collective-permute-start | bytes 393224 | tf_op jit(solution)/shard_map/ppermute | solution.py:35
  133.0 1.0 collective-permute-done.5.other_ref
  134.0 0.0 copy-done.9
  134.0 10.3 %all_to_all.42 = bf16[4,128,384]{2,1,0:T(8,128)(2,1)S(1)} all-to-all(bf16[4,128,384]{2,1,0:T(8,128)(2,1)S(1)} %join_gradients.1), channel_id=1, replica_groups=mesh['xh'=2,'y'=8,'zh'=4,'zl'=2,'xl'=2,'core'=2] {'xh','zl'}, dimensions={0} | all-to-all | bytes 786432 | tf_op jit(solution)/shard_map/all_to_all | solution.py:27
  144.3 0.7 weight_gradient.3
  145.0 4.1 %collective-permute-start.6 = (bf16[1024,384]{1,0:T(8,128)(2,1)S(1)}, bf16[1024,384]{1,0:T(8,128)(2,1)S(1)}, u32[]{:S(2)}, u32[]{:S(2)}) collective-permute-start(bf16[1024,384]{1,0:T(8,128)(2,1)S(1)} %weight_gradient.3), channel_id=1, source_target_pairs={{0,1},{1,0},{2,3},{3,2},{4,5},{5,4},{6,7},{7,6},{8,9},{9,8},{10,11... | collective-permute-start | bytes 2359304 | tf_op jit(solution)/shard_map/ppermute | solution.py:35
  149.1 0.7 weight_gradient.2
  149.8 1.1 collective-permute-done.6
  151.0 0.2 add_convert_fusion
  151.1 30.5 %all_to_all.43 = bf16[64,16,384]{2,1,0:T(8,128)(2,1)S(1)} all-to-all(bf16[64,16,384]{2,1,0:T(8,128)(2,1)S(1)} %bitcast.33), channel_id=1, replica_groups=mesh['xh'=2,'y'=8,'zh'=4,'zl'=2,'xl'=2,'core'=2] {'y','zh','xl'}, dimensions={0} | all-to-all | bytes 1572864 | tf_op jit(solution)/shard_map/all_to_all | solution.py:27
  181.6 0.1 reduce_sum.12
  181.7 13.8 %all_to_all.44 = bf16[16,16,384]{2,1,0:T(8,128)(2,1)S(1)} all-to-all(bf16[16,16,384]{2,1,0:T(8,128)(2,1)S(1)} %broadcast_in_dim.10), channel_id=1, replica_groups=mesh['xh'=2,'y'=8,'zh'=4,'zl'=2,'xl'=2,'core'=2] {'zh','zl','xl'}, dimensions={0} | all-to-all | bytes 393216 | tf_op jit(solution)/shard_map/all_to_all | solution.py:27
  195.5 5.6 %collective-permute-start.7 = (bf16[2,4,2,16,384]{4,3,2,0,1:T(8,128)(2,1)S(1)}, bf16[2,4,2,16,384]{4,3,2,0,1:T(8,128)(2,1)S(1)}, u32[]{:S(2)}, u32[]{:S(2)}) collective-permute-start(bf16[2,4,2,16,384]{4,3,2,0,1:T(8,128)(2,1)S(1)} %bitcast.34), channel_id=1, source_target_pairs={{0,1},{1,0},{2,3},{3,2},{4,5},{5,4},{6,7},{7,6},{8,9},{9,8},{10,11... | collective-permute-start | bytes 589832 | tf_op jit(solution)/shard_map/ppermute | solution.py:35
  201.2 1.0 collective-permute-done.7
  202.3 0.8 copy.6
  (5 shorter events, 0.2 us)
Async XLA Ops:
  0.6 10.2 %copy-start = (bf16[512,384]{1,0:T(8,128)(2,1)S(1)}, bf16[512,384]{1,0:T(8,128)(2,1)}, u32[]{:S(2)}) copy-start(bf16[512,384]{1,0:T(8,128)(2,1)} %param.4) | copy-start | bytes 1179652
  0.6 1.6 copy-start.2
  2.8 1.3 copy-start.1
  4.2 38.7 %all-to-all-start = ((bf16[4,128,2048]{2,1,0:T(8,128)(2,1)}), bf16[4,128,2048]{2,1,0:T(8,128)(2,1)S(1)}, u32[]{:S(2)}, u32[]{:S(2)}) async-start(bf16[4,128,2048]{2,1,0:T(8,128)(2,1)} %copy-done.1), calls=%async_computation | async-start | bytes 4194304 | tf_op jit(solution)/shard_map/all_to_all | solution.py:27
  34.2 10.7 %collective-permute-start = (bf16[1024,384]{1,0:T(8,128)(2,1)S(1)}, bf16[1024,384]{1,0:T(8,128)(2,1)}, u32[]{:S(2)}, u32[]{:S(2)}) collective-permute-start(bf16[1024,384]{1,0:T(8,128)(2,1)S(1)} %all_gather.3.weight_ref), channel_id=1, source_target_pairs={{0,1},{1,0},{2,3},{3,2},{4,5},{5,4},{6,7},{7,6},{8,9},{9,8},{10,11... | collective-permute-start | bytes 2359304 | tf_op jit(solution)/shard_map/ppermute | solution.py:35
  43.6 15.8 %copy-start.4 = (bf16[1,128,128]{2,1,0:T(8,128)(2,1)S(1)}, bf16[1,128,128]{2,1,0:T(8,128)(2,1)}, u32[]{:S(2)}) copy-start(bf16[1,128,128]{2,1,0:T(8,128)(2,1)} %param.5) | copy-start | bytes 98308
  59.5 22.0 %copy-start.3 = (bf16[8,128,256]{2,1,0:T(8,128)(2,1)}, bf16[8,128,256]{2,1,0:T(8,128)(2,1)S(1)}, u32[]{:S(2)}) copy-start(bf16[8,128,256]{2,1,0:T(8,128)(2,1)S(1)} %get-tuple-element.14) | copy-start | bytes 1572868
  59.5 22.0 %copy-start.6 = (bf16[128,128]{1,0:T(8,128)(2,1)}, bf16[128,128]{1,0:T(8,128)(2,1)S(1)}, u32[]{:S(2)}) copy-start(bf16[128,128]{1,0:T(8,128)(2,1)S(1)} %get-tuple-element.10.q_ref) | copy-start | bytes 98308
  81.5 21.7 %all-to-all-start.3 = ((bf16[8,128,256]{2,1,0:T(8,128)(2,1)}), bf16[8,128,256]{2,1,0:T(8,128)(2,1)S(1)}, u32[]{:S(2)}, u32[]{:S(2)}) async-start(bf16[8,128,256]{2,1,0:T(8,128)(2,1)} %copy-done.3), calls=%async_computation.3 | async-start | bytes 1048576 | tf_op jit(solution)/shard_map/all_to_all | solution.py:27
  85.0 11.4 %collective-permute-start.1 = (bf16[1024,256]{1,0:T(8,128)(2,1)S(1)}, bf16[1024,256]{1,0:T(8,128)(2,1)}, u32[]{:S(2)}, u32[]{:S(2)}) collective-permute-start(bf16[1024,256]{1,0:T(8,128)(2,1)S(1)} %bitcast.21), channel_id=1, source_target_pairs={{0,2},{2,0},{1,3},{3,1},{4,6},{6,4},{5,7},{7,5},{8,10},{10,8},{9,1... | collective-permute-start | bytes 1572872 | tf_op jit(solution)/shard_map/ppermute | solution.py:35
  87.1 18.3 %collective-permute-start.2 = (bf16[1024,256]{1,0:T(8,128)(2,1)S(1)}, bf16[1024,256]{1,0:T(8,128)(2,1)}, u32[]{:S(2)}, u32[]{:S(2)}) collective-permute-start(bf16[1024,256]{1,0:T(8,128)(2,1)S(1)} %bitcast.22), channel_id=1, source_target_pairs={{0,1},{1,0},{2,3},{3,2},{4,5},{5,4},{6,7},{7,6},{8,9},{9,8},{10,11... | collective-permute-start | bytes 1572872 | tf_op jit(solution)/shard_map/ppermute | solution.py:35
  96.4 9.1 %collective-permute-start.3 = (bf16[1024,256]{1,0:T(8,128)(2,1)}, bf16[1024,256]{1,0:T(8,128)(2,1)}, u32[]{:S(2)}, u32[]{:S(2)}) collective-permute-start(bf16[1024,256]{1,0:T(8,128)(2,1)} %collective-permute-done.1.kv1), channel_id=1, source_target_pairs={{0,1},{1,0},{2,3},{3,2},{4,5},{5,4},{6,7},{7,6},{8,9},{9,8},{10,11... | collective-permute-start | bytes 1572872 | tf_op jit(solution)/shard_map/ppermute | solution.py:35
  103.2 16.0 %collective-permute-start.4 = (bf16[1024,256]{1,0:T(8,128)(2,1)S(1)}, bf16[1024,256]{1,0:T(8,128)(2,1)}, u32[]{:S(2)}, u32[]{:S(2)}) collective-permute-start(bf16[1024,256]{1,0:T(8,128)(2,1)S(1)} %bitcast.28), channel_id=1, source_target_pairs={{0,2},{2,0},{1,3},{3,1},{4,6},{6,4},{5,7},{7,5},{8,10},{10,8},{9,1... | collective-permute-start | bytes 1572872 | tf_op jit(solution)/shard_map/ppermute | solution.py:35
  105.4 0.8 copy-start.5
  106.2 0.8 copy-start.7
  110.5 0.6 copy-start.8
  111.1 0.6 copy-start.10
  111.7 15.0 %all-to-all-start.4 = ((f32[16,2,128]{2,1,0:T(2,128)}), f32[16,2,128]{2,1,0:T(2,128)S(1)}, u32[]{:S(2)}, u32[]{:S(2)}) async-start(f32[16,2,128]{2,1,0:T(2,128)} %copy-done.10), calls=%async_computation.4 | async-start | bytes 32768 | tf_op jit(solution)/shard_map/all_to_all | solution.py:27
  126.7 7.3 %copy-start.9 = (bf16[128,128]{1,0:T(8,128)(2,1)S(1)}, bf16[128,128]{1,0:T(8,128)(2,1)}, u32[]{:S(2)}) copy-start(bf16[128,128]{1,0:T(8,128)(2,1)} %copy-done.8) | copy-start | bytes 98308
  129.4 4.6 %collective-permute-start.5 = (f32[128,256]{1,0:T(8,128)S(1)}, f32[128,256]{1,0:T(8,128)S(1)}, u32[]{:S(2)}, u32[]{:S(2)}) collective-permute-start(f32[128,256]{1,0:T(8,128)S(1)} %get-tuple-element.17), channel_id=1, source_target_pairs={{0,1},{1,0},{2,3},{3,2},{4,5},{5,4},{6,7},{7,6},{8,9},{9,8},{10,11... | collective-permute-start | bytes 393224 | tf_op jit(solution)/shard_map/ppermute | solution.py:35
  145.0 6.0 %collective-permute-start.6 = (bf16[1024,384]{1,0:T(8,128)(2,1)S(1)}, bf16[1024,384]{1,0:T(8,128)(2,1)S(1)}, u32[]{:S(2)}, u32[]{:S(2)}) collective-permute-start(bf16[1024,384]{1,0:T(8,128)(2,1)S(1)} %weight_gradient.3), channel_id=1, source_target_pairs={{0,1},{1,0},{2,3},{3,2},{4,5},{5,4},{6,7},{7,6},{8,9},{9,8},{10,11... | collective-permute-start | bytes 2359304 | tf_op jit(solution)/shard_map/ppermute | solution.py:35
  195.5 6.7 %collective-permute-start.7 = (bf16[2,4,2,16,384]{4,3,2,0,1:T(8,128)(2,1)S(1)}, bf16[2,4,2,16,384]{4,3,2,0,1:T(8,128)(2,1)S(1)}, u32[]{:S(2)}, u32[]{:S(2)}) collective-permute-start(bf16[2,4,2,16,384]{4,3,2,0,1:T(8,128)(2,1)S(1)} %bitcast.34), channel_id=1, source_target_pairs={{0,1},{1,0},{2,3},{3,2},{4,5},{5,4},{6,7},{7,6},{8,9},{9,8},{10,11... | collective-permute-start | bytes 589832 | tf_op jit(solution)/shard_map/ppermute | solution.py:35

commit v11 on v10

--- a/solution.py
+++ b/solution.py
@@ -45,17 +45,17 @@
 
 
 def forward_kernel(
-    z_count, q_ref, kv0, kv1, kv2, kv3, cot_ref, attn_ref, stats_ref, dq_ref, held
+    z_count, rows_ref, kv0, kv1, kv2, kv3, attn_ref, stats_ref, dq_ref, held
 ):
     pieces = (kv0, kv1, kv2, kv3)
-    rows, head = q_ref.shape
+    rows, head = attn_ref.shape
     half_rows, ctx_count = rows // 2, 4 * z_count
     scale = 1.0 / math.sqrt(head)
     own = piece_device(0, lax.axis_index(z_axes))
     down = lax.broadcasted_iota(jnp.int32, (rows, rows), 0)
     across = lax.broadcasted_iota(jnp.int32, (rows, rows), 1)
     own_positions = positions(own, down, half_rows, ctx_count)
-    queries, cotangent = q_ref[...], cot_ref[...]
+    queries, cotangent = rows_ref[:, :head], rows_ref[:, head:]
     top = None
     for piece, kv in enumerate(pieces):
         raw = dot_f32(queries, kv[:, :head], 1, 1) * scale
@@ -137,19 +137,36 @@
     other_ref[:, :head], other_ref[:, head:] = grad_key[rows:], grad_value[rows:]
 
 
-def relayout_kernel(y_count, tokens_ref, out_ref):
-    members, _, columns = out_ref.shape
+def relayout_kernel(y_count, tokens_ref, out_ref, taken, placed, in_sems, out_sems):
+    members, rows, columns = out_ref.shape
     quarter = columns // (2 * y_count)
     core = lax.axis_index("core")
-    for member in range(members):
-        x_hi, z_lo = member // 2, member % 2
-        for half in range(2):
-            for y in range(y_count):
-                start = ((x_hi * y_count + y) * 4 + z_lo * 2 + (core ^ half)) * quarter
-                target = (half * y_count + y) * quarter
-                out_ref[member, :, target : target + quarter] = tokens_ref[
-                    :, pl.ds(pl.multiple_of(start, quarter), quarter)
-                ]
+    steps = in_sems.shape[0]
+    spans = [pl.ds(step * (rows // steps), rows // steps) for step in range(steps)]
+    reads = [
+        pltpu.make_async_copy(tokens_ref.at[span], taken.at[span], in_sems.at[step])
+        for step, span in enumerate(spans)
+    ]
+    writes = [
+        pltpu.make_async_copy(placed.at[:, span], out_ref.at[:, span], out_sems.at[step])
+        for step, span in enumerate(spans)
+    ]
+    for read in reads:
+        read.start()
+    for span, read, write in zip(spans, reads, writes):
+        read.wait()
+        for member in range(members):
+            x_hi, z_lo = member // 2, member % 2
+            for half in range(2):
+                for y in range(y_count):
+                    start = ((x_hi * y_count + y) * 4 + z_lo * 2 + (core ^ half)) * quarter
+                    target = (half * y_count + y) * quarter
+                    placed[member, span, target : target + quarter] = taken[
+                        span, pl.ds(pl.multiple_of(start, quarter), quarter)
+                    ]
+        write.start()
+    for write in writes:
+        write.wait()
 
 
 def near_kernel(x_ref, weight_ref, out_ref):
@@ -160,15 +177,15 @@
     out_ref[...] = (sum_ref[...] + dot_f32(x_ref[...], weight_ref[...], 1, 0)).astype(low)
 
 
-def split_kernel(parts_ref, cot_ref, q_ref, kv_copies, qc_copies):
-    head = q_ref.shape[1]
+def split_kernel(parts_ref, cot_ref, rows_ref, kv_copies, qc_copies):
+    head = cot_ref.shape[1]
     total = parts_ref[0].astype(jnp.float32)
     for part in range(1, parts_ref.shape[0]):
         total = total + parts_ref[part].astype(jnp.float32)
     qkv = total.astype(low)
     queries, pairs = qkv[:, :head], qkv[:, head:]
-    q_ref[...] = queries
     both = jnp.concatenate([queries, cot_ref[...]], axis=1)
+    rows_ref[...] = both
     for copy in range(kv_copies.shape[0]):
         kv_copies[copy] = pairs
         qc_copies[copy] = both
@@ -203,9 +220,15 @@
     far = swap(near, "core")
     split = pl.pallas_call(
         functools.partial(relayout_kernel, y_count),
-        in_specs=in_vmem(1),
-        out_specs=in_vmem(1)[0],
+        in_specs=[pl.BlockSpec(memory_space=pl.ANY)],
+        out_specs=pl.BlockSpec(memory_space=pl.ANY),
         out_shape=jax.ShapeDtypeStruct((4, row_count, 2 * depth), low),
+        scratch_shapes=[
+            pltpu.VMEM((row_count, model), low),
+            pltpu.VMEM((4, row_count, 2 * depth), low),
+            pltpu.SemaphoreType.DMA((4,)),
+            pltpu.SemaphoreType.DMA((4,)),
+        ],
         compiler_params=vmem,
         name="token_columns",
     )(tokens[0])
@@ -235,14 +258,14 @@
         name="far_projection",
     )(columns, far, near_sum)
     parts = exchange(parts.reshape(4, row_count, width), group_axes)
-    queries, pair_copies, query_copies = pl.pallas_call(
+    own_rows, pair_copies, query_copies = pl.pallas_call(
         split_kernel,
         in_specs=in_vmem(2),
         out_specs=in_vmem(3),
         out_shape=[
             jax.ShapeDtypeStruct(shape, low)
             for shape in (
-                (row_count, head),
+                (row_count, 2 * head),
                 (z_count, row_count, 2 * head),
                 (z_count, row_count, 2 * head),
             )
@@ -255,11 +278,10 @@
     by_x, by_core = swap(along_z, "xl"), swap(along_z, "core")
     pair_pieces = (along_z, by_x, by_core, swap(by_x, "core"))
     queries_z = exchange(query_copies, z_axes).reshape(-1, 2 * head)
-    query_pieces = (queries_z, swap(queries_z, "xl"))
 
     attn_rows, stats, grad_query = pl.pallas_call(
         functools.partial(forward_kernel, z_count),
-        in_specs=in_vmem(6),
+        in_specs=in_vmem(5),
         out_specs=in_vmem(3),
         out_shape=[
             jax.ShapeDtypeStruct((row_count, head), low),
@@ -269,7 +291,9 @@
         scratch_shapes=[pltpu.VMEM((4, row_count, z_count * row_count), jnp.float32)],
         compiler_params=vmem,
         name="attention_rows",
-    )(queries, *pair_pieces, cotangent)
+    )(own_rows, *pair_pieces)
+    queries_z, _ = lax.optimization_barrier((queries_z, stats))
+    query_pieces = (queries_z, swap(queries_z, "xl"))
     stats_all = exchange(stats, z_axes + ("xl",))
 
     own_part, other_part = pl.pallas_call(

time: 204 us -> 200 us (0.980)
  blocking collectives: 112 us -> 126 us
  waiting for transfers between devices: 14.9 us -> 6.17 us
  starting transfers between devices: 57.1 us -> 48.7 us
    all_to_all x5 -> x6, blocking collectives: 89 us -> 103 us  [exchange(): return lax.all_to_all(blocks, axes, split_axis=0, concat_axis=0, tiled=True)]
    all_to_all x3 -> x2, starting transfers between devices: 17.7 us -> 10.2 us  [exchange(): return lax.all_to_all(blocks, axes, split_axis=0, concat_axis=0, tiled=True)]
    all_to_all x3 -> x2, waiting for transfers between devices: 7.4 us -> 0.01 us  [exchange(): return lax.all_to_all(blocks, axes, split_axis=0, concat_axis=0, tiled=True)]
  transfers between devices with their start and end apart: 11 -> 10, of which waited for: 6 -> 5; matrix products, arithmetic and copies ran while one was open for 0% -> 0% of each run, Pallas kernels for 2% -> 2%
where the time goes in v11:
time: 200 us; the launch traced here: 199 us
  blocking collectives  126 us (63%)
  starting transfers between devices  48.7 us (24%)
  Pallas kernels  9.85 us (5%)
  local copies, waits for them, and re-layouts  7.12 us (4%)
  waiting for transfers between devices  6.17 us (3%)
    all_to_all x6, blocking collectives, exchange(): return lax.all_to_all(blocks, axes, split_axis=0, concat_axis=0, tiled=True)  103 us
    ppermute x8, starting transfers between devices, swap(): return lax.ppermute(block, axis, ((0, 1), (1, 0)))  38.5 us
    all_gather x1, blocking collectives, on_device(): near = lax.all_gather(own_weight, 'y', axis=0, tiled=True)  23.3 us
    all_to_all x2, starting transfers between devices, exchange(): return lax.all_to_all(blocks, axes, split_axis=0, concat_axis=0, tiled=True)  10.2 us
    unnamed x22, local copies, waits for them, and re-layouts  6.29 us
    ppermute x8, waiting for transfers between devices, swap(): return lax.ppermute(block, axis, ((0, 1), (1, 0)))  6.16 us
  transfers between devices with their start and end apart: 10, of which 5 were waited for; matrix products, arithmetic and copies ran while one was open for 0% of the time, Pallas kernels for 2%

profile of v11, /device:TPU:1, one launch (start us, length us, event | category | flops | bytes accessed | tf_op | source)
XLA Modules:
  0.0 199.4 jit_solution(17454248519298341707)
XLA Ops:
  0.6 0.0 copy-start
  0.6 0.0 copy-start.2
  0.7 1.6 copy-done.2
  2.3 0.9 token_columns.1
  3.2 0.0 copy-start.1
  3.2 1.3 copy-done.1
  4.6 6.7 %all-to-all-start = ((bf16[4,128,2048]{2,1,0:T(8,128)(2,1)}), bf16[4,128,2048]{2,1,0:T(8,128)(2,1)S(1)}, u32[]{:S(2)}, u32[]{:S(2)}) async-start(bf16[4,128,2048]{2,1,0:T(8,128)(2,1)} %copy-done.1), calls=%async_computation | async-start | bytes 4194304 | tf_op jit(solution)/shard_map/all_to_all | solution.py:27
  11.2 0.0 copy-done
  11.2 23.3 %all_gather.3.weight_ref = bf16[1024,384]{1,0:T(8,128)(2,1)S(1)} all-gather(bf16[128,384]{1,0:T(8,128)(2,1)S(1)} %constant_dynamic-slice_fusion), channel_id=1, replica_groups=mesh['xh'=2,'y'=8,'zh'=4,'zl'=2,'xl'=2,'core'=2] {'y'}, dimensions={0}, use_global_device_ids=true | all-gather | bytes 884736 | tf_op jit(solution)/shard_map/all_gather | solution.py:219
  34.6 8.7 %collective-permute-start = (bf16[1024,384]{1,0:T(8,128)(2,1)S(1)}, bf16[1024,384]{1,0:T(8,128)(2,1)}, u32[]{:S(2)}, u32[]{:S(2)}) collective-permute-start(bf16[1024,384]{1,0:T(8,128)(2,1)S(1)} %all_gather.3.weight_ref), channel_id=1, source_target_pairs={{0,1},{1,0},{2,3},{3,2},{4,5},{5,4},{6,7},{7,6},{8,9},{9,8},{10,11... | collective-permute-start | bytes 2359304 | tf_op jit(solution)/shard_map/ppermute | solution.py:35
  43.3 0.0 all-to-all-done
  43.3 0.7 near_projection.1.sum_ref
  44.0 0.0 copy-start.8
  44.0 1.3 collective-permute-done.weight_ref
  45.3 1.9 far_projection.1
  47.2 12.6 %all_to_all.40.parts_ref = bf16[4,128,384]{2,1,0:T(8,128)(2,1)S(1)} all-to-all(bf16[4,128,384]{2,1,0:T(8,128)(2,1)S(1)} %bitcast.30), channel_id=1, replica_groups=mesh['xh'=2,'y'=8,'zh'=4,'zl'=2,'xl'=2,'core'=2] {'xh','zl'}, dimensions={0} | all-to-all | bytes 786432 | tf_op jit(solution)/shard_map/all_to_all | solution.py:27
  59.8 0.0 copy-done.8
  59.8 0.1 projection_sum.1
  59.9 0.0 copy-start.6
  59.9 0.0 copy-start.5
  59.9 22.0 %all_to_all.41 = bf16[8,128,256]{2,1,0:T(8,128)(2,1)S(1)} all-to-all(bf16[8,128,256]{2,1,0:T(8,128)(2,1)S(1)} %get-tuple-element.12), channel_id=1, replica_groups=mesh['xh'=2,'y'=8,'zh'=4,'zl'=2,'xl'=2,'core'=2] {'zh','zl'}, dimensions={0} | all-to-all | bytes 1048576 | tf_op jit(solution)/shard_map/all_to_all | solution.py:27
  81.9 0.0 copy-done.6
  81.9 2.1 %collective-permute-start.1 = (bf16[1024,256]{1,0:T(8,128)(2,1)S(1)}, bf16[1024,256]{1,0:T(8,128)(2,1)}, u32[]{:S(2)}, u32[]{:S(2)}) collective-permute-start(bf16[1024,256]{1,0:T(8,128)(2,1)S(1)} %bitcast.21), channel_id=1, source_target_pairs={{0,2},{2,0},{1,3},{3,1},{4,6},{6,4},{5,7},{7,5},{8,10},{10,8},{9,1... | collective-permute-start | bytes 1572872 | tf_op jit(solution)/shard_map/ppermute | solution.py:35
  84.0 0.0 copy-done.5
  84.0 3.5 %all-to-all-start.3 = ((bf16[8,128,256]{2,1,0:T(8,128)(2,1)}), bf16[8,128,256]{2,1,0:T(8,128)(2,1)S(1)}, u32[]{:S(2)}, u32[]{:S(2)}) async-start(bf16[8,128,256]{2,1,0:T(8,128)(2,1)} %copy-done.5), calls=%async_computation.3 | async-start | bytes 1048576 | tf_op jit(solution)/shard_map/all_to_all | solution.py:27
  87.5 6.2 %collective-permute-start.2 = (bf16[1024,256]{1,0:T(8,128)(2,1)S(1)}, bf16[1024,256]{1,0:T(8,128)(2,1)S(1)}, u32[]{:S(2)}, u32[]{:S(2)}) collective-permute-start(bf16[1024,256]{1,0:T(8,128)(2,1)S(1)} %bitcast.22), channel_id=1, source_target_pairs={{0,1},{1,0},{2,3},{3,2},{4,5},{5,4},{6,7},{7,6},{8,9},{9,8},{10,11... | collective-permute-start | bytes 1572872 | tf_op jit(solution)/shard_map/ppermute | solution.py:35
  93.7 0.0 collective-permute-done.1.kv1
  93.8 6.3 %collective-permute-start.3 = (bf16[1024,256]{1,0:T(8,128)(2,1)}, bf16[1024,256]{1,0:T(8,128)(2,1)S(1)}, u32[]{:S(2)}, u32[]{:S(2)}) collective-permute-start(bf16[1024,256]{1,0:T(8,128)(2,1)} %collective-permute-done.1.kv1), channel_id=1, source_target_pairs={{0,1},{1,0},{2,3},{3,2},{4,5},{5,4},{6,7},{7,6},{8,9},{9,8},{10,11... | collective-permute-start | bytes 1572872 | tf_op jit(solution)/shard_map/ppermute | solution.py:35
  100.1 0.0 collective-permute-done.2.kv2.across_ref
  100.1 1.7 collective-permute-done.3.kv3
  101.8 0.0 copy-start.7
  101.8 0.8 copy-done.7
  102.7 3.2 %attention_rows.1 = (bf16[128,128]{1,0:T(8,128)(2,1)}, f32[16,2,128]{2,1,0:T(2,128)S(1)}, bf16[128,128]{1,0:T(8,128)(2,1)S(1)}) custom-call(bf16[128,256]{1,0:T(8,128)(2,1)S(1)} %copy-done.7, bf16[1024,256]{1,0:T(8,128)(2,1)S(1)} %bitcast.23, bf16[1024,256]{1,0:T(8,128)(2,1)} %collective-permute-done.1.kv1, ...), custom_call_target="tpu_custom_call" | custom-call | tf_op jit(solution)/shard_map/attention_rows/pallas_call | solution.py:282
  105.9 0.0 copy-start.3
  105.9 0.8 copy-done.3
  106.7 0.0 copy-start.9
  106.7 0.6 copy-done.9
  107.3 0.0 all-to-all-done.3
  107.3 0.0 copy-start.10
  107.3 2.3 %collective-permute-start.4 = (bf16[1024,256]{1,0:T(8,128)(2,1)S(1)}, bf16[1024,256]{1,0:T(8,128)(2,1)S(1)}, u32[]{:S(2)}, u32[]{:S(2)}) collective-permute-start(bf16[1024,256]{1,0:T(8,128)(2,1)S(1)} %bitcast.28), channel_id=1, source_target_pairs={{0,2},{2,0},{1,3},{3,1},{4,6},{6,4},{5,7},{7,5},{8,10},{10,8},{9,1... | collective-permute-start | bytes 1572872 | tf_op jit(solution)/shard_map/ppermute | solution.py:35
  109.6 13.0 %all_to_all.42.stats_ref = f32[16,2,128]{2,1,0:T(2,128)S(1)} all-to-all(f32[16,2,128]{2,1,0:T(2,128)S(1)} %get-tuple-element.16), channel_id=1, replica_groups=mesh['xh'=2,'y'=8,'zh'=4,'zl'=2,'xl'=2,'core'=2] {'zh','zl','xl'}, dimensions={0} | all-to-all | bytes 32768 | tf_op jit(solution)/shard_map/all_to_all | solution.py:27
  122.6 0.0 collective-permute-done.4.qc1
  122.6 0.0 copy-start.4
  122.6 1.0 copy-done.4
  123.7 1.5 attention_columns.1
  125.2 3.2 %collective-permute-start.5 = (f32[128,256]{1,0:T(8,128)S(1)}, f32[128,256]{1,0:T(8,128)S(1)}, u32[]{:S(2)}, u32[]{:S(2)}) collective-permute-start(f32[128,256]{1,0:T(8,128)S(1)} %get-tuple-element.19), channel_id=1, source_target_pairs={{0,1},{1,0},{2,3},{3,2},{4,5},{5,4},{6,7},{7,6},{8,9},{9,8},{10,11... | collective-permute-start | bytes 393224 | tf_op jit(solution)/shard_map/ppermute | solution.py:35
  128.3 1.0 collective-permute-done.5.other_ref
  129.3 0.0 copy-done.10
  129.3 10.1 %all_to_all.43 = bf16[4,128,384]{2,1,0:T(8,128)(2,1)S(1)} all-to-all(bf16[4,128,384]{2,1,0:T(8,128)(2,1)S(1)} %join_gradients.1), channel_id=1, replica_groups=mesh['xh'=2,'y'=8,'zh'=4,'zl'=2,'xl'=2,'core'=2] {'xh','zl'}, dimensions={0} | all-to-all | bytes 786432 | tf_op jit(solution)/shard_map/all_to_all | solution.py:27
  139.5 0.7 weight_gradient.3
  140.2 4.1 %collective-permute-start.6 = (bf16[1024,384]{1,0:T(8,128)(2,1)S(1)}, bf16[1024,384]{1,0:T(8,128)(2,1)S(1)}, u32[]{:S(2)}, u32[]{:S(2)}) collective-permute-start(bf16[1024,384]{1,0:T(8,128)(2,1)S(1)} %weight_gradient.3), channel_id=1, source_target_pairs={{0,1},{1,0},{2,3},{3,2},{4,5},{5,4},{6,7},{7,6},{8,9},{9,8},{10,11... | collective-permute-start | bytes 2359304 | tf_op jit(solution)/shard_map/ppermute | solution.py:35
  144.3 0.7 weight_gradient.2
  145.0 1.1 collective-permute-done.6
  146.2 0.2 add_convert_fusion
  146.3 31.5 %all_to_all.44 = bf16[64,16,384]{2,1,0:T(8,128)(2,1)S(1)} all-to-all(bf16[64,16,384]{2,1,0:T(8,128)(2,1)S(1)} %bitcast.32), channel_id=1, replica_groups=mesh['xh'=2,'y'=8,'zh'=4,'zl'=2,'xl'=2,'core'=2] {'y','zh','xl'}, dimensions={0} | all-to-all | bytes 1572864 | tf_op jit(solution)/shard_map/all_to_all | solution.py:27
  177.8 0.1 reduce_sum.12
  178.0 13.8 %all_to_all.45 = bf16[16,16,384]{2,1,0:T(8,128)(2,1)S(1)} all-to-all(bf16[16,16,384]{2,1,0:T(8,128)(2,1)S(1)} %broadcast_in_dim.10), channel_id=1, replica_groups=mesh['xh'=2,'y'=8,'zh'=4,'zl'=2,'xl'=2,'core'=2] {'zh','zl','xl'}, dimensions={0} | all-to-all | bytes 393216 | tf_op jit(solution)/shard_map/all_to_all | solution.py:27
  191.8 5.6 %collective-permute-start.7 = (bf16[2,4,2,16,384]{4,3,2,0,1:T(8,128)(2,1)S(1)}, bf16[2,4,2,16,384]{4,3,2,0,1:T(8,128)(2,1)S(1)}, u32[]{:S(2)}, u32[]{:S(2)}) collective-permute-start(bf16[2,4,2,16,384]{4,3,2,0,1:T(8,128)(2,1)S(1)} %bitcast.33), channel_id=1, source_target_pairs={{0,1},{1,0},{2,3},{3,2},{4,5},{5,4},{6,7},{7,6},{8,9},{9,8},{10,11... | collective-permute-start | bytes 589832 | tf_op jit(solution)/shard_map/ppermute | solution.py:35
  197.4 1.0 collective-permute-done.7
  198.6 0.8 copy.6
  (5 shorter events, 0.2 us)
Async XLA Ops:
  0.6 10.6 %copy-start = (bf16[512,384]{1,0:T(8,128)(2,1)S(1)}, bf16[512,384]{1,0:T(8,128)(2,1)}, u32[]{:S(2)}) copy-start(bf16[512,384]{1,0:T(8,128)(2,1)} %param.4) | copy-start | bytes 1179652
  0.6 1.6 copy-start.2
  3.2 1.3 copy-start.1
  4.6 38.7 %all-to-all-start = ((bf16[4,128,2048]{2,1,0:T(8,128)(2,1)}), bf16[4,128,2048]{2,1,0:T(8,128)(2,1)S(1)}, u32[]{:S(2)}, u32[]{:S(2)}) async-start(bf16[4,128,2048]{2,1,0:T(8,128)(2,1)} %copy-done.1), calls=%async_computation | async-start | bytes 4194304 | tf_op jit(solution)/shard_map/all_to_all | solution.py:27
  34.6 10.7 %collective-permute-start = (bf16[1024,384]{1,0:T(8,128)(2,1)S(1)}, bf16[1024,384]{1,0:T(8,128)(2,1)}, u32[]{:S(2)}, u32[]{:S(2)}) collective-permute-start(bf16[1024,384]{1,0:T(8,128)(2,1)S(1)} %all_gather.3.weight_ref), channel_id=1, source_target_pairs={{0,1},{1,0},{2,3},{3,2},{4,5},{5,4},{6,7},{7,6},{8,9},{9,8},{10,11... | collective-permute-start | bytes 2359304 | tf_op jit(solution)/shard_map/ppermute | solution.py:35
  44.0 15.8 %copy-start.8 = (bf16[1,128,128]{2,1,0:T(8,128)(2,1)S(1)}, bf16[1,128,128]{2,1,0:T(8,128)(2,1)}, u32[]{:S(2)}) copy-start(bf16[1,128,128]{2,1,0:T(8,128)(2,1)} %param.5) | copy-start | bytes 98308
  59.9 22.0 %copy-start.6 = (bf16[128,256]{1,0:T(8,128)(2,1)}, bf16[128,256]{1,0:T(8,128)(2,1)S(1)}, u32[]{:S(2)}) copy-start(bf16[128,256]{1,0:T(8,128)(2,1)S(1)} %get-tuple-element.11.rows_ref) | copy-start | bytes 196612
  59.9 24.1 %copy-start.5 = (bf16[8,128,256]{2,1,0:T(8,128)(2,1)}, bf16[8,128,256]{2,1,0:T(8,128)(2,1)S(1)}, u32[]{:S(2)}) copy-start(bf16[8,128,256]{2,1,0:T(8,128)(2,1)S(1)} %get-tuple-element.15) | copy-start | bytes 1572868
  81.9 11.9 %collective-permute-start.1 = (bf16[1024,256]{1,0:T(8,128)(2,1)S(1)}, bf16[1024,256]{1,0:T(8,128)(2,1)}, u32[]{:S(2)}, u32[]{:S(2)}) collective-permute-start(bf16[1024,256]{1,0:T(8,128)(2,1)S(1)} %bitcast.21), channel_id=1, source_target_pairs={{0,2},{2,0},{1,3},{3,1},{4,6},{6,4},{5,7},{7,5},{8,10},{10,8},{9,1... | collective-permute-start | bytes 1572872 | tf_op jit(solution)/shard_map/ppermute | solution.py:35
  84.0 23.3 %all-to-all-start.3 = ((bf16[8,128,256]{2,1,0:T(8,128)(2,1)}), bf16[8,128,256]{2,1,0:T(8,128)(2,1)S(1)}, u32[]{:S(2)}, u32[]{:S(2)}) async-start(bf16[8,128,256]{2,1,0:T(8,128)(2,1)} %copy-done.5), calls=%async_computation.3 | async-start | bytes 1048576 | tf_op jit(solution)/shard_map/all_to_all | solution.py:27
  87.5 12.6 %collective-permute-start.2 = (bf16[1024,256]{1,0:T(8,128)(2,1)S(1)}, bf16[1024,256]{1,0:T(8,128)(2,1)S(1)}, u32[]{:S(2)}, u32[]{:S(2)}) collective-permute-start(bf16[1024,256]{1,0:T(8,128)(2,1)S(1)} %bitcast.22), channel_id=1, source_target_pairs={{0,1},{1,0},{2,3},{3,2},{4,5},{5,4},{6,7},{7,6},{8,9},{9,8},{10,11... | collective-permute-start | bytes 1572872 | tf_op jit(solution)/shard_map/ppermute | solution.py:35
  93.8 8.1 %collective-permute-start.3 = (bf16[1024,256]{1,0:T(8,128)(2,1)}, bf16[1024,256]{1,0:T(8,128)(2,1)S(1)}, u32[]{:S(2)}, u32[]{:S(2)}) collective-permute-start(bf16[1024,256]{1,0:T(8,128)(2,1)} %collective-permute-done.1.kv1), channel_id=1, source_target_pairs={{0,1},{1,0},{2,3},{3,2},{4,5},{5,4},{6,7},{7,6},{8,9},{9,8},{10,11... | collective-permute-start | bytes 1572872 | tf_op jit(solution)/shard_map/ppermute | solution.py:35
  101.8 0.8 copy-start.7
  105.9 0.8 copy-start.3
  106.7 0.6 copy-start.9
  107.3 22.0 %copy-start.10 = (bf16[128,128]{1,0:T(8,128)(2,1)S(1)}, bf16[128,128]{1,0:T(8,128)(2,1)}, u32[]{:S(2)}) copy-start(bf16[128,128]{1,0:T(8,128)(2,1)} %copy-done.9) | copy-start | bytes 98308
  107.3 15.3 %collective-permute-start.4 = (bf16[1024,256]{1,0:T(8,128)(2,1)S(1)}, bf16[1024,256]{1,0:T(8,128)(2,1)S(1)}, u32[]{:S(2)}, u32[]{:S(2)}) collective-permute-start(bf16[1024,256]{1,0:T(8,128)(2,1)S(1)} %bitcast.28), channel_id=1, source_target_pairs={{0,2},{2,0},{1,3},{3,1},{4,6},{6,4},{5,7},{7,5},{8,10},{10,8},{9,1... | collective-permute-start | bytes 1572872 | tf_op jit(solution)/shard_map/ppermute | solution.py:35
  122.6 1.0 copy-start.4
  125.2 4.1 %collective-permute-start.5 = (f32[128,256]{1,0:T(8,128)S(1)}, f32[128,256]{1,0:T(8,128)S(1)}, u32[]{:S(2)}, u32[]{:S(2)}) collective-permute-start(f32[128,256]{1,0:T(8,128)S(1)} %get-tuple-element.19), channel_id=1, source_target_pairs={{0,1},{1,0},{2,3},{3,2},{4,5},{5,4},{6,7},{7,6},{8,9},{9,8},{10,11... | collective-permute-start | bytes 393224 | tf_op jit(solution)/shard_map/ppermute | solution.py:35
  140.2 6.0 %collective-permute-start.6 = (bf16[1024,384]{1,0:T(8,128)(2,1)S(1)}, bf16[1024,384]{1,0:T(8,128)(2,1)S(1)}, u32[]{:S(2)}, u32[]{:S(2)}) collective-permute-start(bf16[1024,384]{1,0:T(8,128)(2,1)S(1)} %weight_gradient.3), channel_id=1, source_target_pairs={{0,1},{1,0},{2,3},{3,2},{4,5},{5,4},{6,7},{7,6},{8,9},{9,8},{10,11... | collective-permute-start | bytes 2359304 | tf_op jit(solution)/shard_map/ppermute | solution.py:35
  191.8 6.7 %collective-permute-start.7 = (bf16[2,4,2,16,384]{4,3,2,0,1:T(8,128)(2,1)S(1)}, bf16[2,4,2,16,384]{4,3,2,0,1:T(8,128)(2,1)S(1)}, u32[]{:S(2)}, u32[]{:S(2)}) collective-permute-start(bf16[2,4,2,16,384]{4,3,2,0,1:T(8,128)(2,1)S(1)} %bitcast.33), channel_id=1, source_target_pairs={{0,1},{1,0},{2,3},{3,2},{4,5},{5,4},{6,7},{7,6},{8,9},{9,8},{10,11... | collective-permute-start | bytes 589832 | tf_op jit(solution)/shard_map/ppermute | solution.py:35

commit v12 on v11

--- a/solution.py
+++ b/solution.py
@@ -45,7 +45,7 @@
 
 
 def forward_kernel(
-    z_count, rows_ref, kv0, kv1, kv2, kv3, attn_ref, stats_ref, dq_ref, held
+    z_count, rows_ref, kv0, kv1, kv2, kv3, attn_ref, stats_ref, dq_ref, pairs_ref, held
 ):
     pieces = (kv0, kv1, kv2, kv3)
     rows, head = attn_ref.shape
@@ -55,6 +55,8 @@
     down = lax.broadcasted_iota(jnp.int32, (rows, rows), 0)
     across = lax.broadcasted_iota(jnp.int32, (rows, rows), 1)
     own_positions = positions(own, down, half_rows, ctx_count)
+    place = pl.ds(pl.multiple_of(lax.axis_index(z_axes) * rows, rows), rows)
+    pairs_ref[:rows, :], pairs_ref[rows:, :] = kv0[place, :], kv2[place, :]
     queries, cotangent = rows_ref[:, :head], rows_ref[:, head:]
     top = None
     for piece, kv in enumerate(pieces):
@@ -96,8 +98,8 @@
     dq_ref[...] = (grad * scale).astype(low)
 
 
-def backward_kernel(z_count, along_ref, across_ref, qc0, qc1, stats_ref, own_ref, other_ref):
-    rows, head = along_ref.shape[0] // z_count, along_ref.shape[1] // 2
+def backward_kernel(z_count, pairs_ref, qc0, qc1, stats_ref, own_ref, other_ref):
+    rows, head = pairs_ref.shape[0] // 2, pairs_ref.shape[1] // 2
     half_rows, ctx_count = rows // 2, 4 * z_count
     scale = 1.0 / math.sqrt(head)
     z_own = lax.axis_index(z_axes)
@@ -110,9 +112,7 @@
         ],
         axis=0,
     )
-    place = pl.ds(pl.multiple_of(z_own * rows, rows), rows)
-    pairs = jnp.concatenate([along_ref[place, :], across_ref[place, :]], axis=0)
-    keys, values = pairs[:, :head], pairs[:, head:]
+    keys, values = pairs_ref[:, :head], pairs_ref[:, head:]
     grad_key = jnp.zeros((2 * rows, head), jnp.float32)
     grad_value = jnp.zeros((2 * rows, head), jnp.float32)
     for piece, both in enumerate((qc0, qc1)):
@@ -137,23 +137,19 @@
     other_ref[:, :head], other_ref[:, head:] = grad_key[rows:], grad_value[rows:]
 
 
-def relayout_kernel(y_count, tokens_ref, out_ref, taken, placed, in_sems, out_sems):
+def relayout_kernel(y_count, tokens_ref, out_ref, taken, sems):
     members, rows, columns = out_ref.shape
     quarter = columns // (2 * y_count)
     core = lax.axis_index("core")
-    steps = in_sems.shape[0]
+    steps = sems.shape[0]
     spans = [pl.ds(step * (rows // steps), rows // steps) for step in range(steps)]
     reads = [
-        pltpu.make_async_copy(tokens_ref.at[span], taken.at[span], in_sems.at[step])
-        for step, span in enumerate(spans)
-    ]
-    writes = [
-        pltpu.make_async_copy(placed.at[:, span], out_ref.at[:, span], out_sems.at[step])
+        pltpu.make_async_copy(tokens_ref.at[span], taken.at[span], sems.at[step])
         for step, span in enumerate(spans)
     ]
     for read in reads:
         read.start()
-    for span, read, write in zip(spans, reads, writes):
+    for span, read in zip(spans, reads):
         read.wait()
         for member in range(members):
             x_hi, z_lo = member // 2, member % 2
@@ -161,12 +157,9 @@
                 for y in range(y_count):
                     start = ((x_hi * y_count + y) * 4 + z_lo * 2 + (core ^ half)) * quarter
                     target = (half * y_count + y) * quarter
-                    placed[member, span, target : target + quarter] = taken[
+                    out_ref[member, span, target : target + quarter] = taken[
                         span, pl.ds(pl.multiple_of(start, quarter), quarter)
                     ]
-        write.start()
-    for write in writes:
-        write.wait()
 
 
 def near_kernel(x_ref, weight_ref, out_ref):
@@ -220,18 +213,16 @@
     far = swap(near, "core")
     split = pl.pallas_call(
         functools.partial(relayout_kernel, y_count),
-        in_specs=[pl.BlockSpec(memory_space=pl.ANY)],
-        out_specs=pl.BlockSpec(memory_space=pl.ANY),
+        in_specs=[pl.BlockSpec(memory_space=pltpu.HBM)],
+        out_specs=in_vmem(1)[0],
         out_shape=jax.ShapeDtypeStruct((4, row_count, 2 * depth), low),
         scratch_shapes=[
             pltpu.VMEM((row_count, model), low),
-            pltpu.VMEM((4, row_count, 2 * depth), low),
-            pltpu.SemaphoreType.DMA((4,)),
             pltpu.SemaphoreType.DMA((4,)),
         ],
         compiler_params=vmem,
         name="token_columns",
-    )(tokens[0])
+    )(pltpu.with_memory_space_constraint(tokens[0], pltpu.HBM))
     columns = exchange(split, group_axes).reshape(group_rows, 2 * depth)
     whole = pl.BlockSpec((depth, width), lambda i: (0, 0))
     summed_rows = pl.BlockSpec((group_rows, width), lambda i: (0, 0))
@@ -279,14 +270,15 @@
     pair_pieces = (along_z, by_x, by_core, swap(by_x, "core"))
     queries_z = exchange(query_copies, z_axes).reshape(-1, 2 * head)
 
-    attn_rows, stats, grad_query = pl.pallas_call(
+    attn_rows, stats, grad_query, both_pairs = pl.pallas_call(
         functools.partial(forward_kernel, z_count),
         in_specs=in_vmem(5),
-        out_specs=in_vmem(3),
+        out_specs=in_vmem(4),
         out_shape=[
             jax.ShapeDtypeStruct((row_count, head), low),
             jax.ShapeDtypeStruct((2 * z_count, 2, row_count), jnp.float32),
             jax.ShapeDtypeStruct((row_count, head), low),
+            jax.ShapeDtypeStruct((2 * row_count, 2 * head), low),
         ],
         scratch_shapes=[pltpu.VMEM((4, row_count, z_count * row_count), jnp.float32)],
         compiler_params=vmem,
@@ -298,12 +290,12 @@
 
     own_part, other_part = pl.pallas_call(
         functools.partial(backward_kernel, z_count),
-        in_specs=in_vmem(5),
+        in_specs=in_vmem(4),
         out_specs=in_vmem(2),
         out_shape=[jax.ShapeDtypeStruct((row_count, 2 * head), jnp.float32)] * 2,
         compiler_params=vmem,
         name="attention_columns",
-    )(pair_pieces[0], pair_pieces[2], *query_pieces, stats_all)
+    )(both_pairs, *query_pieces, stats_all)
     grad_copies = pl.pallas_call(
         join_kernel,
         in_specs=in_vmem(3),

time: 200 us -> 200 us (level)
    unnamed x22 -> x20, local copies, waits for them, and re-layouts: 6.29 us -> 5.1 us
where the time goes in v12:
time: 200 us; the launch traced here: 199 us
  blocking collectives  126 us (63%)
  starting transfers between devices  48.5 us (24%)
  Pallas kernels  10.6 us (5%)
  waiting for transfers between devices  6.17 us (3%)
  local copies, waits for them, and re-layouts  5.92 us (3%)
    all_to_all x6, blocking collectives, exchange(): return lax.all_to_all(blocks, axes, split_axis=0, concat_axis=0, tiled=True)  103 us
    ppermute x8, starting transfers between devices, swap(): return lax.ppermute(block, axis, ((0, 1), (1, 0)))  38.4 us
    all_gather x1, blocking collectives, on_device(): near = lax.all_gather(own_weight, 'y', axis=0, tiled=True)  23.3 us
    all_to_all x2, starting transfers between devices, exchange(): return lax.all_to_all(blocks, axes, split_axis=0, concat_axis=0, tiled=True)  10.2 us
    ppermute x8, waiting for transfers between devices, swap(): return lax.ppermute(block, axis, ((0, 1), (1, 0)))  6.16 us
    unnamed x20, local copies, waits for them, and re-layouts  5.1 us
  transfers between devices with their start and end apart: 10, of which 5 were waited for; matrix products, arithmetic and copies ran while one was open for 0% of the time, Pallas kernels for 2%

profile of v12, /device:TPU:1, one launch (start us, length us, event | category | flops | bytes accessed | tf_op | source)
XLA Modules:
  0.0 198.8 jit_solution(3881241686600199415)
XLA Ops:
  0.6 0.0 copy-start
  0.6 1.7 token_columns.1
  2.4 0.0 copy-start.1
  2.4 1.3 copy-done.1
  3.7 6.7 %all-to-all-start = ((bf16[4,128,2048]{2,1,0:T(8,128)(2,1)}), bf16[4,128,2048]{2,1,0:T(8,128)(2,1)S(1)}, u32[]{:S(2)}, u32[]{:S(2)}) async-start(bf16[4,128,2048]{2,1,0:T(8,128)(2,1)} %copy-done.1), calls=%async_computation | async-start | bytes 4194304 | tf_op jit(solution)/shard_map/all_to_all | solution.py:27
  10.4 0.0 copy-done
  10.4 23.3 %all_gather.3.weight_ref = bf16[1024,384]{1,0:T(8,128)(2,1)S(1)} all-gather(bf16[128,384]{1,0:T(8,128)(2,1)S(1)} %constant_dynamic-slice_fusion), channel_id=1, replica_groups=mesh['xh'=2,'y'=8,'zh'=4,'zl'=2,'xl'=2,'core'=2] {'y'}, dimensions={0}, use_global_device_ids=true | all-gather | bytes 884736 | tf_op jit(solution)/shard_map/all_gather | solution.py:212
  33.7 8.7 %collective-permute-start = (bf16[1024,384]{1,0:T(8,128)(2,1)S(1)}, bf16[1024,384]{1,0:T(8,128)(2,1)}, u32[]{:S(2)}, u32[]{:S(2)}) collective-permute-start(bf16[1024,384]{1,0:T(8,128)(2,1)S(1)} %all_gather.3.weight_ref), channel_id=1, source_target_pairs={{0,1},{1,0},{2,3},{3,2},{4,5},{5,4},{6,7},{7,6},{8,9},{9,8},{10,11... | collective-permute-start | bytes 2359304 | tf_op jit(solution)/shard_map/ppermute | solution.py:35
  42.4 0.0 all-to-all-done
  42.4 0.7 near_projection.1.sum_ref
  43.1 0.0 copy-start.7
  43.1 1.3 collective-permute-done.weight_ref
  44.4 1.9 far_projection.1
  46.3 12.6 %all_to_all.40.parts_ref = bf16[4,128,384]{2,1,0:T(8,128)(2,1)S(1)} all-to-all(bf16[4,128,384]{2,1,0:T(8,128)(2,1)S(1)} %bitcast.28), channel_id=1, replica_groups=mesh['xh'=2,'y'=8,'zh'=4,'zl'=2,'xl'=2,'core'=2] {'xh','zl'}, dimensions={0} | all-to-all | bytes 786432 | tf_op jit(solution)/shard_map/all_to_all | solution.py:27
  58.9 0.0 copy-done.7
  58.9 0.1 projection_sum.1
  59.0 0.0 copy-start.5
  59.0 0.0 copy-start.2
  59.1 22.0 %all_to_all.41 = bf16[8,128,256]{2,1,0:T(8,128)(2,1)S(1)} all-to-all(bf16[8,128,256]{2,1,0:T(8,128)(2,1)S(1)} %get-tuple-element.13), channel_id=1, replica_groups=mesh['xh'=2,'y'=8,'zh'=4,'zl'=2,'xl'=2,'core'=2] {'zh','zl'}, dimensions={0} | all-to-all | bytes 1048576 | tf_op jit(solution)/shard_map/all_to_all | solution.py:27
  81.0 0.0 copy-done.5
  81.0 2.1 %collective-permute-start.1 = (bf16[1024,256]{1,0:T(8,128)(2,1)S(1)}, bf16[1024,256]{1,0:T(8,128)(2,1)}, u32[]{:S(2)}, u32[]{:S(2)}) collective-permute-start(bf16[1024,256]{1,0:T(8,128)(2,1)S(1)} %bitcast.25), channel_id=1, source_target_pairs={{0,2},{2,0},{1,3},{3,1},{4,6},{6,4},{5,7},{7,5},{8,10},{10,8},{9,1... | collective-permute-start | bytes 1572872 | tf_op jit(solution)/shard_map/ppermute | solution.py:35
  83.2 0.0 copy-done.2
  83.2 3.5 %all-to-all-start.3 = ((bf16[8,128,256]{2,1,0:T(8,128)(2,1)}), bf16[8,128,256]{2,1,0:T(8,128)(2,1)S(1)}, u32[]{:S(2)}, u32[]{:S(2)}) async-start(bf16[8,128,256]{2,1,0:T(8,128)(2,1)} %copy-done.2), calls=%async_computation.3 | async-start | bytes 1048576 | tf_op jit(solution)/shard_map/all_to_all | solution.py:27
  86.7 6.2 %collective-permute-start.2 = (bf16[1024,256]{1,0:T(8,128)(2,1)S(1)}, bf16[1024,256]{1,0:T(8,128)(2,1)S(1)}, u32[]{:S(2)}, u32[]{:S(2)}) collective-permute-start(bf16[1024,256]{1,0:T(8,128)(2,1)S(1)} %bitcast.26), channel_id=1, source_target_pairs={{0,1},{1,0},{2,3},{3,2},{4,5},{5,4},{6,7},{7,6},{8,9},{9,8},{10,11... | collective-permute-start | bytes 1572872 | tf_op jit(solution)/shard_map/ppermute | solution.py:35
  92.9 0.0 collective-permute-done.1.kv1
  92.9 6.3 %collective-permute-start.3 = (bf16[1024,256]{1,0:T(8,128)(2,1)}, bf16[1024,256]{1,0:T(8,128)(2,1)S(1)}, u32[]{:S(2)}, u32[]{:S(2)}) collective-permute-start(bf16[1024,256]{1,0:T(8,128)(2,1)} %collective-permute-done.1.kv1), channel_id=1, source_target_pairs={{0,1},{1,0},{2,3},{3,2},{4,5},{5,4},{6,7},{7,6},{8,9},{9,8},{10,11... | collective-permute-start | bytes 1572872 | tf_op jit(solution)/shard_map/ppermute | solution.py:35
  99.3 0.0 collective-permute-done.2.kv2
  99.3 1.7 collective-permute-done.3.kv3
  101.0 0.0 copy-start.6
  101.0 0.8 copy-done.6
  101.8 3.2 %attention_rows.1 = (bf16[128,128]{1,0:T(8,128)(2,1)}, f32[16,2,128]{2,1,0:T(2,128)S(1)}, bf16[128,128]{1,0:T(8,128)(2,1)S(1)}, bf16[256,256]{1,0:T(8,128)(2,1)S(1)}) custom-call(bf16[128,256]{1,0:T(8,128)(2,1)S(1)} %copy-done.6, bf16[1024,256]{1,0:T(8,128)(2,1)S(1)} %bitcast.27, bf16[1024,256]{1,0:T(8,128)(2,1)} %collective-permute-done.1.kv1, ...), custom_call_target="tpu_custom_call" | custom-call | tf_op jit(solution)/shard_map/attention_rows/pallas_call | solution.py:273
  105.0 0.0 copy-start.3
  105.0 0.6 copy-done.3
  105.7 0.0 copy-start.8
  105.7 0.6 copy-done.8
  106.3 0.0 all-to-all-done.3
  106.3 2.1 %collective-permute-start.4 = (bf16[1024,256]{1,0:T(8,128)(2,1)S(1)}, bf16[1024,256]{1,0:T(8,128)(2,1)S(1)}, u32[]{:S(2)}, u32[]{:S(2)}) collective-permute-start(bf16[1024,256]{1,0:T(8,128)(2,1)S(1)} %bitcast.23), channel_id=1, source_target_pairs={{0,2},{2,0},{1,3},{3,1},{4,6},{6,4},{5,7},{7,5},{8,10},{10,8},{9,1... | collective-permute-start | bytes 1572872 | tf_op jit(solution)/shard_map/ppermute | solution.py:35
  108.4 13.0 %all_to_all.42.stats_ref = f32[16,2,128]{2,1,0:T(2,128)S(1)} all-to-all(f32[16,2,128]{2,1,0:T(2,128)S(1)} %get-tuple-element.18), channel_id=1, replica_groups=mesh['xh'=2,'y'=8,'zh'=4,'zl'=2,'xl'=2,'core'=2] {'zh','zl','xl'}, dimensions={0} | all-to-all | bytes 32768 | tf_op jit(solution)/shard_map/all_to_all | solution.py:27
  121.5 0.0 collective-permute-done.4.qc1
  121.5 0.0 copy-start.4
  121.5 0.9 copy-done.4
  122.4 1.5 attention_columns.1
  123.9 3.2 %collective-permute-start.5 = (f32[128,256]{1,0:T(8,128)S(1)}, f32[128,256]{1,0:T(8,128)S(1)}, u32[]{:S(2)}, u32[]{:S(2)}) collective-permute-start(f32[128,256]{1,0:T(8,128)S(1)} %get-tuple-element.21), channel_id=1, source_target_pairs={{0,1},{1,0},{2,3},{3,2},{4,5},{5,4},{6,7},{7,6},{8,9},{9,8},{10,11... | collective-permute-start | bytes 393224 | tf_op jit(solution)/shard_map/ppermute | solution.py:35
  127.0 1.0 collective-permute-done.5.other_ref
  128.0 0.0 copy-start.9
  128.0 0.8 copy-done.9
  128.8 10.1 %all_to_all.43 = bf16[4,128,384]{2,1,0:T(8,128)(2,1)S(1)} all-to-all(bf16[4,128,384]{2,1,0:T(8,128)(2,1)S(1)} %join_gradients.1), channel_id=1, replica_groups=mesh['xh'=2,'y'=8,'zh'=4,'zl'=2,'xl'=2,'core'=2] {'xh','zl'}, dimensions={0} | all-to-all | bytes 786432 | tf_op jit(solution)/shard_map/all_to_all | solution.py:27
  138.9 0.7 weight_gradient.3
  139.6 4.1 %collective-permute-start.6 = (bf16[1024,384]{1,0:T(8,128)(2,1)S(1)}, bf16[1024,384]{1,0:T(8,128)(2,1)S(1)}, u32[]{:S(2)}, u32[]{:S(2)}) collective-permute-start(bf16[1024,384]{1,0:T(8,128)(2,1)S(1)} %weight_gradient.3), channel_id=1, source_target_pairs={{0,1},{1,0},{2,3},{3,2},{4,5},{5,4},{6,7},{7,6},{8,9},{9,8},{10,11... | collective-permute-start | bytes 2359304 | tf_op jit(solution)/shard_map/ppermute | solution.py:35
  143.7 0.7 weight_gradient.2
  144.5 1.1 collective-permute-done.6
  145.6 0.2 add_convert_fusion
  145.8 31.5 %all_to_all.44 = bf16[64,16,384]{2,1,0:T(8,128)(2,1)S(1)} all-to-all(bf16[64,16,384]{2,1,0:T(8,128)(2,1)S(1)} %bitcast.30), channel_id=1, replica_groups=mesh['xh'=2,'y'=8,'zh'=4,'zl'=2,'xl'=2,'core'=2] {'y','zh','xl'}, dimensions={0} | all-to-all | bytes 1572864 | tf_op jit(solution)/shard_map/all_to_all | solution.py:27
  177.3 0.1 reduce_sum.12
  177.4 13.8 %all_to_all.45 = bf16[16,16,384]{2,1,0:T(8,128)(2,1)S(1)} all-to-all(bf16[16,16,384]{2,1,0:T(8,128)(2,1)S(1)} %broadcast_in_dim.10), channel_id=1, replica_groups=mesh['xh'=2,'y'=8,'zh'=4,'zl'=2,'xl'=2,'core'=2] {'zh','zl','xl'}, dimensions={0} | all-to-all | bytes 393216 | tf_op jit(solution)/shard_map/all_to_all | solution.py:27
  191.2 5.6 %collective-permute-start.7 = (bf16[2,4,2,16,384]{4,3,2,0,1:T(8,128)(2,1)S(1)}, bf16[2,4,2,16,384]{4,3,2,0,1:T(8,128)(2,1)S(1)}, u32[]{:S(2)}, u32[]{:S(2)}) collective-permute-start(bf16[2,4,2,16,384]{4,3,2,0,1:T(8,128)(2,1)S(1)} %bitcast.32), channel_id=1, source_target_pairs={{0,1},{1,0},{2,3},{3,2},{4,5},{5,4},{6,7},{7,6},{8,9},{9,8},{10,11... | collective-permute-start | bytes 589832 | tf_op jit(solution)/shard_map/ppermute | solution.py:35
  196.9 1.0 collective-permute-done.7
  198.0 0.8 copy.6
  (5 shorter events, 0.2 us)
Async XLA Ops:
  0.6 9.7 %copy-start = (bf16[512,384]{1,0:T(8,128)(2,1)S(1)}, bf16[512,384]{1,0:T(8,128)(2,1)}, u32[]{:S(2)}) copy-start(bf16[512,384]{1,0:T(8,128)(2,1)} %param.4) | copy-start | bytes 1179652
  2.4 1.3 copy-start.1
  3.7 38.7 %all-to-all-start = ((bf16[4,128,2048]{2,1,0:T(8,128)(2,1)}), bf16[4,128,2048]{2,1,0:T(8,128)(2,1)S(1)}, u32[]{:S(2)}, u32[]{:S(2)}) async-start(bf16[4,128,2048]{2,1,0:T(8,128)(2,1)} %copy-done.1), calls=%async_computation | async-start | bytes 4194304 | tf_op jit(solution)/shard_map/all_to_all | solution.py:27
  33.7 10.7 %collective-permute-start = (bf16[1024,384]{1,0:T(8,128)(2,1)S(1)}, bf16[1024,384]{1,0:T(8,128)(2,1)}, u32[]{:S(2)}, u32[]{:S(2)}) collective-permute-start(bf16[1024,384]{1,0:T(8,128)(2,1)S(1)} %all_gather.3.weight_ref), channel_id=1, source_target_pairs={{0,1},{1,0},{2,3},{3,2},{4,5},{5,4},{6,7},{7,6},{8,9},{9,8},{10,11... | collective-permute-start | bytes 2359304 | tf_op jit(solution)/shard_map/ppermute | solution.py:35
  43.1 15.8 %copy-start.7 = (bf16[1,128,128]{2,1,0:T(8,128)(2,1)S(1)}, bf16[1,128,128]{2,1,0:T(8,128)(2,1)}, u32[]{:S(2)}) copy-start(bf16[1,128,128]{2,1,0:T(8,128)(2,1)} %param.5) | copy-start | bytes 98308
  59.0 22.0 %copy-start.5 = (bf16[128,256]{1,0:T(8,128)(2,1)}, bf16[128,256]{1,0:T(8,128)(2,1)S(1)}, u32[]{:S(2)}) copy-start(bf16[128,256]{1,0:T(8,128)(2,1)S(1)} %get-tuple-element.12.rows_ref) | copy-start | bytes 196612
  59.0 24.1 %copy-start.2 = (bf16[8,128,256]{2,1,0:T(8,128)(2,1)}, bf16[8,128,256]{2,1,0:T(8,128)(2,1)S(1)}, u32[]{:S(2)}) copy-start(bf16[8,128,256]{2,1,0:T(8,128)(2,1)S(1)} %get-tuple-element.17) | copy-start | bytes 1572868
  81.0 11.9 %collective-permute-start.1 = (bf16[1024,256]{1,0:T(8,128)(2,1)S(1)}, bf16[1024,256]{1,0:T(8,128)(2,1)}, u32[]{:S(2)}, u32[]{:S(2)}) collective-permute-start(bf16[1024,256]{1,0:T(8,128)(2,1)S(1)} %bitcast.25), channel_id=1, source_target_pairs={{0,2},{2,0},{1,3},{3,1},{4,6},{6,4},{5,7},{7,5},{8,10},{10,8},{9,1... | collective-permute-start | bytes 1572872 | tf_op jit(solution)/shard_map/ppermute | solution.py:35
  83.2 23.1 %all-to-all-start.3 = ((bf16[8,128,256]{2,1,0:T(8,128)(2,1)}), bf16[8,128,256]{2,1,0:T(8,128)(2,1)S(1)}, u32[]{:S(2)}, u32[]{:S(2)}) async-start(bf16[8,128,256]{2,1,0:T(8,128)(2,1)} %copy-done.2), calls=%async_computation.3 | async-start | bytes 1048576 | tf_op jit(solution)/shard_map/all_to_all | solution.py:27
  86.7 12.6 %collective-permute-start.2 = (bf16[1024,256]{1,0:T(8,128)(2,1)S(1)}, bf16[1024,256]{1,0:T(8,128)(2,1)S(1)}, u32[]{:S(2)}, u32[]{:S(2)}) collective-permute-start(bf16[1024,256]{1,0:T(8,128)(2,1)S(1)} %bitcast.26), channel_id=1, source_target_pairs={{0,1},{1,0},{2,3},{3,2},{4,5},{5,4},{6,7},{7,6},{8,9},{9,8},{10,11... | collective-permute-start | bytes 1572872 | tf_op jit(solution)/shard_map/ppermute | solution.py:35
  92.9 8.1 %collective-permute-start.3 = (bf16[1024,256]{1,0:T(8,128)(2,1)}, bf16[1024,256]{1,0:T(8,128)(2,1)S(1)}, u32[]{:S(2)}, u32[]{:S(2)}) collective-permute-start(bf16[1024,256]{1,0:T(8,128)(2,1)} %collective-permute-done.1.kv1), channel_id=1, source_target_pairs={{0,1},{1,0},{2,3},{3,2},{4,5},{5,4},{6,7},{7,6},{8,9},{9,8},{10,11... | collective-permute-start | bytes 1572872 | tf_op jit(solution)/shard_map/ppermute | solution.py:35
  101.0 0.8 copy-start.6
  105.0 0.7 copy-start.3
  105.7 0.6 copy-start.8
  106.3 15.2 %collective-permute-start.4 = (bf16[1024,256]{1,0:T(8,128)(2,1)S(1)}, bf16[1024,256]{1,0:T(8,128)(2,1)S(1)}, u32[]{:S(2)}, u32[]{:S(2)}) collective-permute-start(bf16[1024,256]{1,0:T(8,128)(2,1)S(1)} %bitcast.23), channel_id=1, source_target_pairs={{0,2},{2,0},{1,3},{3,1},{4,6},{6,4},{5,7},{7,5},{8,10},{10,8},{9,1... | collective-permute-start | bytes 1572872 | tf_op jit(solution)/shard_map/ppermute | solution.py:35
  121.5 0.9 copy-start.4
  123.9 4.1 %collective-permute-start.5 = (f32[128,256]{1,0:T(8,128)S(1)}, f32[128,256]{1,0:T(8,128)S(1)}, u32[]{:S(2)}, u32[]{:S(2)}) collective-permute-start(f32[128,256]{1,0:T(8,128)S(1)} %get-tuple-element.21), channel_id=1, source_target_pairs={{0,1},{1,0},{2,3},{3,2},{4,5},{5,4},{6,7},{7,6},{8,9},{9,8},{10,11... | collective-permute-start | bytes 393224 | tf_op jit(solution)/shard_map/ppermute | solution.py:35
  128.0 0.8 copy-start.9
  139.6 6.0 %collective-permute-start.6 = (bf16[1024,384]{1,0:T(8,128)(2,1)S(1)}, bf16[1024,384]{1,0:T(8,128)(2,1)S(1)}, u32[]{:S(2)}, u32[]{:S(2)}) collective-permute-start(bf16[1024,384]{1,0:T(8,128)(2,1)S(1)} %weight_gradient.3), channel_id=1, source_target_pairs={{0,1},{1,0},{2,3},{3,2},{4,5},{5,4},{6,7},{7,6},{8,9},{9,8},{10,11... | collective-permute-start | bytes 2359304 | tf_op jit(solution)/shard_map/ppermute | solution.py:35
  191.2 6.7 %collective-permute-start.7 = (bf16[2,4,2,16,384]{4,3,2,0,1:T(8,128)(2,1)S(1)}, bf16[2,4,2,16,384]{4,3,2,0,1:T(8,128)(2,1)S(1)}, u32[]{:S(2)}, u32[]{:S(2)}) collective-permute-start(bf16[2,4,2,16,384]{4,3,2,0,1:T(8,128)(2,1)S(1)} %bitcast.32), channel_id=1, source_target_pairs={{0,1},{1,0},{2,3},{3,2},{4,5},{5,4},{6,7},{7,6},{8,9},{9,8},{10,11... | collective-permute-start | bytes 589832 | tf_op jit(solution)/shard_map/ppermute | solution.py:35

commit v13 on v12

--- a/solution.py
+++ b/solution.py
@@ -186,9 +186,7 @@
 
 def join_kernel(dq_ref, own_ref, other_ref, out_ref):
     pairs = (own_ref[...] + other_ref[...]).astype(low)
-    rows = jnp.concatenate([dq_ref[...], pairs], axis=1)
-    for copy in range(out_ref.shape[0]):
-        out_ref[copy] = rows
+    out_ref[...] = jnp.concatenate([dq_ref[...], pairs], axis=1)
 
 
 def weight_kernel(x_ref, grad_ref, out_ref):
@@ -296,15 +294,15 @@
         compiler_params=vmem,
         name="attention_columns",
     )(both_pairs, *query_pieces, stats_all)
-    grad_copies = pl.pallas_call(
+    grad_rows = pl.pallas_call(
         join_kernel,
         in_specs=in_vmem(3),
         out_specs=in_vmem(1)[0],
-        out_shape=jax.ShapeDtypeStruct((4, row_count, width), low),
+        out_shape=jax.ShapeDtypeStruct((row_count, width), low),
         compiler_params=vmem,
         name="join_gradients",
     )(grad_query, own_part, swap(other_part, "core"))
-    grad_all = exchange(grad_copies, group_axes).reshape(group_rows, width)
+    grad_all = lax.all_gather(grad_rows, group_axes, axis=0, tiled=True)
 
     def weight_half(half, dtype):
         return pl.pallas_call(

time: 200 us -> 204 us (1.020)
  blocking collectives: 126 us -> 130 us
    all_gather x0 -> x1, blocking collectives: none -> 13 us  [on_device(): grad_all = lax.all_gather(grad_rows, group_axes, axis=0, tiled=True)]
    all_to_all x6 -> x5, blocking collectives: 103 us -> 93.6 us  [exchange(): return lax.all_to_all(blocks, axes, split_axis=0, concat_axis=0, tiled=True)]
where the time goes in v13:
time: 204 us; the launch traced here: 203 us
  blocking collectives  130 us (64%)
  starting transfers between devices  49.6 us (24%)
  Pallas kernels  10.6 us (5%)
  waiting for transfers between devices  6.17 us (3%)
  local copies, waits for them, and re-layouts  5.92 us (3%)
    all_to_all x5, blocking collectives, exchange(): return lax.all_to_all(blocks, axes, split_axis=0, concat_axis=0, tiled=True)  93.6 us
    ppermute x8, starting transfers between devices, swap(): return lax.ppermute(block, axis, ((0, 1), (1, 0)))  39.5 us
    all_gather x1, blocking collectives, on_device(): near = lax.all_gather(own_weight, 'y', axis=0, tiled=True)  23.3 us
    all_gather x1, blocking collectives, on_device(): grad_all = lax.all_gather(grad_rows, group_axes, axis=0, tiled=True)  13 us
    all_to_all x2, starting transfers between devices, exchange(): return lax.all_to_all(blocks, axes, split_axis=0, concat_axis=0, tiled=True)  10.2 us
    ppermute x8, waiting for transfers between devices, swap(): return lax.ppermute(block, axis, ((0, 1), (1, 0)))  6.16 us
    unnamed x20, local copies, waits for them, and re-layouts  5.1 us
  transfers between devices with their start and end apart: 10, of which 5 were waited for; matrix products, arithmetic and copies ran while one was open for 0% of the time, Pallas kernels for 2%

profile of v13, /device:TPU:1, one launch (start us, length us, event | category | flops | bytes accessed | tf_op | source)
XLA Modules:
  0.0 203.5 jit_solution(17639678146495587633)
XLA Ops:
  0.6 0.0 copy-start
  0.6 1.7 token_columns.1
  2.4 0.0 copy-start.1
  2.4 1.3 copy-done.1
  3.7 6.7 %all-to-all-start = ((bf16[4,128,2048]{2,1,0:T(8,128)(2,1)}), bf16[4,128,2048]{2,1,0:T(8,128)(2,1)S(1)}, u32[]{:S(2)}, u32[]{:S(2)}) async-start(bf16[4,128,2048]{2,1,0:T(8,128)(2,1)} %copy-done.1), calls=%async_computation | async-start | bytes 4194304 | tf_op jit(solution)/shard_map/all_to_all | solution.py:27
  10.4 0.0 copy-done
  10.4 23.3 %all_gather.6.weight_ref = bf16[1024,384]{1,0:T(8,128)(2,1)S(1)} all-gather(bf16[128,384]{1,0:T(8,128)(2,1)S(1)} %constant_dynamic-slice_fusion), channel_id=1, replica_groups=mesh['xh'=2,'y'=8,'zh'=4,'zl'=2,'xl'=2,'core'=2] {'y'}, dimensions={0}, use_global_device_ids=true | all-gather | bytes 884736 | tf_op jit(solution)/shard_map/all_gather | solution.py:210
  33.7 8.7 %collective-permute-start = (bf16[1024,384]{1,0:T(8,128)(2,1)S(1)}, bf16[1024,384]{1,0:T(8,128)(2,1)}, u32[]{:S(2)}, u32[]{:S(2)}) collective-permute-start(bf16[1024,384]{1,0:T(8,128)(2,1)S(1)} %all_gather.6.weight_ref), channel_id=1, source_target_pairs={{0,1},{1,0},{2,3},{3,2},{4,5},{5,4},{6,7},{7,6},{8,9},{9,8},{10,11... | collective-permute-start | bytes 2359304 | tf_op jit(solution)/shard_map/ppermute | solution.py:35
  42.4 0.0 all-to-all-done
  42.4 0.7 near_projection.1.sum_ref
  43.1 0.0 copy-start.9
  43.1 1.3 collective-permute-done.weight_ref
  44.4 1.9 far_projection.1
  46.3 12.6 %all_to_all.35.parts_ref = bf16[4,128,384]{2,1,0:T(8,128)(2,1)S(1)} all-to-all(bf16[4,128,384]{2,1,0:T(8,128)(2,1)S(1)} %bitcast.25), channel_id=1, replica_groups=mesh['xh'=2,'y'=8,'zh'=4,'zl'=2,'xl'=2,'core'=2] {'xh','zl'}, dimensions={0} | all-to-all | bytes 786432 | tf_op jit(solution)/shard_map/all_to_all | solution.py:27
  58.9 0.0 copy-done.9
  58.9 0.1 projection_sum.1
  59.0 0.0 copy-start.5
  59.0 0.0 copy-start.2
  59.1 22.0 %all_to_all.36 = bf16[8,128,256]{2,1,0:T(8,128)(2,1)S(1)} all-to-all(bf16[8,128,256]{2,1,0:T(8,128)(2,1)S(1)} %get-tuple-element.13), channel_id=1, replica_groups=mesh['xh'=2,'y'=8,'zh'=4,'zl'=2,'xl'=2,'core'=2] {'zh','zl'}, dimensions={0} | all-to-all | bytes 1048576 | tf_op jit(solution)/shard_map/all_to_all | solution.py:27
  81.0 0.0 copy-done.5
  81.0 2.1 %collective-permute-start.1 = (bf16[1024,256]{1,0:T(8,128)(2,1)S(1)}, bf16[1024,256]{1,0:T(8,128)(2,1)}, u32[]{:S(2)}, u32[]{:S(2)}) collective-permute-start(bf16[1024,256]{1,0:T(8,128)(2,1)S(1)} %bitcast.22), channel_id=1, source_target_pairs={{0,2},{2,0},{1,3},{3,1},{4,6},{6,4},{5,7},{7,5},{8,10},{10,8},{9,1... | collective-permute-start | bytes 1572872 | tf_op jit(solution)/shard_map/ppermute | solution.py:35
  83.2 0.0 copy-done.2
  83.2 3.5 %all-to-all-start.3 = ((bf16[8,128,256]{2,1,0:T(8,128)(2,1)}), bf16[8,128,256]{2,1,0:T(8,128)(2,1)S(1)}, u32[]{:S(2)}, u32[]{:S(2)}) async-start(bf16[8,128,256]{2,1,0:T(8,128)(2,1)} %copy-done.2), calls=%async_computation.3 | async-start | bytes 1048576 | tf_op jit(solution)/shard_map/all_to_all | solution.py:27
  86.7 6.2 %collective-permute-start.2 = (bf16[1024,256]{1,0:T(8,128)(2,1)S(1)}, bf16[1024,256]{1,0:T(8,128)(2,1)S(1)}, u32[]{:S(2)}, u32[]{:S(2)}) collective-permute-start(bf16[1024,256]{1,0:T(8,128)(2,1)S(1)} %bitcast.23), channel_id=1, source_target_pairs={{0,1},{1,0},{2,3},{3,2},{4,5},{5,4},{6,7},{7,6},{8,9},{9,8},{10,11... | collective-permute-start | bytes 1572872 | tf_op jit(solution)/shard_map/ppermute | solution.py:35
  92.9 0.0 collective-permute-done.1.kv1
  92.9 6.3 %collective-permute-start.3 = (bf16[1024,256]{1,0:T(8,128)(2,1)}, bf16[1024,256]{1,0:T(8,128)(2,1)S(1)}, u32[]{:S(2)}, u32[]{:S(2)}) collective-permute-start(bf16[1024,256]{1,0:T(8,128)(2,1)} %collective-permute-done.1.kv1), channel_id=1, source_target_pairs={{0,1},{1,0},{2,3},{3,2},{4,5},{5,4},{6,7},{7,6},{8,9},{9,8},{10,11... | collective-permute-start | bytes 1572872 | tf_op jit(solution)/shard_map/ppermute | solution.py:35
  99.3 0.0 collective-permute-done.2.kv2
  99.3 1.7 collective-permute-done.3.kv3
  101.0 0.0 copy-start.6
  101.0 0.8 copy-done.6
  101.8 3.2 %attention_rows.1 = (bf16[128,128]{1,0:T(8,128)(2,1)}, f32[16,2,128]{2,1,0:T(2,128)S(1)}, bf16[128,128]{1,0:T(8,128)(2,1)S(1)}, bf16[256,256]{1,0:T(8,128)(2,1)S(1)}) custom-call(bf16[128,256]{1,0:T(8,128)(2,1)S(1)} %copy-done.6, bf16[1024,256]{1,0:T(8,128)(2,1)S(1)} %bitcast.24, bf16[1024,256]{1,0:T(8,128)(2,1)} %collective-permute-done.1.kv1, ...), custom_call_target="tpu_custom_call" | custom-call | tf_op jit(solution)/shard_map/attention_rows/pallas_call | solution.py:271
  105.0 0.0 copy-start.3
  105.0 0.6 copy-done.3
  105.7 0.0 copy-start.7
  105.7 0.6 copy-done.7
  106.3 0.0 all-to-all-done.3
  106.3 2.1 %collective-permute-start.4 = (bf16[1024,256]{1,0:T(8,128)(2,1)S(1)}, bf16[1024,256]{1,0:T(8,128)(2,1)S(1)}, u32[]{:S(2)}, u32[]{:S(2)}) collective-permute-start(bf16[1024,256]{1,0:T(8,128)(2,1)S(1)} %bitcast.20), channel_id=1, source_target_pairs={{0,2},{2,0},{1,3},{3,1},{4,6},{6,4},{5,7},{7,5},{8,10},{10,8},{9,1... | collective-permute-start | bytes 1572872 | tf_op jit(solution)/shard_map/ppermute | solution.py:35
  108.4 13.0 %all_to_all.37.stats_ref = f32[16,2,128]{2,1,0:T(2,128)S(1)} all-to-all(f32[16,2,128]{2,1,0:T(2,128)S(1)} %get-tuple-element.18), channel_id=1, replica_groups=mesh['xh'=2,'y'=8,'zh'=4,'zl'=2,'xl'=2,'core'=2] {'zh','zl','xl'}, dimensions={0} | all-to-all | bytes 32768 | tf_op jit(solution)/shard_map/all_to_all | solution.py:27
  121.5 0.0 collective-permute-done.4.qc1
  121.5 0.0 copy-start.4
  121.5 0.9 copy-done.4
  122.4 1.5 attention_columns.1
  123.9 3.2 %collective-permute-start.5 = (f32[128,256]{1,0:T(8,128)S(1)}, f32[128,256]{1,0:T(8,128)S(1)}, u32[]{:S(2)}, u32[]{:S(2)}) collective-permute-start(f32[128,256]{1,0:T(8,128)S(1)} %get-tuple-element.21), channel_id=1, source_target_pairs={{0,1},{1,0},{2,3},{3,2},{4,5},{5,4},{6,7},{7,6},{8,9},{9,8},{10,11... | collective-permute-start | bytes 393224 | tf_op jit(solution)/shard_map/ppermute | solution.py:35
  127.0 1.0 collective-permute-done.5.other_ref
  128.0 0.0 copy-start.8
  128.0 0.8 copy-done.8
  128.8 13.0 %all_gather.7.grad_ref = bf16[512,384]{1,0:T(8,128)(2,1)S(1)} all-gather(bf16[128,384]{1,0:T(8,128)(2,1)S(1)} %join_gradients.1), channel_id=1, replica_groups=mesh['xh'=2,'y'=8,'zh'=4,'zl'=2,'xl'=2,'core'=2] {'xh','zl'}, dimensions={0}, use_global_device_ids=true | all-gather | bytes 491520 | tf_op jit(solution)/shard_map/all_gather | solution.py:305
  141.7 0.7 weight_gradient.3
  142.5 5.2 %collective-permute-start.6 = (bf16[1024,384]{1,0:T(8,128)(2,1)S(1)}, bf16[1024,384]{1,0:T(8,128)(2,1)S(1)}, u32[]{:S(2)}, u32[]{:S(2)}) collective-permute-start(bf16[1024,384]{1,0:T(8,128)(2,1)S(1)} %weight_gradient.3), channel_id=1, source_target_pairs={{0,1},{1,0},{2,3},{3,2},{4,5},{5,4},{6,7},{7,6},{8,9},{9,8},{10,11... | collective-permute-start | bytes 2359304 | tf_op jit(solution)/shard_map/ppermute | solution.py:35
  147.7 0.7 weight_gradient.2
  148.4 1.1 collective-permute-done.6
  149.6 0.2 add_convert_fusion
  149.7 32.2 %all_to_all.38 = bf16[64,16,384]{2,1,0:T(8,128)(2,1)S(1)} all-to-all(bf16[64,16,384]{2,1,0:T(8,128)(2,1)S(1)} %bitcast.27), channel_id=1, replica_groups=mesh['xh'=2,'y'=8,'zh'=4,'zl'=2,'xl'=2,'core'=2] {'y','zh','xl'}, dimensions={0} | all-to-all | bytes 1572864 | tf_op jit(solution)/shard_map/all_to_all | solution.py:27
  182.0 0.1 reduce_sum.12
  182.1 13.8 %all_to_all.39 = bf16[16,16,384]{2,1,0:T(8,128)(2,1)S(1)} all-to-all(bf16[16,16,384]{2,1,0:T(8,128)(2,1)S(1)} %broadcast_in_dim.10), channel_id=1, replica_groups=mesh['xh'=2,'y'=8,'zh'=4,'zl'=2,'xl'=2,'core'=2] {'zh','zl','xl'}, dimensions={0} | all-to-all | bytes 393216 | tf_op jit(solution)/shard_map/all_to_all | solution.py:27
  195.9 5.6 %collective-permute-start.7 = (bf16[2,4,2,16,384]{4,3,2,0,1:T(8,128)(2,1)S(1)}, bf16[2,4,2,16,384]{4,3,2,0,1:T(8,128)(2,1)S(1)}, u32[]{:S(2)}, u32[]{:S(2)}) collective-permute-start(bf16[2,4,2,16,384]{4,3,2,0,1:T(8,128)(2,1)S(1)} %bitcast.29), channel_id=1, source_target_pairs={{0,1},{1,0},{2,3},{3,2},{4,5},{5,4},{6,7},{7,6},{8,9},{9,8},{10,11... | collective-permute-start | bytes 589832 | tf_op jit(solution)/shard_map/ppermute | solution.py:35
  201.6 1.0 collective-permute-done.7
  202.7 0.8 copy.6
  (5 shorter events, 0.1 us)
Async XLA Ops:
  0.6 9.7 %copy-start = (bf16[512,384]{1,0:T(8,128)(2,1)S(1)}, bf16[512,384]{1,0:T(8,128)(2,1)}, u32[]{:S(2)}) copy-start(bf16[512,384]{1,0:T(8,128)(2,1)} %param.4) | copy-start | bytes 1179652
  2.4 1.3 copy-start.1
  3.7 38.7 %all-to-all-start = ((bf16[4,128,2048]{2,1,0:T(8,128)(2,1)}), bf16[4,128,2048]{2,1,0:T(8,128)(2,1)S(1)}, u32[]{:S(2)}, u32[]{:S(2)}) async-start(bf16[4,128,2048]{2,1,0:T(8,128)(2,1)} %copy-done.1), calls=%async_computation | async-start | bytes 4194304 | tf_op jit(solution)/shard_map/all_to_all | solution.py:27
  33.7 10.7 %collective-permute-start = (bf16[1024,384]{1,0:T(8,128)(2,1)S(1)}, bf16[1024,384]{1,0:T(8,128)(2,1)}, u32[]{:S(2)}, u32[]{:S(2)}) collective-permute-start(bf16[1024,384]{1,0:T(8,128)(2,1)S(1)} %all_gather.6.weight_ref), channel_id=1, source_target_pairs={{0,1},{1,0},{2,3},{3,2},{4,5},{5,4},{6,7},{7,6},{8,9},{9,8},{10,11... | collective-permute-start | bytes 2359304 | tf_op jit(solution)/shard_map/ppermute | solution.py:35
  43.1 15.8 %copy-start.9 = (bf16[1,128,128]{2,1,0:T(8,128)(2,1)S(1)}, bf16[1,128,128]{2,1,0:T(8,128)(2,1)}, u32[]{:S(2)}) copy-start(bf16[1,128,128]{2,1,0:T(8,128)(2,1)} %param.5) | copy-start | bytes 98308
  59.0 22.0 %copy-start.5 = (bf16[128,256]{1,0:T(8,128)(2,1)}, bf16[128,256]{1,0:T(8,128)(2,1)S(1)}, u32[]{:S(2)}) copy-start(bf16[128,256]{1,0:T(8,128)(2,1)S(1)} %get-tuple-element.12.rows_ref) | copy-start | bytes 196612
  59.0 24.1 %copy-start.2 = (bf16[8,128,256]{2,1,0:T(8,128)(2,1)}, bf16[8,128,256]{2,1,0:T(8,128)(2,1)S(1)}, u32[]{:S(2)}) copy-start(bf16[8,128,256]{2,1,0:T(8,128)(2,1)S(1)} %get-tuple-element.17) | copy-start | bytes 1572868
  81.0 11.9 %collective-permute-start.1 = (bf16[1024,256]{1,0:T(8,128)(2,1)S(1)}, bf16[1024,256]{1,0:T(8,128)(2,1)}, u32[]{:S(2)}, u32[]{:S(2)}) collective-permute-start(bf16[1024,256]{1,0:T(8,128)(2,1)S(1)} %bitcast.22), channel_id=1, source_target_pairs={{0,2},{2,0},{1,3},{3,1},{4,6},{6,4},{5,7},{7,5},{8,10},{10,8},{9,1... | collective-permute-start | bytes 1572872 | tf_op jit(solution)/shard_map/ppermute | solution.py:35
  83.2 23.1 %all-to-all-start.3 = ((bf16[8,128,256]{2,1,0:T(8,128)(2,1)}), bf16[8,128,256]{2,1,0:T(8,128)(2,1)S(1)}, u32[]{:S(2)}, u32[]{:S(2)}) async-start(bf16[8,128,256]{2,1,0:T(8,128)(2,1)} %copy-done.2), calls=%async_computation.3 | async-start | bytes 1048576 | tf_op jit(solution)/shard_map/all_to_all | solution.py:27
  86.7 12.6 %collective-permute-start.2 = (bf16[1024,256]{1,0:T(8,128)(2,1)S(1)}, bf16[1024,256]{1,0:T(8,128)(2,1)S(1)}, u32[]{:S(2)}, u32[]{:S(2)}) collective-permute-start(bf16[1024,256]{1,0:T(8,128)(2,1)S(1)} %bitcast.23), channel_id=1, source_target_pairs={{0,1},{1,0},{2,3},{3,2},{4,5},{5,4},{6,7},{7,6},{8,9},{9,8},{10,11... | collective-permute-start | bytes 1572872 | tf_op jit(solution)/shard_map/ppermute | solution.py:35
  92.9 8.1 %collective-permute-start.3 = (bf16[1024,256]{1,0:T(8,128)(2,1)}, bf16[1024,256]{1,0:T(8,128)(2,1)S(1)}, u32[]{:S(2)}, u32[]{:S(2)}) collective-permute-start(bf16[1024,256]{1,0:T(8,128)(2,1)} %collective-permute-done.1.kv1), channel_id=1, source_target_pairs={{0,1},{1,0},{2,3},{3,2},{4,5},{5,4},{6,7},{7,6},{8,9},{9,8},{10,11... | collective-permute-start | bytes 1572872 | tf_op jit(solution)/shard_map/ppermute | solution.py:35
  101.0 0.8 copy-start.6
  105.0 0.7 copy-start.3
  105.7 0.6 copy-start.7
  106.3 15.2 %collective-permute-start.4 = (bf16[1024,256]{1,0:T(8,128)(2,1)S(1)}, bf16[1024,256]{1,0:T(8,128)(2,1)S(1)}, u32[]{:S(2)}, u32[]{:S(2)}) collective-permute-start(bf16[1024,256]{1,0:T(8,128)(2,1)S(1)} %bitcast.20), channel_id=1, source_target_pairs={{0,2},{2,0},{1,3},{3,1},{4,6},{6,4},{5,7},{7,5},{8,10},{10,8},{9,1... | collective-permute-start | bytes 1572872 | tf_op jit(solution)/shard_map/ppermute | solution.py:35
  121.5 0.9 copy-start.4
  123.9 4.1 %collective-permute-start.5 = (f32[128,256]{1,0:T(8,128)S(1)}, f32[128,256]{1,0:T(8,128)S(1)}, u32[]{:S(2)}, u32[]{:S(2)}) collective-permute-start(f32[128,256]{1,0:T(8,128)S(1)} %get-tuple-element.21), channel_id=1, source_target_pairs={{0,1},{1,0},{2,3},{3,2},{4,5},{5,4},{6,7},{7,6},{8,9},{9,8},{10,11... | collective-permute-start | bytes 393224 | tf_op jit(solution)/shard_map/ppermute | solution.py:35
  128.0 0.8 copy-start.8
  142.5 7.1 %collective-permute-start.6 = (bf16[1024,384]{1,0:T(8,128)(2,1)S(1)}, bf16[1024,384]{1,0:T(8,128)(2,1)S(1)}, u32[]{:S(2)}, u32[]{:S(2)}) collective-permute-start(bf16[1024,384]{1,0:T(8,128)(2,1)S(1)} %weight_gradient.3), channel_id=1, source_target_pairs={{0,1},{1,0},{2,3},{3,2},{4,5},{5,4},{6,7},{7,6},{8,9},{9,8},{10,11... | collective-permute-start | bytes 2359304 | tf_op jit(solution)/shard_map/ppermute | solution.py:35
  195.9 6.7 %collective-permute-start.7 = (bf16[2,4,2,16,384]{4,3,2,0,1:T(8,128)(2,1)S(1)}, bf16[2,4,2,16,384]{4,3,2,0,1:T(8,128)(2,1)S(1)}, u32[]{:S(2)}, u32[]{:S(2)}) collective-permute-start(bf16[2,4,2,16,384]{4,3,2,0,1:T(8,128)(2,1)S(1)} %bitcast.29), channel_id=1, source_target_pairs={{0,1},{1,0},{2,3},{3,2},{4,5},{5,4},{6,7},{7,6},{8,9},{9,8},{10,11... | collective-permute-start | bytes 589832 | tf_op jit(solution)/shard_map/ppermute | solution.py:35
